TPU v7x, 32 devices: a whole 2x2x4 slice. The times are simulated.
32 devices in a mesh: dp: 4 (over z), seq: 8 (over y, x, core).
Axes of the slice: x: 2, y: 2, z: 4, core: 2. Of those that a mesh axis runs over, the one named last changes fastest.
Arguments:
- patches: bfloat16 [12, 16, 64, 1152], P('dp', 'seq'), may hold values from -6 to 6
- valid: int32 [12, 2], P('dp'), may hold values from 1 to 64, as said below
- labels: int32 [12], P('dp'), may hold values from 0 to 999
- partners: int32 [12], P('dp'), may hold values from 0 to 11
- mix: float32 [12], P('dp'), may hold values from 0.5 to 1
- embed_w: float32 [1152, 320], P('dp'), may hold values from -0.1875 to 0.1875
- in_proj: float32 [6, 320, 2560], P(None, 'dp'), may hold values from -0.3125 to 0.3125
- down_proj: float32 [6, 2, 1280, 320], P(None, None, 'dp'), may hold values from -0.15625 to 0.15625
- dw_kernel: float32 [6, 9, 1280], P(None, None, 'dp'), may hold values from -2 to 2
- head_w: float32 [320, 1000], P('dp'), may hold values from -0.3125 to 0.3125
- norm_gain: float32 [20, 320], P(None, 'dp'), may hold values from 0.5 to 1.5
- norm_bias: float32 [20, 320], P(None, 'dp'), may hold values from -1.5 to 1.5
- m_embed: float32 [1152, 320], P('dp'), may hold values from -5.340576e-05 to 5.340576e-05
- m_proj: float32 [6, 320, 2560], P(None, 'dp'), may hold values from -5.340576e-05 to 5.340576e-05
- m_down: float32 [6, 2, 1280, 320], P(None, None, 'dp'), may hold values from -5.340576e-05 to 5.340576e-05
- m_taps: float32 [6, 9, 1280], P(None, None, 'dp'), may hold values from -5.340576e-05 to 5.340576e-05
- m_head: float32 [320, 1000], P('dp'), may hold values from -5.340576e-05 to 5.340576e-05
- m_gain: float32 [20, 320], P(None, 'dp'), may hold values from -5.340576e-05 to 5.340576e-05
- m_bias: float32 [20, 320], P(None, 'dp'), may hold values from -5.340576e-05 to 5.340576e-05
- v_embed: float32 [1152, 320], P('dp'), may hold values from 9.433108e-13 to 3.773243e-12
- v_proj: float32 [6, 320, 2560], P(None, 'dp'), may hold values from 9.433108e-13 to 3.773243e-12
- v_down: float32 [6, 2, 1280, 320], P(None, None, 'dp'), may hold values from 9.433108e-13 to 3.773243e-12
- v_taps: float32 [6, 9, 1280], P(None, None, 'dp'), may hold values from 9.433108e-13 to 3.773243e-12
- v_head: float32 [320, 1000], P('dp'), may hold values from 9.433108e-13 to 3.773243e-12
- v_gain: float32 [20, 320], P(None, 'dp'), may hold values from 9.433108e-13 to 3.773243e-12
- v_bias: float32 [20, 320], P(None, 'dp'), may hold values from 9.433108e-13 to 3.773243e-12
Outputs:
- loss: float32 [], replicated
- grad_norm: float32 [], replicated
- stats: float32 [2, 22], replicated
- trust: float32 [22], replicated
- new_embed: float32 [1152, 320], P('dp')
- new_proj: float32 [6, 320, 2560], P(None, 'dp')
- new_down: float32 [6, 2, 1280, 320], P(None, None, 'dp')
- new_taps: float32 [6, 9, 1280], P(None, None, 'dp')
- new_head: float32 [320, 1000], P('dp')
- new_gain: float32 [20, 320], P(None, 'dp')
- new_bias: float32 [20, 320], P(None, 'dp')
- m_embed_out: float32 [1152, 320], P('dp')
- m_proj_out: float32 [6, 320, 2560], P(None, 'dp')
- m_down_out: float32 [6, 2, 1280, 320], P(None, None, 'dp')
- m_taps_out: float32 [6, 9, 1280], P(None, None, 'dp')
- m_head_out: float32 [320, 1000], P('dp')
- m_gain_out: float32 [20, 320], P(None, 'dp')
- m_bias_out: float32 [20, 320], P(None, 'dp')
- v_embed_out: float32 [1152, 320], P('dp')
- v_proj_out: float32 [6, 320, 2560], P(None, 'dp')
- v_down_out: float32 [6, 2, 1280, 320], P(None, None, 'dp')
- v_taps_out: float32 [6, 9, 1280], P(None, None, 'dp')
- v_head_out: float32 [320, 1000], P('dp')
- v_gain_out: float32 [20, 320], P(None, 'dp')
- v_bias_out: float32 [20, 320], P(None, 'dp')
Inputs may be any that keep to these rules, and one draw needn't show every extreme that they name: Each image's valid rows are at least 8 and valid columns at least 32; the first image fills the whole grid.
All inputs are finite; a program needn't handle non-finite values.
Results may differ from a plain program's by a relative error of at most 0.006.
The roundings to bfloat16 on the way count: a program that leaves them out, or rounds other values in their place, can miss the bound.
Values may be sent and summed in bfloat16 or wider, within the bound.
No kernel may reach another device: no remote copies, remote signals or barrier semaphores. Data moves between devices by JAX's collectives and lax.ppermute only.
A program may use at most 512 MiB of HBM per device.

v0:
```python
import jax
import jax.numpy as jnp
from jax import lax
from jax.sharding import PartitionSpec as P

D = 320
HEADS = 5
HD = 64
FF = 1280
CLS = 1000
W = 64
LAYERS = 6
MICRO = 3
STEP = 5


norm_eps = 1e-06
scale_qk = 0.125
big_neg = -1e30
beta_one = 0.9
beta_two = 0.999
lamb_eps = 1e-06
decay_rate = 0.01
learn_rate = 0.3
clip_limit = 0.1
precise = lax.Precision.HIGHEST


def extended(block, sides, width):
    for axis, dim in sides:
        count = lax.axis_size(axis)
        forward = [(i, i + 1) for i in range(count - 1)]
        backward = [(target, source) for source, target in forward]
        low = lax.ppermute(
            lax.slice_in_dim(block, block.shape[dim] - width, None, axis=dim), axis, forward
        )
        high = lax.ppermute(lax.slice_in_dim(block, 0, width, axis=dim), axis, backward)
        block = jnp.concatenate([low, block, high], axis=dim)
    return block


def to_bf(v):
    return v.astype(jnp.bfloat16)


def matmul(a, b):
    return jnp.dot(a, b, preferred_element_type=jnp.float32)


def times_t(a, b, precision=None):
    return lax.dot_general(
        a,
        b,
        (((a.ndim - 1,), (1,)), ((), ())),
        precision=precision,
        preferred_element_type=jnp.float32,
    )


def contract(a, b, precision=None):
    flat_a = a.reshape(-1, a.shape[-1])
    flat_b = b.reshape(-1, b.shape[-1])
    return lax.dot_general(
        flat_a,
        flat_b,
        (((0,), (0,)), ((), ())),
        precision=precision,
        preferred_element_type=jnp.float32,
    )


def layer_norm(v, gain, bias):
    center = v - jnp.mean(v, -1, keepdims=True)
    spread = jnp.mean(center * center, -1, keepdims=True)
    return center * lax.rsqrt(spread + norm_eps) * gain + bias


def norm_back(v, gain, bias, grad):
    _, pull = jax.vjp(layer_norm, v, gain, bias)
    return pull(grad)


def widen(v):
    return jnp.pad(v, ((0, 0), (0, 0), (1, 1), (0, 0)))


def taps_apply(padded, taps, rows, flip):
    total = jnp.zeros((padded.shape[0], rows, W, padded.shape[3]), jnp.float32)
    for i in range(3):
        for j in range(3):
            top = 2 - i if flip else i
            left = 2 - j if flip else j
            total = (
                total
                + taps[3 * i + j].astype(jnp.float32) * padded[:, top : top + rows, left : left + W]
            )
    return total


def gelu_exact(v):
    return jax.nn.gelu(v, approximate=False)


def scores(q16, kv_all, key_ok):
    batch, tok, _ = q16.shape
    qh = q16.reshape(batch, tok, HEADS, HD)
    kh = kv_all[:, :, :D].reshape(batch, -1, HEADS, HD)
    s = jnp.einsum("bqhd,bkhd->bhqk", qh, kh, preferred_element_type=jnp.float32) * scale_qk
    return jnp.where(key_ok[:, None, None, :], s, big_neg)


def layer_forward(x, wts, key_ok):
    proj, downs, taps, gains, biases = wts
    batch, tok, _ = x.shape
    rows = tok // W
    a16 = to_bf(layer_norm(x, gains[0], biases[0]))
    q16 = to_bf(matmul(a16, proj[:, :D]))
    grid = (
        a16.reshape(batch, rows // 2, 2, W // 2, 2, D)
        .transpose(0, 1, 3, 2, 4, 5)
        .reshape(batch, -1, 4 * D)
    )
    reduced = matmul(grid, downs[0])
    rn16 = to_bf(layer_norm(reduced, gains[1], biases[1]))
    kv16 = to_bf(matmul(rn16, proj[:, D : 3 * D]))
    kv_all = lax.all_gather(kv16, "seq", axis=1, tiled=True)
    s = scores(q16, kv_all, key_ok)
    top = jnp.max(s, -1, keepdims=True)
    expo = jnp.exp(s - top)
    total = jnp.sum(expo, -1, keepdims=True)
    lse = top + jnp.log(total)
    vh = kv_all[:, :, D:].reshape(batch, -1, HEADS, HD)
    att = jnp.einsum("bhqk,bkhd->bqhd", to_bf(expo / total), vh, preferred_element_type=jnp.float32)
    o16 = to_bf(att.reshape(batch, tok, D))
    x2 = x + matmul(o16, proj[:, 3 * D : 4 * D])
    b16 = to_bf(layer_norm(x2, gains[2], biases[2]))
    h16 = to_bf(matmul(b16, proj[:, 4 * D :])).reshape(batch, rows, W, FF)
    hpad = widen(extended(h16, (("seq", 1),), 1))
    z = taps_apply(hpad, taps, rows, False)
    g16 = to_bf(gelu_exact(z)).reshape(batch, tok, FF)
    x3 = x2 + matmul(g16, downs[1])
    return (x3, (x, a16, q16, grid, reduced, rn16, kv_all, lse, o16, x2, b16, hpad, z, g16))


def layer_backward(cache, dx3, wts, key_ok):
    x, a16, q16, grid, reduced, rn_keep, kv_all, lse, o16, x2, b16, hpad, z, g16 = cache
    proj, downs, taps, gains, biases = wts
    batch, tok, _ = x.shape
    rows = tok // W
    dy16 = to_bf(dx3)
    d_fc2 = contract(g16, dy16)
    dg16 = to_bf(times_t(dy16, downs[1]))
    _, gelu_pull = jax.vjp(gelu_exact, z)
    dz16 = to_bf(gelu_pull(dg16.reshape(z.shape).astype(jnp.float32))[0])
    dpad = widen(extended(dz16, (("seq", 1),), 1))
    dh16 = to_bf(taps_apply(dpad, taps, rows, True)).reshape(batch, tok, FF)
    d_taps = jnp.stack(
        [
            jnp.sum(hpad[:, i : i + rows, j : j + W] * dz16.astype(jnp.float32), (0, 1, 2))
            for i in range(3)
            for j in range(3)
        ]
    )
    d_fc1 = contract(b16, dh16)
    dln2, dgain2, dbias2 = norm_back(x2, gains[2], biases[2], times_t(dh16, proj[:, 4 * D :]))
    dx2 = dx3 + dln2
    dy16 = to_bf(dx2)
    d_out = contract(o16, dy16)
    do16 = to_bf(times_t(dy16, proj[:, 3 * D : 4 * D])).reshape(batch, tok, HEADS, HD)
    prob = jnp.exp(scores(q16, kv_all, key_ok) - lse)
    kh = kv_all[:, :, :D].reshape(batch, -1, HEADS, HD)
    vh = kv_all[:, :, D:].reshape(batch, -1, HEADS, HD)
    dprob = jnp.einsum("bqhd,bkhd->bhqk", do16, vh, preferred_element_type=jnp.float32)
    dv = jnp.einsum("bhqk,bqhd->bkhd", to_bf(prob), do16, preferred_element_type=jnp.float32)
    ds16 = to_bf(prob * (dprob - jnp.sum(prob * dprob, -1, keepdims=True)))
    dq = jnp.einsum("bhqk,bkhd->bqhd", ds16, kh, preferred_element_type=jnp.float32) * scale_qk
    dq16 = to_bf(dq.reshape(batch, tok, D))
    qh = q16.reshape(batch, tok, HEADS, HD)
    dk = jnp.einsum("bhqk,bqhd->bkhd", ds16, qh, preferred_element_type=jnp.float32) * scale_qk
    dkv = jnp.concatenate([dk.reshape(batch, -1, D), dv.reshape(batch, -1, D)], -1)
    w_kv = proj[:, D : 3 * D].astype(jnp.float32)
    dkv_own = lax.psum_scatter(
        dkv.astype(jnp.bfloat16), "seq", scatter_dimension=1, tiled=True
    ).astype(jnp.float32)
    d_kv = contract(rn_keep.astype(jnp.float32), dkv_own, precise)
    drn = times_t(dkv_own, w_kv, precise)
    d_q = contract(a16, dq16)
    dred, dgain1, dbias1 = norm_back(reduced, gains[1], biases[1], drn)
    dred16 = to_bf(dred)
    d_sr = contract(grid, dred16)
    dgrid = times_t(dred16, downs[0])
    dgrid = (
        dgrid.reshape(batch, rows // 2, W // 2, 2, 2, D)
        .transpose(0, 1, 3, 2, 4, 5)
        .reshape(batch, tok, D)
    )
    da = times_t(dq16, proj[:, :D]) + dgrid
    dln1, dgain0, dbias0 = norm_back(x, gains[0], biases[0], da)
    d_proj = jnp.concatenate([d_q, d_kv, d_out, d_fc1], 1)
    d_down = jnp.stack([d_sr, d_fc2])
    return (
        dx2 + dln1,
        (
            d_proj,
            d_down,
            d_taps,
            jnp.stack([dgain0, dgain1, dgain2]),
            jnp.stack([dbias0, dbias1, dbias2]),
        ),
    )


def layer_weights(wts, gain32, bias32, layer):
    base = 1 + 3 * layer
    return (
        wts[1][layer],
        wts[2][layer],
        wts[3][layer],
        gain32[base : base + 3],
        bias32[base : base + 3],
    )


def group_sums(arrs):
    embed, proj, downs, taps, head, gains, biases = arrs
    first = jnp.stack([jnp.sum(embed), jnp.sum(head), jnp.sum(gains), jnp.sum(biases)])
    rest = [jnp.sum(a.reshape(a.shape[0], -1), 1) for a in (proj, downs, taps)]
    return jnp.concatenate([first] + rest)


def spread_ratio(ratio):
    return (
        ratio[0],
        ratio[4 : 4 + LAYERS].reshape(LAYERS, 1, 1),
        ratio[4 + LAYERS : 4 + 2 * LAYERS].reshape(LAYERS, 1, 1, 1),
        ratio[4 + 2 * LAYERS : 4 + 3 * LAYERS].reshape(LAYERS, 1, 1),
        ratio[1],
        ratio[2],
        ratio[3],
    )


def reduce_grads(grads):
    shards = (
        lax.psum_scatter(grads[0], "dp", scatter_dimension=0, tiled=True),
        lax.psum_scatter(grads[1], "dp", scatter_dimension=1, tiled=True),
        lax.psum_scatter(grads[2], "dp", scatter_dimension=2, tiled=True),
        lax.psum_scatter(grads[3], "dp", scatter_dimension=2, tiled=True),
        lax.psum_scatter(grads[4], "dp", scatter_dimension=0, tiled=True),
        lax.psum_scatter(grads[5], "dp", scatter_dimension=1, tiled=True),
        lax.psum_scatter(grads[6], "dp", scatter_dimension=1, tiled=True),
    )
    return lax.psum(
        (shards[0], shards[1], shards[2], shards[3], shards[4], shards[5], shards[6]), "seq"
    )


def per_device(
    patches,
    valid,
    labels,
    partners,
    mix,
    embed_w,
    in_proj,
    down_proj,
    dw_kernel,
    head_w,
    norm_gain,
    norm_bias,
    m_embed,
    m_proj,
    m_down,
    m_taps,
    m_head,
    m_gain,
    m_bias,
    v_embed,
    v_proj,
    v_down,
    v_taps,
    v_head,
    v_gain,
    v_bias,
):
    masters = (embed_w, in_proj, down_proj, dw_kernel, head_w, norm_gain, norm_bias)
    firsts = (m_embed, m_proj, m_down, m_taps, m_head, m_gain, m_bias)
    seconds = (v_embed, v_proj, v_down, v_taps, v_head, v_gain, v_bias)
    n_seq = lax.axis_size("seq")
    seq_pos = lax.axis_index("seq")
    img_dev, rows = (patches.shape[0], patches.shape[1])
    images = img_dev * lax.axis_size("dp")
    img_mb = img_dev // MICRO
    tok = rows * W
    keys = rows * n_seq * W // 4
    all_labels = lax.all_gather(labels, "dp", axis=0, tiled=True)
    slot = lax.broadcasted_iota(jnp.int32, (img_dev, images), 1)
    partner_labels = jnp.sum(jnp.where(slot == partners[:, None], all_labels[None, :], 0), 1)
    tid = lax.broadcasted_iota(jnp.int32, (1, tok), 1)
    tok_ok = ((seq_pos * rows + tid // W < valid[:, 0:1]) & (tid % W < valid[:, 1:2])).astype(
        jnp.float32
    )
    kid = lax.broadcasted_iota(jnp.int32, (1, keys), 1)
    key_ok = (2 * (kid // (W // 2)) < valid[:, 0:1]) & (2 * (kid % (W // 2)) < valid[:, 1:2])
    counts = (valid[:, 0] * valid[:, 1]).astype(jnp.float32)
    classes = lax.broadcasted_iota(jnp.int32, (1, CLS), 1)
    target = mix[:, None] * (classes == labels[:, None]).astype(jnp.float32) + (
        1.0 - mix[:, None]
    ) * (classes == partner_labels[:, None]).astype(jnp.float32)
    head_keep = (seq_pos == 0).astype(jnp.float32)
    loss_local = jnp.zeros((), jnp.float32)
    summed = None
    for micro in range(MICRO):
        wts = (
            lax.all_gather(to_bf(embed_w), "dp", axis=0, tiled=True),
            lax.all_gather(to_bf(in_proj), "dp", axis=1, tiled=True),
            lax.all_gather(to_bf(down_proj), "dp", axis=2, tiled=True),
            lax.all_gather(to_bf(dw_kernel), "dp", axis=2, tiled=True),
            lax.all_gather(to_bf(head_w), "dp", axis=0, tiled=True),
            lax.all_gather(to_bf(norm_gain), "dp", axis=1, tiled=True),
            lax.all_gather(to_bf(norm_bias), "dp", axis=1, tiled=True),
        )
        low_i, high_i = (micro * img_mb, (micro + 1) * img_mb)
        gain32 = wts[5].astype(jnp.float32)
        bias32 = wts[6].astype(jnp.float32)
        patch_mb = patches[low_i:high_i].reshape(img_mb, tok, -1)
        embedded = matmul(patch_mb, wts[0])
        x = layer_norm(embedded, gain32[0], bias32[0])
        caches = []
        for layer in range(LAYERS):
            x, cache = layer_forward(
                x, layer_weights(wts, gain32, bias32, layer), key_ok[low_i:high_i]
            )
            caches.append(cache)
        fin = layer_norm(x, gain32[-1], bias32[-1])
        okay = tok_ok[low_i:high_i]
        pooled_sum = lax.psum(jnp.sum(fin * okay[:, :, None], 1), "seq")
        count_mb = counts[low_i:high_i][:, None]
        pooled16 = to_bf(pooled_sum / count_mb)
        logits = matmul(pooled16, wts[4])
        shifted = logits - jnp.max(logits, -1, keepdims=True)
        logp = shifted - jnp.log(jnp.sum(jnp.exp(shifted), -1, keepdims=True))
        target_mb = target[low_i:high_i]
        loss_local = loss_local - jnp.sum(target_mb * logp) / images
        dlog16 = to_bf((jnp.exp(logp) - target_mb) / images)
        d_head = contract(pooled16, dlog16) * head_keep
        dpool = times_t(dlog16, wts[4]) / count_mb
        dx, dgain_f, dbias_f = norm_back(
            x, gain32[-1], bias32[-1], okay[:, :, None] * dpool[:, None, :]
        )
        layer_grads = [None] * LAYERS
        for layer in reversed(range(LAYERS)):
            dx, layer_grads[layer] = layer_backward(
                caches[layer], dx, layer_weights(wts, gain32, bias32, layer), key_ok[low_i:high_i]
            )
        dembed, dgain_e, dbias_e = norm_back(embedded, gain32[0], bias32[0], dx)
        d_embed = contract(patch_mb, to_bf(dembed))
        d_proj = jnp.stack([lg[0] for lg in layer_grads])
        d_down = jnp.stack([lg[1] for lg in layer_grads])
        d_taps = jnp.stack([lg[2] for lg in layer_grads])
        d_gain = jnp.concatenate(
            [dgain_e[None]] + [lg[3] for lg in layer_grads] + [dgain_f[None]], 0
        )
        d_bias = jnp.concatenate(
            [dbias_e[None]] + [lg[4] for lg in layer_grads] + [dbias_f[None]], 0
        )
        grads = (d_embed, d_proj, d_down, d_taps, d_head, d_gain, d_bias)
        summed = grads if summed is None else tuple((a + g for a, g in zip(summed, grads)))
    shards = reduce_grads(summed)
    loss = lax.psum(loss_local, "dp")
    gsq_local = sum((jnp.sum(g * g) for g in shards))
    wsq_local = group_sums(tuple((w * w for w in masters)))
    gsq, wsq = lax.psum((gsq_local, wsq_local), "dp")
    grad_norm = jnp.sqrt(gsq)
    factor = jnp.minimum(1.0, clip_limit / grad_norm)
    new_m, new_v, updates = ([], [], [])
    for w, g, m, v in zip(masters, shards, firsts, seconds):
        g = g * factor
        m2 = beta_one * m + (1.0 - beta_one) * g
        v2 = beta_two * v + (1.0 - beta_two) * g * g
        u = (
            m2 / (1.0 - beta_one**STEP) / (jnp.sqrt(v2 / (1.0 - beta_two**STEP)) + lamb_eps)
            + decay_rate * w
        )
        new_m.append(m2)
        new_v.append(v2)
        updates.append(u)
    usq = lax.psum(group_sums(tuple((u * u for u in updates))), "dp")
    wnorm = jnp.sqrt(wsq)
    unorm = jnp.sqrt(usq)
    ratio = wnorm / unorm
    spreads = spread_ratio(ratio)
    new_w = [w - learn_rate * r * u for w, r, u in zip(masters, spreads, updates)]
    stats = jnp.stack([wnorm, unorm])
    return (
        loss,
        grad_norm,
        stats,
        ratio,
        new_w[0],
        new_w[1],
        new_w[2],
        new_w[3],
        new_w[4],
        new_w[5],
        new_w[6],
        new_m[0],
        new_m[1],
        new_m[2],
        new_m[3],
        new_m[4],
        new_m[5],
        new_m[6],
        new_v[0],
        new_v[1],
        new_v[2],
        new_v[3],
        new_v[4],
        new_v[5],
        new_v[6],
    )


def solution(mesh):
    in_specs = (
        P("dp", "seq", None, None),
        P("dp", None),
        P("dp"),
        P("dp"),
        P("dp"),
        P("dp", None),
        P(None, "dp", None),
        P(None, None, "dp", None),
        P(None, None, "dp"),
        P("dp", None),
        P(None, "dp"),
        P(None, "dp"),
        P("dp", None),
        P(None, "dp", None),
        P(None, None, "dp", None),
        P(None, None, "dp"),
        P("dp", None),
        P(None, "dp"),
        P(None, "dp"),
        P("dp", None),
        P(None, "dp", None),
        P(None, None, "dp", None),
        P(None, None, "dp"),
        P("dp", None),
        P(None, "dp"),
        P(None, "dp"),
    )
    out_specs = (
        P(),
        P(),
        P(),
        P(),
        P("dp", None),
        P(None, "dp", None),
        P(None, None, "dp", None),
        P(None, None, "dp"),
        P("dp", None),
        P(None, "dp"),
        P(None, "dp"),
        P("dp", None),
        P(None, "dp", None),
        P(None, None, "dp", None),
        P(None, None, "dp"),
        P("dp", None),
        P(None, "dp"),
        P(None, "dp"),
        P("dp", None),
        P(None, "dp", None),
        P(None, None, "dp", None),
        P(None, None, "dp"),
        P("dp", None),
        P(None, "dp"),
        P(None, "dp"),
    )
    return jax.shard_map(
        per_device, mesh=mesh, in_specs=in_specs, out_specs=out_specs, check_vma=False
    )
```

profile of v0, /device:TPU:0, one launch (start us, length us, event | category | flops | bytes accessed | tf_op | source)
XLA Modules:
  0.0 4305.2 jit_solution(5869907032530714998)
XLA Ops:
  110.9 84.4 %all_gather.99 = bf16[6,9,1280]{1,0,2:T(8,128)(2,1)S(1)} all-gather(bf16[6,9,320]{1,0,2:T(8,128)(2,1)} %copy.796), channel_id=1, replica_groups=mesh['dp'=4,'seq'=8] {'dp'}, dimensions={2}, use_global_device_ids=true | all-gather | bytes 172800 | tf_op jit(solution)/shard_map/all_gather | solution.py:318
  230.6 70.0 %fusion.714 = (f32[1280]{0:T(1024)S(1)}, f32[1280]{0:T(1024)S(1)}, f32[1280]{0:T(1024)}, f32[1280]{0:T(1024)}, f32[1280]{0:T(1024)}, /*index=5*/f32[1280]{0:T(10...) fusion(bf16[6,9,1280]{1,0,2:T(8,128)(2,1)S(1)} %all_gather.99), kind=kLoop, calls=%fused_computation.1588 | loop fusion | flops 20480 | bytes 122880 | tf_op jit(solution)/shard_map/convert_element_type | solution.py:95
  300.7 86.9 %fusion.696 = (f32[1280]{0:T(1024)}, f32[1280]{0:T(1024)}, f32[1280]{0:T(1024)}, f32[1280]{0:T(1024)}, f32[1280]{0:T(1024)}, /*index=5*/f32[1280]{0:T(1024)}, f3...) fusion(bf16[6,9,1280]{1,0,2:T(8,128)(2,1)S(1)} %all_gather.99), kind=kLoop, calls=%fused_computation.1552 | loop fusion | flops 24320 | bytes 145920 | tf_op jit(solution)/shard_map/convert_element_type | solution.py:95
  387.6 86.7 %fusion.678 = (f32[1280]{0:T(1024)}, f32[1280]{0:T(1024)}, f32[1280]{0:T(1024)}, f32[1280]{0:T(1024)}, f32[1280]{0:T(1024)}, /*index=5*/f32[1280]{0:T(1024)}, f3...) fusion(bf16[6,9,1280]{1,0,2:T(8,128)(2,1)S(1)} %all_gather.99), kind=kLoop, calls=%fused_computation.1516 | loop fusion | flops 24320 | bytes 145920 | tf_op jit(solution)/shard_map/convert_element_type | solution.py:95
  805.1 54.8 %all-reduce.90.cloned.1.call-done = bf16[1,256,640]{2,0,1:T(2,128)(2,1)} async-done(((bf16[1,256,640]{2,0,1:T(2,128)(2,1)}), bf16[1,256,640]{2,0,1:T(2,128)(2,1)}) %all-reduce.90.cloned.1.call-update) | async-done | bytes 327696
  912.7 53.2 %all-reduce.92.cloned.1.call-done = bf16[1,256,640]{2,0,1:T(2,128)(2,1)} async-done(((bf16[1,256,640]{2,0,1:T(2,128)(2,1)}), bf16[1,256,640]{2,0,1:T(2,128)(2,1)}) %all-reduce.92.cloned.1.call-update) | async-done | bytes 327696
  1014.4 53.2 %all-reduce.94.cloned.1.call-done = bf16[1,256,640]{2,0,1:T(2,128)(2,1)} async-done(((bf16[1,256,640]{2,0,1:T(2,128)(2,1)}), bf16[1,256,640]{2,0,1:T(2,128)(2,1)}) %all-reduce.94.cloned.1.call-update) | async-done | bytes 327696
  1116.4 53.2 %all-reduce.96.cloned.1.call-done = bf16[1,256,640]{2,0,1:T(2,128)(2,1)} async-done(((bf16[1,256,640]{2,0,1:T(2,128)(2,1)}), bf16[1,256,640]{2,0,1:T(2,128)(2,1)}) %all-reduce.96.cloned.1.call-update) | async-done | bytes 327696
  1218.1 53.2 %all-reduce.98.cloned.1.call-done = bf16[1,256,640]{2,0,1:T(2,128)(2,1)} async-done(((bf16[1,256,640]{2,0,1:T(2,128)(2,1)}), bf16[1,256,640]{2,0,1:T(2,128)(2,1)}) %all-reduce.98.cloned.1.call-update) | async-done | bytes 327696
  1327.2 52.6 %all-reduce.100.cloned.1.call-done = bf16[1,256,640]{2,0,1:T(2,128)(2,1)} async-done(((bf16[1,256,640]{2,0,1:T(2,128)(2,1)}), bf16[1,256,640]{2,0,1:T(2,128)(2,1)}) %all-reduce.100.cloned.1.call-update) | async-done | bytes 327696
  1736.0 55.2 %all-reduce.102.cloned.1.call-done = bf16[1,256,640]{2,0,1:T(2,128)(2,1)} async-done(((bf16[1,256,640]{2,0,1:T(2,128)(2,1)}), bf16[1,256,640]{2,0,1:T(2,128)(2,1)}) %all-reduce.102.cloned.1.call-update) | async-done | bytes 327696
  1843.9 53.3 %all-reduce.104.cloned.1.call-done = bf16[1,256,640]{2,0,1:T(2,128)(2,1)} async-done(((bf16[1,256,640]{2,0,1:T(2,128)(2,1)}), bf16[1,256,640]{2,0,1:T(2,128)(2,1)}) %all-reduce.104.cloned.1.call-update) | async-done | bytes 327696
  1945.6 53.2 %all-reduce.106.cloned.1.call-done = bf16[1,256,640]{2,0,1:T(2,128)(2,1)} async-done(((bf16[1,256,640]{2,0,1:T(2,128)(2,1)}), bf16[1,256,640]{2,0,1:T(2,128)(2,1)}) %all-reduce.106.cloned.1.call-update) | async-done | bytes 327696
  2047.4 53.2 %all-reduce.108.cloned.1.call-done = bf16[1,256,640]{2,0,1:T(2,128)(2,1)} async-done(((bf16[1,256,640]{2,0,1:T(2,128)(2,1)}), bf16[1,256,640]{2,0,1:T(2,128)(2,1)}) %all-reduce.108.cloned.1.call-update) | async-done | bytes 327696
  2149.3 53.2 %all-reduce.110.cloned.1.call-done = bf16[1,256,640]{2,0,1:T(2,128)(2,1)} async-done(((bf16[1,256,640]{2,0,1:T(2,128)(2,1)}), bf16[1,256,640]{2,0,1:T(2,128)(2,1)}) %all-reduce.110.cloned.1.call-update) | async-done | bytes 327696
  2258.4 52.6 %all-reduce.112.cloned.1.call-done = bf16[1,256,640]{2,0,1:T(2,128)(2,1)} async-done(((bf16[1,256,640]{2,0,1:T(2,128)(2,1)}), bf16[1,256,640]{2,0,1:T(2,128)(2,1)}) %all-reduce.112.cloned.1.call-update) | async-done | bytes 327696
  2613.4 55.2 %all-reduce.78.cloned.1.call-done = bf16[1,256,640]{2,0,1:T(2,128)(2,1)} async-done(((bf16[1,256,640]{2,0,1:T(2,128)(2,1)}), bf16[1,256,640]{2,0,1:T(2,128)(2,1)}) %all-reduce.78.cloned.1.call-update) | async-done | bytes 327696
  2716.1 53.3 %all-reduce.80.cloned.1.call-done = bf16[1,256,640]{2,0,1:T(2,128)(2,1)} async-done(((bf16[1,256,640]{2,0,1:T(2,128)(2,1)}), bf16[1,256,640]{2,0,1:T(2,128)(2,1)}) %all-reduce.80.cloned.1.call-update) | async-done | bytes 327696
  2814.0 53.9 %all-reduce.82.cloned.1.call-done = bf16[1,256,640]{2,0,1:T(2,128)(2,1)} async-done(((bf16[1,256,640]{2,0,1:T(2,128)(2,1)}), bf16[1,256,640]{2,0,1:T(2,128)(2,1)}) %all-reduce.82.cloned.1.call-update) | async-done | bytes 327696
  2915.5 53.8 %all-reduce.84.cloned.1.call-done = bf16[1,256,640]{2,0,1:T(2,128)(2,1)} async-done(((bf16[1,256,640]{2,0,1:T(2,128)(2,1)}), bf16[1,256,640]{2,0,1:T(2,128)(2,1)}) %all-reduce.84.cloned.1.call-update) | async-done | bytes 327696
  3014.2 53.3 %all-reduce.86.cloned.1.call-done = bf16[1,256,640]{2,0,1:T(2,128)(2,1)} async-done(((bf16[1,256,640]{2,0,1:T(2,128)(2,1)}), bf16[1,256,640]{2,0,1:T(2,128)(2,1)}) %all-reduce.86.cloned.1.call-update) | async-done | bytes 327696
  3108.5 44.0 %all-reduce.88.cloned.1.call-done = bf16[1,256,640]{2,0,1:T(2,128)(2,1)} async-done(((bf16[1,256,640]{2,0,1:T(2,128)(2,1)}), bf16[1,256,640]{2,0,1:T(2,128)(2,1)}) %all-reduce.88.cloned.1.call-update) | async-done | bytes 327696
  3649.8 308.8 %reduce-scatter.18.cloned.1.call-done = f32[6,80,2560]{2,1,0:T(8,128)} async-done(((f32[6,320,2560]{2,1,0:T(8,128)}), f32[6,80,2560]{2,1,0:T(8,128)}) %reduce-scatter.18.cloned.1.call-update) | async-done | bytes 4915216 | tf_op jit(solution)/shard_map/reduce_scatter | solution.py:246
  4027.3 144.9 %all-reduce.114.cloned.1.call-done = (f32[288,320]{0,1:T(8,128)}, f32[6,80,2560]{2,1,0:T(8,128)}, f32[6,2,320,320]{2,3,1,0:T(8,128)}, f32[6,9,320]{2,1,0:T(8,128)}, f32[80,1000]{1,0:T(8,128)}) async-done(((f32[288,320]{0,1:T(8,128)}, f32[6,80,2560]{2,1,0:T(8,128)}, f32[6,2,320,320]{2,3,1,0:T(8,128)}, f32[6,9,320]{2,1,0:T(8,128)}, f32[80,1000]{1,0:T(8,128)}), (f32[288,320]{0,1:T(8,128)}, ...) | async-done | bytes 10588176 | tf_op jit(solution)/shard_map/psum | solution.py:253
  (5989 shorter events, 2513.1 us)
Async XLA Ops:
  7.2 467.1 %all-gather.23.cloned.1.call-start = ((), (), s32[]{:S(2)}) async-start(), calls=%async_computation.7 | async-start | bytes 14745600 | tf_op jit(solution)/shard_map/all_gather | solution.py:317
  14.7 462.8 %all-gather.25.cloned.1.call-start = ((), (), s32[]{:S(2)}) async-start(), calls=%async_computation.8 | async-start | bytes 12288000 | tf_op jit(solution)/shard_map/all_gather | solution.py:316
  19.0 840.9 %all-reduce.90.cloned.1.call-start = ((), (), s32[]{:S(2)}) async-start(), calls=%async_computation.22 | async-start | bytes 1310720
  803.7 162.2 %all-reduce.92.cloned.1.call-start = ((), (), s32[]{:S(2)}) async-start(), calls=%async_computation.23 | async-start | bytes 1310720
  911.3 156.3 %all-reduce.94.cloned.1.call-start = ((), (), s32[]{:S(2)}) async-start(), calls=%async_computation.24 | async-start | bytes 1310720
  1013.0 156.7 %all-reduce.96.cloned.1.call-start = ((), (), s32[]{:S(2)}) async-start(), calls=%async_computation.25 | async-start | bytes 1310720
  1216.7 163.1 %all-reduce.100.cloned.1.call-start = ((), (), s32[]{:S(2)}) async-start(), calls=%async_computation.27 | async-start | bytes 1310720
  1325.2 465.9 %all-reduce.102.cloned.1.call-start = ((), (), s32[]{:S(2)}) async-start(), calls=%async_computation.28 | async-start | bytes 1310720
  1734.6 162.6 %all-reduce.104.cloned.1.call-start = ((), (), s32[]{:S(2)}) async-start(), calls=%async_computation.29 | async-start | bytes 1310720
  1842.6 156.3 %all-reduce.106.cloned.1.call-start = ((), (), s32[]{:S(2)}) async-start(), calls=%async_computation.30 | async-start | bytes 1310720
  1944.2 156.4 %all-reduce.108.cloned.1.call-start = ((), (), s32[]{:S(2)}) async-start(), calls=%async_computation.31 | async-start | bytes 1310720
  2046.0 156.5 %all-reduce.110.cloned.1.call-start = ((), (), s32[]{:S(2)}) async-start(), calls=%async_computation.32 | async-start | bytes 1310720
  2147.9 163.2 %all-reduce.112.cloned.1.call-start = ((), (), s32[]{:S(2)}) async-start(), calls=%async_computation.33 | async-start | bytes 1310720
  2256.4 412.2 %all-reduce.78.cloned.1.call-start = ((), (), s32[]{:S(2)}) async-start(), calls=%async_computation.16 | async-start | bytes 1310720
  2611.4 158.0 %all-reduce.80.cloned.1.call-start = ((), (), s32[]{:S(2)}) async-start(), calls=%async_computation.17 | async-start | bytes 1310720
  2812.6 156.7 %all-reduce.84.cloned.1.call-start = ((), (), s32[]{:S(2)}) async-start(), calls=%async_computation.19 | async-start | bytes 1310720
  3095.6 528.3 %reduce-scatter.26.cloned.1.call-start = ((), (), s32[]{:S(2)}) async-start(), calls=%async_computation.13 | async-start | bytes 819200
  3106.6 519.7 %reduce-scatter.22.cloned.1.call-start = ((), (), s32[]{:S(2)}) async-start(), calls=%async_computation.11 | async-start | bytes 2211840
  3168.2 460.1 %reduce-scatter.24.cloned.1.call-start = ((), (), s32[]{:S(2)}) async-start(), calls=%async_computation.12 | async-start | bytes 24576000
  3270.3 379.5 %reduce-scatter.20.cloned.1.call-start = ((), (), s32[]{:S(2)}) async-start(), calls=%async_computation.10 | async-start | bytes 1638400 | tf_op jit(solution)/shard_map/reduce_scatter | solution.py:249
  3459.5 499.0 %reduce-scatter.18.cloned.1.call-start = ((), (), s32[]{:S(2)}) async-start(), calls=%async_computation.9 | async-start | bytes 24576000 | tf_op jit(solution)/shard_map/reduce_scatter | solution.py:246
  3564.6 417.9 %reduce-scatter.28.cloned.1.call-start = ((), (), s32[]{:S(2)}) async-start(), calls=%async_computation.14 | async-start | bytes 204800
  3622.8 379.2 %reduce-scatter.30.cloned.1.call-start = ((), (), s32[]{:S(2)}) async-start(), calls=%async_computation.15 | async-start | bytes 204800
  3623.9 548.3 %all-reduce.114.cloned.1.call-start = ((), (), s32[]{:S(2)}) async-start(), calls=%async_computation.34 | async-start | bytes 23560192 | tf_op jit(solution)/shard_map/psum | solution.py:253
  (2053 other events, 26879.3 us)
Sparse Core Ops, SparseCore 0:
  14.9 275.3 all-gather.22
  292.3 171.4 all-gather.24
  803.8 55.9 all-reduce.89
  911.4 54.4 all-reduce.91
  1013.1 54.4 all-reduce.93
  1115.2 54.4 all-reduce.95
  1216.8 54.4 all-reduce.97
  1325.3 54.4 all-reduce.99
  1734.7 56.3 all-reduce.101
  1842.7 54.4 all-reduce.103
  1944.3 54.4 all-reduce.105
  2046.1 54.4 all-reduce.107
  2148.0 54.4 all-reduce.109
  2256.5 54.4 all-reduce.111
  2611.5 57.0 all-reduce.77
  2714.2 55.0 all-reduce.79
  2812.8 55.1 all-reduce.81
  2914.2 55.0 all-reduce.83
  3013.0 54.4 all-reduce.85
  3095.7 56.7 all-reduce.87
  3179.2 37.2 reduce-scatter.21
  3270.4 325.9 reduce-scatter.23
  3633.5 325.0 reduce-scatter.17
  4008.7 163.3 all-reduce.113
  (4 shorter events, 91.5 us)
where the time goes:
time: 4340 us; the launch traced here: 4310 us
  waiting for transfers between devices  1430 us (33%)
  local copies, waits for them, and re-layouts  774 us (18%)
  other arithmetic  736 us (17%)
  matrix products  626 us (14%)
  blocking collectives  509 us (12%)
  starting transfers between devices  171 us (4%)
  between operations  56 us (1%)
    unnamed x51, waiting for transfers between devices  973 us
    unnamed x4035, local copies, waits for them, and re-layouts  317 us
    reduce_scatter x1, waiting for transfers between devices, reduce_grads(): lax.psum_scatter(grads[1], 'dp', scatter_dimension=1, tiled=True)  309 us
    convert_element_type x3, other arithmetic, taps_apply(): taps[3 * i + j].astype(jnp.float32)  244 us
    all_gather x18, blocking collectives, layer_forward(): kv_all = lax.all_gather(kv16, 'seq', axis=1, tiled=True)  225 us
    dot_general x111, matrix products, contract(): lax.dot_general(flat_a, flat_b, (((0,), (0,)), ((), ())), precision=preci...  214 us
    dot_general x111, matrix products, times_t(): lax.dot_general(a, b, (((a.ndim - 1,), (1,)), ((), ())), precision=precis...  152 us
    psum x1, waiting for transfers between devices, reduce_grads(): lax.psum((shards[0], shards[1], shards[2], shards[3], shards[4], shards[5...  145 us

commit v1 on v0

v1 whole, which is shorter than its diff:
```python
import functools

import jax
import jax.numpy as jnp
from jax import lax
from jax.experimental import pallas as pl
from jax.experimental.pallas import tpu as pltpu
from jax.sharding import PartitionSpec as P

D = 320
HEADS = 5
HD = 64
FF = 1280
CLS = 1000
W = 64
HALF = W // 2
LAYERS = 6
STEP = 5
LANES = 128


norm_eps = 1e-06
scale_qk = 0.125
big_neg = -1e30
beta_one = 0.9
beta_two = 0.999
lamb_eps = 1e-06
decay_rate = 0.01
learn_rate = 0.3
clip_limit = 0.1
root_half = 0.7071067811865476
root_two_pi = 0.3989422804014327
precise = lax.Precision.HIGHEST

f32 = jnp.float32
bf16 = jnp.bfloat16


def to_bf(v):
    return v.astype(bf16)


def dot(a, b):
    return jnp.dot(a, b, preferred_element_type=f32)


def dot_nt(a, b, precision=None):
    return lax.dot_general(
        a, b, (((1,), (1,)), ((), ())), precision=precision, preferred_element_type=f32
    )


def contract(a, b, precision=None):
    return lax.dot_general(
        a, b, (((0,), (0,)), ((), ())), precision=precision, preferred_element_type=f32
    )


def norm_parts(v):
    center = v - jnp.mean(v, -1, keepdims=True)
    spread = jnp.mean(center * center, -1, keepdims=True)
    scale = lax.rsqrt(spread + norm_eps)
    return center * scale, scale


def layer_norm(v, gain, bias):
    return norm_parts(v)[0] * gain + bias


def norm_back(v, gain, grad):
    unit, scale = norm_parts(v)
    dgain = jnp.sum(grad * unit, 0, keepdims=True)
    dbias = jnp.sum(grad, 0, keepdims=True)
    t = grad * gain
    dv = scale * (
        t - jnp.mean(t, -1, keepdims=True) - unit * jnp.mean(t * unit, -1, keepdims=True)
    )
    return dv, dgain, dbias


def run(body, outs, *args):
    vm = pl.BlockSpec(memory_space=pltpu.VMEM)
    return pl.pallas_call(
        body,
        out_shape=[jax.ShapeDtypeStruct(s, d) for s, d in outs],
        in_specs=[vm] * len(args),
        out_specs=[vm] * len(outs),
        compiler_params=pltpu.CompilerParams(vmem_limit_bytes=48 << 20),
    )(*args)


def cells_of(v):
    rows = v.shape[0] // W
    split = v.reshape(rows // 2, 2, 2, HALF, v.shape[1])
    return [split[:, k // 2, k % 2].reshape(-1, v.shape[1]) for k in range(4)]


def attention_inputs(x, gain, bias, wq, wsr, wkv, a_ref, q_ref, r_ref, rn_ref, kv_ref):
    a = to_bf(layer_norm(x, gain[0:1], bias[0:1]))
    a_ref[...] = a
    q_ref[...] = to_bf(dot(a, wq[...]))
    total = None
    for k, cell in enumerate(cells_of(a)):
        part = dot(cell, wsr[k * D : (k + 1) * D, :])
        total = part if total is None else total + part
    r_ref[...] = total
    rn = to_bf(layer_norm(total, gain[1:2], bias[1:2]))
    rn_ref[...] = rn
    kv_ref[...] = to_bf(dot(rn, wkv[...]))


def first_body(e_ref, ln_ref, gain, bias, wq, wsr, wkv, x_ref, *outs):
    x = layer_norm(e_ref[...], ln_ref[0:1], ln_ref[1:2])
    x_ref[...] = x
    attention_inputs(x, gain, bias, wq, wsr, wkv, *outs)


def middle_body(q_ref, kv_ref, ok_ref, x_ref, gain, bias, wo, w1, o_ref, lse_ref, x2_ref, b_ref, h_ref):
    q = q_ref[...] * jnp.asarray(scale_qk, bf16)
    keys = kv_ref.shape[0]
    kv = kv_ref[...]
    shut = jnp.broadcast_to(ok_ref[...], (keys, q.shape[0]))
    q_t = q.T
    v_t = kv[:, D:].T
    parts = []
    for head in range(HEADS):
        low, high = head * HD, (head + 1) * HD
        s = dot(kv[:, low:high], q_t[low:high, :]) + shut
        top = jnp.max(s, 0, keepdims=True)
        expo = jnp.exp(s - top)
        total = jnp.sum(expo, 0, keepdims=True)
        lse_ref[head : head + 1, :] = top + jnp.log(total)
        p = to_bf(expo * (1.0 / total))
        parts.append(dot(v_t[low:high, :], p))
    o = to_bf(jnp.concatenate(parts, 0).T)
    o_ref[...] = o
    x2 = x_ref[...] + dot(o, wo[...])
    x2_ref[...] = x2
    b = to_bf(layer_norm(x2, gain[2:3], bias[2:3]))
    b_ref[...] = b
    h_ref[...] = to_bf(dot(b, w1[...]))


def shift_down(v):
    index = lax.broadcasted_iota(jnp.int32, v.shape, 0)
    return jnp.where(index == 0, 0.0, pltpu.roll(v, 1, 0))


def shift_up(v):
    index = lax.broadcasted_iota(jnp.int32, v.shape, 0)
    return jnp.where(index == v.shape[0] - 1, 0.0, pltpu.roll(v, v.shape[0] - 1, 0))


def from_left(v):
    return jnp.concatenate([shift_down(v[HALF:]), v[:HALF]], 0)


def from_right(v):
    return jnp.concatenate([v[HALF:], shift_up(v[:HALF])], 0)


def row_of(main, low, high, i, rows, lanes):
    if i < 0:
        return low[:, lanes].astype(f32)
    if i >= rows:
        return high[:, lanes].astype(f32)
    return main[i * W : (i + 1) * W, lanes].astype(f32)


def conv_gelu(h_ref, low_ref, high_ref, taps_ref, g_ref, slope_ref):
    rows = h_ref.shape[0] // W

    def chunk(c, carry):
        lanes = pl.ds(pl.multiple_of(c * LANES, LANES), LANES)
        taps = [taps_ref[k : k + 1, lanes] for k in range(9)]
        near = [row_of(h_ref, low_ref, high_ref, i, rows, lanes) for i in (-1, 0)]
        for i in range(rows):
            near.append(row_of(h_ref, low_ref, high_ref, i + 1, rows, lanes))
            sums = [
                taps[j] * near[0] + taps[3 + j] * near[1] + taps[6 + j] * near[2] for j in range(3)
            ]
            z = sums[1] + from_left(sums[0]) + from_right(sums[2])
            phi = 0.5 + 0.5 * lax.erf(z * root_half)
            here = slice(i * W, (i + 1) * W)
            g_ref[here, lanes] = to_bf(z * phi)
            slope_ref[here, lanes] = phi + z * (jnp.exp(-0.5 * z * z) * root_two_pi)
            near = near[1:]
        return carry

    lax.fori_loop(0, FF // LANES, chunk, 0)


def last_body(h_ref, low_ref, high_ref, taps_ref, x2_ref, w2, ln_ref, ok_ref, g_ref, slope_ref, x_ref, sum_ref):
    conv_gelu(h_ref, low_ref, high_ref, taps_ref, g_ref, slope_ref)
    x = x2_ref[...] + dot(g_ref[...], w2[...])
    x_ref[...] = x
    fin = layer_norm(x, ln_ref[0:1], ln_ref[1:2])
    sum_ref[...] = jnp.sum(fin * ok_ref[...], 0, keepdims=True)


def join_body(
    h_ref, low_ref, high_ref, taps_ref, x2_ref, w2, gain, bias, wq, wsr, wkv, g_ref, slope_ref, x_ref, *outs
):
    conv_gelu(h_ref, low_ref, high_ref, taps_ref, g_ref, slope_ref)
    x = x2_ref[...] + dot(g_ref[...], w2[...])
    x_ref[...] = x
    attention_inputs(x, gain, bias, wq, wsr, wkv, *outs)


def gelu_back(dx, w2, slope_ref, dy_ref, dz_ref):
    dy = to_bf(dx)
    dy_ref[...] = dy
    dg = to_bf(dot_nt(dy, w2[...])).astype(f32)
    dz_ref[...] = to_bf(dg * slope_ref[...])


def head_body(
    images,
    pool_ref,
    count_ref,
    head_ref,
    target_ref,
    x_ref,
    ln_ref,
    ok_ref,
    w2,
    slope_ref,
    loss_ref,
    pooled_ref,
    dlog_ref,
    dln_ref,
    dx_ref,
    dy_ref,
    dz_ref,
):
    count = count_ref[...]
    pooled = to_bf(pool_ref[...] / count)
    pooled_ref[...] = pooled
    logits = dot(jnp.broadcast_to(pooled.astype(f32), (16, D)).astype(bf16), head_ref[...])[0:1]
    shifted = logits - jnp.max(logits, -1, keepdims=True)
    logp = shifted - jnp.log(jnp.sum(jnp.exp(shifted), -1, keepdims=True))
    target = target_ref[...]
    loss_ref[...] = jnp.sum(target * logp, -1, keepdims=True) * (-1.0 / images)
    dlog = to_bf((jnp.exp(logp) - target) * (1.0 / images))
    dlog_ref[...] = dlog
    wide = jnp.broadcast_to(dlog.astype(f32), (16, CLS)).astype(bf16)
    dpool = dot_nt(wide, head_ref[...])[0:1] / count
    dx, dgain, dbias = norm_back(x_ref[...], ln_ref[0:1], ok_ref[...] * dpool)
    dln_ref[0:1, :] = dgain
    dln_ref[1:2, :] = dbias
    dx_ref[...] = dx
    gelu_back(dx, w2, slope_ref, dy_ref, dz_ref)


def conv_back(h_ref, hlow_ref, hhigh_ref, dz_ref, zlow_ref, zhigh_ref, taps_ref, dh_ref, dtaps_ref):
    rows = h_ref.shape[0] // W

    def chunk(c, carry):
        lanes = pl.ds(pl.multiple_of(c * LANES, LANES), LANES)
        taps = [taps_ref[k : k + 1, lanes] for k in range(9)]
        acc = [jnp.zeros((8, LANES), f32) for _ in range(9)]

        def views(i):
            v = row_of(dz_ref, zlow_ref, zhigh_ref, i, rows, lanes)
            return [from_right(v), v, from_left(v)]

        near = [views(-1), views(0)]
        hear = [row_of(h_ref, hlow_ref, hhigh_ref, i, rows, lanes) for i in (-1, 0)]
        for i in range(rows):
            near.append(views(i + 1))
            hear.append(row_of(h_ref, hlow_ref, hhigh_ref, i + 1, rows, lanes))
            dh = None
            for di in range(3):
                for dj in range(3):
                    part = taps[3 * di + dj] * near[2 - di][dj]
                    dh = part if dh is None else dh + part
            dh_ref[i * W : (i + 1) * W, lanes] = to_bf(dh)
            for di in range(3):
                for dj in range(3):
                    prod = (hear[di] * near[1][dj]).reshape(W // 8, 8, LANES)
                    acc[3 * di + dj] = acc[3 * di + dj] + jnp.sum(prod, 0)
            near = near[1:]
            hear = hear[1:]
        for k in range(9):
            dtaps_ref[k : k + 1, lanes] = jnp.sum(acc[k], 0, keepdims=True)
        return carry

    lax.fori_loop(0, FF // LANES, chunk, 0)


def block_back_body(
    h_ref,
    hlow_ref,
    hhigh_ref,
    dz_ref,
    zlow_ref,
    zhigh_ref,
    taps_ref,
    w1,
    x2_ref,
    gain,
    dx_ref,
    wo,
    q_ref,
    kv_ref,
    ok_ref,
    lse_ref,
    dh_ref,
    dtaps_ref,
    dln_ref,
    dx2_ref,
    dy_ref,
    dq_ref,
    dkv_ref,
):
    conv_back(h_ref, hlow_ref, hhigh_ref, dz_ref, zlow_ref, zhigh_ref, taps_ref, dh_ref, dtaps_ref)
    db = dot_nt(dh_ref[...], w1[...])
    dln, dgain, dbias = norm_back(x2_ref[...], gain[2:3], db)
    dln_ref[0:1, :] = dgain
    dln_ref[1:2, :] = dbias
    dx2 = dx_ref[...] + dln
    dx2_ref[...] = dx2
    dy = to_bf(dx2)
    dy_ref[...] = dy
    do_t = to_bf(dot_nt(wo[...], dy))
    q = q_ref[...] * jnp.asarray(scale_qk, bf16)
    q_t = q.T
    keys = kv_ref.shape[0]
    kv = kv_ref[...]
    k_t = (kv[:, :D] * jnp.asarray(scale_qk, bf16)).T
    shut = jnp.broadcast_to(ok_ref[...], (keys, q.shape[0]))
    dq_parts, dk_parts, dv_parts = ([], [], [])
    for head in range(HEADS):
        low, high = head * HD, (head + 1) * HD
        s = dot(kv[:, low:high], q_t[low:high, :]) + shut
        p = jnp.exp(s - lse_ref[head : head + 1, :])
        dp = dot(kv[:, D + low : D + high], do_t[low:high, :])
        dv_parts.append(dot_nt(do_t[low:high, :], to_bf(p)))
        ds = to_bf(p * (dp - jnp.sum(p * dp, 0, keepdims=True)))
        dq_parts.append(dot(k_t[low:high, :], ds))
        dk_parts.append(dot_nt(q_t[low:high, :], ds))
    dq_ref[...] = to_bf(jnp.concatenate(dq_parts, 0).T)
    dkv_ref[...] = jnp.concatenate(dk_parts + dv_parts, 0).T


def inputs_back(dkv, wkv, r_ref, gain, dq_ref, wq, wsr, x_ref, dx2_ref, dr_ref, dln_ref):
    w_kv = wkv[...].astype(f32)
    drn = dot_nt(dkv, w_kv, precise)
    dr, dgain1, dbias1 = norm_back(r_ref[...], gain[1:2], drn)
    dr = to_bf(dr)
    dr_ref[...] = dr
    rows = x_ref.shape[0] // W
    cells = [
        dot_nt(dr, wsr[k * D : (k + 1) * D, :]).reshape(rows // 2, 1, 1, HALF, D) for k in range(4)
    ]
    placed = jnp.concatenate(
        [jnp.concatenate(cells[0:2], 2), jnp.concatenate(cells[2:4], 2)], 1
    ).reshape(rows * W, D)
    da = dot_nt(dq_ref[...], wq[...]) + placed
    dln, dgain0, dbias0 = norm_back(x_ref[...], gain[0:1], da)
    for k, row in enumerate((dgain0, dgain1, dbias0, dbias1)):
        dln_ref[k : k + 1, :] = row
    return dx2_ref[...] + dln


def join_back_body(
    dkv_ref, wkv, r_ref, gain, dq_ref, wq, wsr, x_ref, dx2_ref, w2, slope_ref, dr_ref, dln_ref, dx_ref, dy_ref, dz_ref
):
    dx = inputs_back(dkv_ref[...], wkv, r_ref, gain, dq_ref, wq, wsr, x_ref, dx2_ref, dr_ref, dln_ref)
    dx_ref[...] = dx
    gelu_back(dx, w2, slope_ref, dy_ref, dz_ref)


def first_back_body(
    dkv_ref, wkv, r_ref, gain, dq_ref, wq, wsr, x_ref, dx2_ref, e_ref, ln_ref, dr_ref, dln_ref, de_ref, dle_ref
):
    dx = inputs_back(dkv_ref[...], wkv, r_ref, gain, dq_ref, wq, wsr, x_ref, dx2_ref, dr_ref, dln_ref)
    de, dgain, dbias = norm_back(e_ref[...], ln_ref[0:1], dx)
    de_ref[...] = to_bf(de)
    dle_ref[0:1, :] = dgain
    dle_ref[1:2, :] = dbias


def weight_grads_body(
    n_dp, cols, subs, core_ref, a_ref, dq_ref, rn_ref, dkv_ref, o_ref, dy2_ref, b_ref, dh_ref, dr_ref, g_ref, dy_ref, *refs
):
    outs, (proj, down) = refs[:-2], refs[-2:]
    a = a_ref[...]
    proj[:, :D] = contract(a, dq_ref[...])
    proj[:, D : 3 * D] = contract(rn_ref[...].astype(f32), dkv_ref[...], precise)
    proj[:, 3 * D : 4 * D] = contract(o_ref[...], dy2_ref[...])
    proj[:, 4 * D :] = contract(b_ref[...], dh_ref[...])
    dr = dr_ref[...]
    for k, cell in enumerate(cells_of(a)):
        down[k * D : (k + 1) * D, :D] = contract(cell, dr)
    down[:, D:] = contract(g_ref[...], dy_ref[...])
    rows = D // n_dp
    sub = rows // subs
    wide = (4 * D + FF) // cols
    down_rows = FF // n_dp
    for c in range(cols):
        for d in range(n_dp):
            for n, out in enumerate(outs):
                for j in range(subs) if len(outs) == 1 else (None,):
                    if j is None:
                        k = core_ref[0] if n == 0 else 1 - core_ref[0]
                        at = (c, d)
                    else:
                        k = j
                        at = (c, j, d)
                    start = d * rows + k * sub
                    low = d * down_rows + (c * subs + k) * (down_rows // (cols * subs))
                    if j is None:
                        start = pl.multiple_of(start, 8)
                        low = pl.multiple_of(low, 8)
                    out[(*at, slice(0, sub))] = proj[pl.ds(start, sub), c * wide : (c + 1) * wide]
                    out[(*at, slice(sub, 2 * sub))] = down[pl.ds(low, sub), :]


def group_sums(arrs):
    embed, proj, downs, taps, head, gains, biases = arrs
    first = jnp.stack([jnp.sum(embed), jnp.sum(head), jnp.sum(gains), jnp.sum(biases)])
    rest = [jnp.sum(a.reshape(a.shape[0], -1), 1) for a in (proj, downs, taps)]
    return jnp.concatenate([first] + rest)


def spread_ratio(ratio):
    return (
        ratio[0],
        ratio[4 : 4 + LAYERS].reshape(LAYERS, 1, 1),
        ratio[4 + LAYERS : 4 + 2 * LAYERS].reshape(LAYERS, 1, 1, 1),
        ratio[4 + 2 * LAYERS : 4 + 3 * LAYERS].reshape(LAYERS, 1, 1),
        ratio[1],
        ratio[2],
        ratio[3],
    )


def per_device(
    patches,
    valid,
    labels,
    partners,
    mix,
    embed_w,
    in_proj,
    down_proj,
    dw_kernel,
    head_w,
    norm_gain,
    norm_bias,
    m_embed,
    m_proj,
    m_down,
    m_taps,
    m_head,
    m_gain,
    m_bias,
    v_embed,
    v_proj,
    v_down,
    v_taps,
    v_head,
    v_gain,
    v_bias,
):
    masters = (embed_w, in_proj, down_proj, dw_kernel, head_w, norm_gain, norm_bias)
    firsts = (m_embed, m_proj, m_down, m_taps, m_head, m_gain, m_bias)
    seconds = (v_embed, v_proj, v_down, v_taps, v_head, v_gain, v_bias)
    n_seq = lax.axis_size("seq")
    n_dp = lax.axis_size("dp")
    seq_pos = lax.axis_index("seq")
    img_dev, rows = (patches.shape[0], patches.shape[1])
    images = img_dev * n_dp

    team = n_seq
    while team * img_dev > n_seq:
        team //= 2
    blocks = n_seq // team
    rows_own = rows * blocks
    tok = rows_own * W
    keys_own = tok // 4
    image = jnp.minimum(seq_pos // team, img_dev - 1)
    busy = seq_pos // team < img_dev
    place = seq_pos % team

    def between(shift, wrap):
        pairs = []
        for base in range(0, n_seq, team):
            for h in range(team):
                if wrap or 0 <= h + shift < team:
                    pairs.append((base + (h + shift) % team, base + h))
        return pairs

    def edges(v):
        low = lax.ppermute(v[-W:], "seq", between(-1, False))
        high = lax.ppermute(v[:W], "seq", between(1, False))
        return low, high

    def all_keys(v):
        return jnp.concatenate(
            [v] + [lax.ppermute(v, "seq", between(j, True)) for j in range(1, team)], 0
        )

    def own_keys(v):
        total = v[:keys_own]
        for j in range(1, team):
            part = v[j * keys_own : (j + 1) * keys_own]
            total = total + lax.ppermute(part, "seq", between(-j, True))
        return total

    back_block = seq_pos % blocks
    routes = [
        [
            (blocks * h + (i + r) % blocks, team * i + h)
            for i in range(img_dev)
            for h in range(team)
        ]
        for r in range(blocks)
    ]

    def to_team(v):
        got = []
        for r, pairs in enumerate(routes):
            send = lax.dynamic_index_in_dim(
                v, jnp.minimum((back_block - r) % blocks, img_dev - 1), 0, keepdims=False
            )
            got.append(lax.ppermute(send, "seq", pairs))
        twice = jnp.stack(got + got)
        own = lax.dynamic_slice_in_dim(twice, (blocks - image) % blocks, blocks, 0)
        return own.reshape(tok, -1)

    def from_team(v):
        parts = v.reshape(blocks, rows * W, -1)
        got = []
        for r, pairs in enumerate(routes):
            send = lax.dynamic_index_in_dim(parts, (image + r) % blocks, 0, keepdims=False)
            got.append(lax.ppermute(send, "seq", [(b, a) for a, b in pairs]))
        got = jnp.stack(got)
        return jnp.stack(
            [
                lax.dynamic_index_in_dim(got, (back_block - i) % blocks, 0, keepdims=False)
                for i in range(img_dev)
            ]
        )

    cols = 4
    subs = n_seq // cols
    row_in = D // n_dp
    sub_in = row_in // subs
    wide = in_proj.shape[2] // cols
    down_rows = down_proj.shape[2] // n_seq
    core = seq_pos % subs

    def part_of(flat):
        size = -(-flat.shape[0] // (wide * n_seq)) * wide * n_seq
        flat = jnp.pad(flat, (0, size - flat.shape[0])).reshape(n_seq, -1, wide)
        return lax.dynamic_index_in_dim(flat, seq_pos, 0, keepdims=False)

    def layer_part(l):
        block = lax.dynamic_slice(
            in_proj[l], (core * sub_in, (seq_pos // subs) * wide), (sub_in, wide)
        )
        lower = lax.dynamic_slice_in_dim(down_proj[l], seq_pos * down_rows, down_rows, 1)
        return [to_bf(block), to_bf(jnp.concatenate([lower[0], lower[1]], 1))]

    def gathered(parts):
        sizes = [p.shape[0] for p in parts]
        got = lax.all_gather(jnp.concatenate(parts, 0), ("dp", "seq"), axis=0, tiled=False)
        got = got.reshape(n_dp, n_seq, sum(sizes), wide)
        starts = [sum(sizes[:i]) for i in range(len(sizes))]
        return [got[:, :, a : a + n] for a, n in zip(starts, sizes)]

    def proj_of(got):
        got = got.reshape(n_dp, cols, subs, sub_in, wide).transpose(0, 2, 3, 1, 4)
        return got.reshape(D, cols * wide)

    small = jnp.concatenate(
        [to_bf(dw_kernel).reshape(-1), to_bf(norm_gain).reshape(-1), to_bf(norm_bias).reshape(-1)]
    )
    groups = [[0], [1, 2], [3, 4, 5]]
    extra = [[part_of(to_bf(embed_w).reshape(-1)), part_of(small)], [], [part_of(to_bf(head_w).reshape(-1))]]
    layers16, extras = ([], [])
    for members, more in zip(groups, extra):
        parts = more + [p for l in members for p in layer_part(l)]
        got = gathered(parts)
        extras += [g.reshape(n_dp, -1) for g in got[: len(more)]]
        got = got[len(more) :]
        layers16 += [(proj_of(got[2 * i]), got[2 * i + 1].reshape(FF, 2 * D)) for i in range(len(members))]
    embed16 = extras[0][:, : embed_w.size].reshape(-1, D)
    head16 = extras[2][:, : head_w.size].reshape(D, CLS)
    small = extras[1].astype(f32)
    n_taps = dw_kernel.size
    n_gain = norm_gain.size
    taps32 = small[:, :n_taps].reshape(n_dp, LAYERS * 9, -1).transpose(1, 0, 2)
    taps32 = taps32.reshape(LAYERS, 9, FF)
    gain32 = small[:, n_taps : n_taps + n_gain].reshape(n_dp, -1, row_in).transpose(1, 0, 2)
    gain32 = gain32.reshape(-1, D)
    bias32 = small[:, n_taps + n_gain : n_taps + 2 * n_gain].reshape(n_dp, -1, row_in)
    bias32 = bias32.transpose(1, 0, 2).reshape(-1, D)

    def own(v):
        return lax.dynamic_index_in_dim(v, image, 0, keepdims=False)

    dp_pos = lax.axis_index("dp")
    wanted = own(partners)
    partner_label = jnp.zeros((), jnp.int32)
    for j in range(n_dp):
        other = labels
        if j:
            other = lax.ppermute(labels, "dp", [((d + j) % n_dp, d) for d in range(n_dp)])
        index = ((dp_pos + j) % n_dp) * img_dev + jnp.arange(img_dev)
        partner_label = partner_label + jnp.sum(jnp.where(index == wanted, other, 0))
    valid_own = own(valid)
    tid = lax.broadcasted_iota(jnp.int32, (tok, 1), 0)
    within = tid % W
    row_id = place * rows_own + tid // W
    col_id = 2 * (within % HALF) + within // HALF
    okay = ((row_id < valid_own[0]) & (col_id < valid_own[1]) & busy).astype(f32)
    kid = lax.broadcasted_iota(jnp.int32, (team * keys_own, 1), 0)
    segment = (place + kid // keys_own) % team
    key_row = segment * (rows_own // 2) + (kid % keys_own) // HALF
    key_ok = (2 * key_row < valid_own[0]) & (2 * (kid % HALF) < valid_own[1])
    shut = jnp.where(key_ok, 0.0, big_neg).astype(f32)
    count = (valid_own[0] * valid_own[1]).astype(f32).reshape(1, 1)
    classes = lax.broadcasted_iota(jnp.int32, (1, CLS), 1)
    mix_own = own(mix)
    target = mix_own * (classes == own(labels)).astype(f32) + (1.0 - mix_own) * (
        classes == partner_label
    ).astype(f32)

    def weights(l):
        base = 1 + 3 * l
        return dict(
            wq=layers16[l][0][:, :D],
            wkv=layers16[l][0][:, D : 3 * D],
            wo=layers16[l][0][:, 3 * D : 4 * D],
            w1=layers16[l][0][:, 4 * D :],
            wsr=layers16[l][1][:, :D],
            w2=layers16[l][1][:, D:],
            taps=taps32[l],
            gain=gain32[base : base + 3],
            bias=bias32[base : base + 3],
        )

    wts = [weights(l) for l in range(LAYERS)]
    ln_first = jnp.stack([gain32[0], bias32[0]])
    ln_last = jnp.stack([gain32[-1], bias32[-1]])

    full = ((tok, D), f32)
    half = ((tok, D), bf16)
    wide16 = ((tok, FF), bf16)
    input_outs = [half, half, ((keys_own, D), f32), ((keys_own, D), bf16), ((keys_own, 2 * D), bf16)]
    ln_out = ((2, D), f32)

    embedded = dot(patches.reshape(-1, patches.shape[-1]), embed16)
    embedded = embedded.reshape(img_dev, rows, HALF, 2, D).transpose(0, 1, 3, 2, 4)
    e = to_team(embedded.reshape(img_dev, rows * W, D))
    w = wts[0]
    x, a16, q16, r, rn16, kv16 = run(
        first_body, [full] + input_outs, e, ln_first, w["gain"], w["bias"], w["wq"], w["wsr"], w["wkv"]
    )
    kept = []
    for l in range(LAYERS):
        w = wts[l]
        kv_all = all_keys(kv16)
        o16, lse, x2, b16, h16 = run(
            middle_body,
            [half, ((HEADS, tok), f32), full, half, wide16],
            q16,
            kv_all,
            shut,
            x,
            w["gain"],
            w["bias"],
            w["wo"],
            w["w1"],
        )
        hlow, hhigh = edges(h16)
        keep = dict(
            x=x, a16=a16, q16=q16, r=r, rn16=rn16, kv=kv_all, o16=o16, lse=lse, x2=x2, b16=b16,
            h16=h16, hlow=hlow, hhigh=hhigh,
        )
        shared = (h16, hlow, hhigh, w["taps"], x2, w["w2"])
        if l + 1 < LAYERS:
            n = wts[l + 1]
            keep["g16"], keep["slope"], x, a16, q16, r, rn16, kv16 = run(
                join_body,
                [wide16, ((tok, FF), f32), full] + input_outs,
                *shared,
                n["gain"],
                n["bias"],
                n["wq"],
                n["wsr"],
                n["wkv"],
            )
        else:
            keep["g16"], keep["slope"], x, pool = run(
                last_body,
                [wide16, ((tok, FF), f32), full, ((1, D), f32)],
                *shared,
                ln_last,
                okay,
            )
        kept.append(keep)

    whole = pool
    for j in range(1, team):
        whole = whole + lax.ppermute(pool, "seq", between(j, True))
    loss_own, pooled16, dlog16, dln_last, dx, dy16, dz16 = run(
        functools.partial(head_body, images),
        [((1, 1), f32), ((1, D), bf16), ((1, CLS), bf16), ln_out, full, half, wide16],
        whole,
        count,
        head16,
        target,
        x,
        ln_last,
        okay,
        wts[-1]["w2"],
        kept[-1]["slope"],
    )
    chosen = ((place == 0) & busy).astype(f32)
    d_head = pooled16.astype(f32).reshape(D, 1) * dlog16.astype(f32) * chosen
    loss_local = loss_own[0, 0] * busy.astype(f32)
    teams = n_seq // team
    loss_parts = jnp.zeros((teams,), f32)
    for j in range(teams):
        other = loss_local
        if j:
            other = lax.ppermute(
                loss_local, "seq", [((d + j * team) % n_seq, d) for d in range(n_seq)]
            )
        loss_parts = jnp.where(jnp.arange(teams) == (seq_pos // team + j) % teams, other, loss_parts)
    loss_seq = jnp.sum(loss_parts)

    piece = ((cols, n_dp, 2 * sub_in, wide), f32)
    paired = subs == 2

    def weight_grads(*args):
        vm = pl.BlockSpec(memory_space=pltpu.VMEM)
        outs = [piece] * 2 if paired else [((cols, subs) + piece[0][1:], f32)]
        got = pl.pallas_call(
            functools.partial(weight_grads_body, n_dp, cols, subs),
            out_shape=[jax.ShapeDtypeStruct(s, d) for s, d in outs],
            in_specs=[pl.BlockSpec(memory_space=pltpu.SMEM)] + [vm] * len(args),
            out_specs=[vm] * len(outs),
            scratch_shapes=[pltpu.VMEM((D, cols * wide), f32), pltpu.VMEM((FF, 2 * D), f32)],
            compiler_params=pltpu.CompilerParams(vmem_limit_bytes=48 << 20),
        )(core.reshape(1), *args)
        if paired:
            return got[0] + lax.ppermute(got[1], "seq", [(d ^ 1, d) for d in range(n_seq)])
        return got[0]

    grads = [None] * LAYERS
    for l in reversed(range(LAYERS)):
        w, k = wts[l], kept[l]
        zlow, zhigh = edges(dz16)
        dh16, d_taps, dln2, dx2, dy2, dq16, dkv = run(
            block_back_body,
            [wide16, ((9, FF), f32), ln_out, full, half, half, ((team * keys_own, 2 * D), f32)],
            k["h16"], k["hlow"], k["hhigh"], dz16, zlow, zhigh, w["taps"], w["w1"], k["x2"], w["gain"], dx,
            w["wo"], k["q16"], k["kv"], shut, k["lse"],
        )
        dkv_own = own_keys(dkv)
        upper = dy16
        shared = (dkv_own, w["wkv"], k["r"], w["gain"], dq16, w["wq"], w["wsr"], k["x"], dx2)
        if l:
            dr16, dln, dx, dy16, dz16 = run(
                join_back_body,
                [((keys_own, D), bf16), ((4, D), f32), full, half, wide16],
                *shared,
                wts[l - 1]["w2"],
                kept[l - 1]["slope"],
            )
        else:
            dr16, dln, de16, dln_first = run(
                first_back_body,
                [((keys_own, D), bf16), ((4, D), f32), half, ln_out],
                *shared,
                e,
                ln_first,
            )
        grads[l] = (
            weight_grads(
                k["a16"], dq16, k["rn16"], dkv_own, k["o16"], dy2, k["b16"], dh16, dr16, k["g16"], upper
            ),
            None,
            d_taps,
            jnp.concatenate([dln[0:2], dln2[0:1]], 0),
            jnp.concatenate([dln[2:4], dln2[1:2]], 0),
        )
    de = from_team(de16).reshape(img_dev, rows, 2, HALF, D).transpose(0, 1, 3, 2, 4)
    d_embed = contract(patches.reshape(-1, patches.shape[-1]), de.reshape(-1, D))
    d_gain = jnp.concatenate([dln_first[0:1]] + [g[3] for g in grads] + [dln_last[0:1]], 0)
    d_bias = jnp.concatenate([dln_first[1:2]] + [g[4] for g in grads] + [dln_last[1:2]], 0)

    d_taps = jnp.stack([g[2] for g in grads])
    rest = [
        d_embed.reshape(n_dp, -1),
        d_head.reshape(n_dp, -1),
        d_taps.reshape(LAYERS * 9, n_dp, -1).transpose(1, 0, 2).reshape(n_dp, -1),
        d_gain.reshape(-1, n_dp, row_in).transpose(1, 0, 2).reshape(n_dp, -1),
        d_bias.reshape(-1, n_dp, row_in).transpose(1, 0, 2).reshape(n_dp, -1),
    ]
    cuts = [0]
    for part in rest:
        cuts.append(cuts[-1] + part.shape[1])
    size = -(-cuts[-1] // (8 * wide * n_seq)) * 8 * wide * n_seq
    rest = jnp.pad(jnp.concatenate(rest, 1), ((0, 0), (0, size - cuts[-1])))
    rest = rest.reshape(n_dp, cols, subs, -1, wide).transpose(1, 2, 0, 3, 4)
    if paired:
        mine = lax.dynamic_index_in_dim(rest, core, 1, keepdims=False)
        send = lax.dynamic_index_in_dim(rest, 1 - core, 1, keepdims=False)
        rest = mine + lax.ppermute(send, "seq", [(d ^ 1, d) for d in range(n_seq)])

    def scattered(parts):
        both = jnp.concatenate([to_bf(p) for p in parts], -2)
        both = both.reshape(-1, wide)
        if paired:
            chips = [[c * subs + k for c in range(cols)] for k in range(subs)]
            both = lax.psum_scatter(
                both, "seq", scatter_dimension=0, tiled=True, axis_index_groups=chips
            )
        else:
            both = lax.psum_scatter(both, "seq", scatter_dimension=0, tiled=True)
        return lax.psum_scatter(both.astype(f32), "dp", scatter_dimension=0, tiled=True)

    chunks = [
        scattered([grads[5][0], grads[4][0]]),
        scattered([grads[3][0], grads[2][0]]),
        scattered([grads[1][0], grads[0][0], rest]),
    ]
    got = lax.all_gather(jnp.concatenate(chunks, 0), "seq", axis=0, tiled=False)
    proj_sums, down_sums = ([], [])
    for n in range(LAYERS):
        block = got[:, 2 * sub_in * n : 2 * sub_in * (n + 1)]
        g_proj = block[:, :sub_in].reshape(cols, subs, sub_in, wide).transpose(1, 2, 0, 3)
        proj_sums.append(g_proj.reshape(row_in, cols * wide))
        g_down = block[:, sub_in:].reshape(-1, 2, D).transpose(1, 0, 2)
        down_sums.append(g_down)
    got = got[:, 2 * sub_in * LAYERS :].reshape(-1)
    got = [got[a:b] for a, b in zip(cuts, cuts[1:])]
    shards = (
        got[0].reshape(embed_w.shape),
        jnp.stack(proj_sums[::-1]),
        jnp.stack(down_sums[::-1]),
        got[2].reshape(dw_kernel.shape),
        got[1].reshape(head_w.shape),
        got[3].reshape(norm_gain.shape),
        got[4].reshape(norm_bias.shape),
    )

    gsq_local = sum((jnp.sum(g * g) for g in shards))
    wsq_local = group_sums(tuple((w * w for w in masters)))
    gsq, wsq, loss = lax.psum((gsq_local, wsq_local, loss_seq), "dp")
    grad_norm = jnp.sqrt(gsq)
    factor = jnp.minimum(1.0, clip_limit / grad_norm)
    new_m, new_v, updates = ([], [], [])
    for w, g, m, v in zip(masters, shards, firsts, seconds):
        g = g * factor
        m2 = beta_one * m + (1.0 - beta_one) * g
        v2 = beta_two * v + (1.0 - beta_two) * g * g
        u = (
            m2 / (1.0 - beta_one**STEP) / (jnp.sqrt(v2 / (1.0 - beta_two**STEP)) + lamb_eps)
            + decay_rate * w
        )
        new_m.append(m2)
        new_v.append(v2)
        updates.append(u)
    usq = lax.psum(group_sums(tuple((u * u for u in updates))), "dp")
    wnorm = jnp.sqrt(wsq)
    unorm = jnp.sqrt(usq)
    ratio = wnorm / unorm
    spreads = spread_ratio(ratio)
    new_w = [w - learn_rate * r * u for w, r, u in zip(masters, spreads, updates)]
    stats = jnp.stack([wnorm, unorm])
    return (loss, grad_norm, stats, ratio, *new_w, *new_m, *new_v)


def solution(mesh):
    placed = (
        P("dp", None),
        P(None, "dp", None),
        P(None, None, "dp", None),
        P(None, None, "dp"),
        P("dp", None),
        P(None, "dp"),
        P(None, "dp"),
    )
    in_specs = (
        P("dp", "seq", None, None),
        P("dp", None),
        P("dp"),
        P("dp"),
        P("dp"),
    ) + placed * 3
    out_specs = (P(), P(), P(), P()) + placed * 3
    return jax.shard_map(
        per_device, mesh=mesh, in_specs=in_specs, out_specs=out_specs, check_vma=False
    )
```

time: 4340 us -> 1180 us (0.27)
  waiting for transfers between devices: 1430 us -> 340 us
  matrix products: 626 us -> 2.04 us
  other arithmetic: 736 us -> 127 us
  blocking collectives: 509 us -> 21.4 us
  local copies, waits for them, and re-layouts: 774 us -> 325 us
  Pallas kernels: 0 us -> 209 us
  starting transfers between devices: 171 us -> 105 us
    unnamed x51 -> x11, waiting for transfers between devices: 973 us -> 45.1 us
    dot_general x444 -> x2, matrix products: 626 us -> 2.04 us  [the longest x1 1.45 us: dot(): return jnp.dot(a, b, preferred_element_type=f32)]
    all_gather x23 -> x0, blocking collectives: 408 us -> none  [the longest x18 225 us: layer_forward(): kv_all = lax.all_gather(kv16, 'seq', axis=1, tiled=True)]
    convert_element_type x100 -> x16, other arithmetic: 382 us -> 30.3 us  [the longest x11 19.7 us: to_bf(): return v.astype(bf16)]
    pallas_call x0 -> x32, Pallas kernels: none -> 209 us  [the longest x26 175 us: run(): pl.pallas_call(body, out_shape=[jax.ShapeDtypeStruct(s, d) for s, d in ou...]
    unnamed x4035 -> x883, local copies, waits for them, and re-layouts: 317 us -> 128 us
    psum x1 -> x0, waiting for transfers between devices: 145 us -> none  [reduce_grads(): lax.psum((shards[0], shards[1], shards[2], shards[3], shards[4], shards[5...]
    concatenate x60 -> x10, local copies, waits for them, and re-layouts: 142 us -> 3.89 us  [the longest x6 1.97 us: all_keys(): jnp.concatenate([v] + [lax.ppermute(v, 'seq', between(j, True)) for j in...]
where the time goes in v1:
time: 1180 us; the launch traced here: 1160 us
  waiting for transfers between devices  340 us (29%)
  local copies, waits for them, and re-layouts  325 us (28%)
  Pallas kernels  209 us (18%)
  other arithmetic  127 us (11%)
  starting transfers between devices  105 us (9%)
  between operations  34 us (3%)
  blocking collectives  21.4 us (2%)
    pallas_call x26, Pallas kernels, run(): pl.pallas_call(body, out_shape=[jax.ShapeDtypeStruct(s, d) for s, d in ou...  175 us
    unnamed x883, local copies, waits for them, and re-layouts  128 us
    reduce_scatter x3, waiting for transfers between devices, scattered(): lax.psum_scatter(both, 'seq', scatter_dimension=0, tiled=True, axis_index...  110 us
    reduce_scatter x2, waiting for transfers between devices, scattered(): lax.psum_scatter(both.astype(f32), 'dp', scatter_dimension=0, tiled=True)  74.8 us
    all_gather x1, waiting for transfers between devices, per_device(): got = lax.all_gather(jnp.concatenate(chunks, 0), 'seq', axis=0, tiled=False)  55.1 us
    unnamed x11, waiting for transfers between devices  45.1 us
    ppermute x12, starting transfers between devices, edges(): low = lax.ppermute(v[-W:], 'seq', between(-1, False))  43.7 us
    all_gather x3, waiting for transfers between devices, gathered(): lax.all_gather(jnp.concatenate(parts, 0), ('dp', 'seq'), axis=0, tiled=Fa...  42.4 us
  transfers between devices with their start and end apart: 68, of which 19 were waited for; matrix products, arithmetic and copies ran while one was open for 22% of the time, Pallas kernels for 13%

profile of v1, /device:TPU:0, one launch (start us, length us, event | category | flops | bytes accessed | tf_op | source)
XLA Modules:
  0.0 1164.5 jit_solution(793178413296934424)
XLA Ops:
  45.3 42.4 %all-gather.16.cloned.1.call-done = bf16[32,102,640]{2,1,0:T(8,128)(2,1)} async-done(((bf16[1,102,640]{2,1,0:T(8,128)(2,1)}), bf16[32,102,640]{2,1,0:T(8,128)(2,1)}) %all-gather.16.cloned.1.call-update) | async-done | bytes 4177936 | tf_op jit(solution)/shard_map/all_gather | solution.py:569
  180.3 8.6 shard_map.443
  204.3 8.0 shard_map.445
  272.0 8.1 shard_map.447
  295.7 8.0 shard_map.449
  317.7 8.0 shard_map.451
  390.7 10.8 shard_map.455
  430.1 10.6 shard_map.458
  478.8 10.9 shard_map.461
  519.5 10.8 shard_map.464
  550.8 10.9 shard_map.467
  589.1 10.7 shard_map.470
  700.0 11.4 reduce-scatter.9.cloned.1.call-done
  714.0 46.0 %reduce-scatter.13.cloned.1.call-done = bf16[640,640]{1,0:T(8,128)(2,1)} async-done(((bf16[2560,640]{1,0:T(8,128)(2,1)}), bf16[640,640]{1,0:T(8,128)(2,1)}) %reduce-scatter.13.cloned.1.call-update) | async-done | bytes 819216 | tf_op jit(solution)/shard_map/reduce_scatter | solution.py:822
  762.5 52.9 %reduce-scatter.17.cloned.1.call-done = bf16[800,640]{1,0:T(8,128)(2,1)} async-done(((bf16[3200,640]{1,0:T(8,128)(2,1)}), bf16[800,640]{1,0:T(8,128)(2,1)}) %reduce-scatter.17.cloned.1.call-update) | async-done | bytes 1024016 | tf_op jit(solution)/shard_map/reduce_scatter | solution.py:822
  818.1 36.5 %reduce-scatter.11.cloned.1.call-done = f32[160,640]{1,0:T(8,128)} async-done(((f32[640,640]{1,0:T(8,128)}), f32[160,640]{1,0:T(8,128)}) %reduce-scatter.11.cloned.1.call-update) | async-done | bytes 409616 | tf_op jit(solution)/shard_map/reduce_scatter | solution.py:827
  854.6 38.3 %reduce-scatter.15.cloned.1.call-done = f32[160,640]{1,0:T(8,128)} async-done(((f32[640,640]{1,0:T(8,128)}), f32[160,640]{1,0:T(8,128)}) %reduce-scatter.15.cloned.1.call-update) | async-done | bytes 409616 | tf_op jit(solution)/shard_map/reduce_scatter | solution.py:827
  893.0 45.0 %reduce-scatter.19.cloned.1.call-done = f32[200,640]{1,0:T(8,128)} async-done(((f32[800,640]{1,0:T(8,128)}), f32[200,640]{1,0:T(8,128)}) %reduce-scatter.19.cloned.1.call-update) | async-done | bytes 512016
  948.7 55.1 %all-gather.14.cloned.1.call-done = f32[4160,640]{1,0:T(8,128)} async-done(((f32[520,640]{1,0:T(8,128)}), f32[4160,640]{1,0:T(8,128)}) %all-gather.14.cloned.1.call-update) | async-done | bytes 10649616 | tf_op jit(solution)/shard_map/all_gather | solution.py:834
  1065.7 12.2 %psum.29 = f32[]{:T(128)} all-reduce(f32[]{:T(128)S(6)} %add.635), channel_id=1, replica_groups=mesh['dp'=4,'seq'=8] {'dp'}, use_global_device_ids=true, to_apply=%region_19.20 | all-reduce | flops 1 | bytes 8 | tf_op jit(solution)/shard_map/psum | solution.py:856
  1083.1 13.3 %multiply_reduce_fusion.4 = (f32[6]{0:T(128)S(1)}, f32[6]{0:T(128)}, f32[6,80,2560]{2,1,0:T(8,128)}, f32[6,80,2560]{2,1,0:T(8,128)}) fusion(f32[6,80,2560]{2,1,0:T(8,128)} %param.32, f32[6,80,2560]{2,1,0:T(8,128)} %copy-done.321, f32[]{:T(128)S(6)} %min.23, f32[6,80,2560]{2,1,0:T(8,128)} %param.39, f32[6,80,2560]{2,1,0:T(8,128)} %param.46), kind=kLoop, calls=%fused_computation.14 | loop fusion | flops 22118388 | bytes 29491252 | tf_op jit(solution)/shard_map/reduce_sum | solution.py:423
  1096.6 14.2 %multiply_reduce_fusion.1 = (f32[6]{0:T(128)}, f32[6]{0:T(128)}, f32[6,2,320,320]{3,2,1,0:T(8,128)}, f32[6,2,320,320]{3,2,1,0:T(8,128)}) fusion(f32[6,2,320,320]{3,2,1,0:T(8,128)} %param.33, f32[6,2,320,320]{3,2,1,0:T(8,128)S(1)} %bitcast.264, f32[]{:T(128)S(6)} %min.23, f32[6,2,320,320]{3,2,1,0:T(8,128)} %param.40, f32[6,2,320,320]{3,2,1,0:T(8,128)} %param.47), kind=kLoop, calls=%fused_computation.7 | loop fusion | flops 22118388 | bytes 29491252 | tf_op jit(solution)/shard_map/reduce_sum | solution.py:423
  1120.8 9.3 all-reduce.3
  1139.2 10.2 multiply_subtract_fusion.1
  (1333 shorter events, 638.3 us)
Async XLA Ops:
  7.2 80.5 %all-gather.16.cloned.1.call-start = ((), (), s32[]{:S(2)}) async-start(), calls=%async_computation.14 | async-start | bytes 4392960 | tf_op jit(solution)/shard_map/all_gather | solution.py:569
  22.6 151.9 %all-gather.10.cloned.1.call-start = ((), (), s32[]{:S(2)}) async-start(), calls=%async_computation.11 | async-start | bytes 6758400 | tf_op jit(solution)/shard_map/all_gather | solution.py:569
  24.4 239.5 %all-gather.12.cloned.1.call-start = ((), (), s32[]{:S(2)}) async-start(), calls=%async_computation.12 | async-start | bytes 10813440 | tf_op jit(solution)/shard_map/all_gather | solution.py:569
  28.6 682.9 %reduce-scatter.9.cloned.1.call-start = ((), (), s32[]{:S(2)}) async-start(), calls=%async_computation.6 | async-start | bytes 4096000 | tf_op jit(solution)/shard_map/reduce_scatter | solution.py:822
  28.6 187.4 %collective-permute-start.23 = (s32[3]{0:T(128)}, s32[3]{0:T(128)}, u32[]{:S(2)}, u32[]{:S(2)}) collective-permute-start(s32[3]{0:T(128)} %param.28), channel_id=1, source_target_pairs={{8,0},{16,8},{24,16},{0,24},{9,1},{17,9},{25,17},{1,25},{10,2},{18... | collective-permute-start | bytes 44 | tf_op jit(solution)/shard_map/ppermute | solution.py:611
  33.7 292.5 %collective-permute-start.25 = (s32[3]{0:T(128)}, s32[3]{0:T(128)}, u32[]{:S(2)}, u32[]{:S(2)}) collective-permute-start(s32[3]{0:T(128)} %param.28), channel_id=1, source_target_pairs={{24,0},{0,8},{8,16},{16,24},{25,1},{1,9},{9,17},{17,25},{26,2},{2,... | collective-permute-start | bytes 44 | tf_op jit(solution)/shard_map/ppermute | solution.py:611
  33.7 308.2 %collective-permute-start.24 = (s32[3]{0:T(128)}, s32[3]{0:T(128)}, u32[]{:S(2)}, u32[]{:S(2)}) collective-permute-start(s32[3]{0:T(128)} %param.28), channel_id=1, source_target_pairs={{16,0},{24,8},{0,16},{8,24},{17,1},{25,9},{1,17},{9,25},{18,2},{26... | collective-permute-start | bytes 44 | tf_op jit(solution)/shard_map/ppermute | solution.py:611
  216.0 28.6 %collective-permute-start.10 = (bf16[128,640]{1,0:T(8,128)(2,1)}, bf16[128,640]{1,0:T(8,128)(2,1)}, u32[]{:S(2)}, u32[]{:S(2)}) collective-permute-start(bf16[128,640]{1,0:T(8,128)(2,1)} %get-tuple-element.206), channel_id=1, source_target_pairs={{1,0},{0,1},{3,2},{2,3},{5,4},{4,5},{7,6},{6,7},{9,8},{8,9},{11,10... | collective-permute-start | bytes 491528 | tf_op jit(solution)/shard_map/ppermute | solution.py:502
  499.0 160.3 %collective-permute-start.32 = (f32[4,4,80,640]{3,2,1,0:T(8,128)}, f32[4,4,80,640]{3,2,1,0:T(8,128)}, u32[]{:S(2)}, u32[]{:S(2)}) collective-permute-start(f32[4,4,80,640]{3,2,1,0:T(8,128)} %get-tuple-element.247), channel_id=1, source_target_pairs={{1,0},{0,1},{3,2},{2,3},{5,4},{4,5},{7,6},{6,7},{9,8},{8,9},{11,10... | collective-permute-start | bytes 9830408 | tf_op jit(solution)/shard_map/ppermute | solution.py:752
  505.6 157.2 %collective-permute-start.36 = (f32[4,4,80,640]{3,2,1,0:T(8,128)}, f32[4,4,80,640]{3,2,1,0:T(8,128)}, u32[]{:S(2)}, u32[]{:S(2)}) collective-permute-start(f32[4,4,80,640]{3,2,1,0:T(8,128)} %get-tuple-element.266), channel_id=1, source_target_pairs={{1,0},{0,1},{3,2},{2,3},{5,4},{4,5},{7,6},{6,7},{9,8},{8,9},{11,10... | collective-permute-start | bytes 9830408 | tf_op jit(solution)/shard_map/ppermute | solution.py:752
  623.5 28.4 %collective-permute-start.56 = (bf16[128,320]{1,0:T(8,128)(2,1)}, bf16[128,320]{1,0:T(8,128)(2,1)}, u32[]{:S(2)}, u32[]{:S(2)}) collective-permute-start(bf16[128,320]{1,0:T(8,128)(2,1)} %get-tuple-element.601), channel_id=1, source_target_pairs={{0,3},{1,7},{2,0},{3,4},{4,1},{5,5},{8,11},{9,15},{10,8},{11,12},{... | collective-permute-start | bytes 245768 | tf_op jit(solution)/shard_map/ppermute | solution.py:538
  628.8 24.3 %collective-permute-start.55 = (bf16[128,320]{1,0:T(8,128)(2,1)}, bf16[128,320]{1,0:T(8,128)(2,1)}, u32[]{:S(2)}, u32[]{:S(2)}) collective-permute-start(bf16[128,320]{1,0:T(8,128)(2,1)} %get-tuple-element.602), channel_id=1, source_target_pairs={{0,2},{1,6},{2,3},{3,7},{4,0},{5,4},{8,10},{9,14},{10,11},{11,15},... | collective-permute-start | bytes 245768 | tf_op jit(solution)/shard_map/ppermute | solution.py:538
  630.7 22.4 %collective-permute-start.54 = (bf16[128,320]{1,0:T(8,128)(2,1)}, bf16[128,320]{1,0:T(8,128)(2,1)}, u32[]{:S(2)}, u32[]{:S(2)}) collective-permute-start(bf16[128,320]{1,0:T(8,128)(2,1)} %get-tuple-element.603), channel_id=1, source_target_pairs={{0,1},{1,5},{2,2},{3,6},{4,3},{5,7},{8,9},{9,13},{10,10},{11,14},{... | collective-permute-start | bytes 245768 | tf_op jit(solution)/shard_map/ppermute | solution.py:538
  653.2 39.2 %collective-permute-start.48 = (f32[4,4,80,640]{3,2,1,0:T(8,128)}, f32[4,4,80,640]{3,2,1,0:T(8,128)}, u32[]{:S(2)}, u32[]{:S(2)}) collective-permute-start(f32[4,4,80,640]{3,2,1,0:T(8,128)} %get-tuple-element.323), channel_id=1, source_target_pairs={{1,0},{0,1},{3,2},{2,3},{5,4},{4,5},{7,6},{6,7},{9,8},{8,9},{11,10... | collective-permute-start | bytes 9830408 | tf_op jit(solution)/shard_map/ppermute | solution.py:752
  659.3 35.7 %collective-permute-start.52 = (f32[4,4,80,640]{3,2,1,0:T(8,128)}, f32[4,4,80,640]{3,2,1,0:T(8,128)}, u32[]{:S(2)}, u32[]{:S(2)}) collective-permute-start(f32[4,4,80,640]{3,2,1,0:T(8,128)} %get-tuple-element.341), channel_id=1, source_target_pairs={{1,0},{0,1},{3,2},{2,3},{5,4},{4,5},{7,6},{6,7},{9,8},{8,9},{11,10... | collective-permute-start | bytes 9830408 | tf_op jit(solution)/shard_map/ppermute | solution.py:752
  667.8 92.2 %reduce-scatter.13.cloned.1.call-start = ((), (), s32[]{:S(2)}) async-start(), calls=%async_computation.8 | async-start | bytes 4096000 | tf_op jit(solution)/shard_map/reduce_scatter | solution.py:822
  679.2 136.2 %reduce-scatter.17.cloned.1.call-start = ((), (), s32[]{:S(2)}) async-start(), calls=%async_computation.10 | async-start | bytes 5120000 | tf_op jit(solution)/shard_map/reduce_scatter | solution.py:822
  700.0 154.6 %reduce-scatter.11.cloned.1.call-start = ((), (), s32[]{:S(2)}) async-start(), calls=%async_computation.7 | async-start | bytes 2048000 | tf_op jit(solution)/shard_map/reduce_scatter | solution.py:827
  713.9 179.0 %reduce-scatter.15.cloned.1.call-start = ((), (), s32[]{:S(2)}) async-start(), calls=%async_computation.9 | async-start | bytes 2048000 | tf_op jit(solution)/shard_map/reduce_scatter | solution.py:827
  762.4 175.5 %reduce-scatter.19.cloned.1.call-start = ((), (), s32[]{:S(2)}) async-start(), calls=%async_computation.15 | async-start | bytes 2560000
  818.1 185.7 %all-gather.14.cloned.1.call-start = ((), (), s32[]{:S(2)}) async-start(), calls=%async_computation.13 | async-start | bytes 11980800 | tf_op jit(solution)/shard_map/all_gather | solution.py:834
  941.1 122.1 %collective-permute-start.28 = (f32[]{:T(128)}, f32[]{:T(128)}, u32[]{:S(2)}, u32[]{:S(2)}) collective-permute-start(f32[]{:T(128)} %mul.558), channel_id=1, source_target_pairs={{2,0},{3,1},{4,2},{5,3},{6,4},{7,5},{0,6},{1,7},{10,8},{11,9},{12,... | collective-permute-start | bytes 20 | tf_op jit(solution)/shard_map/ppermute | solution.py:731
  944.8 118.4 %collective-permute-start.27 = (f32[]{:T(128)}, f32[]{:T(128)}, u32[]{:S(2)}, u32[]{:S(2)}) collective-permute-start(f32[]{:T(128)} %mul.558), channel_id=1, source_target_pairs={{4,0},{5,1},{6,2},{7,3},{0,4},{1,5},{2,6},{3,7},{12,8},{13,9},{14,... | collective-permute-start | bytes 20 | tf_op jit(solution)/shard_map/ppermute | solution.py:731
  946.7 116.6 %collective-permute-start.26 = (f32[]{:T(128)}, f32[]{:T(128)}, u32[]{:S(2)}, u32[]{:S(2)}) collective-permute-start(f32[]{:T(128)} %mul.558), channel_id=1, source_target_pairs={{6,0},{7,1},{0,2},{1,3},{2,4},{3,5},{4,6},{5,7},{14,8},{15,9},{8,1... | collective-permute-start | bytes 20 | tf_op jit(solution)/shard_map/ppermute | solution.py:731
  (462 other events, 4251.3 us)
Sparse Core Ops, SparseCore 0:
  22.8 64.9 all-gather.15
  91.1 69.0 all-gather.9
  163.7 85.2 all-gather.11
  667.9 43.5 reduce-scatter.8
  714.9 45.0 reduce-scatter.12
  763.5 51.8 reduce-scatter.16
  818.3 36.2 reduce-scatter.10
  857.6 35.3 reduce-scatter.14
  895.9 42.0 reduce-scatter.18
  940.5 63.2 all-gather.13

commit v2 on v1

--- a/solution.py
+++ b/solution.py
@@ -78,7 +78,11 @@
     return dv, dgain, dbias
 
 
-def run(body, outs, *args):
+def cost(us):
+    return pl.CostEstimate(flops=int(us * 1e9), bytes_accessed=int(us * 3e6), transcendentals=0)
+
+
+def run(us, body, outs, *args):
     vm = pl.BlockSpec(memory_space=pltpu.VMEM)
     return pl.pallas_call(
         body,
@@ -86,6 +90,7 @@
         in_specs=[vm] * len(args),
         out_specs=[vm] * len(outs),
         compiler_params=pltpu.CompilerParams(vmem_limit_bytes=48 << 20),
+        cost_estimate=cost(us),
     )(*args)
 
 
@@ -109,10 +114,18 @@
     kv_ref[...] = to_bf(dot(rn, wkv[...]))
 
 
-def first_body(e_ref, ln_ref, gain, bias, wq, wsr, wkv, x_ref, *outs):
-    x = layer_norm(e_ref[...], ln_ref[0:1], ln_ref[1:2])
-    x_ref[...] = x
-    attention_inputs(x, gain, bias, wq, wsr, wkv, *outs)
+def embed_body(p_ref, w_ref, ln_ref, e_ref, x_ref):
+    e = dot(p_ref[...], w_ref[...])
+    e_ref[...] = e
+    x_ref[...] = layer_norm(e, ln_ref[0:1], ln_ref[1:2])
+
+
+def embed_back_body(p_ref, de_ref, dw_ref):
+    dw_ref[...] = contract(p_ref[...], de_ref[...])
+
+
+def first_body(x_ref, gain, bias, wq, wsr, wkv, *outs):
+    attention_inputs(x_ref[...], gain, bias, wq, wsr, wkv, *outs)
 
 
 def middle_body(q_ref, kv_ref, ok_ref, x_ref, gain, bias, wo, w1, o_ref, lse_ref, x2_ref, b_ref, h_ref):
@@ -404,7 +417,7 @@
                 for j in range(subs) if len(outs) == 1 else (None,):
                     if j is None:
                         k = core_ref[0] if n == 0 else 1 - core_ref[0]
-                        at = (c, d)
+                        at = (c ^ core_ref[1], lax.rem(d + n_dp - core_ref[2], n_dp))
                     else:
                         k = j
                         at = (c, j, d)
@@ -417,11 +430,55 @@
                     out[(*at, slice(sub, 2 * sub))] = down[pl.ds(low, sub), :]
 
 
-def group_sums(arrs):
+def moments(w, g, m, v):
+    m2 = beta_one * m + (1.0 - beta_one) * g
+    v2 = beta_two * v + (1.0 - beta_two) * g * g
+    u = (
+        m2 / (1.0 - beta_one**STEP) / (jnp.sqrt(v2 / (1.0 - beta_two**STEP)) + lamb_eps)
+        + decay_rate * w
+    )
+    return m2, v2, u
+
+
+def update_body(
+    cols, subs, late, factor_ref, early_ref, late_ref, wp, mp, vp, wd, md, vd, mp2, vp2, up, md2, vd2, ud, sums
+):
+    factor = factor_ref[0]
+    layer = pl.program_id(0)
+    sub = wp.shape[1] // subs
+    wide = wp.shape[2] // cols
+
+    def go(g_ref):
+        squares = [0.0, 0.0]
+
+        def put(n, at, refs, outs, g):
+            new = moments(refs[0][at], g * factor, refs[1][at], refs[2][at])
+            for out, value in zip(outs, new):
+                out[at] = value
+            squares[n] = squares[n] + jnp.sum(new[2] * new[2], 0, keepdims=True)
+
+        for c in range(cols):
+            for k in range(subs):
+                g = g_ref[c * subs + k].astype(f32).reshape(2 * sub, wide)
+                at = (0, slice(k * sub, (k + 1) * sub), slice(c * wide, (c + 1) * wide))
+                put(0, at, (wp, mp, vp), (mp2, vp2, up), g[:sub])
+                rows = slice((c * subs + k) * sub, (c * subs + k + 1) * sub)
+                for half in range(2):
+                    at = (0, half, rows, slice(0, D))
+                    put(1, at, (wd, md, vd), (md2, vd2, ud), g[sub:, half * D : (half + 1) * D])
+        for n in range(2):
+            sums[0, n : n + 1, :] = jnp.broadcast_to(jnp.sum(squares[n], 1, keepdims=True), (1, LANES))
+
+    pl.when(layer >= late)(lambda: go(early_ref))
+    pl.when(layer < late)(lambda: go(late_ref))
+
+
+def group_sums(arrs, layered=None):
     embed, proj, downs, taps, head, gains, biases = arrs
     first = jnp.stack([jnp.sum(embed), jnp.sum(head), jnp.sum(gains), jnp.sum(biases)])
-    rest = [jnp.sum(a.reshape(a.shape[0], -1), 1) for a in (proj, downs, taps)]
-    return jnp.concatenate([first] + rest)
+    if layered is None:
+        layered = [jnp.sum(a.reshape(a.shape[0], -1), 1) for a in (proj, downs)]
+    return jnp.concatenate([first, *layered, jnp.sum(taps.reshape(taps.shape[0], -1), 1)])
 
 
 def spread_ratio(ratio):
@@ -530,20 +587,6 @@
         own = lax.dynamic_slice_in_dim(twice, (blocks - image) % blocks, blocks, 0)
         return own.reshape(tok, -1)
 
-    def from_team(v):
-        parts = v.reshape(blocks, rows * W, -1)
-        got = []
-        for r, pairs in enumerate(routes):
-            send = lax.dynamic_index_in_dim(parts, (image + r) % blocks, 0, keepdims=False)
-            got.append(lax.ppermute(send, "seq", [(b, a) for a, b in pairs]))
-        got = jnp.stack(got)
-        return jnp.stack(
-            [
-                lax.dynamic_index_in_dim(got, (back_block - i) % blocks, 0, keepdims=False)
-                for i in range(img_dev)
-            ]
-        )
-
     cols = 4
     subs = n_seq // cols
     row_in = D // n_dp
@@ -575,11 +618,23 @@
         got = got.reshape(n_dp, cols, subs, sub_in, wide).transpose(0, 2, 3, 1, 4)
         return got.reshape(D, cols * wide)
 
-    small = jnp.concatenate(
-        [to_bf(dw_kernel).reshape(-1), to_bf(norm_gain).reshape(-1), to_bf(norm_bias).reshape(-1)]
-    )
-    groups = [[0], [1, 2], [3, 4, 5]]
-    extra = [[part_of(to_bf(embed_w).reshape(-1)), part_of(small)], [], [part_of(to_bf(head_w).reshape(-1))]]
+    dp_pos = lax.axis_index("dp")
+
+    def over_dp(v):
+        got = [v] + [
+            lax.ppermute(v, "dp", [((d + j) % n_dp, d) for d in range(n_dp)])
+            for j in range(1, n_dp)
+        ]
+        return lax.dynamic_slice_in_dim(jnp.stack(got + got), (n_dp - dp_pos) % n_dp, n_dp, 0)
+
+    embed16 = over_dp(to_bf(embed_w)).reshape(-1, D)
+    taps16 = over_dp(to_bf(dw_kernel).reshape(LAYERS * 9, -1))
+    norms16 = over_dp(to_bf(jnp.stack([norm_gain, norm_bias])))
+    taps32 = taps16.transpose(1, 0, 2).reshape(LAYERS, 9, FF).astype(f32)
+    norms32 = norms16.transpose(1, 2, 0, 3).reshape(2, -1, D).astype(f32)
+    gain32, bias32 = norms32[0], norms32[1]
+    groups = [[0, 1, 2, 3], [4, 5]]
+    extra = [[], [part_of(to_bf(head_w).reshape(-1))]]
     layers16, extras = ([], [])
     for members, more in zip(groups, extra):
         parts = more + [p for l in members for p in layer_part(l)]
@@ -587,22 +642,11 @@
         extras += [g.reshape(n_dp, -1) for g in got[: len(more)]]
         got = got[len(more) :]
         layers16 += [(proj_of(got[2 * i]), got[2 * i + 1].reshape(FF, 2 * D)) for i in range(len(members))]
-    embed16 = extras[0][:, : embed_w.size].reshape(-1, D)
-    head16 = extras[2][:, : head_w.size].reshape(D, CLS)
-    small = extras[1].astype(f32)
-    n_taps = dw_kernel.size
-    n_gain = norm_gain.size
-    taps32 = small[:, :n_taps].reshape(n_dp, LAYERS * 9, -1).transpose(1, 0, 2)
-    taps32 = taps32.reshape(LAYERS, 9, FF)
-    gain32 = small[:, n_taps : n_taps + n_gain].reshape(n_dp, -1, row_in).transpose(1, 0, 2)
-    gain32 = gain32.reshape(-1, D)
-    bias32 = small[:, n_taps + n_gain : n_taps + 2 * n_gain].reshape(n_dp, -1, row_in)
-    bias32 = bias32.transpose(1, 0, 2).reshape(-1, D)
+    head16 = extras[0][:, : head_w.size].reshape(D, CLS)
 
     def own(v):
         return lax.dynamic_index_in_dim(v, image, 0, keepdims=False)
 
-    dp_pos = lax.axis_index("dp")
     wanted = own(partners)
     partner_label = jnp.zeros((), jnp.int32)
     for j in range(n_dp):
@@ -653,18 +697,19 @@
     input_outs = [half, half, ((keys_own, D), f32), ((keys_own, D), bf16), ((keys_own, 2 * D), bf16)]
     ln_out = ((2, D), f32)
 
-    embedded = dot(patches.reshape(-1, patches.shape[-1]), embed16)
-    embedded = embedded.reshape(img_dev, rows, HALF, 2, D).transpose(0, 1, 3, 2, 4)
-    e = to_team(embedded.reshape(img_dev, rows * W, D))
+    spread = patches.reshape(img_dev, rows, HALF, 2, -1).transpose(0, 1, 3, 2, 4)
+    patch_own = to_team(spread.reshape(img_dev, rows * W, -1))
+    e, x = run(2, embed_body, [full, full], patch_own, embed16, ln_first)
     w = wts[0]
-    x, a16, q16, r, rn16, kv16 = run(
-        first_body, [full] + input_outs, e, ln_first, w["gain"], w["bias"], w["wq"], w["wsr"], w["wkv"]
+    a16, q16, r, rn16, kv16 = run(
+        2, first_body, input_outs, x, w["gain"], w["bias"], w["wq"], w["wsr"], w["wkv"]
     )
     kept = []
     for l in range(LAYERS):
         w = wts[l]
         kv_all = all_keys(kv16)
         o16, lse, x2, b16, h16 = run(
+            4,
             middle_body,
             [half, ((HEADS, tok), f32), full, half, wide16],
             q16,
@@ -685,6 +730,7 @@
         if l + 1 < LAYERS:
             n = wts[l + 1]
             keep["g16"], keep["slope"], x, a16, q16, r, rn16, kv16 = run(
+                8,
                 join_body,
                 [wide16, ((tok, FF), f32), full] + input_outs,
                 *shared,
@@ -696,6 +742,7 @@
             )
         else:
             keep["g16"], keep["slope"], x, pool = run(
+                7,
                 last_body,
                 [wide16, ((tok, FF), f32), full, ((1, D), f32)],
                 *shared,
@@ -708,6 +755,7 @@
     for j in range(1, team):
         whole = whole + lax.ppermute(pool, "seq", between(j, True))
     loss_own, pooled16, dlog16, dln_last, dx, dy16, dz16 = run(
+        4,
         functools.partial(head_body, images),
         [((1, 1), f32), ((1, D), bf16), ((1, CLS), bf16), ln_out, full, half, wide16],
         whole,
@@ -735,38 +783,96 @@
     loss_seq = jnp.sum(loss_parts)
 
     piece = ((cols, n_dp, 2 * sub_in, wide), f32)
-    paired = subs == 2
+    paired = subs == 2 and cols == 4
+    chip = seq_pos // subs
+    where = jnp.stack([core, chip, dp_pos]).astype(jnp.int32)
 
     def weight_grads(*args):
         vm = pl.BlockSpec(memory_space=pltpu.VMEM)
         outs = [piece] * 2 if paired else [((cols, subs) + piece[0][1:], f32)]
-        got = pl.pallas_call(
+        return pl.pallas_call(
             functools.partial(weight_grads_body, n_dp, cols, subs),
             out_shape=[jax.ShapeDtypeStruct(s, d) for s, d in outs],
             in_specs=[pl.BlockSpec(memory_space=pltpu.SMEM)] + [vm] * len(args),
             out_specs=[vm] * len(outs),
             scratch_shapes=[pltpu.VMEM((D, cols * wide), f32), pltpu.VMEM((FF, 2 * D), f32)],
             compiler_params=pltpu.CompilerParams(vmem_limit_bytes=48 << 20),
-        )(core.reshape(1), *args)
-        if paired:
-            return got[0] + lax.ppermute(got[1], "seq", [(d ^ 1, d) for d in range(n_seq)])
-        return got[0]
+            cost_estimate=cost(6),
+        )(where, *args)
+
+    def padded_rest(parts):
+        flat = jnp.concatenate(parts, 1)
+        size = -(-flat.shape[1] // (8 * wide * n_seq)) * 8 * wide * n_seq
+        flat = jnp.pad(flat, ((0, 0), (0, size - flat.shape[1])))
+        flat = flat.reshape(n_dp, cols, subs, -1, wide).transpose(1, 2, 0, 3, 4)
+        if not paired:
+            return [flat]
+        flat = jnp.stack([lax.dynamic_index_in_dim(flat, chip ^ j, 0, False) for j in range(cols)])
+        twice = jnp.concatenate([flat, flat], 2)
+        flat = lax.dynamic_slice_in_dim(twice, dp_pos, n_dp, 2)
+        return [lax.dynamic_index_in_dim(flat, k, 1, False) for k in (core, 1 - core)]
+
+    def pair_sum(parts):
+        mine, send = parts
+        return mine + lax.ppermute(send, "seq", [(d ^ 1, d) for d in range(n_seq)])
+
+    def plane_sum(y):
+        total = y[0]
+        for j in range(1, cols):
+            pairs = [(d ^ (j * subs), d) for d in range(n_seq)]
+            total = total + lax.ppermute(to_bf(y[j]), "seq", pairs).astype(f32)
+        return total
+
+    def dp_sum(y):
+        total = y[0]
+        for j in range(1, n_dp):
+            pairs = [(d, (d + j) % n_dp) for d in range(n_dp)]
+            total = total + lax.ppermute(y[j], "dp", pairs)
+        return total
+
+    def whole_sum(parts):
+        y = jnp.concatenate([p[0] for p in parts], -2)
+        y = lax.psum_scatter(y.reshape(-1, wide), "seq", scatter_dimension=0, tiled=True)
+        return lax.psum_scatter(y, "dp", scatter_dimension=0, tiled=True)
+
+    def tied(value, others):
+        return lax.optimization_barrier((value, others))
+
+    stages = [pair_sum, plane_sum, dp_sum]
+    pieces = []
+
+    def advance(now):
+        if not paired:
+            return now
+        ready = [p for p in pieces if p[0] < len(stages)]
+        now, values = tied(now, [p[1] for p in ready])
+        for p, v in zip(ready, values):
+            p[1] = stages[p[0]](v)
+            p[0] += 1
+        return now
 
     grads = [None] * LAYERS
+    pieces.append([0, padded_rest([d_head.reshape(n_dp, -1)])])
+    waiting = None
     for l in reversed(range(LAYERS)):
         w, k = wts[l], kept[l]
         zlow, zhigh = edges(dz16)
         dh16, d_taps, dln2, dx2, dy2, dq16, dkv = run(
+            11,
             block_back_body,
             [wide16, ((9, FF), f32), ln_out, full, half, half, ((team * keys_own, 2 * D), f32)],
             k["h16"], k["hlow"], k["hhigh"], dz16, zlow, zhigh, w["taps"], w["w1"], k["x2"], w["gain"], dx,
             w["wo"], k["q16"], k["kv"], shut, k["lse"],
         )
+        if waiting is not None:
+            pieces.append([0, weight_grads(*waiting)])
         dkv_own = own_keys(dkv)
+        dkv_own = advance(dkv_own)
         upper = dy16
         shared = (dkv_own, w["wkv"], k["r"], w["gain"], dq16, w["wq"], w["wsr"], k["x"], dx2)
         if l:
             dr16, dln, dx, dy16, dz16 = run(
+                6,
                 join_back_body,
                 [((keys_own, D), bf16), ((4, D), f32), full, half, wide16],
                 *shared,
@@ -775,30 +881,25 @@
             )
         else:
             dr16, dln, de16, dln_first = run(
+                3,
                 first_back_body,
                 [((keys_own, D), bf16), ((4, D), f32), half, ln_out],
                 *shared,
                 e,
                 ln_first,
             )
+        waiting = (k["a16"], dq16, k["rn16"], dkv_own, k["o16"], dy2, k["b16"], dh16, dr16, k["g16"], upper)
         grads[l] = (
-            weight_grads(
-                k["a16"], dq16, k["rn16"], dkv_own, k["o16"], dy2, k["b16"], dh16, dr16, k["g16"], upper
-            ),
-            None,
             d_taps,
             jnp.concatenate([dln[0:2], dln2[0:1]], 0),
             jnp.concatenate([dln[2:4], dln2[1:2]], 0),
         )
-    de = from_team(de16).reshape(img_dev, rows, 2, HALF, D).transpose(0, 1, 3, 2, 4)
-    d_embed = contract(patches.reshape(-1, patches.shape[-1]), de.reshape(-1, D))
-    d_gain = jnp.concatenate([dln_first[0:1]] + [g[3] for g in grads] + [dln_last[0:1]], 0)
-    d_bias = jnp.concatenate([dln_first[1:2]] + [g[4] for g in grads] + [dln_last[1:2]], 0)
-
-    d_taps = jnp.stack([g[2] for g in grads])
+    (d_embed,) = run(3, embed_back_body, [((embed16.shape[0], D), f32)], patch_own, de16)
+    d_gain = jnp.concatenate([dln_first[0:1]] + [g[1] for g in grads] + [dln_last[0:1]], 0)
+    d_bias = jnp.concatenate([dln_first[1:2]] + [g[2] for g in grads] + [dln_last[1:2]], 0)
+    d_taps = jnp.stack([g[0] for g in grads])
     rest = [
         d_embed.reshape(n_dp, -1),
-        d_head.reshape(n_dp, -1),
         d_taps.reshape(LAYERS * 9, n_dp, -1).transpose(1, 0, 2).reshape(n_dp, -1),
         d_gain.reshape(-1, n_dp, row_in).transpose(1, 0, 2).reshape(n_dp, -1),
         d_bias.reshape(-1, n_dp, row_in).transpose(1, 0, 2).reshape(n_dp, -1),
@@ -806,69 +907,85 @@
     cuts = [0]
     for part in rest:
         cuts.append(cuts[-1] + part.shape[1])
-    size = -(-cuts[-1] // (8 * wide * n_seq)) * 8 * wide * n_seq
-    rest = jnp.pad(jnp.concatenate(rest, 1), ((0, 0), (0, size - cuts[-1])))
-    rest = rest.reshape(n_dp, cols, subs, -1, wide).transpose(1, 2, 0, 3, 4)
+    last = weight_grads(*waiting)
+    rest = padded_rest(rest)
+    pieces.append([0, [jnp.concatenate([a, b], -2) for a, b in zip(last, rest)]])
     if paired:
-        mine = lax.dynamic_index_in_dim(rest, core, 1, keepdims=False)
-        send = lax.dynamic_index_in_dim(rest, 1 - core, 1, keepdims=False)
-        rest = mine + lax.ppermute(send, "seq", [(d ^ 1, d) for d in range(n_seq)])
-
-    def scattered(parts):
-        both = jnp.concatenate([to_bf(p) for p in parts], -2)
-        both = both.reshape(-1, wide)
-        if paired:
-            chips = [[c * subs + k for c in range(cols)] for k in range(subs)]
-            both = lax.psum_scatter(
-                both, "seq", scatter_dimension=0, tiled=True, axis_index_groups=chips
-            )
-        else:
-            both = lax.psum_scatter(both, "seq", scatter_dimension=0, tiled=True)
-        return lax.psum_scatter(both.astype(f32), "dp", scatter_dimension=0, tiled=True)
-
-    chunks = [
-        scattered([grads[5][0], grads[4][0]]),
-        scattered([grads[3][0], grads[2][0]]),
-        scattered([grads[1][0], grads[0][0], rest]),
-    ]
-    got = lax.all_gather(jnp.concatenate(chunks, 0), "seq", axis=0, tiled=False)
-    proj_sums, down_sums = ([], [])
-    for n in range(LAYERS):
-        block = got[:, 2 * sub_in * n : 2 * sub_in * (n + 1)]
-        g_proj = block[:, :sub_in].reshape(cols, subs, sub_in, wide).transpose(1, 2, 0, 3)
-        proj_sums.append(g_proj.reshape(row_in, cols * wide))
-        g_down = block[:, sub_in:].reshape(-1, 2, D).transpose(1, 0, 2)
-        down_sums.append(g_down)
-    got = got[:, 2 * sub_in * LAYERS :].reshape(-1)
-    got = [got[a:b] for a, b in zip(cuts, cuts[1:])]
+        while any(p[0] < len(stages) for p in pieces):
+            for p in pieces:
+                if p[0] < len(stages):
+                    p[1] = stages[p[0]](p[1])
+                    p[0] += 1
+        sums = [p[1] for p in pieces]
+    else:
+        sums = [whole_sum([p[1]]) for p in pieces]
+
+    late = 2
+
+    def together(parts):
+        return lax.all_gather(to_bf(jnp.concatenate(parts, 0)), "seq", axis=0, tiled=False)
+
+    early_got = together(sums[1 : LAYERS + 1 - late] + sums[:1])
+    late_got = together(sums[LAYERS + 1 - late :])
+    head_start = (LAYERS - late) * 2 * sub_in
+    g_head = early_got[:, head_start:].reshape(-1)[: head_w.size].reshape(head_w.shape).astype(f32)
+    flat = late_got[:, late * 2 * sub_in :].reshape(-1).astype(f32)
+    flat = [flat[a:b] for a, b in zip(cuts, cuts[1:])]
     shards = (
-        got[0].reshape(embed_w.shape),
-        jnp.stack(proj_sums[::-1]),
-        jnp.stack(down_sums[::-1]),
-        got[2].reshape(dw_kernel.shape),
-        got[1].reshape(head_w.shape),
-        got[3].reshape(norm_gain.shape),
-        got[4].reshape(norm_bias.shape),
+        flat[0].reshape(embed_w.shape),
+        None,
+        None,
+        flat[1].reshape(dw_kernel.shape),
+        g_head,
+        flat[2].reshape(norm_gain.shape),
+        flat[3].reshape(norm_bias.shape),
     )
 
-    gsq_local = sum((jnp.sum(g * g) for g in shards))
+    gsq_local = sum(jnp.sum(jnp.square(g.astype(f32))) for g in (early_got, late_got))
     wsq_local = group_sums(tuple((w * w for w in masters)))
     gsq, wsq, loss = lax.psum((gsq_local, wsq_local, loss_seq), "dp")
     grad_norm = jnp.sqrt(gsq)
     factor = jnp.minimum(1.0, clip_limit / grad_norm)
+
+    proj_spec = pl.BlockSpec((1,) + in_proj.shape[1:], lambda l: (l, 0, 0))
+    down_spec = pl.BlockSpec((1,) + down_proj.shape[1:], lambda l: (l, 0, 0, 0))
+    block = (n_seq, 2 * sub_in, wide)
+    blocks_of = [early_got, late_got]
+    if 2 * sub_in % 8:
+        block = (n_seq, 1, 2 * sub_in, wide)
+        counts = (LAYERS - late, late)
+        blocks_of = [
+            g[:, : n * 2 * sub_in].reshape(n_seq, n, 2 * sub_in, wide)
+            for g, n in zip(blocks_of, counts)
+        ]
+    tail = (0,) * (len(block) - 2)
+    got = pl.pallas_call(
+        functools.partial(update_body, cols, subs, late),
+        grid=(LAYERS,),
+        out_shape=[jax.ShapeDtypeStruct(in_proj.shape, f32)] * 3
+        + [jax.ShapeDtypeStruct(down_proj.shape, f32)] * 3
+        + [jax.ShapeDtypeStruct((LAYERS, 2, LANES), f32)],
+        in_specs=[
+            pl.BlockSpec(memory_space=pltpu.SMEM),
+            pl.BlockSpec(block, lambda l: (0, jnp.minimum(LAYERS - 1 - l, LAYERS - 1 - late), *tail)),
+            pl.BlockSpec(block, lambda l: (0, jnp.maximum(late - 1 - l, 0), *tail)),
+        ]
+        + [proj_spec] * 3
+        + [down_spec] * 3,
+        out_specs=[proj_spec] * 3 + [down_spec] * 3 + [pl.BlockSpec((1, 2, LANES), lambda l: (l, 0, 0))],
+        compiler_params=pltpu.CompilerParams(vmem_limit_bytes=56 << 20),
+        cost_estimate=cost(25),
+    )(factor.reshape(1), *blocks_of, in_proj, m_proj, v_proj, down_proj, m_down, v_down)
+    big = {1: got[0:3], 2: got[3:6]}
     new_m, new_v, updates = ([], [], [])
-    for w, g, m, v in zip(masters, shards, firsts, seconds):
-        g = g * factor
-        m2 = beta_one * m + (1.0 - beta_one) * g
-        v2 = beta_two * v + (1.0 - beta_two) * g * g
-        u = (
-            m2 / (1.0 - beta_one**STEP) / (jnp.sqrt(v2 / (1.0 - beta_two**STEP)) + lamb_eps)
-            + decay_rate * w
-        )
+    for n, (w, g, m, v) in enumerate(zip(masters, shards, firsts, seconds)):
+        m2, v2, u = big[n] if n in big else moments(w, g * factor, m, v)
         new_m.append(m2)
         new_v.append(v2)
         updates.append(u)
-    usq = lax.psum(group_sums(tuple((u * u for u in updates))), "dp")
+    usq = lax.psum(
+        group_sums(tuple((u * u for u in updates)), [got[6][:, 0, 0], got[6][:, 1, 0]]), "dp"
+    )
     wnorm = jnp.sqrt(wsq)
     unorm = jnp.sqrt(usq)
     ratio = wnorm / unorm

time: 1180 us -> 970 us (0.82)
  local copies, waits for them, and re-layouts: 325 us -> 169 us
  waiting for transfers between devices: 340 us -> 251 us
  starting transfers between devices: 105 us -> 150 us
  Pallas kernels: 209 us -> 241 us
  other arithmetic: 127 us -> 100 us
    reduce_scatter x5 -> x0, waiting for transfers between devices: 185 us -> none  [the longest x3 110 us: scattered(): lax.psum_scatter(both, 'seq', scatter_dimension=0, tiled=True, axis_index...]
    ppermute x11 -> x58, waiting for transfers between devices: 3.16 us -> 147 us  [the longest x21 87.1 us: plane_sum(): total = total + lax.ppermute(to_bf(y[j]), 'seq', pairs).astype(f32)]
    unnamed x883 -> x751, local copies, waits for them, and re-layouts: 128 us -> 70.8 us
    ppermute x11 -> x58, starting transfers between devices: 13.3 us -> 68.4 us  [the longest x21 26.2 us: dp_sum(): total = total + lax.ppermute(y[j], 'dp', pairs)]
    all_gather x1 -> x2, waiting for transfers between devices: 55.1 us -> 3.22 us  [together(): lax.all_gather(to_bf(jnp.concatenate(parts, 0)), 'seq', axis=0, tiled=False)]
    all_gather x3 -> x2, waiting for transfers between devices: 42.4 us -> 89.4 us  [gathered(): lax.all_gather(jnp.concatenate(parts, 0), ('dp', 'seq'), axis=0, tiled=Fa...]
    unnamed x11 -> x4, waiting for transfers between devices: 45.1 us -> 0.07 us
    reshape x23 -> x4, local copies, waits for them, and re-layouts: 30.4 us -> 3.82 us  [the longest x1 3.28 us: per_device(): head16 = extras[0][:, :head_w.size].reshape(D, CLS)]
  transfers between devices with their start and end apart: 68 -> 109, of which waited for: 19 -> 33; matrix products, arithmetic and copies ran while one was open for 22% -> 14% of each run, Pallas kernels for 13% -> 18%
where the time goes in v2:
time: 970 us; the launch traced here: 962 us
  waiting for transfers between devices  251 us (26%)
  Pallas kernels  241 us (25%)
  local copies, waits for them, and re-layouts  169 us (17%)
  starting transfers between devices  150 us (15%)
  other arithmetic  100 us (10%)
  between operations  30.2 us (3%)
  blocking collectives  21.4 us (2%)
    pallas_call x28, Pallas kernels, run(): pl.pallas_call(body, out_shape=[jax.ShapeDtypeStruct(s, d) for s, d in ou...  176 us
    all_gather x2, waiting for transfers between devices, gathered(): lax.all_gather(jnp.concatenate(parts, 0), ('dp', 'seq'), axis=0, tiled=Fa...  89.4 us
    ppermute x21, waiting for transfers between devices, plane_sum(): total = total + lax.ppermute(to_bf(y[j]), 'seq', pairs).astype(f32)  87.1 us
    unnamed x751, local copies, waits for them, and re-layouts  70.8 us
    ppermute x12, starting transfers between devices, edges(): low = lax.ppermute(v[-W:], 'seq', between(-1, False))  41.7 us
    pallas_call x6, Pallas kernels, weight_grads(): pl.pallas_call(functools.partial(weight_grads_body, n_dp, cols, subs), ou...  38.3 us
    ppermute x21, waiting for transfers between devices, dp_sum(): total = total + lax.ppermute(y[j], 'dp', pairs)  36.1 us
    pallas_call x1, Pallas kernels, per_device(): pl.pallas_call(functools.partial(update_body, cols, subs, late), grid=(LA...  26.4 us
  transfers between devices with their start and end apart: 109, of which 33 were waited for; matrix products, arithmetic and copies ran while one was open for 14% of the time, Pallas kernels for 18%

profile of v2, /device:TPU:0, one launch (start us, length us, event | category | flops | bytes accessed | tf_op | source)
XLA Modules:
  0.0 961.6 jit_solution(312271107333359790)
XLA Ops:
  74.4 20.2 %collective-permute-done.4 = bf16[288,320]{1,0:T(8,128)(2,1)S(1)} collective-permute-done((bf16[288,320]{1,0:T(8,128)(2,1)S(1)}, bf16[288,320]{1,0:T(8,128)(2,1)S(1)}, u32[]{:S(2)}, u32[]{:S(2)}) %collective-permute-start.4) | collective-permute-done | bytes 184352 | tf_op jit(solution)/shard_map/ppermute | solution.py:625
  122.8 89.4 %all-gather.11.cloned.1.call-done = bf16[10240,640]{1,0:T(8,128)(2,1)} async-done(((bf16[320,640]{1,0:T(8,128)(2,1)}), bf16[10240,640]{1,0:T(8,128)(2,1)}) %all-gather.11.cloned.1.call-update) | async-done | bytes 13107216 | tf_op jit(solution)/shard_map/all_gather | solution.py:612
  241.2 8.3 shard_map.444
  264.3 8.1 shard_map.446
  286.8 8.1 shard_map.448
  309.6 8.1 shard_map.450
  332.3 8.1 shard_map.452
  414.9 10.8 %shard_map.456 = (bf16[512,1280]{1,0:T(8,128)(2,1)}, f32[9,1280]{1,0:T(8,128)S(1)}, f32[2,320]{1,0:T(2,128)S(1)}, f32[512,320]{1,0:T(8,128)S(1)}, bf16[512,320]{...) custom-call(bf16[512,1280]{1,0:T(8,128)(2,1)} %copy-done.65, ...), custom_call_target="tpu_custom_call" | custom-call | flops 11000000512 | bytes 33000000 | tf_op jit(solution)/shard_map/pallas_call | solution.py:87
  446.4 10.6 %shard_map.458 = (bf16[512,1280]{1,0:T(8,128)(2,1)}, f32[9,1280]{1,0:T(8,128)S(1)}, f32[2,320]{1,0:T(2,128)S(1)}, f32[512,320]{1,0:T(8,128)S(1)}, bf16[512,320]{...) custom-call(bf16[512,1280]{1,0:T(8,128)(2,1)} %copy-done.64, ...), custom_call_target="tpu_custom_call" | custom-call | flops 11000000512 | bytes 33000000 | tf_op jit(solution)/shard_map/pallas_call | solution.py:87
  483.3 10.6 %shard_map.461 = (bf16[512,1280]{1,0:T(8,128)(2,1)}, f32[9,1280]{1,0:T(8,128)S(1)}, f32[2,320]{1,0:T(2,128)S(1)}, f32[512,320]{1,0:T(8,128)S(1)}, bf16[512,320]{...) custom-call(bf16[512,1280]{1,0:T(8,128)(2,1)} %copy-done.63, ...), custom_call_target="tpu_custom_call" | custom-call | flops 11000000512 | bytes 33000000 | tf_op jit(solution)/shard_map/pallas_call | solution.py:87
  523.3 10.6 %shard_map.464 = (bf16[512,1280]{1,0:T(8,128)(2,1)}, f32[9,1280]{1,0:T(8,128)S(1)}, f32[2,320]{1,0:T(2,128)S(1)}, f32[512,320]{1,0:T(8,128)S(1)}, bf16[512,320]{...) custom-call(bf16[512,1280]{1,0:T(8,128)(2,1)} %copy-done.62, ...), custom_call_target="tpu_custom_call" | custom-call | flops 11000000512 | bytes 33000000 | tf_op jit(solution)/shard_map/pallas_call | solution.py:87
  571.1 10.6 %shard_map.467 = (bf16[512,1280]{1,0:T(8,128)(2,1)}, f32[9,1280]{1,0:T(8,128)S(1)}, f32[2,320]{1,0:T(2,128)S(1)}, f32[512,320]{1,0:T(8,128)S(1)}, bf16[512,320]{...) custom-call(bf16[512,1280]{1,0:T(8,128)(2,1)} %copy-done.61, ...), custom_call_target="tpu_custom_call" | custom-call | flops 11000000512 | bytes 33000000 | tf_op jit(solution)/shard_map/pallas_call | solution.py:87
  593.8 8.7 collective-permute-done.66
  634.3 11.0 %shard_map.470 = (bf16[512,1280]{1,0:T(8,128)(2,1)}, f32[9,1280]{1,0:T(8,128)S(1)}, f32[2,320]{1,0:T(2,128)S(1)}, f32[512,320]{1,0:T(8,128)S(1)}, bf16[512,320]{...) custom-call(bf16[512,1280]{1,0:T(8,128)(2,1)} %copy-done.60, ...), custom_call_target="tpu_custom_call" | custom-call | flops 11000000512 | bytes 33000000 | tf_op jit(solution)/shard_map/pallas_call | solution.py:87
  653.1 8.5 collective-permute-done.77
  661.6 8.7 collective-permute-done.76
  735.0 7.8 collective-permute-done.86
  771.5 8.3 collective-permute-done.94
  784.6 14.4 %collective-permute-done.99 = bf16[4,104,640]{2,1,0:T(8,128)(2,1)S(1)} collective-permute-done((bf16[4,104,640]{2,1,0:T(8,128)(2,1)S(1)}, bf16[4,104,640]{2,1,0:T(8,128)(2,1)S(1)}, u32[]{:S(2)}, u32[]{:S(2)}) %collective-permute-start.99) | collective-permute-done | bytes 532512 | tf_op jit(solution)/shard_map/ppermute | solution.py:823
  798.9 10.2 %collective-permute-done.101 = bf16[4,104,640]{2,1,0:T(8,128)(2,1)S(1)} collective-permute-done((bf16[4,104,640]{2,1,0:T(8,128)(2,1)S(1)}, bf16[4,104,640]{2,1,0:T(8,128)(2,1)S(1)}, u32[]{:S(2)}, u32[]{:S(2)}) %collective-permute-start.101) | collective-permute-done | bytes 532512 | tf_op jit(solution)/shard_map/ppermute | solution.py:823
  822.0 9.7 %collective-permute-done.103 = f32[104,640]{1,0:T(8,128)S(1)} collective-permute-done((f32[104,640]{1,0:T(8,128)S(1)}, f32[104,640]{1,0:T(8,128)S(1)}, u32[]{:S(2)}, u32[]{:S(2)}) %collective-permute-start.103) | collective-permute-done | bytes 266272 | tf_op jit(solution)/shard_map/ppermute | solution.py:830
  863.2 12.4 %psum.29 = f32[]{:T(128)} all-reduce(f32[]{:T(128)S(6)} %add.744), channel_id=1, replica_groups=mesh['dp'=4,'seq'=8] {'dp'}, use_global_device_ids=true, to_apply=%region_8.9 | all-reduce | flops 1 | bytes 8 | tf_op jit(solution)/shard_map/psum | solution.py:946
  881.0 26.4 %shard_map.475 = (f32[6,80,2560]{2,1,0:T(8,128)}, f32[6,80,2560]{2,1,0:T(8,128)}, f32[6,80,2560]{2,1,0:T(8,128)}, f32[6,2,320,320]{3,2,1,0:T(8,128)}, f32[6,2,32...) custom-call(f32[1]{0:T(128)} %bitcast.188.factor_ref, ...), custom_call_target="tpu_custom_call" | custom-call | flops 24999999488 | bytes 75000000 | tf_op jit(solution)/shard_map/pallas_call | solution.py:962
  921.3 9.0 all-reduce.3
  (1251 shorter events, 592.8 us)
Async XLA Ops:
  7.2 109.2 %all-gather.13.cloned.1.call-start = ((), (), s32[]{:S(2)}) async-start(), calls=%async_computation.3 | async-start | bytes 7434240 | tf_op jit(solution)/shard_map/all_gather | solution.py:612
  22.0 190.2 %all-gather.11.cloned.1.call-start = ((), (), s32[]{:S(2)}) async-start(), calls=%async_computation.2 | async-start | bytes 13516800 | tf_op jit(solution)/shard_map/all_gather | solution.py:612
  29.9 821.1 %all-gather.7.cloned.1.call-start = ((), (), s32[]{:S(2)}) async-start(), calls=%async_computation | async-start | bytes 3870720 | tf_op jit(solution)/shard_map/all_gather | solution.py:926
  35.1 305.8 %collective-permute-start.34 = (s32[3]{0:T(128)}, s32[3]{0:T(128)}, u32[]{:S(2)}, u32[]{:S(2)}) collective-permute-start(s32[3]{0:T(128)} %param.28), channel_id=1, source_target_pairs={{24,0},{0,8},{8,16},{16,24},{25,1},{1,9},{9,17},{17,25},{26,2},{2,... | collective-permute-start | bytes 44 | tf_op jit(solution)/shard_map/ppermute | solution.py:655
  35.1 320.9 %collective-permute-start.33 = (s32[3]{0:T(128)}, s32[3]{0:T(128)}, u32[]{:S(2)}, u32[]{:S(2)}) collective-permute-start(s32[3]{0:T(128)} %param.28), channel_id=1, source_target_pairs={{16,0},{24,8},{0,16},{8,24},{17,1},{25,9},{1,17},{9,25},{18,2},{26... | collective-permute-start | bytes 44 | tf_op jit(solution)/shard_map/ppermute | solution.py:655
  67.8 33.6 %collective-permute-start.6 = (bf16[288,320]{1,0:T(8,128)(2,1)S(1)}, bf16[288,320]{1,0:T(8,128)(2,1)S(1)}, u32[]{:S(2)}, u32[]{:S(2)}) collective-permute-start(bf16[288,320]{1,0:T(8,128)(2,1)S(1)} %get-tuple-element.565), channel_id=1, source_target_pairs={{24,0},{0,8},{8,16},{16,24},{25,1},{1,9},{9,17},{17,25},{26,2},{2,... | collective-permute-start | bytes 552968 | tf_op jit(solution)/shard_map/ppermute | solution.py:625
  460.3 33.7 %collective-permute-start.48 = (bf16[4,16,640]{2,1,0:T(8,128)(2,1)S(1)}, bf16[4,16,640]{2,1,0:T(8,128)(2,1)S(1)}, u32[]{:S(2)}, u32[]{:S(2)}) collective-permute-start(bf16[4,16,640]{2,1,0:T(8,128)(2,1)S(1)} %get-tuple-element.702), channel_id=1, source_target_pairs={{2,0},{3,1},{0,2},{1,3},{6,4},{7,5},{4,6},{5,7},{10,8},{11,9},{8,1... | collective-permute-start | bytes 245768 | tf_op jit(solution)/shard_map/ppermute | solution.py:823
  461.8 32.2 %collective-permute-start.50 = (bf16[4,16,640]{2,1,0:T(8,128)(2,1)S(1)}, bf16[4,16,640]{2,1,0:T(8,128)(2,1)S(1)}, u32[]{:S(2)}, u32[]{:S(2)}) collective-permute-start(bf16[4,16,640]{2,1,0:T(8,128)(2,1)S(1)} %get-tuple-element.703), channel_id=1, source_target_pairs={{6,0},{7,1},{4,2},{5,3},{2,4},{3,5},{0,6},{1,7},{14,8},{15,9},{12,... | collective-permute-start | bytes 245768 | tf_op jit(solution)/shard_map/ppermute | solution.py:823
  463.3 32.4 %collective-permute-start.51 = (f32[4,4,80,640]{3,2,1,0:T(8,128)}, f32[4,4,80,640]{3,2,1,0:T(8,128)}, u32[]{:S(2)}, u32[]{:S(2)}) collective-permute-start(f32[4,4,80,640]{3,2,1,0:T(8,128)} %get-tuple-element.303), channel_id=1, source_target_pairs={{1,0},{0,1},{3,2},{2,3},{5,4},{4,5},{7,6},{6,7},{9,8},{8,9},{11,10... | collective-permute-start | bytes 9830408 | tf_op jit(solution)/shard_map/ppermute | solution.py:817
  499.1 42.8 %collective-permute-start.58 = (f32[4,4,80,640]{3,2,1,0:T(8,128)}, f32[4,4,80,640]{3,2,1,0:T(8,128)}, u32[]{:S(2)}, u32[]{:S(2)}) collective-permute-start(f32[4,4,80,640]{3,2,1,0:T(8,128)} %get-tuple-element.326), channel_id=1, source_target_pairs={{1,0},{0,1},{3,2},{2,3},{5,4},{4,5},{7,6},{6,7},{9,8},{8,9},{11,10... | collective-permute-start | bytes 9830408 | tf_op jit(solution)/shard_map/ppermute | solution.py:817
  556.5 46.3 %collective-permute-start.68 = (f32[4,4,80,640]{3,2,1,0:T(8,128)}, f32[4,4,80,640]{3,2,1,0:T(8,128)}, u32[]{:S(2)}, u32[]{:S(2)}) collective-permute-start(f32[4,4,80,640]{3,2,1,0:T(8,128)} %get-tuple-element.350), channel_id=1, source_target_pairs={{1,0},{0,1},{3,2},{2,3},{5,4},{4,5},{7,6},{6,7},{9,8},{8,9},{11,10... | collective-permute-start | bytes 9830408 | tf_op jit(solution)/shard_map/ppermute | solution.py:817
  619.3 29.3 %collective-permute-start.69 = (f32[80,640]{1,0:T(8,128)}, f32[80,640]{1,0:T(8,128)}, u32[]{:S(2)}, u32[]{:S(2)}) collective-permute-start(f32[80,640]{1,0:T(8,128)} %get-tuple-element.683), channel_id=1, source_target_pairs={{0,8},{8,16},{16,24},{24,0},{1,9},{9,17},{17,25},{25,1},{2,10},{10... | collective-permute-start | bytes 614408 | tf_op jit(solution)/shard_map/ppermute | solution.py:830
  619.8 30.2 %collective-permute-start.71 = (f32[80,640]{1,0:T(8,128)}, f32[80,640]{1,0:T(8,128)}, u32[]{:S(2)}, u32[]{:S(2)}) collective-permute-start(f32[80,640]{1,0:T(8,128)} %get-tuple-element.684), channel_id=1, source_target_pairs={{0,24},{8,0},{16,8},{24,16},{1,25},{9,1},{17,9},{25,17},{2,26},{10... | collective-permute-start | bytes 614408 | tf_op jit(solution)/shard_map/ppermute | solution.py:830
  634.3 38.6 %collective-permute-start.78 = (f32[4,4,80,640]{3,2,1,0:T(8,128)}, f32[4,4,80,640]{3,2,1,0:T(8,128)}, u32[]{:S(2)}, u32[]{:S(2)}) collective-permute-start(f32[4,4,80,640]{3,2,1,0:T(8,128)} %get-tuple-element.374), channel_id=1, source_target_pairs={{1,0},{0,1},{3,2},{2,3},{5,4},{4,5},{7,6},{6,7},{9,8},{8,9},{11,10... | collective-permute-start | bytes 9830408 | tf_op jit(solution)/shard_map/ppermute | solution.py:817
  692.3 28.4 %collective-permute-start.79 = (f32[80,640]{1,0:T(8,128)}, f32[80,640]{1,0:T(8,128)}, u32[]{:S(2)}, u32[]{:S(2)}) collective-permute-start(f32[80,640]{1,0:T(8,128)} %get-tuple-element.680), channel_id=1, source_target_pairs={{0,8},{8,16},{16,24},{24,0},{1,9},{9,17},{17,25},{25,1},{2,10},{10... | collective-permute-start | bytes 614408 | tf_op jit(solution)/shard_map/ppermute | solution.py:830
  692.3 28.5 %collective-permute-start.81 = (f32[80,640]{1,0:T(8,128)}, f32[80,640]{1,0:T(8,128)}, u32[]{:S(2)}, u32[]{:S(2)}) collective-permute-start(f32[80,640]{1,0:T(8,128)} %get-tuple-element.681), channel_id=1, source_target_pairs={{0,24},{8,0},{16,8},{24,16},{1,25},{9,1},{17,9},{25,17},{2,26},{10... | collective-permute-start | bytes 614408 | tf_op jit(solution)/shard_map/ppermute | solution.py:830
  717.4 31.8 %collective-permute-start.91 = (f32[4,4,80,640]{3,2,1,0:T(8,128)}, f32[4,4,80,640]{3,2,1,0:T(8,128)}, u32[]{:S(2)}, u32[]{:S(2)}) collective-permute-start(f32[4,4,80,640]{3,2,1,0:T(8,128)} %get-tuple-element.390), channel_id=1, source_target_pairs={{1,0},{0,1},{3,2},{2,3},{5,4},{4,5},{7,6},{6,7},{9,8},{8,9},{11,10... | collective-permute-start | bytes 9830408 | tf_op jit(solution)/shard_map/ppermute | solution.py:817
  719.3 37.2 %collective-permute-start.98 = (f32[4,4,104,640]{3,2,1,0:T(8,128)}, f32[4,4,104,640]{3,2,1,0:T(8,128)}, u32[]{:S(2)}, u32[]{:S(2)}) collective-permute-start(f32[4,4,104,640]{3,2,1,0:T(8,128)} %pad_maximum_fusion), channel_id=1, source_target_pairs={{1,0},{0,1},{3,2},{2,3},{5,4},{4,5},{7,6},{6,7},{9,8},{8,9},{11,10... | collective-permute-start | bytes 12779528 | tf_op jit(solution)/shard_map/ppermute | solution.py:817
  749.1 109.5 %all-gather.9.cloned.1.call-start = ((), (), s32[]{:S(2)}) async-start(), calls=%async_computation.1 | async-start | bytes 2119680 | tf_op jit(solution)/shard_map/all_gather | solution.py:926
  759.6 39.3 %collective-permute-start.99 = (bf16[4,104,640]{2,1,0:T(8,128)(2,1)S(1)}, bf16[4,104,640]{2,1,0:T(8,128)(2,1)S(1)}, u32[]{:S(2)}, u32[]{:S(2)}) collective-permute-start(bf16[4,104,640]{2,1,0:T(8,128)(2,1)S(1)} %get-tuple-element.594), channel_id=1, source_target_pairs={{2,0},{3,1},{0,2},{1,3},{6,4},{7,5},{4,6},{5,7},{10,8},{11,9},{8,1... | collective-permute-start | bytes 1597448 | tf_op jit(solution)/shard_map/ppermute | solution.py:823
  761.2 48.0 %collective-permute-start.101 = (bf16[4,104,640]{2,1,0:T(8,128)(2,1)S(1)}, bf16[4,104,640]{2,1,0:T(8,128)(2,1)S(1)}, u32[]{:S(2)}, u32[]{:S(2)}) collective-permute-start(bf16[4,104,640]{2,1,0:T(8,128)(2,1)S(1)} %get-tuple-element.595), channel_id=1, source_target_pairs={{6,0},{7,1},{4,2},{5,3},{2,4},{3,5},{0,6},{1,7},{14,8},{15,9},{12,... | collective-permute-start | bytes 1597448 | tf_op jit(solution)/shard_map/ppermute | solution.py:823
  770.0 40.4 %collective-permute-start.100 = (bf16[4,104,640]{2,1,0:T(8,128)(2,1)S(1)}, bf16[4,104,640]{2,1,0:T(8,128)(2,1)S(1)}, u32[]{:S(2)}, u32[]{:S(2)}) collective-permute-start(bf16[4,104,640]{2,1,0:T(8,128)(2,1)S(1)} %get-tuple-element.596), channel_id=1, source_target_pairs={{4,0},{5,1},{6,2},{7,3},{0,4},{1,5},{2,6},{3,7},{12,8},{13,9},{14,... | collective-permute-start | bytes 1597448 | tf_op jit(solution)/shard_map/ppermute | solution.py:823
  780.7 34.0 %collective-permute-start.95 = (f32[80,640]{1,0:T(8,128)S(1)}, f32[80,640]{1,0:T(8,128)S(1)}, u32[]{:S(2)}, u32[]{:S(2)}) collective-permute-start(f32[80,640]{1,0:T(8,128)S(1)} %get-tuple-element.689), channel_id=1, source_target_pairs={{0,8},{8,16},{16,24},{24,0},{1,9},{9,17},{17,25},{25,1},{2,10},{10... | collective-permute-start | bytes 614408 | tf_op jit(solution)/shard_map/ppermute | solution.py:830
  780.9 33.7 %collective-permute-start.97 = (f32[80,640]{1,0:T(8,128)S(1)}, f32[80,640]{1,0:T(8,128)S(1)}, u32[]{:S(2)}, u32[]{:S(2)}) collective-permute-start(f32[80,640]{1,0:T(8,128)S(1)} %get-tuple-element.690), channel_id=1, source_target_pairs={{0,24},{8,0},{16,8},{24,16},{1,25},{9,1},{17,9},{25,17},{2,26},{10... | collective-permute-start | bytes 614408 | tf_op jit(solution)/shard_map/ppermute | solution.py:830
  (426 other events, 4845.4 us)
Sparse Core Ops, SparseCore 0:
  22.1 88.1 all-gather.12
  113.8 98.3 all-gather.10
  749.3 62.2 all-gather.6
  832.7 25.9 all-gather.8

commit v3 on v2

--- a/solution.py
+++ b/solution.py
@@ -79,19 +79,20 @@
 
 
 def cost(us):
-    return pl.CostEstimate(flops=int(us * 1e9), bytes_accessed=int(us * 3e6), transcendentals=0)
-
-
-def run(us, body, outs, *args):
+    return pl.CostEstimate(flops=int(us * 1e8), bytes_accessed=int(us * 1e5), transcendentals=0)
+
+
+def run(us, body, outs, *args, place=None):
     vm = pl.BlockSpec(memory_space=pltpu.VMEM)
+    scalars = [] if place is None else [place]
     return pl.pallas_call(
         body,
         out_shape=[jax.ShapeDtypeStruct(s, d) for s, d in outs],
-        in_specs=[vm] * len(args),
+        in_specs=[pl.BlockSpec(memory_space=pltpu.SMEM)] * len(scalars) + [vm] * len(args),
         out_specs=[vm] * len(outs),
         compiler_params=pltpu.CompilerParams(vmem_limit_bytes=48 << 20),
         cost_estimate=cost(us),
-    )(*args)
+    )(*scalars, *args)
 
 
 def cells_of(v):
@@ -128,7 +129,9 @@
     attention_inputs(x_ref[...], gain, bias, wq, wsr, wkv, *outs)
 
 
-def middle_body(q_ref, kv_ref, ok_ref, x_ref, gain, bias, wo, w1, o_ref, lse_ref, x2_ref, b_ref, h_ref):
+def middle_body(
+    place, q_ref, kv_ref, ok_ref, x_ref, gain, bias, wo, w1, o_ref, lse_ref, x2_ref, b_ref, h_ref, edge_ref
+):
     q = q_ref[...] * jnp.asarray(scale_qk, bf16)
     keys = kv_ref.shape[0]
     kv = kv_ref[...]
@@ -152,6 +155,7 @@
     b = to_bf(layer_norm(x2, gain[2:3], bias[2:3]))
     b_ref[...] = b
     h_ref[...] = to_bf(dot(b, w1[...]))
+    send_edge(place, h_ref, edge_ref)
 
 
 def shift_down(v):
@@ -172,23 +176,29 @@
     return jnp.concatenate([v[HALF:], shift_up(v[:HALF])], 0)
 
 
-def row_of(main, low, high, i, rows, lanes):
+def row_of(main, near, i, rows, lanes):
+    place, low, high = near
     if i < 0:
-        return low[:, lanes].astype(f32)
+        return jnp.where(place[0] > 0, low[:, lanes].astype(f32), 0.0)
     if i >= rows:
-        return high[:, lanes].astype(f32)
+        return jnp.where(place[1] > 0, high[:, lanes].astype(f32), 0.0)
     return main[i * W : (i + 1) * W, lanes].astype(f32)
 
 
-def conv_gelu(h_ref, low_ref, high_ref, taps_ref, g_ref, slope_ref):
+def send_edge(place, main, edge_ref):
+    start = pl.multiple_of(jnp.where(place[0] > 0, 0, main.shape[0] - W), W)
+    edge_ref[...] = main[pl.ds(start, W), :]
+
+
+def conv_gelu(h_ref, ends, taps_ref, g_ref, slope_ref):
     rows = h_ref.shape[0] // W
 
     def chunk(c, carry):
         lanes = pl.ds(pl.multiple_of(c * LANES, LANES), LANES)
         taps = [taps_ref[k : k + 1, lanes] for k in range(9)]
-        near = [row_of(h_ref, low_ref, high_ref, i, rows, lanes) for i in (-1, 0)]
+        near = [row_of(h_ref, ends, i, rows, lanes) for i in (-1, 0)]
         for i in range(rows):
-            near.append(row_of(h_ref, low_ref, high_ref, i + 1, rows, lanes))
+            near.append(row_of(h_ref, ends, i + 1, rows, lanes))
             sums = [
                 taps[j] * near[0] + taps[3 + j] * near[1] + taps[6 + j] * near[2] for j in range(3)
             ]
@@ -203,8 +213,8 @@
     lax.fori_loop(0, FF // LANES, chunk, 0)
 
 
-def last_body(h_ref, low_ref, high_ref, taps_ref, x2_ref, w2, ln_ref, ok_ref, g_ref, slope_ref, x_ref, sum_ref):
-    conv_gelu(h_ref, low_ref, high_ref, taps_ref, g_ref, slope_ref)
+def last_body(place, h_ref, low_ref, high_ref, taps_ref, x2_ref, w2, ln_ref, ok_ref, g_ref, slope_ref, x_ref, sum_ref):
+    conv_gelu(h_ref, (place, low_ref, high_ref), taps_ref, g_ref, slope_ref)
     x = x2_ref[...] + dot(g_ref[...], w2[...])
     x_ref[...] = x
     fin = layer_norm(x, ln_ref[0:1], ln_ref[1:2])
@@ -212,23 +222,25 @@
 
 
 def join_body(
-    h_ref, low_ref, high_ref, taps_ref, x2_ref, w2, gain, bias, wq, wsr, wkv, g_ref, slope_ref, x_ref, *outs
+    place, h_ref, low_ref, high_ref, taps_ref, x2_ref, w2, gain, bias, wq, wsr, wkv, g_ref, slope_ref, x_ref, *outs
 ):
-    conv_gelu(h_ref, low_ref, high_ref, taps_ref, g_ref, slope_ref)
+    conv_gelu(h_ref, (place, low_ref, high_ref), taps_ref, g_ref, slope_ref)
     x = x2_ref[...] + dot(g_ref[...], w2[...])
     x_ref[...] = x
     attention_inputs(x, gain, bias, wq, wsr, wkv, *outs)
 
 
-def gelu_back(dx, w2, slope_ref, dy_ref, dz_ref):
+def gelu_back(place, dx, w2, slope_ref, dy_ref, dz_ref, edge_ref):
     dy = to_bf(dx)
     dy_ref[...] = dy
     dg = to_bf(dot_nt(dy, w2[...])).astype(f32)
     dz_ref[...] = to_bf(dg * slope_ref[...])
+    send_edge(place, dz_ref, edge_ref)
 
 
 def head_body(
     images,
+    place,
     pool_ref,
     count_ref,
     head_ref,
@@ -245,6 +257,7 @@
     dx_ref,
     dy_ref,
     dz_ref,
+    edge_ref,
 ):
     count = count_ref[...]
     pooled = to_bf(pool_ref[...] / count)
@@ -262,10 +275,10 @@
     dln_ref[0:1, :] = dgain
     dln_ref[1:2, :] = dbias
     dx_ref[...] = dx
-    gelu_back(dx, w2, slope_ref, dy_ref, dz_ref)
-
-
-def conv_back(h_ref, hlow_ref, hhigh_ref, dz_ref, zlow_ref, zhigh_ref, taps_ref, dh_ref, dtaps_ref):
+    gelu_back(place, dx, w2, slope_ref, dy_ref, dz_ref, edge_ref)
+
+
+def conv_back(h_ref, hends, dz_ref, zends, taps_ref, dh_ref, dtaps_ref):
     rows = h_ref.shape[0] // W
 
     def chunk(c, carry):
@@ -274,14 +287,14 @@
         acc = [jnp.zeros((8, LANES), f32) for _ in range(9)]
 
         def views(i):
-            v = row_of(dz_ref, zlow_ref, zhigh_ref, i, rows, lanes)
+            v = row_of(dz_ref, zends, i, rows, lanes)
             return [from_right(v), v, from_left(v)]
 
         near = [views(-1), views(0)]
-        hear = [row_of(h_ref, hlow_ref, hhigh_ref, i, rows, lanes) for i in (-1, 0)]
+        hear = [row_of(h_ref, hends, i, rows, lanes) for i in (-1, 0)]
         for i in range(rows):
             near.append(views(i + 1))
-            hear.append(row_of(h_ref, hlow_ref, hhigh_ref, i + 1, rows, lanes))
+            hear.append(row_of(h_ref, hends, i + 1, rows, lanes))
             dh = None
             for di in range(3):
                 for dj in range(3):
@@ -302,6 +315,7 @@
 
 
 def block_back_body(
+    place,
     h_ref,
     hlow_ref,
     hhigh_ref,
@@ -326,7 +340,9 @@
     dq_ref,
     dkv_ref,
 ):
-    conv_back(h_ref, hlow_ref, hhigh_ref, dz_ref, zlow_ref, zhigh_ref, taps_ref, dh_ref, dtaps_ref)
+    conv_back(
+        h_ref, (place, hlow_ref, hhigh_ref), dz_ref, (place, zlow_ref, zhigh_ref), taps_ref, dh_ref, dtaps_ref
+    )
     db = dot_nt(dh_ref[...], w1[...])
     dln, dgain, dbias = norm_back(x2_ref[...], gain[2:3], db)
     dln_ref[0:1, :] = dgain
@@ -377,11 +393,12 @@
 
 
 def join_back_body(
-    dkv_ref, wkv, r_ref, gain, dq_ref, wq, wsr, x_ref, dx2_ref, w2, slope_ref, dr_ref, dln_ref, dx_ref, dy_ref, dz_ref
+    place, dkv_ref, wkv, r_ref, gain, dq_ref, wq, wsr, x_ref, dx2_ref, w2, slope_ref,
+    dr_ref, dln_ref, dx_ref, dy_ref, dz_ref, edge_ref
 ):
     dx = inputs_back(dkv_ref[...], wkv, r_ref, gain, dq_ref, wq, wsr, x_ref, dx2_ref, dr_ref, dln_ref)
     dx_ref[...] = dx
-    gelu_back(dx, w2, slope_ref, dy_ref, dz_ref)
+    gelu_back(place, dx, w2, slope_ref, dy_ref, dz_ref, edge_ref)
 
 
 def first_back_body(
@@ -475,10 +492,16 @@
 
 def group_sums(arrs, layered=None):
     embed, proj, downs, taps, head, gains, biases = arrs
-    first = jnp.stack([jnp.sum(embed), jnp.sum(head), jnp.sum(gains), jnp.sum(biases)])
     if layered is None:
         layered = [jnp.sum(a.reshape(a.shape[0], -1), 1) for a in (proj, downs)]
-    return jnp.concatenate([first, *layered, jnp.sum(taps.reshape(taps.shape[0], -1), 1)])
+    layered = [*layered, jnp.sum(taps.reshape(taps.shape[0], -1), 1)]
+    slot = jnp.arange(4 + 3 * LAYERS)
+    total = jnp.zeros((4 + 3 * LAYERS,), f32)
+    for n, a in enumerate((embed, head, gains, biases)):
+        total = jnp.where(slot == n, jnp.sum(a), total)
+    for n, a in enumerate(layered):
+        total = total + jnp.pad(a, (4 + LAYERS * n, LAYERS * (2 - n)))
+    return total
 
 
 def spread_ratio(ratio):
@@ -549,7 +572,12 @@
                     pairs.append((base + (h + shift) % team, base + h))
         return pairs
 
-    def edges(v):
+    ends = jnp.stack([place > 0, place < team - 1]).astype(jnp.int32)
+
+    def edges(v, edge):
+        if team == 2:
+            other = lax.ppermute(edge, "seq", between(1, True))
+            return other, other
         low = lax.ppermute(v[-W:], "seq", between(-1, False))
         high = lax.ppermute(v[:W], "seq", between(1, False))
         return low, high
@@ -610,6 +638,9 @@
     def gathered(parts):
         sizes = [p.shape[0] for p in parts]
         got = lax.all_gather(jnp.concatenate(parts, 0), ("dp", "seq"), axis=0, tiled=False)
+        return got, sizes
+
+    def cut(got, sizes):
         got = got.reshape(n_dp, n_seq, sum(sizes), wide)
         starts = [sum(sizes[:i]) for i in range(len(sizes))]
         return [got[:, :, a : a + n] for a, n in zip(starts, sizes)]
@@ -635,14 +666,15 @@
     gain32, bias32 = norms32[0], norms32[1]
     groups = [[0, 1, 2, 3], [4, 5]]
     extra = [[], [part_of(to_bf(head_w).reshape(-1))]]
-    layers16, extras = ([], [])
-    for members, more in zip(groups, extra):
-        parts = more + [p for l in members for p in layer_part(l)]
-        got = gathered(parts)
-        extras += [g.reshape(n_dp, -1) for g in got[: len(more)]]
-        got = got[len(more) :]
-        layers16 += [(proj_of(got[2 * i]), got[2 * i + 1].reshape(FF, 2 * D)) for i in range(len(members))]
-    head16 = extras[0][:, : head_w.size].reshape(D, CLS)
+
+    def layers_of(got, count):
+        return [(proj_of(got[2 * i]), got[2 * i + 1].reshape(FF, 2 * D)) for i in range(count)]
+
+    raw = [
+        gathered(more + [p for l in members for p in layer_part(l)])
+        for members, more in zip(groups, extra)
+    ]
+    first_late = groups[1][0]
 
     def own(v):
         return lax.dynamic_index_in_dim(v, image, 0, keepdims=False)
@@ -673,21 +705,21 @@
         classes == partner_label
     ).astype(f32)
 
-    def weights(l):
+    def weights(l, layer):
         base = 1 + 3 * l
         return dict(
-            wq=layers16[l][0][:, :D],
-            wkv=layers16[l][0][:, D : 3 * D],
-            wo=layers16[l][0][:, 3 * D : 4 * D],
-            w1=layers16[l][0][:, 4 * D :],
-            wsr=layers16[l][1][:, :D],
-            w2=layers16[l][1][:, D:],
+            wq=layer[0][:, :D],
+            wkv=layer[0][:, D : 3 * D],
+            wo=layer[0][:, 3 * D : 4 * D],
+            w1=layer[0][:, 4 * D :],
+            wsr=layer[1][:, :D],
+            w2=layer[1][:, D:],
             taps=taps32[l],
             gain=gain32[base : base + 3],
             bias=bias32[base : base + 3],
         )
 
-    wts = [weights(l) for l in range(LAYERS)]
+    wts = [weights(l, layer) for l, layer in zip(groups[0], layers_of(cut(*raw[0]), len(groups[0])))]
     ln_first = jnp.stack([gain32[0], bias32[0]])
     ln_last = jnp.stack([gain32[-1], bias32[-1]])
 
@@ -696,6 +728,7 @@
     wide16 = ((tok, FF), bf16)
     input_outs = [half, half, ((keys_own, D), f32), ((keys_own, D), bf16), ((keys_own, 2 * D), bf16)]
     ln_out = ((2, D), f32)
+    row16 = ((W, FF), bf16)
 
     spread = patches.reshape(img_dev, rows, HALF, 2, -1).transpose(0, 1, 3, 2, 4)
     patch_own = to_team(spread.reshape(img_dev, rows * W, -1))
@@ -708,10 +741,10 @@
     for l in range(LAYERS):
         w = wts[l]
         kv_all = all_keys(kv16)
-        o16, lse, x2, b16, h16 = run(
+        o16, lse, x2, b16, h16, edge = run(
             4,
             middle_body,
-            [half, ((HEADS, tok), f32), full, half, wide16],
+            [half, ((HEADS, tok), f32), full, half, wide16, row16],
             q16,
             kv_all,
             shut,
@@ -720,13 +753,19 @@
             w["bias"],
             w["wo"],
             w["w1"],
+            place=ends,
         )
-        hlow, hhigh = edges(h16)
+        hlow, hhigh = edges(h16, edge)
         keep = dict(
             x=x, a16=a16, q16=q16, r=r, rn16=rn16, kv=kv_all, o16=o16, lse=lse, x2=x2, b16=b16,
             h16=h16, hlow=hlow, hhigh=hhigh,
         )
         shared = (h16, hlow, hhigh, w["taps"], x2, w["w2"])
+        if l + 1 == first_late:
+            got, _ = lax.optimization_barrier((raw[1][0], kv_all))
+            got = cut(got, raw[1][1])
+            head16 = got[0].reshape(n_dp, -1)[:, : head_w.size].reshape(D, CLS)
+            wts += [weights(m, layer) for m, layer in zip(groups[1], layers_of(got[1:], len(groups[1])))]
         if l + 1 < LAYERS:
             n = wts[l + 1]
             keep["g16"], keep["slope"], x, a16, q16, r, rn16, kv16 = run(
@@ -739,6 +778,7 @@
                 n["wq"],
                 n["wsr"],
                 n["wkv"],
+                place=ends,
             )
         else:
             keep["g16"], keep["slope"], x, pool = run(
@@ -748,16 +788,17 @@
                 *shared,
                 ln_last,
                 okay,
+                place=ends,
             )
         kept.append(keep)
 
     whole = pool
     for j in range(1, team):
         whole = whole + lax.ppermute(pool, "seq", between(j, True))
-    loss_own, pooled16, dlog16, dln_last, dx, dy16, dz16 = run(
+    loss_own, pooled16, dlog16, dln_last, dx, dy16, dz16, edge = run(
         4,
         functools.partial(head_body, images),
-        [((1, 1), f32), ((1, D), bf16), ((1, CLS), bf16), ln_out, full, half, wide16],
+        [((1, 1), f32), ((1, D), bf16), ((1, CLS), bf16), ln_out, full, half, wide16, row16],
         whole,
         count,
         head16,
@@ -767,6 +808,7 @@
         okay,
         wts[-1]["w2"],
         kept[-1]["slope"],
+        place=ends,
     )
     chosen = ((place == 0) & busy).astype(f32)
     d_head = pooled16.astype(f32).reshape(D, 1) * dlog16.astype(f32) * chosen
@@ -802,7 +844,7 @@
 
     def padded_rest(parts):
         flat = jnp.concatenate(parts, 1)
-        size = -(-flat.shape[1] // (8 * wide * n_seq)) * 8 * wide * n_seq
+        size = -(-flat.shape[1] // (16 * wide * n_seq)) * 16 * wide * n_seq
         flat = jnp.pad(flat, ((0, 0), (0, size - flat.shape[1])))
         flat = flat.reshape(n_dp, cols, subs, -1, wide).transpose(1, 2, 0, 3, 4)
         if not paired:
@@ -816,12 +858,20 @@
         mine, send = parts
         return mine + lax.ppermute(send, "seq", [(d ^ 1, d) for d in range(n_seq)])
 
-    def plane_sum(y):
-        total = y[0]
-        for j in range(1, cols):
-            pairs = [(d ^ (j * subs), d) for d in range(n_seq)]
-            total = total + lax.ppermute(to_bf(y[j]), "seq", pairs).astype(f32)
-        return total
+    def over_chips(v, bit):
+        return lax.ppermute(v, "seq", [(d ^ (bit * subs), d) for d in range(n_seq)])
+
+    def plane_first(y):
+        cut = y.shape[2] // 2
+        one, two = y[:, :, :cut], y[:, :, cut:]
+        moved = (to_bf(jnp.stack([one[1], one[3]])), to_bf(jnp.stack([two[2], two[3]])))
+        got = (over_chips(moved[0], 1).astype(f32), over_chips(moved[1], 2).astype(f32))
+        return [one[0] + got[0][0], one[2] + got[0][1], two[0] + got[1][0], two[1] + got[1][1]]
+
+    def plane_second(parts):
+        one = parts[0] + over_chips(to_bf(parts[1]), 2).astype(f32)
+        two = parts[2] + over_chips(to_bf(parts[3]), 1).astype(f32)
+        return jnp.concatenate([one, two], 1)
 
     def dp_sum(y):
         total = y[0]
@@ -838,16 +888,16 @@
     def tied(value, others):
         return lax.optimization_barrier((value, others))
 
-    stages = [pair_sum, plane_sum, dp_sum]
+    stages = [pair_sum, plane_first, plane_second, dp_sum]
     pieces = []
 
-    def advance(now):
+    def advance(now, which):
         if not paired:
             return now
-        ready = [p for p in pieces if p[0] < len(stages)]
+        ready = [p for p in pieces if p[0] in which]
         now, values = tied(now, [p[1] for p in ready])
         for p, v in zip(ready, values):
-            p[1] = stages[p[0]](v)
+            p[1] = stages[p[0]](v) if p[0] < len(stages) else v
             p[0] += 1
         return now
 
@@ -856,28 +906,31 @@
     waiting = None
     for l in reversed(range(LAYERS)):
         w, k = wts[l], kept[l]
-        zlow, zhigh = edges(dz16)
+        zlow, zhigh = edges(dz16, edge)
+        if waiting is not None:
+            pieces.append([0, weight_grads(*waiting)])
+        upper = dy16
+        dz16 = advance(dz16, (0, 2, 3))
         dh16, d_taps, dln2, dx2, dy2, dq16, dkv = run(
             11,
             block_back_body,
             [wide16, ((9, FF), f32), ln_out, full, half, half, ((team * keys_own, 2 * D), f32)],
             k["h16"], k["hlow"], k["hhigh"], dz16, zlow, zhigh, w["taps"], w["w1"], k["x2"], w["gain"], dx,
             w["wo"], k["q16"], k["kv"], shut, k["lse"],
+            place=ends,
         )
-        if waiting is not None:
-            pieces.append([0, weight_grads(*waiting)])
         dkv_own = own_keys(dkv)
-        dkv_own = advance(dkv_own)
-        upper = dy16
+        dkv_own = advance(dkv_own, (1, 4))
         shared = (dkv_own, w["wkv"], k["r"], w["gain"], dq16, w["wq"], w["wsr"], k["x"], dx2)
         if l:
-            dr16, dln, dx, dy16, dz16 = run(
+            dr16, dln, dx, dy16, dz16, edge = run(
                 6,
                 join_back_body,
-                [((keys_own, D), bf16), ((4, D), f32), full, half, wide16],
+                [((keys_own, D), bf16), ((4, D), f32), full, half, wide16, row16],
                 *shared,
                 wts[l - 1]["w2"],
                 kept[l - 1]["slope"],
+                place=ends,
             )
         else:
             dr16, dln, de16, dln_first = run(
@@ -894,7 +947,10 @@
             jnp.concatenate([dln[0:2], dln2[0:1]], 0),
             jnp.concatenate([dln[2:4], dln2[1:2]], 0),
         )
+    pieces.append([0, weight_grads(*waiting)])
+    de16 = advance(de16, (0, 2, 3))
     (d_embed,) = run(3, embed_back_body, [((embed16.shape[0], D), f32)], patch_own, de16)
+    d_embed = advance(d_embed, (1, 3, 4))
     d_gain = jnp.concatenate([dln_first[0:1]] + [g[1] for g in grads] + [dln_last[0:1]], 0)
     d_bias = jnp.concatenate([dln_first[1:2]] + [g[2] for g in grads] + [dln_last[1:2]], 0)
     d_taps = jnp.stack([g[0] for g in grads])
@@ -907,9 +963,18 @@
     cuts = [0]
     for part in rest:
         cuts.append(cuts[-1] + part.shape[1])
-    last = weight_grads(*waiting)
     rest = padded_rest(rest)
-    pieces.append([0, [jnp.concatenate([a, b], -2) for a, b in zip(last, rest)]])
+
+    late = 2
+
+    def together(parts):
+        return to_bf(jnp.concatenate(parts, 0))
+
+    if paired:
+        assert all(p[0] > len(stages) for p in pieces[: LAYERS + 1 - late])
+        early = together([p[1] for p in pieces[1 : LAYERS + 1 - late] + pieces[:1]])
+        rest, early = tied(rest, early)
+    pieces.append([0, rest])
     if paired:
         while any(p[0] < len(stages) for p in pieces):
             for p in pieces:
@@ -919,14 +984,10 @@
         sums = [p[1] for p in pieces]
     else:
         sums = [whole_sum([p[1]]) for p in pieces]
-
-    late = 2
-
-    def together(parts):
-        return lax.all_gather(to_bf(jnp.concatenate(parts, 0)), "seq", axis=0, tiled=False)
-
-    early_got = together(sums[1 : LAYERS + 1 - late] + sums[:1])
-    late_got = together(sums[LAYERS + 1 - late :])
+        early = together(sums[1 : LAYERS + 1 - late] + sums[:1])
+    early_got = lax.all_gather(early, "seq", axis=0, tiled=False)
+    late_part, early_got = tied(together(sums[LAYERS + 1 - late :]), early_got)
+    late_got = lax.all_gather(late_part, "seq", axis=0, tiled=False)
     head_start = (LAYERS - late) * 2 * sub_in
     g_head = early_got[:, head_start:].reshape(-1)[: head_w.size].reshape(head_w.shape).astype(f32)
     flat = late_got[:, late * 2 * sub_in :].reshape(-1).astype(f32)

time: 970 us -> 880 us (0.907)
  waiting for transfers between devices: 251 us -> 125 us
  local copies, waits for them, and re-layouts: 169 us -> 201 us
  starting transfers between devices: 150 us -> 128 us
  other arithmetic: 100 us -> 118 us
    all_gather x2, waiting for transfers between devices: 89.4 us -> 0.01 us  [gathered(): lax.all_gather(jnp.concatenate(parts, 0), ('dp', 'seq'), axis=0, tiled=Fa...]
    ppermute x45 -> x44, waiting for transfers between devices: 89.3 us -> 28.1 us  [the longest x32 17.7 us: over_chips(): return lax.ppermute(v, 'seq', [(d ^ bit * subs, d) for d in range(n_seq)])]
    ppermute x45 -> x44, starting transfers between devices: 83 us -> 38.9 us  [the longest x32 34.7 us: over_chips(): return lax.ppermute(v, 'seq', [(d ^ bit * subs, d) for d in range(n_seq)])]
    unnamed x751 -> x779, local copies, waits for them, and re-layouts: 70.8 us -> 102 us
    add x7 -> x32, other arithmetic: 5.62 us -> 24.5 us  [the longest x6 9.19 us: plane_first(): two[1] + got[1][1]]
    ppermute x21 -> x24, starting transfers between devices: 26.2 us -> 42.6 us  [dp_sum(): total = total + lax.ppermute(y[j], 'dp', pairs)]
    ppermute x9, waiting for transfers between devices: 23.7 us -> 38.2 us  [over_dp(): lax.ppermute(v, 'dp', [((d + j) % n_dp, d) for d in range(n_dp)])]
    ppermute x21 -> x24, waiting for transfers between devices: 36.1 us -> 44.4 us  [dp_sum(): total = total + lax.ppermute(y[j], 'dp', pairs)]
  transfers between devices with their start and end apart: 109 -> 112, of which waited for: 33 -> 33; matrix products, arithmetic and copies ran while one was open for 14% -> 19% of each run, Pallas kernels for 18% -> 24%
where the time goes in v3:
time: 880 us; the launch traced here: 871 us
  Pallas kernels  248 us (28%)
  local copies, waits for them, and re-layouts  201 us (23%)
  starting transfers between devices  128 us (15%)
  waiting for transfers between devices  125 us (14%)
  other arithmetic  118 us (13%)
  between operations  30.4 us (3%)
  blocking collectives  21.1 us (2%)
    pallas_call x28, Pallas kernels, run(): pl.pallas_call(body, out_shape=[jax.ShapeDtypeStruct(s, d) for s, d in ou...  183 us
    unnamed x779, local copies, waits for them, and re-layouts  102 us
    ppermute x24, waiting for transfers between devices, dp_sum(): total = total + lax.ppermute(y[j], 'dp', pairs)  44.4 us
    ppermute x24, starting transfers between devices, dp_sum(): total = total + lax.ppermute(y[j], 'dp', pairs)  42.6 us
    pallas_call x6, Pallas kernels, weight_grads(): pl.pallas_call(functools.partial(weight_grads_body, n_dp, cols, subs), ou...  38.3 us
    ppermute x9, waiting for transfers between devices, over_dp(): lax.ppermute(v, 'dp', [((d + j) % n_dp, d) for d in range(n_dp)])  38.2 us
    ppermute x32, starting transfers between devices, over_chips(): return lax.ppermute(v, 'seq', [(d ^ bit * subs, d) for d in range(n_seq)])  34.7 us
    pallas_call x1, Pallas kernels, per_device(): pl.pallas_call(functools.partial(update_body, cols, subs, late), grid=(LA...  26.5 us
  transfers between devices with their start and end apart: 112, of which 33 were waited for; matrix products, arithmetic and copies ran while one was open for 19% of the time, Pallas kernels for 24%

profile of v3, /device:TPU:0, one launch (start us, length us, event | category | flops | bytes accessed | tf_op | source)
XLA Modules:
  0.0 871.0 jit_solution(6973874073559941064)
XLA Ops:
  62.1 7.0 collective-permute-done.13
  85.4 23.9 %collective-permute-done.5 = bf16[288,320]{1,0:T(8,128)(2,1)S(1)} collective-permute-done((bf16[288,320]{1,0:T(8,128)(2,1)S(1)}, bf16[288,320]{1,0:T(8,128)(2,1)S(1)}, u32[]{:S(2)}, u32[]{:S(2)}) %collective-permute-start.5) | collective-permute-done | bytes 184352 | tf_op jit(solution)/shard_map/ppermute | solution.py:656
  125.0 9.1 %collective-permute-start.2 = (bf16[128,1152]{1,0:T(8,128)(2,1)S(1)}, bf16[128,1152]{1,0:T(8,128)(2,1)S(1)}, u32[]{:S(2)}, u32[]{:S(2)}) collective-permute-start(bf16[128,1152]{1,0:T(8,128)(2,1)S(1)} %get-tuple-element.768), channel_id=1, source_target_pairs={{2,0},{6,1},{3,2},{7,3},{0,4},{4,5},{10,8},{14,9},{11,10},{15,11},... | collective-permute-start | bytes 884744 | tf_op jit(solution)/shard_map/ppermute | solution.py:613
  141.3 7.6 fusion.155
  166.0 8.7 shard_map.444
  187.2 8.3 shard_map.446
  208.6 8.2 shard_map.448
  252.0 8.5 shard_map.450
  273.2 8.5 shard_map.452
  358.3 11.1 %shard_map.456 = (bf16[512,1280]{1,0:T(8,128)(2,1)}, f32[9,1280]{1,0:T(8,128)S(1)}, f32[2,320]{1,0:T(2,128)S(1)}, f32[512,320]{1,0:T(8,128)S(1)}, bf16[512,320]{...) custom-call(s32[2]{0:T(128)S(1)} %add_convert_fusion.place, bf16[512,1280]{1,0:T(8,128)(2,1)} %copy-done.26, ...), custom_call_target="tpu_custom_call" | custom-call | flops 1100000000 | bytes 1100000 | tf_op jit(solution)/shard_map/pallas_call | solution.py:88
  373.9 6.6 shard_map.457
  394.7 11.1 %shard_map.459 = (bf16[512,1280]{1,0:T(8,128)(2,1)}, f32[9,1280]{1,0:T(8,128)S(1)}, f32[2,320]{1,0:T(2,128)S(1)}, f32[512,320]{1,0:T(8,128)S(1)}, bf16[512,320]{...) custom-call(s32[2]{0:T(128)S(1)} %add_convert_fusion.place, bf16[512,1280]{1,0:T(8,128)(2,1)} %copy-done.32, ...), custom_call_target="tpu_custom_call" | custom-call | flops 1100000000 | bytes 1100000 | tf_op jit(solution)/shard_map/pallas_call | solution.py:88
  442.4 10.9 %shard_map.462 = (bf16[512,1280]{1,0:T(8,128)(2,1)}, f32[9,1280]{1,0:T(8,128)S(1)}, f32[2,320]{1,0:T(2,128)S(1)}, f32[512,320]{1,0:T(8,128)S(1)}, bf16[512,320]{...) custom-call(s32[2]{0:T(128)S(1)} %add_convert_fusion.place, bf16[512,1280]{1,0:T(8,128)(2,1)} %copy-done.31, ...), custom_call_target="tpu_custom_call" | custom-call | flops 1100000000 | bytes 1100000 | tf_op jit(solution)/shard_map/pallas_call | solution.py:88
  490.4 10.9 %shard_map.465 = (bf16[512,1280]{1,0:T(8,128)(2,1)}, f32[9,1280]{1,0:T(8,128)S(1)}, f32[2,320]{1,0:T(2,128)S(1)}, f32[512,320]{1,0:T(8,128)S(1)}, bf16[512,320]{...) custom-call(s32[2]{0:T(128)S(1)} %add_convert_fusion.place, bf16[512,1280]{1,0:T(8,128)(2,1)} %copy-done.30, ...), custom_call_target="tpu_custom_call" | custom-call | flops 1100000000 | bytes 1100000 | tf_op jit(solution)/shard_map/pallas_call | solution.py:88
  541.4 11.1 %shard_map.468 = (bf16[512,1280]{1,0:T(8,128)(2,1)}, f32[9,1280]{1,0:T(8,128)S(1)}, f32[2,320]{1,0:T(2,128)S(1)}, f32[512,320]{1,0:T(8,128)S(1)}, bf16[512,320]{...) custom-call(s32[2]{0:T(128)S(1)} %add_convert_fusion.place, bf16[512,1280]{1,0:T(8,128)(2,1)} %copy-done.29, ...), custom_call_target="tpu_custom_call" | custom-call | flops 1100000000 | bytes 1100000 | tf_op jit(solution)/shard_map/pallas_call | solution.py:88
  589.2 10.9 %shard_map.471 = (bf16[512,1280]{1,0:T(8,128)(2,1)}, f32[9,1280]{1,0:T(8,128)S(1)}, f32[2,320]{1,0:T(2,128)S(1)}, f32[512,320]{1,0:T(8,128)S(1)}, bf16[512,320]{...) custom-call(s32[2]{0:T(128)S(1)} %add_convert_fusion.place, bf16[512,1280]{1,0:T(8,128)(2,1)} %copy-done.28, ...), custom_call_target="tpu_custom_call" | custom-call | flops 1100000000 | bytes 1100000 | tf_op jit(solution)/shard_map/pallas_call | solution.py:88
  648.8 7.9 collective-permute-done.85
  685.6 9.0 %collective-permute-done.91 = f32[80,640]{1,0:T(8,128)S(1)} collective-permute-done((f32[80,640]{1,0:T(8,128)S(1)}, f32[80,640]{1,0:T(8,128)S(1)}, u32[]{:S(2)}, u32[]{:S(2)}) %collective-permute-start.91) | collective-permute-done | bytes 204832 | tf_op jit(solution)/shard_map/ppermute | solution.py:880
  700.3 7.6 collective-permute-done.94
  727.4 11.1 %collective-permute-start.106 = (f32[32,640]{1,0:T(8,128)S(1)}, f32[32,640]{1,0:T(8,128)S(1)}, u32[]{:S(2)}, u32[]{:S(2)}) collective-permute-start(f32[32,640]{1,0:T(8,128)S(1)} %get-tuple-element.803), channel_id=1, source_target_pairs={{0,16},{8,24},{16,0},{24,8},{1,17},{9,25},{17,1},{25,9},{2,18},{10... | collective-permute-start | bytes 245768 | tf_op jit(solution)/shard_map/ppermute | solution.py:880
  777.7 12.2 %psum.29 = f32[]{:T(128)} all-reduce(f32[]{:T(128)S(6)} %add.1014), channel_id=1, replica_groups=mesh['dp'=4,'seq'=8] {'dp'}, use_global_device_ids=true, to_apply=%region_8.9 | all-reduce | flops 1 | bytes 8 | tf_op jit(solution)/shard_map/psum | solution.py:1007
  791.5 26.5 %shard_map.475 = (f32[6,80,2560]{2,1,0:T(8,128)}, f32[6,80,2560]{2,1,0:T(8,128)}, f32[6,80,2560]{2,1,0:T(8,128)}, f32[6,2,320,320]{3,2,1,0:T(8,128)}, f32[6,2,32...) custom-call(f32[1]{0:T(128)} %bitcast.186.factor_ref, bf16[8,336,640]{2,1,0:T(8,128)(2,1)} %bitcast.504, ...), custom_call_target="tpu_custom_call" | custom-call | flops 2500000000 | bytes 2500000 | tf_op jit(solution)/shard_map/pallas_call | solution.py:1023
  828.5 9.0 %all-reduce.9 = (f32[]{:T(128)}, f32[22]{0:T(128)S(1)}, f32[22]{0:T(128)S(1)}) all-reduce(f32[]{:T(128)} %fusion.142, f32[22]{0:T(128)S(1)} %get-tuple-element.883, f32[22]{0:T(128)S(1)} %get-tuple-element.884), channel_id=1, replica_groups=mesh['dp'=4,'seq'=8] {'dp'}, use_global_device_ids=true, to_apply=%region_5.6 | all-reduce | flops 45 | bytes 360 | tf_op jit(solution)/shard_map/psum | solution.py:1007
  846.1 7.5 multiply_subtract_fusion.1
  (1337 shorter events, 587.5 us)
Async XLA Ops:
  7.2 134.1 %all-gather.9.cloned.1.call-start = ((), (), s32[]{:S(2)}) async-start(), calls=%async_computation | async-start | bytes 13516800 | tf_op jit(solution)/shard_map/all_gather | solution.py:640
  20.5 214.8 %all-gather.11.cloned.1.call-start = ((), (), s32[]{:S(2)}) async-start(), calls=%async_computation.1 | async-start | bytes 7434240 | tf_op jit(solution)/shard_map/all_gather | solution.py:640
  20.6 200.4 %collective-permute-start.26 = (s32[3]{0:T(128)}, s32[3]{0:T(128)}, u32[]{:S(2)}, u32[]{:S(2)}) collective-permute-start(s32[3]{0:T(128)} %param.28), channel_id=1, source_target_pairs={{8,0},{16,8},{24,16},{0,24},{9,1},{17,9},{25,17},{1,25},{10,2},{18... | collective-permute-start | bytes 44 | tf_op jit(solution)/shard_map/ppermute | solution.py:687
  25.7 258.4 %collective-permute-start.28 = (s32[3]{0:T(128)}, s32[3]{0:T(128)}, u32[]{:S(2)}, u32[]{:S(2)}) collective-permute-start(s32[3]{0:T(128)} %param.28), channel_id=1, source_target_pairs={{24,0},{0,8},{8,16},{16,24},{25,1},{1,9},{9,17},{17,25},{26,2},{2,... | collective-permute-start | bytes 44 | tf_op jit(solution)/shard_map/ppermute | solution.py:687
  25.7 270.6 %collective-permute-start.27 = (s32[3]{0:T(128)}, s32[3]{0:T(128)}, u32[]{:S(2)}, u32[]{:S(2)}) collective-permute-start(s32[3]{0:T(128)} %param.28), channel_id=1, source_target_pairs={{16,0},{24,8},{0,16},{8,24},{17,1},{25,9},{1,17},{9,25},{18,2},{26... | collective-permute-start | bytes 44 | tf_op jit(solution)/shard_map/ppermute | solution.py:687
  26.7 27.6 %collective-permute-start.9 = (bf16[2,20,80]{2,1,0:T(8,128)(2,1)S(1)}, bf16[2,20,80]{2,1,0:T(8,128)(2,1)S(1)}, u32[]{:S(2)}, u32[]{:S(2)}) collective-permute-start(bf16[2,20,80]{2,1,0:T(8,128)(2,1)S(1)} %pad_maximum_fusion.17), channel_id=1, source_target_pairs={{24,0},{0,8},{8,16},{16,24},{25,1},{1,9},{9,17},{17,25},{26,2},{2,... | collective-permute-start | bytes 19208 | tf_op jit(solution)/shard_map/ppermute | solution.py:656
  33.8 711.6 %all-gather.13.cloned.1.call-start = ((), (), s32[]{:S(2)}) async-start(), calls=%async_computation.2 | async-start | bytes 3870720 | tf_op jit(solution)/shard_map/all_gather | solution.py:988
  69.1 44.6 %collective-permute-start.6 = (bf16[288,320]{1,0:T(8,128)(2,1)S(1)}, bf16[288,320]{1,0:T(8,128)(2,1)S(1)}, u32[]{:S(2)}, u32[]{:S(2)}) collective-permute-start(bf16[288,320]{1,0:T(8,128)(2,1)S(1)} %get-tuple-element.660), channel_id=1, source_target_pairs={{24,0},{0,8},{8,16},{16,24},{25,1},{1,9},{9,17},{17,25},{26,2},{2,... | collective-permute-start | bytes 552968 | tf_op jit(solution)/shard_map/ppermute | solution.py:656
  83.7 25.7 %collective-permute-start.5 = (bf16[288,320]{1,0:T(8,128)(2,1)S(1)}, bf16[288,320]{1,0:T(8,128)(2,1)S(1)}, u32[]{:S(2)}, u32[]{:S(2)}) collective-permute-start(bf16[288,320]{1,0:T(8,128)(2,1)S(1)} %get-tuple-element.660), channel_id=1, source_target_pairs={{16,0},{24,8},{0,16},{8,24},{17,1},{25,9},{1,17},{9,25},{18,2},{26... | collective-permute-start | bytes 552968 | tf_op jit(solution)/shard_map/ppermute | solution.py:656
  109.4 28.7 %collective-permute-start.3 = (bf16[128,1152]{1,0:T(8,128)(2,1)S(1)}, bf16[128,1152]{1,0:T(8,128)(2,1)S(1)}, u32[]{:S(2)}, u32[]{:S(2)}) collective-permute-start(bf16[128,1152]{1,0:T(8,128)(2,1)S(1)} %get-tuple-element.767), channel_id=1, source_target_pairs={{3,0},{7,1},{0,2},{4,3},{1,4},{5,5},{11,8},{15,9},{8,10},{12,11},{... | collective-permute-start | bytes 884744 | tf_op jit(solution)/shard_map/ppermute | solution.py:613
  388.9 21.5 %collective-permute-start.39 = (f32[4,4,80,640]{3,2,1,0:T(8,128)}, f32[4,4,80,640]{3,2,1,0:T(8,128)}, u32[]{:S(2)}, u32[]{:S(2)}) collective-permute-start(f32[4,4,80,640]{3,2,1,0:T(8,128)} %get-tuple-element.366), channel_id=1, source_target_pairs={{1,0},{0,1},{3,2},{2,3},{5,4},{4,5},{7,6},{6,7},{9,8},{8,9},{11,10... | collective-permute-start | bytes 9830408 | tf_op jit(solution)/shard_map/ppermute | solution.py:859
  434.8 20.4 %collective-permute-start.49 = (f32[4,4,80,640]{3,2,1,0:T(8,128)}, f32[4,4,80,640]{3,2,1,0:T(8,128)}, u32[]{:S(2)}, u32[]{:S(2)}) collective-permute-start(f32[4,4,80,640]{3,2,1,0:T(8,128)} %get-tuple-element.396), channel_id=1, source_target_pairs={{1,0},{0,1},{3,2},{2,3},{5,4},{4,5},{7,6},{6,7},{9,8},{8,9},{11,10... | collective-permute-start | bytes 9830408 | tf_op jit(solution)/shard_map/ppermute | solution.py:859
  435.5 18.1 %collective-permute-start.48 = (f32[16,640]{1,0:T(8,128)S(1)}, f32[16,640]{1,0:T(8,128)S(1)}, u32[]{:S(2)}, u32[]{:S(2)}) collective-permute-start(f32[16,640]{1,0:T(8,128)S(1)} %get-tuple-element.807), channel_id=1, source_target_pairs={{0,24},{8,0},{16,8},{24,16},{1,25},{9,1},{17,9},{25,17},{2,26},{10... | collective-permute-start | bytes 122888 | tf_op jit(solution)/shard_map/ppermute | solution.py:880
  482.7 22.7 %collective-permute-start.59 = (f32[4,4,80,640]{3,2,1,0:T(8,128)}, f32[4,4,80,640]{3,2,1,0:T(8,128)}, u32[]{:S(2)}, u32[]{:S(2)}) collective-permute-start(f32[4,4,80,640]{3,2,1,0:T(8,128)} %get-tuple-element.426), channel_id=1, source_target_pairs={{1,0},{0,1},{3,2},{2,3},{5,4},{4,5},{7,6},{6,7},{9,8},{8,9},{11,10... | collective-permute-start | bytes 9830408 | tf_op jit(solution)/shard_map/ppermute | solution.py:859
  531.0 24.8 %collective-permute-start.69 = (f32[4,4,80,640]{3,2,1,0:T(8,128)}, f32[4,4,80,640]{3,2,1,0:T(8,128)}, u32[]{:S(2)}, u32[]{:S(2)}) collective-permute-start(f32[4,4,80,640]{3,2,1,0:T(8,128)} %get-tuple-element.456), channel_id=1, source_target_pairs={{1,0},{0,1},{3,2},{2,3},{5,4},{4,5},{7,6},{6,7},{9,8},{8,9},{11,10... | collective-permute-start | bytes 9830408 | tf_op jit(solution)/shard_map/ppermute | solution.py:859
  579.8 27.0 %collective-permute-start.79 = (f32[4,4,80,640]{3,2,1,0:T(8,128)}, f32[4,4,80,640]{3,2,1,0:T(8,128)}, u32[]{:S(2)}, u32[]{:S(2)}) collective-permute-start(f32[4,4,80,640]{3,2,1,0:T(8,128)} %get-tuple-element.486), channel_id=1, source_target_pairs={{1,0},{0,1},{3,2},{2,3},{5,4},{4,5},{7,6},{6,7},{9,8},{8,9},{11,10... | collective-permute-start | bytes 9830408 | tf_op jit(solution)/shard_map/ppermute | solution.py:859
  583.5 23.3 %collective-permute-start.80 = (bf16[4,40,640]{2,1,0:T(8,128)(2,1)S(1)}, bf16[4,40,640]{2,1,0:T(8,128)(2,1)S(1)}, u32[]{:S(2)}, u32[]{:S(2)}) collective-permute-start(bf16[4,40,640]{2,1,0:T(8,128)(2,1)S(1)} %get-tuple-element.494), channel_id=1, source_target_pairs={{4,0},{5,1},{6,2},{7,3},{0,4},{1,5},{2,6},{3,7},{12,8},{13,9},{14,... | collective-permute-start | bytes 614408 | tf_op jit(solution)/shard_map/ppermute | solution.py:862
  628.5 29.2 %collective-permute-start.89 = (f32[4,4,80,640]{3,2,1,0:T(8,128)}, f32[4,4,80,640]{3,2,1,0:T(8,128)}, u32[]{:S(2)}, u32[]{:S(2)}) collective-permute-start(f32[4,4,80,640]{3,2,1,0:T(8,128)} %get-tuple-element.516), channel_id=1, source_target_pairs={{1,0},{0,1},{3,2},{2,3},{5,4},{4,5},{7,6},{6,7},{9,8},{8,9},{11,10... | collective-permute-start | bytes 9830408 | tf_op jit(solution)/shard_map/ppermute | solution.py:859
  672.2 98.7 %all-gather.15.cloned.1.call-start = ((), (), s32[]{:S(2)}) async-start(), calls=%async_computation.3 | async-start | bytes 2211840 | tf_op jit(solution)/shard_map/all_gather | solution.py:990
  672.3 26.0 %collective-permute-start.100 = (f32[4,4,32,640]{3,2,1,0:T(8,128)}, f32[4,4,32,640]{3,2,1,0:T(8,128)S(1)}, u32[]{:S(2)}, u32[]{:S(2)}) collective-permute-start(f32[4,4,32,640]{3,2,1,0:T(8,128)} %get-tuple-element.546), channel_id=1, source_target_pairs={{1,0},{0,1},{3,2},{2,3},{5,4},{4,5},{7,6},{6,7},{9,8},{8,9},{11,10... | collective-permute-start | bytes 3932168 | tf_op jit(solution)/shard_map/ppermute | solution.py:859
  718.9 19.6 %collective-permute-start.99 = (f32[80,640]{1,0:T(8,128)S(1)}, f32[80,640]{1,0:T(8,128)S(1)}, u32[]{:S(2)}, u32[]{:S(2)}) collective-permute-start(f32[80,640]{1,0:T(8,128)S(1)} %get-tuple-element.775), channel_id=1, source_target_pairs={{0,24},{8,0},{16,8},{24,16},{1,25},{9,1},{17,9},{25,17},{2,26},{10... | collective-permute-start | bytes 614408 | tf_op jit(solution)/shard_map/ppermute | solution.py:880
  721.3 20.6 %collective-permute-start.98 = (f32[80,640]{1,0:T(8,128)S(1)}, f32[80,640]{1,0:T(8,128)S(1)}, u32[]{:S(2)}, u32[]{:S(2)}) collective-permute-start(f32[80,640]{1,0:T(8,128)S(1)} %get-tuple-element.776), channel_id=1, source_target_pairs={{0,16},{8,24},{16,0},{24,8},{1,17},{9,25},{17,1},{25,9},{2,18},{10... | collective-permute-start | bytes 614408 | tf_op jit(solution)/shard_map/ppermute | solution.py:880
  721.7 20.3 %collective-permute-start.105 = (f32[32,640]{1,0:T(8,128)S(1)}, f32[32,640]{1,0:T(8,128)S(1)}, u32[]{:S(2)}, u32[]{:S(2)}) collective-permute-start(f32[32,640]{1,0:T(8,128)S(1)} %get-tuple-element.801), channel_id=1, source_target_pairs={{0,8},{8,16},{16,24},{24,0},{1,9},{9,17},{17,25},{25,1},{2,10},{10... | collective-permute-start | bytes 245768 | tf_op jit(solution)/shard_map/ppermute | solution.py:880
  723.6 18.5 %collective-permute-start.107 = (f32[32,640]{1,0:T(8,128)S(1)}, f32[32,640]{1,0:T(8,128)S(1)}, u32[]{:S(2)}, u32[]{:S(2)}) collective-permute-start(f32[32,640]{1,0:T(8,128)S(1)} %get-tuple-element.802), channel_id=1, source_target_pairs={{0,24},{8,0},{16,8},{24,16},{1,25},{9,1},{17,9},{25,17},{2,26},{10... | collective-permute-start | bytes 245768 | tf_op jit(solution)/shard_map/ppermute | solution.py:880
  (438 other events, 3368.9 us)
Sparse Core Ops, SparseCore 0:
  20.6 112.7 all-gather.8
  136.9 72.8 all-gather.10
  672.3 44.5 all-gather.12
  745.5 25.2 all-gather.14

commit v4 on v3

--- a/solution.py
+++ b/solution.py
@@ -664,7 +664,7 @@
     taps32 = taps16.transpose(1, 0, 2).reshape(LAYERS, 9, FF).astype(f32)
     norms32 = norms16.transpose(1, 2, 0, 3).reshape(2, -1, D).astype(f32)
     gain32, bias32 = norms32[0], norms32[1]
-    groups = [[0, 1, 2, 3], [4, 5]]
+    groups = [[0, 1, 2], [3, 4, 5]]
     extra = [[], [part_of(to_bf(head_w).reshape(-1))]]
 
     def layers_of(got, count):
@@ -869,15 +869,15 @@
         return [one[0] + got[0][0], one[2] + got[0][1], two[0] + got[1][0], two[1] + got[1][1]]
 
     def plane_second(parts):
-        one = parts[0] + over_chips(to_bf(parts[1]), 2).astype(f32)
-        two = parts[2] + over_chips(to_bf(parts[3]), 1).astype(f32)
+        one = parts[0] + over_chips(parts[1], 2)
+        two = parts[2] + over_chips(parts[3], 1)
         return jnp.concatenate([one, two], 1)
 
     def dp_sum(y):
         total = y[0]
         for j in range(1, n_dp):
             pairs = [(d, (d + j) % n_dp) for d in range(n_dp)]
-            total = total + lax.ppermute(y[j], "dp", pairs)
+            total = total + lax.ppermute(to_bf(y[j]), "dp", pairs).astype(f32)
         return total
 
     def whole_sum(parts):
@@ -888,7 +888,9 @@
     def tied(value, others):
         return lax.optimization_barrier((value, others))
 
-    stages = [pair_sum, plane_first, plane_second, dp_sum]
+    same = lambda v: v
+    stages = [pair_sum, plane_first, same, plane_second, same, dp_sum]
+    even, odd = ((0, 2, 4, 6), (1, 3, 5))
     pieces = []
 
     def advance(now, which):
@@ -910,7 +912,7 @@
         if waiting is not None:
             pieces.append([0, weight_grads(*waiting)])
         upper = dy16
-        dz16 = advance(dz16, (0, 2, 3))
+        dz16 = advance(dz16, even)
         dh16, d_taps, dln2, dx2, dy2, dq16, dkv = run(
             11,
             block_back_body,
@@ -920,7 +922,7 @@
             place=ends,
         )
         dkv_own = own_keys(dkv)
-        dkv_own = advance(dkv_own, (1, 4))
+        dq16 = advance(dq16, odd)
         shared = (dkv_own, w["wkv"], k["r"], w["gain"], dq16, w["wq"], w["wsr"], k["x"], dx2)
         if l:
             dr16, dln, dx, dy16, dz16, edge = run(
@@ -948,9 +950,9 @@
             jnp.concatenate([dln[2:4], dln2[1:2]], 0),
         )
     pieces.append([0, weight_grads(*waiting)])
-    de16 = advance(de16, (0, 2, 3))
+    de16 = advance(de16, even)
     (d_embed,) = run(3, embed_back_body, [((embed16.shape[0], D), f32)], patch_own, de16)
-    d_embed = advance(d_embed, (1, 3, 4))
+    d_embed = advance(d_embed, odd)
     d_gain = jnp.concatenate([dln_first[0:1]] + [g[1] for g in grads] + [dln_last[0:1]], 0)
     d_bias = jnp.concatenate([dln_first[1:2]] + [g[2] for g in grads] + [dln_last[1:2]], 0)
     d_taps = jnp.stack([g[0] for g in grads])
@@ -965,7 +967,7 @@
         cuts.append(cuts[-1] + part.shape[1])
     rest = padded_rest(rest)
 
-    late = 2
+    late = 3
 
     def together(parts):
         return to_bf(jnp.concatenate(parts, 0))
@@ -974,16 +976,13 @@
         assert all(p[0] > len(stages) for p in pieces[: LAYERS + 1 - late])
         early = together([p[1] for p in pieces[1 : LAYERS + 1 - late] + pieces[:1]])
         rest, early = tied(rest, early)
-    pieces.append([0, rest])
-    if paired:
-        while any(p[0] < len(stages) for p in pieces):
-            for p in pieces:
-                if p[0] < len(stages):
-                    p[1] = stages[p[0]](p[1])
-                    p[0] += 1
-        sums = [p[1] for p in pieces]
+        rest = advance(rest, even)
+        rest = advance(rest, odd)
+        last = plane_second(plane_first(pair_sum(rest)))
+        last = dp_sum(jnp.concatenate([pieces[-1][1], last], 1))
+        sums = [None] * (LAYERS + 1 - late) + [p[1] for p in pieces[LAYERS + 1 - late : -1]] + [last]
     else:
-        sums = [whole_sum([p[1]]) for p in pieces]
+        sums = [whole_sum([p[1]]) for p in pieces + [[0, rest]]]
         early = together(sums[1 : LAYERS + 1 - late] + sums[:1])
     early_got = lax.all_gather(early, "seq", axis=0, tiled=False)
     late_part, early_got = tied(together(sums[LAYERS + 1 - late :]), early_got)

time: 880 us -> 876 us (level)
  starting transfers between devices: 128 us -> 117 us
    ppermute x24 -> x21, waiting for transfers between devices: 44.4 us -> 14.4 us  [dp_sum(): total = total + lax.ppermute(to_bf(y[j]), 'dp', pairs).astype(f32)]
    ppermute x12, waiting for transfers between devices: 10.4 us -> 23.6 us  [edges(): other = lax.ppermute(edge, 'seq', between(1, True))]
    ppermute x24 -> x21, starting transfers between devices: 42.6 us -> 29.8 us  [dp_sum(): total = total + lax.ppermute(to_bf(y[j]), 'dp', pairs).astype(f32)]
    ppermute x32, waiting for transfers between devices: 17.7 us -> 29.8 us  [over_chips(): return lax.ppermute(v, 'seq', [(d ^ bit * subs, d) for d in range(n_seq)])]
    unnamed x779 -> x783, local copies, waits for them, and re-layouts: 102 us -> 99.3 us
  transfers between devices with their start and end apart: 112 -> 109, of which waited for: 33 -> 30; matrix products, arithmetic and copies ran while one was open for 19% -> 20% of each run, Pallas kernels for 24% -> 24%
where the time goes in v4:
time: 876 us; the launch traced here: 868 us
  Pallas kernels  249 us (28%)
  local copies, waits for them, and re-layouts  198 us (23%)
  waiting for transfers between devices  130 us (15%)
  other arithmetic  123 us (14%)
  starting transfers between devices  117 us (13%)
  between operations  30.4 us (3%)
  blocking collectives  21.4 us (2%)
    pallas_call x28, Pallas kernels, run(): pl.pallas_call(body, out_shape=[jax.ShapeDtypeStruct(s, d) for s, d in ou...  184 us
    unnamed x783, local copies, waits for them, and re-layouts  99.3 us
    pallas_call x6, Pallas kernels, weight_grads(): pl.pallas_call(functools.partial(weight_grads_body, n_dp, cols, subs), ou...  38.2 us
    ppermute x32, starting transfers between devices, over_chips(): return lax.ppermute(v, 'seq', [(d ^ bit * subs, d) for d in range(n_seq)])  34.9 us
    ppermute x9, waiting for transfers between devices, over_dp(): lax.ppermute(v, 'dp', [((d + j) % n_dp, d) for d in range(n_dp)])  31.6 us
    ppermute x21, starting transfers between devices, dp_sum(): total = total + lax.ppermute(to_bf(y[j]), 'dp', pairs).astype(f32)  29.8 us
    ppermute x32, waiting for transfers between devices, over_chips(): return lax.ppermute(v, 'seq', [(d ^ bit * subs, d) for d in range(n_seq)])  29.8 us
    pallas_call x1, Pallas kernels, per_device(): pl.pallas_call(functools.partial(update_body, cols, subs, late), grid=(LA...  26.7 us
  transfers between devices with their start and end apart: 109, of which 30 were waited for; matrix products, arithmetic and copies ran while one was open for 20% of the time, Pallas kernels for 24%

profile of v4, /device:TPU:0, one launch (start us, length us, event | category | flops | bytes accessed | tf_op | source)
XLA Modules:
  0.0 867.6 jit_solution(1137303901251035300)
XLA Ops:
  80.2 22.5 %collective-permute-done.5 = bf16[288,320]{1,0:T(8,128)(2,1)S(1)} collective-permute-done((bf16[288,320]{1,0:T(8,128)(2,1)S(1)}, bf16[288,320]{1,0:T(8,128)(2,1)S(1)}, u32[]{:S(2)}, u32[]{:S(2)}) %collective-permute-start.5) | collective-permute-done | bytes 184352 | tf_op jit(solution)/shard_map/ppermute | solution.py:656
  118.0 9.5 %collective-permute-start.2 = (bf16[128,1152]{1,0:T(8,128)(2,1)S(1)}, bf16[128,1152]{1,0:T(8,128)(2,1)S(1)}, u32[]{:S(2)}, u32[]{:S(2)}) collective-permute-start(bf16[128,1152]{1,0:T(8,128)(2,1)S(1)} %get-tuple-element.864), channel_id=1, source_target_pairs={{2,0},{6,1},{3,2},{7,3},{0,4},{4,5},{10,8},{14,9},{11,10},{15,11},... | collective-permute-start | bytes 884744 | tf_op jit(solution)/shard_map/ppermute | solution.py:613
  158.6 8.3 shard_map.444
  181.0 8.4 shard_map.446
  230.4 8.3 shard_map.448
  253.7 8.4 shard_map.450
  276.4 8.3 shard_map.452
  314.2 6.8 shard_map.454
  361.4 11.1 %shard_map.456 = (bf16[512,1280]{1,0:T(8,128)(2,1)}, f32[9,1280]{1,0:T(8,128)S(1)}, f32[2,320]{1,0:T(2,128)S(1)}, f32[512,320]{1,0:T(8,128)S(1)}, bf16[512,320]{...) custom-call(s32[2]{0:T(128)S(1)} %add_convert_fusion.place, bf16[512,1280]{1,0:T(8,128)(2,1)} %copy-done.26, ...), custom_call_target="tpu_custom_call" | custom-call | flops 1100000000 | bytes 1100000 | tf_op jit(solution)/shard_map/pallas_call | solution.py:88
  396.7 10.9 %shard_map.459 = (bf16[512,1280]{1,0:T(8,128)(2,1)}, f32[9,1280]{1,0:T(8,128)S(1)}, f32[2,320]{1,0:T(2,128)S(1)}, f32[512,320]{1,0:T(8,128)S(1)}, bf16[512,320]{...) custom-call(s32[2]{0:T(128)S(1)} %add_convert_fusion.place, bf16[512,1280]{1,0:T(8,128)(2,1)} %copy-done.32, ...), custom_call_target="tpu_custom_call" | custom-call | flops 1100000000 | bytes 1100000 | tf_op jit(solution)/shard_map/pallas_call | solution.py:88
  419.0 6.6 shard_map.460
  441.6 11.1 %shard_map.462 = (bf16[512,1280]{1,0:T(8,128)(2,1)}, f32[9,1280]{1,0:T(8,128)S(1)}, f32[2,320]{1,0:T(2,128)S(1)}, f32[512,320]{1,0:T(8,128)S(1)}, bf16[512,320]{...) custom-call(s32[2]{0:T(128)S(1)} %add_convert_fusion.place, bf16[512,1280]{1,0:T(8,128)(2,1)} %copy-done.31, ...), custom_call_target="tpu_custom_call" | custom-call | flops 1100000000 | bytes 1100000 | tf_op jit(solution)/shard_map/pallas_call | solution.py:88
  466.1 6.6 shard_map.463
  492.6 11.0 %shard_map.465 = (bf16[512,1280]{1,0:T(8,128)(2,1)}, f32[9,1280]{1,0:T(8,128)S(1)}, f32[2,320]{1,0:T(2,128)S(1)}, f32[512,320]{1,0:T(8,128)S(1)}, bf16[512,320]{...) custom-call(s32[2]{0:T(128)S(1)} %add_convert_fusion.place, bf16[512,1280]{1,0:T(8,128)(2,1)} %copy-done.30, ...), custom_call_target="tpu_custom_call" | custom-call | flops 1100000000 | bytes 1100000 | tf_op jit(solution)/shard_map/pallas_call | solution.py:88
  517.7 6.6 shard_map.466
  543.7 11.1 %shard_map.468 = (bf16[512,1280]{1,0:T(8,128)(2,1)}, f32[9,1280]{1,0:T(8,128)S(1)}, f32[2,320]{1,0:T(2,128)S(1)}, f32[512,320]{1,0:T(8,128)S(1)}, bf16[512,320]{...) custom-call(s32[2]{0:T(128)S(1)} %add_convert_fusion.place, bf16[512,1280]{1,0:T(8,128)(2,1)} %copy-done.29, ...), custom_call_target="tpu_custom_call" | custom-call | flops 1100000000 | bytes 1100000 | tf_op jit(solution)/shard_map/pallas_call | solution.py:88
  595.9 10.9 %shard_map.471 = (bf16[512,1280]{1,0:T(8,128)(2,1)}, f32[9,1280]{1,0:T(8,128)S(1)}, f32[2,320]{1,0:T(2,128)S(1)}, f32[512,320]{1,0:T(8,128)S(1)}, bf16[512,320]{...) custom-call(s32[2]{0:T(128)S(1)} %add_convert_fusion.place, bf16[512,1280]{1,0:T(8,128)(2,1)} %copy-done.28, ...), custom_call_target="tpu_custom_call" | custom-call | flops 1100000000 | bytes 1100000 | tf_op jit(solution)/shard_map/pallas_call | solution.py:88
  673.8 12.0 %collective-permute-done.90 = bf16[2,4,40,640]{3,2,1,0:T(8,128)(2,1)S(1)} collective-permute-done((bf16[2,4,40,640]{3,2,1,0:T(8,128)(2,1)}, bf16[2,4,40,640]{3,2,1,0:T(8,128)(2,1)S(1)}, u32[]{:S(2)}, u32[]{:S(2)}) %collective-permute-start.90) | collective-permute-done | bytes 409632 | tf_op jit(solution)/shard_map/ppermute | solution.py:862
  728.4 7.3 collective-permute-done.103
  757.8 8.7 %all-gather.15.cloned.1.call-done = bf16[2176,640]{1,0:T(8,128)(2,1)} async-done(((bf16[272,640]{1,0:T(8,128)(2,1)}), bf16[2176,640]{1,0:T(8,128)(2,1)}) %all-gather.15.cloned.1.call-update) | async-done | bytes 2785296 | tf_op jit(solution)/shard_map/all_gather | solution.py:989
  773.9 12.4 %psum.29 = f32[]{:T(128)} all-reduce(f32[]{:T(128)S(6)} %add.1014), channel_id=1, replica_groups=mesh['dp'=4,'seq'=8] {'dp'}, use_global_device_ids=true, to_apply=%region_8.9 | all-reduce | flops 1 | bytes 8 | tf_op jit(solution)/shard_map/psum | solution.py:1006
  788.0 26.7 %shard_map.475 = (f32[6,80,2560]{2,1,0:T(8,128)}, f32[6,80,2560]{2,1,0:T(8,128)}, f32[6,80,2560]{2,1,0:T(8,128)}, f32[6,2,320,320]{3,2,1,0:T(8,128)}, f32[6,2,32...) custom-call(f32[1]{0:T(128)} %bitcast.182.factor_ref, bf16[8,256,640]{2,1,0:T(8,128)(2,1)} %bitcast.487, ...), custom_call_target="tpu_custom_call" | custom-call | flops 2500000000 | bytes 2500000 | tf_op jit(solution)/shard_map/pallas_call | solution.py:1022
  825.0 9.0 %all-reduce.9 = (f32[]{:T(128)}, f32[22]{0:T(128)S(1)}, f32[22]{0:T(128)S(1)}) all-reduce(f32[]{:T(128)} %fusion.118, f32[22]{0:T(128)S(1)} %get-tuple-element.978, f32[22]{0:T(128)S(1)} %get-tuple-element.979), channel_id=1, replica_groups=mesh['dp'=4,'seq'=8] {'dp'}, use_global_device_ids=true, to_apply=%region_5.6 | all-reduce | flops 45 | bytes 360 | tf_op jit(solution)/shard_map/psum | solution.py:1006
  842.7 7.5 multiply_subtract_fusion.1
  (1336 shorter events, 587.0 us)
Async XLA Ops:
  7.2 129.9 %all-gather.9.cloned.1.call-start = ((), (), s32[]{:S(2)}) async-start(), calls=%async_computation | async-start | bytes 10137600 | tf_op jit(solution)/shard_map/all_gather | solution.py:640
  19.5 201.3 %all-gather.11.cloned.1.call-start = ((), (), s32[]{:S(2)}) async-start(), calls=%async_computation.1 | async-start | bytes 10813440 | tf_op jit(solution)/shard_map/all_gather | solution.py:640
  23.7 712.8 %all-gather.13.cloned.1.call-start = ((), (), s32[]{:S(2)}) async-start(), calls=%async_computation.2 | async-start | bytes 2949120 | tf_op jit(solution)/shard_map/all_gather | solution.py:987
  23.8 169.5 %collective-permute-start.26 = (s32[3]{0:T(128)}, s32[3]{0:T(128)}, u32[]{:S(2)}, u32[]{:S(2)}) collective-permute-start(s32[3]{0:T(128)} %param.28), channel_id=1, source_target_pairs={{8,0},{16,8},{24,16},{0,24},{9,1},{17,9},{25,17},{1,25},{10,2},{18... | collective-permute-start | bytes 44 | tf_op jit(solution)/shard_map/ppermute | solution.py:687
  28.9 258.2 %collective-permute-start.28 = (s32[3]{0:T(128)}, s32[3]{0:T(128)}, u32[]{:S(2)}, u32[]{:S(2)}) collective-permute-start(s32[3]{0:T(128)} %param.28), channel_id=1, source_target_pairs={{24,0},{0,8},{8,16},{16,24},{25,1},{1,9},{9,17},{17,25},{26,2},{2,... | collective-permute-start | bytes 44 | tf_op jit(solution)/shard_map/ppermute | solution.py:687
  28.9 270.3 %collective-permute-start.27 = (s32[3]{0:T(128)}, s32[3]{0:T(128)}, u32[]{:S(2)}, u32[]{:S(2)}) collective-permute-start(s32[3]{0:T(128)} %param.28), channel_id=1, source_target_pairs={{16,0},{24,8},{0,16},{8,24},{17,1},{25,9},{1,17},{9,25},{18,2},{26... | collective-permute-start | bytes 44 | tf_op jit(solution)/shard_map/ppermute | solution.py:687
  29.9 24.2 %collective-permute-start.9 = (bf16[2,20,80]{2,1,0:T(8,128)(2,1)S(1)}, bf16[2,20,80]{2,1,0:T(8,128)(2,1)S(1)}, u32[]{:S(2)}, u32[]{:S(2)}) collective-permute-start(bf16[2,20,80]{2,1,0:T(8,128)(2,1)S(1)} %pad_maximum_fusion.17), channel_id=1, source_target_pairs={{24,0},{0,8},{8,16},{16,24},{25,1},{1,9},{9,17},{17,25},{26,2},{2,... | collective-permute-start | bytes 19208 | tf_op jit(solution)/shard_map/ppermute | solution.py:656
  67.4 39.5 %collective-permute-start.6 = (bf16[288,320]{1,0:T(8,128)(2,1)S(1)}, bf16[288,320]{1,0:T(8,128)(2,1)S(1)}, u32[]{:S(2)}, u32[]{:S(2)}) collective-permute-start(bf16[288,320]{1,0:T(8,128)(2,1)S(1)} %get-tuple-element.744), channel_id=1, source_target_pairs={{24,0},{0,8},{8,16},{16,24},{25,1},{1,9},{9,17},{17,25},{26,2},{2,... | collective-permute-start | bytes 552968 | tf_op jit(solution)/shard_map/ppermute | solution.py:656
  77.8 25.0 %collective-permute-start.5 = (bf16[288,320]{1,0:T(8,128)(2,1)S(1)}, bf16[288,320]{1,0:T(8,128)(2,1)S(1)}, u32[]{:S(2)}, u32[]{:S(2)}) collective-permute-start(bf16[288,320]{1,0:T(8,128)(2,1)S(1)} %get-tuple-element.744), channel_id=1, source_target_pairs={{16,0},{24,8},{0,16},{8,24},{17,1},{25,9},{1,17},{9,25},{18,2},{26... | collective-permute-start | bytes 552968 | tf_op jit(solution)/shard_map/ppermute | solution.py:656
  102.7 31.2 %collective-permute-start.3 = (bf16[128,1152]{1,0:T(8,128)(2,1)S(1)}, bf16[128,1152]{1,0:T(8,128)(2,1)S(1)}, u32[]{:S(2)}, u32[]{:S(2)}) collective-permute-start(bf16[128,1152]{1,0:T(8,128)(2,1)S(1)} %get-tuple-element.863), channel_id=1, source_target_pairs={{3,0},{7,1},{0,2},{4,3},{1,4},{5,5},{11,8},{15,9},{8,10},{12,11},{... | collective-permute-start | bytes 884744 | tf_op jit(solution)/shard_map/ppermute | solution.py:613
  435.8 18.6 %collective-permute-start.46 = (f32[4,4,80,640]{3,2,1,0:T(8,128)S(1)}, f32[4,4,80,640]{3,2,1,0:T(8,128)}, u32[]{:S(2)}, u32[]{:S(2)}) collective-permute-start(f32[4,4,80,640]{3,2,1,0:T(8,128)S(1)} %copy-done.349), channel_id=1, source_target_pairs={{1,0},{0,1},{3,2},{2,3},{5,4},{4,5},{7,6},{6,7},{9,8},{8,9},{11,10... | collective-permute-start | bytes 9830408 | tf_op jit(solution)/shard_map/ppermute | solution.py:859
  457.7 25.1 %collective-permute-start.50 = (f32[4,40,640]{2,1,0:T(8,128)S(1)}, f32[4,40,640]{2,1,0:T(8,128)}, u32[]{:S(2)}, u32[]{:S(2)}) collective-permute-start(f32[4,40,640]{2,1,0:T(8,128)S(1)} %get-tuple-element.455), channel_id=1, source_target_pairs={{4,0},{5,1},{6,2},{7,3},{0,4},{1,5},{2,6},{3,7},{12,8},{13,9},{14,... | collective-permute-start | bytes 1228808 | tf_op jit(solution)/shard_map/ppermute | solution.py:862
  458.5 25.4 %collective-permute-start.51 = (f32[4,40,640]{2,1,0:T(8,128)}, f32[4,40,640]{2,1,0:T(8,128)S(1)}, u32[]{:S(2)}, u32[]{:S(2)}) collective-permute-start(f32[4,40,640]{2,1,0:T(8,128)} %get-tuple-element.457), channel_id=1, source_target_pairs={{2,0},{3,1},{0,2},{1,3},{6,4},{7,5},{4,6},{5,7},{10,8},{11,9},{8,1... | collective-permute-start | bytes 1228808 | tf_op jit(solution)/shard_map/ppermute | solution.py:862
  460.9 20.8 %collective-permute-start.52 = (bf16[2,4,40,640]{3,2,1,0:T(8,128)(2,1)}, bf16[2,4,40,640]{3,2,1,0:T(8,128)(2,1)}, u32[]{:S(2)}, u32[]{:S(2)}) collective-permute-start(bf16[2,4,40,640]{3,2,1,0:T(8,128)(2,1)} %pad_maximum_fusion.7), channel_id=1, source_target_pairs={{2,0},{3,1},{0,2},{1,3},{6,4},{7,5},{4,6},{5,7},{10,8},{11,9},{8,1... | collective-permute-start | bytes 1228808 | tf_op jit(solution)/shard_map/ppermute | solution.py:862
  511.4 22.3 %collective-permute-start.60 = (f32[4,40,640]{2,1,0:T(8,128)S(1)}, f32[4,40,640]{2,1,0:T(8,128)}, u32[]{:S(2)}, u32[]{:S(2)}) collective-permute-start(f32[4,40,640]{2,1,0:T(8,128)S(1)} %copy-done.298), channel_id=1, source_target_pairs={{4,0},{5,1},{6,2},{7,3},{0,4},{1,5},{2,6},{3,7},{12,8},{13,9},{14,... | collective-permute-start | bytes 1228808 | tf_op jit(solution)/shard_map/ppermute | solution.py:862
  512.6 22.1 %collective-permute-start.61 = (f32[4,40,640]{2,1,0:T(8,128)}, f32[4,40,640]{2,1,0:T(8,128)}, u32[]{:S(2)}, u32[]{:S(2)}) collective-permute-start(f32[4,40,640]{2,1,0:T(8,128)} %get-tuple-element.492), channel_id=1, source_target_pairs={{2,0},{3,1},{0,2},{1,3},{6,4},{7,5},{4,6},{5,7},{10,8},{11,9},{8,1... | collective-permute-start | bytes 1228808 | tf_op jit(solution)/shard_map/ppermute | solution.py:862
  562.5 21.7 %collective-permute-start.70 = (f32[4,40,640]{2,1,0:T(8,128)}, f32[4,40,640]{2,1,0:T(8,128)}, u32[]{:S(2)}, u32[]{:S(2)}) collective-permute-start(f32[4,40,640]{2,1,0:T(8,128)} %get-tuple-element.525), channel_id=1, source_target_pairs={{4,0},{5,1},{6,2},{7,3},{0,4},{1,5},{2,6},{3,7},{12,8},{13,9},{14,... | collective-permute-start | bytes 1228808 | tf_op jit(solution)/shard_map/ppermute | solution.py:862
  563.4 21.9 %collective-permute-start.71 = (f32[4,40,640]{2,1,0:T(8,128)}, f32[4,40,640]{2,1,0:T(8,128)}, u32[]{:S(2)}, u32[]{:S(2)}) collective-permute-start(f32[4,40,640]{2,1,0:T(8,128)} %get-tuple-element.527), channel_id=1, source_target_pairs={{2,0},{3,1},{0,2},{1,3},{6,4},{7,5},{4,6},{5,7},{10,8},{11,9},{8,1... | collective-permute-start | bytes 1228808 | tf_op jit(solution)/shard_map/ppermute | solution.py:862
  588.4 18.9 %collective-permute-start.76 = (f32[4,4,80,640]{3,2,1,0:T(8,128)}, f32[4,4,80,640]{3,2,1,0:T(8,128)}, u32[]{:S(2)}, u32[]{:S(2)}) collective-permute-start(f32[4,4,80,640]{3,2,1,0:T(8,128)} %get-tuple-element.553), channel_id=1, source_target_pairs={{1,0},{0,1},{3,2},{2,3},{5,4},{4,5},{7,6},{6,7},{9,8},{8,9},{11,10... | collective-permute-start | bytes 9830408 | tf_op jit(solution)/shard_map/ppermute | solution.py:859
  614.5 22.1 %collective-permute-start.80 = (f32[4,40,640]{2,1,0:T(8,128)}, f32[4,40,640]{2,1,0:T(8,128)}, u32[]{:S(2)}, u32[]{:S(2)}) collective-permute-start(f32[4,40,640]{2,1,0:T(8,128)} %get-tuple-element.560), channel_id=1, source_target_pairs={{4,0},{5,1},{6,2},{7,3},{0,4},{1,5},{2,6},{3,7},{12,8},{13,9},{14,... | collective-permute-start | bytes 1228808 | tf_op jit(solution)/shard_map/ppermute | solution.py:862
  615.9 21.8 %collective-permute-start.81 = (f32[4,40,640]{2,1,0:T(8,128)S(1)}, f32[4,40,640]{2,1,0:T(8,128)}, u32[]{:S(2)}, u32[]{:S(2)}) collective-permute-start(f32[4,40,640]{2,1,0:T(8,128)S(1)} %get-tuple-element.562), channel_id=1, source_target_pairs={{2,0},{3,1},{0,2},{1,3},{6,4},{7,5},{4,6},{5,7},{10,8},{11,9},{8,1... | collective-permute-start | bytes 1228808 | tf_op jit(solution)/shard_map/ppermute | solution.py:862
  662.9 24.1 %collective-permute-start.88 = (f32[4,40,640]{2,1,0:T(8,128)}, f32[4,40,640]{2,1,0:T(8,128)}, u32[]{:S(2)}, u32[]{:S(2)}) collective-permute-start(f32[4,40,640]{2,1,0:T(8,128)} %get-tuple-element.612), channel_id=1, source_target_pairs={{4,0},{5,1},{6,2},{7,3},{0,4},{1,5},{2,6},{3,7},{12,8},{13,9},{14,... | collective-permute-start | bytes 1228808 | tf_op jit(solution)/shard_map/ppermute | solution.py:862
  663.8 24.4 %collective-permute-start.89 = (f32[4,40,640]{2,1,0:T(8,128)S(1)}, f32[4,40,640]{2,1,0:T(8,128)}, u32[]{:S(2)}, u32[]{:S(2)}) collective-permute-start(f32[4,40,640]{2,1,0:T(8,128)S(1)} %copy-done.297), channel_id=1, source_target_pairs={{2,0},{3,1},{0,2},{1,3},{6,4},{7,5},{4,6},{5,7},{10,8},{11,9},{8,1... | collective-permute-start | bytes 1228808 | tf_op jit(solution)/shard_map/ppermute | solution.py:862
  672.7 93.8 %all-gather.15.cloned.1.call-start = ((), (), s32[]{:S(2)}) async-start(), calls=%async_computation.3 | async-start | bytes 3133440 | tf_op jit(solution)/shard_map/all_gather | solution.py:989
  (439 other events, 3243.4 us)
Sparse Core Ops, SparseCore 0:
  19.6 97.2 all-gather.8
  120.3 86.2 all-gather.10
  672.8 32.3 all-gather.12
  736.7 29.7 all-gather.14

commit v5 on v4

--- a/solution.py
+++ b/solution.py
@@ -434,7 +434,7 @@
                 for j in range(subs) if len(outs) == 1 else (None,):
                     if j is None:
                         k = core_ref[0] if n == 0 else 1 - core_ref[0]
-                        at = (c ^ core_ref[1], lax.rem(d + n_dp - core_ref[2], n_dp))
+                        at = (c ^ core_ref[1], d)
                     else:
                         k = j
                         at = (c, j, d)
@@ -670,10 +670,8 @@
     def layers_of(got, count):
         return [(proj_of(got[2 * i]), got[2 * i + 1].reshape(FF, 2 * D)) for i in range(count)]
 
-    raw = [
-        gathered(more + [p for l in members for p in layer_part(l)])
-        for members, more in zip(groups, extra)
-    ]
+    parts_of = [more + [p for l in members for p in layer_part(l)] for members, more in zip(groups, extra)]
+    raw = [gathered(parts_of[0])]
     first_late = groups[1][0]
 
     def own(v):
@@ -719,20 +717,22 @@
             bias=bias32[base : base + 3],
         )
 
+    full = ((tok, D), f32)
+    ln_first = jnp.stack([gain32[0], bias32[0]])
+    spread = patches.reshape(img_dev, rows, HALF, 2, -1).transpose(0, 1, 3, 2, 4)
+    patch_own = to_team(spread.reshape(img_dev, rows * W, -1))
+    e, x = run(2, embed_body, [full, full], patch_own, embed16, ln_first)
+    second, x = lax.optimization_barrier((parts_of[1], x))
+    raw.append(gathered(second))
     wts = [weights(l, layer) for l, layer in zip(groups[0], layers_of(cut(*raw[0]), len(groups[0])))]
-    ln_first = jnp.stack([gain32[0], bias32[0]])
     ln_last = jnp.stack([gain32[-1], bias32[-1]])
 
-    full = ((tok, D), f32)
     half = ((tok, D), bf16)
     wide16 = ((tok, FF), bf16)
     input_outs = [half, half, ((keys_own, D), f32), ((keys_own, D), bf16), ((keys_own, 2 * D), bf16)]
     ln_out = ((2, D), f32)
     row16 = ((W, FF), bf16)
 
-    spread = patches.reshape(img_dev, rows, HALF, 2, -1).transpose(0, 1, 3, 2, 4)
-    patch_own = to_team(spread.reshape(img_dev, rows * W, -1))
-    e, x = run(2, embed_body, [full, full], patch_own, embed16, ln_first)
     w = wts[0]
     a16, q16, r, rn16, kv16 = run(
         2, first_body, input_outs, x, w["gain"], w["bias"], w["wq"], w["wsr"], w["wkv"]
@@ -827,7 +827,7 @@
     piece = ((cols, n_dp, 2 * sub_in, wide), f32)
     paired = subs == 2 and cols == 4
     chip = seq_pos // subs
-    where = jnp.stack([core, chip, dp_pos]).astype(jnp.int32)
+    where = jnp.stack([core, chip]).astype(jnp.int32)
 
     def weight_grads(*args):
         vm = pl.BlockSpec(memory_space=pltpu.VMEM)
@@ -850,8 +850,6 @@
         if not paired:
             return [flat]
         flat = jnp.stack([lax.dynamic_index_in_dim(flat, chip ^ j, 0, False) for j in range(cols)])
-        twice = jnp.concatenate([flat, flat], 2)
-        flat = lax.dynamic_slice_in_dim(twice, dp_pos, n_dp, 2)
         return [lax.dynamic_index_in_dim(flat, k, 1, False) for k in (core, 1 - core)]
 
     def pair_sum(parts):
@@ -873,11 +871,14 @@
         two = parts[2] + over_chips(parts[3], 1)
         return jnp.concatenate([one, two], 1)
 
-    def dp_sum(y):
-        total = y[0]
+    def dp_sum(y, dtype=f32):
+        def of(j):
+            return lax.dynamic_index_in_dim(y, (dp_pos + j) % n_dp, 0, keepdims=False)
+
+        total = of(0)
         for j in range(1, n_dp):
             pairs = [(d, (d + j) % n_dp) for d in range(n_dp)]
-            total = total + lax.ppermute(to_bf(y[j]), "dp", pairs).astype(f32)
+            total = total + lax.ppermute(of(j).astype(dtype), "dp", pairs).astype(f32)
         return total
 
     def whole_sum(parts):
@@ -888,18 +889,23 @@
     def tied(value, others):
         return lax.optimization_barrier((value, others))
 
-    same = lambda v: v
-    stages = [pair_sum, plane_first, same, plane_second, same, dp_sum]
-    even, odd = ((0, 2, 4, 6), (1, 3, 5))
+    stages = [pair_sum, plane_first, plane_second]
     pieces = []
 
-    def advance(now, which):
+    def advance(now):
         if not paired:
             return now
-        ready = [p for p in pieces if p[0] in which]
+        ready = [p for p in pieces if p[0] <= len(stages) + 1]
         now, values = tied(now, [p[1] for p in ready])
-        for p, v in zip(ready, values):
-            p[1] = stages[p[0]](v) if p[0] < len(stages) else v
+        for n, (p, v) in enumerate(zip(ready, values)):
+            if p[0] < len(stages):
+                p[1] = stages[p[0]](v)
+            elif p[0] > len(stages) or p is pieces[0]:
+                p[1] = v
+            elif p is pieces[1]:
+                p[1] = dp_sum(jnp.concatenate([v, pieces[0][1]], 1))
+            else:
+                p[1] = dp_sum(v)
             p[0] += 1
         return now
 
@@ -909,10 +915,8 @@
     for l in reversed(range(LAYERS)):
         w, k = wts[l], kept[l]
         zlow, zhigh = edges(dz16, edge)
-        if waiting is not None:
-            pieces.append([0, weight_grads(*waiting)])
         upper = dy16
-        dz16 = advance(dz16, even)
+        dz16 = advance(dz16)
         dh16, d_taps, dln2, dx2, dy2, dq16, dkv = run(
             11,
             block_back_body,
@@ -921,8 +925,11 @@
             w["wo"], k["q16"], k["kv"], shut, k["lse"],
             place=ends,
         )
+        if waiting is not None:
+            first, _ = tied(waiting[0], dkv)
+            pieces.append([0, weight_grads(first, *waiting[1:])])
         dkv_own = own_keys(dkv)
-        dq16 = advance(dq16, odd)
+        dq16 = advance(dq16)
         shared = (dkv_own, w["wkv"], k["r"], w["gain"], dq16, w["wq"], w["wsr"], k["x"], dx2)
         if l:
             dr16, dln, dx, dy16, dz16, edge = run(
@@ -950,9 +957,9 @@
             jnp.concatenate([dln[2:4], dln2[1:2]], 0),
         )
     pieces.append([0, weight_grads(*waiting)])
-    de16 = advance(de16, even)
+    de16 = advance(de16)
     (d_embed,) = run(3, embed_back_body, [((embed16.shape[0], D), f32)], patch_own, de16)
-    d_embed = advance(d_embed, odd)
+    d_embed = advance(d_embed)
     d_gain = jnp.concatenate([dln_first[0:1]] + [g[1] for g in grads] + [dln_last[0:1]], 0)
     d_bias = jnp.concatenate([dln_first[1:2]] + [g[2] for g in grads] + [dln_last[1:2]], 0)
     d_taps = jnp.stack([g[0] for g in grads])
@@ -973,13 +980,14 @@
         return to_bf(jnp.concatenate(parts, 0))
 
     if paired:
-        assert all(p[0] > len(stages) for p in pieces[: LAYERS + 1 - late])
-        early = together([p[1] for p in pieces[1 : LAYERS + 1 - late] + pieces[:1]])
+        assert all(p[0] > len(stages) + 1 for p in pieces[: LAYERS + 1 - late])
+        own_rows = 2 * sub_in
+        parts = [p[1] for p in pieces[1 : LAYERS + 1 - late]]
+        early = together([parts[0][:own_rows], *parts[1:], parts[0][own_rows:]])
         rest, early = tied(rest, early)
-        rest = advance(rest, even)
-        rest = advance(rest, odd)
+        rest = advance(rest)
         last = plane_second(plane_first(pair_sum(rest)))
-        last = dp_sum(jnp.concatenate([pieces[-1][1], last], 1))
+        last = dp_sum(jnp.concatenate([pieces[-1][1], last], 1), bf16)
         sums = [None] * (LAYERS + 1 - late) + [p[1] for p in pieces[LAYERS + 1 - late : -1]] + [last]
     else:
         sums = [whole_sum([p[1]]) for p in pieces + [[0, rest]]]

time: 876 us -> 878 us (level)
  local copies, waits for them, and re-layouts: 198 us -> 226 us
  starting transfers between devices: 117 us -> 99.2 us
  other arithmetic: 123 us -> 110 us
    all_gather x2, waiting for transfers between devices: 0.01 us -> 29.3 us  [gathered(): lax.all_gather(jnp.concatenate(parts, 0), ('dp', 'seq'), axis=0, tiled=Fa...]
    ppermute x9, waiting for transfers between devices: 31.6 us -> 10.2 us  [over_dp(): lax.ppermute(v, 'dp', [((d + j) % n_dp, d) for d in range(n_dp)])]
    ppermute x12, waiting for transfers between devices: 23.6 us -> 5.92 us  [edges(): other = lax.ppermute(edge, 'seq', between(1, True))]
    unnamed x783 -> x848, local copies, waits for them, and re-layouts: 99.3 us -> 116 us
    ppermute x6, waiting for transfers between devices: 2.65 us -> 14.9 us  [own_keys(): total = total + lax.ppermute(part, 'seq', between(-j, True))]
    ppermute x4, waiting for transfers between devices: 10.7 us -> 0.01 us  [to_team(): got.append(lax.ppermute(send, 'seq', pairs))]
    ppermute x21 -> x18, starting transfers between devices: 29.8 us -> 22 us  [dp_sum(): total = total + lax.ppermute(of(j).astype(dtype), 'dp', pairs).astype(f32)]
    ppermute x21 -> x18, waiting for transfers between devices: 14.4 us -> 20.9 us  [dp_sum(): total = total + lax.ppermute(of(j).astype(dtype), 'dp', pairs).astype(f32)]
  transfers between devices with their start and end apart: 109 -> 106, of which waited for: 30 -> 31; matrix products, arithmetic and copies ran while one was open for 20% -> 18% of each run, Pallas kernels for 24% -> 24%
where the time goes in v5:
time: 878 us; the launch traced here: 868 us
  Pallas kernels  249 us (28%)
  local copies, waits for them, and re-layouts  226 us (26%)
  waiting for transfers between devices  133 us (15%)
  other arithmetic  110 us (13%)
  starting transfers between devices  99.2 us (11%)
  between operations  30.4 us (3%)
  blocking collectives  21.4 us (2%)
    pallas_call x28, Pallas kernels, run(): pl.pallas_call(body, out_shape=[jax.ShapeDtypeStruct(s, d) for s, d in ou...  184 us
    unnamed x848, local copies, waits for them, and re-layouts  116 us
    pallas_call x6, Pallas kernels, weight_grads(): pl.pallas_call(functools.partial(weight_grads_body, n_dp, cols, subs), ou...  38.6 us
    ppermute x32, waiting for transfers between devices, over_chips(): return lax.ppermute(v, 'seq', [(d ^ bit * subs, d) for d in range(n_seq)])  36.6 us
    ppermute x32, starting transfers between devices, over_chips(): return lax.ppermute(v, 'seq', [(d ^ bit * subs, d) for d in range(n_seq)])  33.6 us
    all_gather x2, waiting for transfers between devices, gathered(): lax.all_gather(jnp.concatenate(parts, 0), ('dp', 'seq'), axis=0, tiled=Fa...  29.3 us
    pallas_call x1, Pallas kernels, per_device(): pl.pallas_call(functools.partial(update_body, cols, subs, late), grid=(LA...  26.7 us
    ppermute x18, starting transfers between devices, dp_sum(): total = total + lax.ppermute(of(j).astype(dtype), 'dp', pairs).astype(f32)  22 us
  transfers between devices with their start and end apart: 106, of which 31 were waited for; matrix products, arithmetic and copies ran while one was open for 18% of the time, Pallas kernels for 24%

profile of v5, /device:TPU:0, one launch (start us, length us, event | category | flops | bytes accessed | tf_op | source)
XLA Modules:
  0.0 868.5 jit_solution(7237191664505316511)
XLA Ops:
  87.1 7.1 collective-permute-done.13
  96.0 24.3 %all-gather.9.cloned.1.call-done = bf16[7680,640]{1,0:T(8,128)(2,1)} async-done(((bf16[240,640]{1,0:T(8,128)(2,1)}), bf16[7680,640]{1,0:T(8,128)(2,1)}) %all-gather.9.cloned.1.call-update) | async-done | bytes 9830416 | tf_op jit(solution)/shard_map/all_gather | solution.py:640
  143.7 8.4 shard_map.444
  164.9 8.6 shard_map.446
  217.8 8.3 shard_map.448
  239.3 8.3 shard_map.450
  260.0 8.3 shard_map.452
  294.4 6.6 shard_map.454
  339.5 11.4 %shard_map.456 = (bf16[512,1280]{1,0:T(8,128)(2,1)}, f32[9,1280]{1,0:T(8,128)S(1)}, f32[2,320]{1,0:T(2,128)S(1)}, f32[512,320]{1,0:T(8,128)S(1)}, bf16[512,320]{...) custom-call(s32[2]{0:T(128)S(1)} %add_convert_fusion.place, bf16[512,1280]{1,0:T(8,128)(2,1)} %copy-done.26, ...), custom_call_target="tpu_custom_call" | custom-call | flops 1100000000 | bytes 1100000 | tf_op jit(solution)/shard_map/pallas_call | solution.py:88
  354.5 6.5 shard_map.457
  363.3 11.0 %shard_map.458 = (bf16[512,1280]{1,0:T(8,128)(2,1)}, f32[9,1280]{1,0:T(8,128)S(1)}, f32[2,320]{1,0:T(2,128)S(1)}, f32[512,320]{1,0:T(8,128)S(1)}, bf16[512,320]{...) custom-call(s32[2]{0:T(128)S(1)} %add_convert_fusion.place, bf16[512,1280]{1,0:T(8,128)(2,1)} %copy-done.32, ...), custom_call_target="tpu_custom_call" | custom-call | flops 1100000000 | bytes 1100000 | tf_op jit(solution)/shard_map/pallas_call | solution.py:88
  403.0 11.1 %shard_map.461 = (bf16[512,1280]{1,0:T(8,128)(2,1)}, f32[9,1280]{1,0:T(8,128)S(1)}, f32[2,320]{1,0:T(2,128)S(1)}, f32[512,320]{1,0:T(8,128)S(1)}, bf16[512,320]{...) custom-call(s32[2]{0:T(128)S(1)} %add_convert_fusion.place, bf16[512,1280]{1,0:T(8,128)(2,1)} %copy-done.31, ...), custom_call_target="tpu_custom_call" | custom-call | flops 1100000000 | bytes 1100000 | tf_op jit(solution)/shard_map/pallas_call | solution.py:88
  470.3 11.4 %shard_map.464 = (bf16[512,1280]{1,0:T(8,128)(2,1)}, f32[9,1280]{1,0:T(8,128)S(1)}, f32[2,320]{1,0:T(2,128)S(1)}, f32[512,320]{1,0:T(8,128)S(1)}, bf16[512,320]{...) custom-call(s32[2]{0:T(128)S(1)} %add_convert_fusion.place, bf16[512,1280]{1,0:T(8,128)(2,1)} %copy-done.30, ...), custom_call_target="tpu_custom_call" | custom-call | flops 1100000000 | bytes 1100000 | tf_op jit(solution)/shard_map/pallas_call | solution.py:88
  519.0 11.0 %shard_map.467 = (bf16[512,1280]{1,0:T(8,128)(2,1)}, f32[9,1280]{1,0:T(8,128)S(1)}, f32[2,320]{1,0:T(2,128)S(1)}, f32[512,320]{1,0:T(8,128)S(1)}, bf16[512,320]{...) custom-call(s32[2]{0:T(128)S(1)} %add_convert_fusion.place, bf16[512,1280]{1,0:T(8,128)(2,1)} %copy-done.29, ...), custom_call_target="tpu_custom_call" | custom-call | flops 1100000000 | bytes 1100000 | tf_op jit(solution)/shard_map/pallas_call | solution.py:88
  565.1 11.1 %shard_map.470 = (bf16[512,1280]{1,0:T(8,128)(2,1)}, f32[9,1280]{1,0:T(8,128)S(1)}, f32[2,320]{1,0:T(2,128)S(1)}, f32[512,320]{1,0:T(8,128)S(1)}, bf16[512,320]{...) custom-call(s32[2]{0:T(128)S(1)} %add_convert_fusion.place, bf16[512,1280]{1,0:T(8,128)(2,1)} %copy-done.28, ...), custom_call_target="tpu_custom_call" | custom-call | flops 1100000000 | bytes 1100000 | tf_op jit(solution)/shard_map/pallas_call | solution.py:88
  597.7 6.8 shard_map.473
  664.5 11.7 %collective-permute-done.87 = bf16[2,4,40,640]{3,2,1,0:T(8,128)(2,1)S(1)} collective-permute-done((bf16[2,4,40,640]{3,2,1,0:T(8,128)(2,1)S(1)}, bf16[2,4,40,640]{3,2,1,0:T(8,128)(2,1)S(1)}, u32[]{:S(2)}, u32[]{:S(2)}) %collective-permute-start.87) | collective-permute-done | bytes 409632 | tf_op jit(solution)/shard_map/ppermute | solution.py:860
  677.9 11.0 %collective-permute-done.85 = f32[4,40,640]{2,1,0:T(8,128)S(1)} collective-permute-done((f32[4,40,640]{2,1,0:T(8,128)S(1)}, f32[4,40,640]{2,1,0:T(8,128)S(1)}, u32[]{:S(2)}, u32[]{:S(2)}) %collective-permute-start.85) | collective-permute-done | bytes 409632 | tf_op jit(solution)/shard_map/ppermute | solution.py:860
  719.9 10.2 %collective-permute-done.90 = f32[80,640]{1,0:T(8,128)S(1)} collective-permute-done((f32[80,640]{1,0:T(8,128)S(1)}, f32[80,640]{1,0:T(8,128)S(1)}, u32[]{:S(2)}, u32[]{:S(2)}) %collective-permute-start.90) | collective-permute-done | bytes 204832 | tf_op jit(solution)/shard_map/ppermute | solution.py:881
  757.7 9.1 %all-gather.15.cloned.1.call-done = bf16[2176,640]{1,0:T(8,128)(2,1)} async-done(((bf16[272,640]{1,0:T(8,128)(2,1)}), bf16[2176,640]{1,0:T(8,128)(2,1)}) %all-gather.15.cloned.1.call-update) | async-done | bytes 2785296 | tf_op jit(solution)/shard_map/all_gather | solution.py:997
  774.3 12.2 %psum.29 = f32[]{:T(128)} all-reduce(f32[]{:T(128)S(6)} %add.1058), channel_id=1, replica_groups=mesh['dp'=4,'seq'=8] {'dp'}, use_global_device_ids=true, to_apply=%region_8.9 | all-reduce | flops 1 | bytes 8 | tf_op jit(solution)/shard_map/psum | solution.py:1014
  789.1 26.7 %shard_map.475 = (f32[6,80,2560]{2,1,0:T(8,128)}, f32[6,80,2560]{2,1,0:T(8,128)}, f32[6,80,2560]{2,1,0:T(8,128)}, f32[6,2,320,320]{3,2,1,0:T(8,128)}, f32[6,2,32...) custom-call(f32[1]{0:T(128)} %bitcast.177.factor_ref, bf16[8,256,640]{2,1,0:T(8,128)(2,1)} %bitcast.466, ...), custom_call_target="tpu_custom_call" | custom-call | flops 2500000000 | bytes 2500000 | tf_op jit(solution)/shard_map/pallas_call | solution.py:1030
  828.0 9.2 %all-reduce.9 = (f32[]{:T(128)}, f32[22]{0:T(128)S(1)}, f32[22]{0:T(128)S(1)}) all-reduce(f32[]{:T(128)} %fusion.118, f32[22]{0:T(128)} %get-tuple-element.929, f32[22]{0:T(128)} %get-tuple-element.930), channel_id=1, replica_groups=mesh['dp'=4,'seq'=8] {'dp'}, use_global_device_ids=true, to_apply=%region_5.6 | all-reduce | flops 45 | bytes 360 | tf_op jit(solution)/shard_map/psum | solution.py:1014
  845.8 7.6 multiply_subtract_fusion.1
  (1397 shorter events, 580.3 us)
Async XLA Ops:
  7.2 113.1 %all-gather.9.cloned.1.call-start = ((), (), s32[]{:S(2)}) async-start(), calls=%async_computation | async-start | bytes 10137600 | tf_op jit(solution)/shard_map/all_gather | solution.py:640
  18.7 190.2 %all-gather.11.cloned.1.call-start = ((), (), s32[]{:S(2)}) async-start(), calls=%async_computation.1 | async-start | bytes 10813440 | tf_op jit(solution)/shard_map/all_gather | solution.py:640
  20.0 23.8 %collective-permute-start.9 = (bf16[2,20,80]{2,1,0:T(8,128)(2,1)}, bf16[2,20,80]{2,1,0:T(8,128)(2,1)}, u32[]{:S(2)}, u32[]{:S(2)}) collective-permute-start(bf16[2,20,80]{2,1,0:T(8,128)(2,1)} %pad_maximum_fusion.22), channel_id=1, source_target_pairs={{24,0},{0,8},{8,16},{16,24},{25,1},{1,9},{9,17},{17,25},{26,2},{2,... | collective-permute-start | bytes 19208 | tf_op jit(solution)/shard_map/ppermute | solution.py:656
  27.7 28.2 %collective-permute-start.6 = (bf16[288,320]{1,0:T(8,128)(2,1)S(1)}, bf16[288,320]{1,0:T(8,128)(2,1)S(1)}, u32[]{:S(2)}, u32[]{:S(2)}) collective-permute-start(bf16[288,320]{1,0:T(8,128)(2,1)S(1)} %get-tuple-element.698), channel_id=1, source_target_pairs={{24,0},{0,8},{8,16},{16,24},{25,1},{1,9},{9,17},{17,25},{26,2},{2,... | collective-permute-start | bytes 552968 | tf_op jit(solution)/shard_map/ppermute | solution.py:656
  28.4 26.1 %collective-permute-start.5 = (bf16[288,320]{1,0:T(8,128)(2,1)S(1)}, bf16[288,320]{1,0:T(8,128)(2,1)S(1)}, u32[]{:S(2)}, u32[]{:S(2)}) collective-permute-start(bf16[288,320]{1,0:T(8,128)(2,1)S(1)} %get-tuple-element.698), channel_id=1, source_target_pairs={{16,0},{24,8},{0,16},{8,24},{17,1},{25,9},{1,17},{9,25},{18,2},{26... | collective-permute-start | bytes 552968 | tf_op jit(solution)/shard_map/ppermute | solution.py:656
  64.8 671.2 %all-gather.13.cloned.1.call-start = ((), (), s32[]{:S(2)}) async-start(), calls=%async_computation.2 | async-start | bytes 2949120 | tf_op jit(solution)/shard_map/all_gather | solution.py:995
  64.9 112.6 %collective-permute-start.26 = (s32[3]{0:T(128)}, s32[3]{0:T(128)}, u32[]{:S(2)}, u32[]{:S(2)}) collective-permute-start(s32[3]{0:T(128)} %param.28), channel_id=1, source_target_pairs={{8,0},{16,8},{24,16},{0,24},{9,1},{17,9},{25,17},{1,25},{10,2},{18... | collective-permute-start | bytes 44 | tf_op jit(solution)/shard_map/ppermute | solution.py:685
  67.1 201.7 %collective-permute-start.28 = (s32[3]{0:T(128)}, s32[3]{0:T(128)}, u32[]{:S(2)}, u32[]{:S(2)}) collective-permute-start(s32[3]{0:T(128)} %param.28), channel_id=1, source_target_pairs={{24,0},{0,8},{8,16},{16,24},{25,1},{1,9},{9,17},{17,25},{26,2},{2,... | collective-permute-start | bytes 44 | tf_op jit(solution)/shard_map/ppermute | solution.py:685
  69.2 211.5 %collective-permute-start.27 = (s32[3]{0:T(128)}, s32[3]{0:T(128)}, u32[]{:S(2)}, u32[]{:S(2)}) collective-permute-start(s32[3]{0:T(128)} %param.28), channel_id=1, source_target_pairs={{16,0},{24,8},{0,16},{8,24},{17,1},{25,9},{1,17},{9,25},{18,2},{26... | collective-permute-start | bytes 44 | tf_op jit(solution)/shard_map/ppermute | solution.py:685
  71.4 22.8 %collective-permute-start.14 = (bf16[54,320]{1,0:T(8,128)(2,1)S(1)}, bf16[54,320]{1,0:T(8,128)(2,1)S(1)}, u32[]{:S(2)}, u32[]{:S(2)}) collective-permute-start(bf16[54,320]{1,0:T(8,128)(2,1)S(1)} %reshape.856), channel_id=1, source_target_pairs={{24,0},{0,8},{8,16},{16,24},{25,1},{1,9},{9,17},{17,25},{26,2},{2,... | collective-permute-start | bytes 103688 | tf_op jit(solution)/shard_map/ppermute | solution.py:656
  424.3 24.7 %collective-permute-start.48 = (f32[4,4,80,640]{3,2,1,0:T(8,128)}, f32[4,4,80,640]{3,2,1,0:T(8,128)}, u32[]{:S(2)}, u32[]{:S(2)}) collective-permute-start(f32[4,4,80,640]{3,2,1,0:T(8,128)} %get-tuple-element.435), channel_id=1, source_target_pairs={{1,0},{0,1},{3,2},{2,3},{5,4},{4,5},{7,6},{6,7},{9,8},{8,9},{11,10... | collective-permute-start | bytes 9830408 | tf_op jit(solution)/shard_map/ppermute | solution.py:857
  455.2 33.0 %collective-permute-start.51 = (f32[96,640]{1,0:T(8,128)}, f32[96,640]{1,0:T(8,128)}, u32[]{:S(2)}, u32[]{:S(2)}) collective-permute-start(f32[96,640]{1,0:T(8,128)} %get-tuple-element.820), channel_id=1, source_target_pairs={{0,8},{8,16},{16,24},{24,0},{1,9},{9,17},{17,25},{25,1},{2,10},{10... | collective-permute-start | bytes 737288 | tf_op jit(solution)/shard_map/ppermute | solution.py:881
  456.5 31.7 %collective-permute-start.53 = (f32[96,640]{1,0:T(8,128)}, f32[96,640]{1,0:T(8,128)}, u32[]{:S(2)}, u32[]{:S(2)}) collective-permute-start(f32[96,640]{1,0:T(8,128)} %get-tuple-element.821), channel_id=1, source_target_pairs={{0,24},{8,0},{16,8},{24,16},{1,25},{9,1},{17,9},{25,17},{2,26},{10... | collective-permute-start | bytes 737288 | tf_op jit(solution)/shard_map/ppermute | solution.py:881
  459.0 29.2 %collective-permute-start.52 = (f32[96,640]{1,0:T(8,128)}, f32[96,640]{1,0:T(8,128)}, u32[]{:S(2)}, u32[]{:S(2)}) collective-permute-start(f32[96,640]{1,0:T(8,128)} %get-tuple-element.822), channel_id=1, source_target_pairs={{0,16},{8,24},{16,0},{24,8},{1,17},{9,25},{17,1},{25,9},{2,18},{10... | collective-permute-start | bytes 737288 | tf_op jit(solution)/shard_map/ppermute | solution.py:881
  459.8 30.5 %collective-permute-start.54 = (bf16[2,4,40,640]{3,2,1,0:T(8,128)(2,1)}, bf16[2,4,40,640]{3,2,1,0:T(8,128)(2,1)}, u32[]{:S(2)}, u32[]{:S(2)}) collective-permute-start(bf16[2,4,40,640]{3,2,1,0:T(8,128)(2,1)} %pad_maximum_fusion.9), channel_id=1, source_target_pairs={{2,0},{3,1},{0,2},{1,3},{6,4},{7,5},{4,6},{5,7},{10,8},{11,9},{8,1... | collective-permute-start | bytes 1228808 | tf_op jit(solution)/shard_map/ppermute | solution.py:860
  462.0 29.4 %collective-permute-start.55 = (bf16[2,4,40,640]{3,2,1,0:T(8,128)(2,1)}, bf16[2,4,40,640]{3,2,1,0:T(8,128)(2,1)}, u32[]{:S(2)}, u32[]{:S(2)}) collective-permute-start(bf16[2,4,40,640]{3,2,1,0:T(8,128)(2,1)} %stack.274), channel_id=1, source_target_pairs={{4,0},{5,1},{6,2},{7,3},{0,4},{1,5},{2,6},{3,7},{12,8},{13,9},{14,... | collective-permute-start | bytes 1228808 | tf_op jit(solution)/shard_map/ppermute | solution.py:860
  510.7 25.8 %collective-permute-start.61 = (f32[80,640]{1,0:T(8,128)}, f32[80,640]{1,0:T(8,128)S(1)}, u32[]{:S(2)}, u32[]{:S(2)}) collective-permute-start(f32[80,640]{1,0:T(8,128)} %get-tuple-element.836), channel_id=1, source_target_pairs={{0,8},{8,16},{16,24},{24,0},{1,9},{9,17},{17,25},{25,1},{2,10},{10... | collective-permute-start | bytes 614408 | tf_op jit(solution)/shard_map/ppermute | solution.py:881
  511.3 25.2 %collective-permute-start.63 = (f32[80,640]{1,0:T(8,128)}, f32[80,640]{1,0:T(8,128)S(1)}, u32[]{:S(2)}, u32[]{:S(2)}) collective-permute-start(f32[80,640]{1,0:T(8,128)} %get-tuple-element.837), channel_id=1, source_target_pairs={{0,24},{8,0},{16,8},{24,16},{1,25},{9,1},{17,9},{25,17},{2,26},{10... | collective-permute-start | bytes 614408 | tf_op jit(solution)/shard_map/ppermute | solution.py:881
  558.7 23.8 %collective-permute-start.71 = (f32[80,640]{1,0:T(8,128)}, f32[80,640]{1,0:T(8,128)S(1)}, u32[]{:S(2)}, u32[]{:S(2)}) collective-permute-start(f32[80,640]{1,0:T(8,128)} %get-tuple-element.833), channel_id=1, source_target_pairs={{0,8},{8,16},{16,24},{24,0},{1,9},{9,17},{17,25},{25,1},{2,10},{10... | collective-permute-start | bytes 614408 | tf_op jit(solution)/shard_map/ppermute | solution.py:881
  558.8 23.8 %collective-permute-start.73 = (f32[80,640]{1,0:T(8,128)}, f32[80,640]{1,0:T(8,128)S(1)}, u32[]{:S(2)}, u32[]{:S(2)}) collective-permute-start(f32[80,640]{1,0:T(8,128)} %get-tuple-element.834), channel_id=1, source_target_pairs={{0,24},{8,0},{16,8},{24,16},{1,25},{9,1},{17,9},{25,17},{2,26},{10... | collective-permute-start | bytes 614408 | tf_op jit(solution)/shard_map/ppermute | solution.py:881
  610.7 33.9 %collective-permute-start.84 = (f32[4,4,80,640]{3,2,1,0:T(8,128)}, f32[4,4,80,640]{3,2,1,0:T(8,128)}, u32[]{:S(2)}, u32[]{:S(2)}) collective-permute-start(f32[4,4,80,640]{3,2,1,0:T(8,128)} %get-tuple-element.545), channel_id=1, source_target_pairs={{1,0},{0,1},{3,2},{2,3},{5,4},{4,5},{7,6},{6,7},{9,8},{8,9},{11,10... | collective-permute-start | bytes 9830408 | tf_op jit(solution)/shard_map/ppermute | solution.py:857
  658.7 108.1 %all-gather.15.cloned.1.call-start = ((), (), s32[]{:S(2)}) async-start(), calls=%async_computation.3 | async-start | bytes 3133440 | tf_op jit(solution)/shard_map/all_gather | solution.py:997
  662.0 26.8 %collective-permute-start.85 = (f32[4,40,640]{2,1,0:T(8,128)S(1)}, f32[4,40,640]{2,1,0:T(8,128)S(1)}, u32[]{:S(2)}, u32[]{:S(2)}) collective-permute-start(f32[4,40,640]{2,1,0:T(8,128)S(1)} %copy-done.344), channel_id=1, source_target_pairs={{4,0},{5,1},{6,2},{7,3},{0,4},{1,5},{2,6},{3,7},{12,8},{13,9},{14,... | collective-permute-start | bytes 1228808 | tf_op jit(solution)/shard_map/ppermute | solution.py:860
  663.9 25.0 %collective-permute-start.86 = (f32[4,40,640]{2,1,0:T(8,128)S(1)}, f32[4,40,640]{2,1,0:T(8,128)S(1)}, u32[]{:S(2)}, u32[]{:S(2)}) collective-permute-start(f32[4,40,640]{2,1,0:T(8,128)S(1)} %copy-done.343), channel_id=1, source_target_pairs={{2,0},{3,1},{0,2},{1,3},{6,4},{7,5},{4,6},{5,7},{10,8},{11,9},{8,1... | collective-permute-start | bytes 1228808 | tf_op jit(solution)/shard_map/ppermute | solution.py:860
  (469 other events, 3862.1 us)
Sparse Core Ops, SparseCore 0:
  18.8 101.4 all-gather.8
  123.7 85.1 all-gather.10
  658.9 34.9 all-gather.12
  736.2 30.6 all-gather.14

commit v6 on v5

--- a/solution.py
+++ b/solution.py
@@ -483,8 +483,12 @@
                 for half in range(2):
                     at = (0, half, rows, slice(0, D))
                     put(1, at, (wd, md, vd), (md2, vd2, ud), g[sub:, half * D : (half + 1) * D])
+        lane = lax.broadcasted_iota(jnp.int32, (1, LANES), 1)
+        total = jnp.zeros((1, LANES), f32)
         for n in range(2):
-            sums[0, n : n + 1, :] = jnp.broadcast_to(jnp.sum(squares[n], 1, keepdims=True), (1, LANES))
+            value = jnp.broadcast_to(jnp.sum(squares[n], 1, keepdims=True), (1, LANES))
+            total = jnp.where(lane == 4 + n * LAYERS + layer, value, total)
+        sums[0] = jnp.broadcast_to(total, sums.shape[1:])
 
     pl.when(layer >= late)(lambda: go(early_ref))
     pl.when(layer < late)(lambda: go(late_ref))
@@ -492,15 +496,19 @@
 
 def group_sums(arrs, layered=None):
     embed, proj, downs, taps, head, gains, biases = arrs
-    if layered is None:
-        layered = [jnp.sum(a.reshape(a.shape[0], -1), 1) for a in (proj, downs)]
-    layered = [*layered, jnp.sum(taps.reshape(taps.shape[0], -1), 1)]
-    slot = jnp.arange(4 + 3 * LAYERS)
-    total = jnp.zeros((4 + 3 * LAYERS,), f32)
+    slot = lax.broadcasted_iota(jnp.int32, (1, 4 + 3 * LAYERS), 1)
+
+    def placed(values, start):
+        at = lax.broadcasted_iota(jnp.int32, (values.shape[0], 1), 0) + start
+        return jnp.sum(jnp.where(at == slot, values[:, None], 0.0), 0)
+
+    total = placed(jnp.sum(taps, (1, 2)), 4 + 2 * LAYERS)
     for n, a in enumerate((embed, head, gains, biases)):
-        total = jnp.where(slot == n, jnp.sum(a), total)
-    for n, a in enumerate(layered):
-        total = total + jnp.pad(a, (4 + LAYERS * n, LAYERS * (2 - n)))
+        total = total + jnp.where(slot[0] == n, jnp.sum(a), 0.0)
+    if layered is not None:
+        return total + layered
+    for n, a in enumerate((proj, downs)):
+        total = total + placed(jnp.sum(a.reshape(a.shape[0], -1), 1), 4 + n * LAYERS)
     return total
 
 
@@ -664,7 +672,7 @@
     taps32 = taps16.transpose(1, 0, 2).reshape(LAYERS, 9, FF).astype(f32)
     norms32 = norms16.transpose(1, 2, 0, 3).reshape(2, -1, D).astype(f32)
     gain32, bias32 = norms32[0], norms32[1]
-    groups = [[0, 1, 2], [3, 4, 5]]
+    groups = [[0, 1, 2, 3], [4, 5]]
     extra = [[], [part_of(to_bf(head_w).reshape(-1))]]
 
     def layers_of(got, count):
@@ -867,18 +875,18 @@
         return [one[0] + got[0][0], one[2] + got[0][1], two[0] + got[1][0], two[1] + got[1][1]]
 
     def plane_second(parts):
-        one = parts[0] + over_chips(parts[1], 2)
-        two = parts[2] + over_chips(parts[3], 1)
+        one = parts[0] + over_chips(parts[1].astype(wire[0]), 2).astype(f32)
+        two = parts[2] + over_chips(parts[3].astype(wire[0]), 1).astype(f32)
         return jnp.concatenate([one, two], 1)
 
-    def dp_sum(y, dtype=f32):
+    def dp_sum(y):
         def of(j):
             return lax.dynamic_index_in_dim(y, (dp_pos + j) % n_dp, 0, keepdims=False)
 
         total = of(0)
         for j in range(1, n_dp):
             pairs = [(d, (d + j) % n_dp) for d in range(n_dp)]
-            total = total + lax.ppermute(of(j).astype(dtype), "dp", pairs).astype(f32)
+            total = total + lax.ppermute(of(j).astype(wire[0]), "dp", pairs).astype(f32)
         return total
 
     def whole_sum(parts):
@@ -889,6 +897,7 @@
     def tied(value, others):
         return lax.optimization_barrier((value, others))
 
+    wire = [f32]
     stages = [pair_sum, plane_first, plane_second]
     pieces = []
 
@@ -956,6 +965,7 @@
             jnp.concatenate([dln[0:2], dln2[0:1]], 0),
             jnp.concatenate([dln[2:4], dln2[1:2]], 0),
         )
+    wire[0] = bf16
     pieces.append([0, weight_grads(*waiting)])
     de16 = advance(de16)
     (d_embed,) = run(3, embed_back_body, [((embed16.shape[0], D), f32)], patch_own, de16)
@@ -987,7 +997,7 @@
         rest, early = tied(rest, early)
         rest = advance(rest)
         last = plane_second(plane_first(pair_sum(rest)))
-        last = dp_sum(jnp.concatenate([pieces[-1][1], last], 1), bf16)
+        last = dp_sum(jnp.concatenate([pieces[-1][1], last], 1))
         sums = [None] * (LAYERS + 1 - late) + [p[1] for p in pieces[LAYERS + 1 - late : -1]] + [last]
     else:
         sums = [whole_sum([p[1]]) for p in pieces + [[0, rest]]]
@@ -1032,7 +1042,7 @@
         grid=(LAYERS,),
         out_shape=[jax.ShapeDtypeStruct(in_proj.shape, f32)] * 3
         + [jax.ShapeDtypeStruct(down_proj.shape, f32)] * 3
-        + [jax.ShapeDtypeStruct((LAYERS, 2, LANES), f32)],
+        + [jax.ShapeDtypeStruct((LAYERS, 8, LANES), f32)],
         in_specs=[
             pl.BlockSpec(memory_space=pltpu.SMEM),
             pl.BlockSpec(block, lambda l: (0, jnp.minimum(LAYERS - 1 - l, LAYERS - 1 - late), *tail)),
@@ -1040,7 +1050,7 @@
         ]
         + [proj_spec] * 3
         + [down_spec] * 3,
-        out_specs=[proj_spec] * 3 + [down_spec] * 3 + [pl.BlockSpec((1, 2, LANES), lambda l: (l, 0, 0))],
+        out_specs=[proj_spec] * 3 + [down_spec] * 3 + [pl.BlockSpec((1, 8, LANES), lambda l: (l, 0, 0))],
         compiler_params=pltpu.CompilerParams(vmem_limit_bytes=56 << 20),
         cost_estimate=cost(25),
     )(factor.reshape(1), *blocks_of, in_proj, m_proj, v_proj, down_proj, m_down, v_down)
@@ -1052,7 +1062,10 @@
         new_v.append(v2)
         updates.append(u)
     usq = lax.psum(
-        group_sums(tuple((u * u for u in updates)), [got[6][:, 0, 0], got[6][:, 1, 0]]), "dp"
+        group_sums(
+            tuple((u * u for u in updates)), jnp.sum(got[6][:, 0, : 4 + 3 * LAYERS], 0)
+        ),
+        "dp",
     )
     wnorm = jnp.sqrt(wsq)
     unorm = jnp.sqrt(usq)

time: 878 us -> 875 us (level)
  waiting for transfers between devices: 133 us -> 121 us
    ppermute x32, waiting for transfers between devices: 36.6 us -> 26.1 us  [over_chips(): return lax.ppermute(v, 'seq', [(d ^ bit * subs, d) for d in range(n_seq)])]
    all_gather x2, waiting for transfers between devices: 29.3 us -> 38.6 us  [gathered(): lax.all_gather(jnp.concatenate(parts, 0), ('dp', 'seq'), axis=0, tiled=Fa...]
    add x21 -> x25, other arithmetic: 15.5 us -> 18.1 us  [the longest x4 6.4 us: dp_sum(): total = total + lax.ppermute(of(j).astype(wire[0]), 'dp', pairs).astype(f32)]
    unnamed x848 -> x841, local copies, waits for them, and re-layouts: 116 us -> 113 us
  transfers between devices with their start and end apart: 106 -> 106, of which waited for: 31 -> 31; matrix products, arithmetic and copies ran while one was open for 18% -> 20% of each run, Pallas kernels for 24% -> 24%
where the time goes in v6:
time: 875 us; the launch traced here: 865 us
  Pallas kernels  248 us (28%)
  local copies, waits for them, and re-layouts  224 us (26%)
  waiting for transfers between devices  121 us (14%)
  other arithmetic  115 us (13%)
  starting transfers between devices  105 us (12%)
  between operations  30.4 us (3%)
  blocking collectives  21.4 us (2%)
    pallas_call x28, Pallas kernels, run(): pl.pallas_call(body, out_shape=[jax.ShapeDtypeStruct(s, d) for s, d in ou...  183 us
    unnamed x841, local copies, waits for them, and re-layouts  113 us
    all_gather x2, waiting for transfers between devices, gathered(): lax.all_gather(jnp.concatenate(parts, 0), ('dp', 'seq'), axis=0, tiled=Fa...  38.6 us
    pallas_call x6, Pallas kernels, weight_grads(): pl.pallas_call(functools.partial(weight_grads_body, n_dp, cols, subs), ou...  38.4 us
    ppermute x32, starting transfers between devices, over_chips(): return lax.ppermute(v, 'seq', [(d ^ bit * subs, d) for d in range(n_seq)])  32.6 us
    ppermute x18, starting transfers between devices, dp_sum(): total = total + lax.ppermute(of(j).astype(wire[0]), 'dp', pairs).astype(f32)  26.9 us
    pallas_call x1, Pallas kernels, per_device(): pl.pallas_call(functools.partial(update_body, cols, subs, late), grid=(LA...  26.7 us
    ppermute x32, waiting for transfers between devices, over_chips(): return lax.ppermute(v, 'seq', [(d ^ bit * subs, d) for d in range(n_seq)])  26.1 us
  transfers between devices with their start and end apart: 106, of which 31 were waited for; matrix products, arithmetic and copies ran while one was open for 20% of the time, Pallas kernels for 24%

profile of v6, /device:TPU:0, one launch (start us, length us, event | category | flops | bytes accessed | tf_op | source)
XLA Modules:
  0.0 864.9 jit_solution(4102255539097132512)
XLA Ops:
  102.1 38.6 %all-gather.9.cloned.1.call-done = bf16[10240,640]{1,0:T(8,128)(2,1)} async-done(((bf16[320,640]{1,0:T(8,128)(2,1)}), bf16[10240,640]{1,0:T(8,128)(2,1)}) %all-gather.9.cloned.1.call-update) | async-done | bytes 13107216 | tf_op jit(solution)/shard_map/all_gather | solution.py:648
  140.7 7.5 fusion.144
  169.3 8.5 shard_map.444
  190.9 8.7 %shard_map.446 = (bf16[512,1280]{1,0:T(8,128)(2,1)}, f32[512,1280]{1,0:T(8,128)}, f32[512,320]{1,0:T(8,128)S(1)}, bf16[512,320]{1,0:T(8,128)(2,1)S(1)}, bf16[512...) custom-call(s32[2]{0:T(128)S(1)} %add_convert_fusion.place, ...), custom_call_target="tpu_custom_call" | custom-call | flops 800000000 | bytes 800000 | tf_op jit(solution)/shard_map/pallas_call | solution.py:88
  212.2 8.2 shard_map.448
  254.3 8.3 shard_map.450
  274.5 8.3 shard_map.452
  308.9 6.8 shard_map.454
  354.1 11.0 %shard_map.456 = (bf16[512,1280]{1,0:T(8,128)(2,1)}, f32[9,1280]{1,0:T(8,128)S(1)}, f32[2,320]{1,0:T(2,128)S(1)}, f32[512,320]{1,0:T(8,128)S(1)}, bf16[512,320]{...) custom-call(s32[2]{0:T(128)S(1)} %add_convert_fusion.place, bf16[512,1280]{1,0:T(8,128)(2,1)} %copy-done.26, ...), custom_call_target="tpu_custom_call" | custom-call | flops 1100000000 | bytes 1100000 | tf_op jit(solution)/shard_map/pallas_call | solution.py:88
  368.6 6.5 shard_map.457
  377.5 11.1 %shard_map.458 = (bf16[512,1280]{1,0:T(8,128)(2,1)}, f32[9,1280]{1,0:T(8,128)S(1)}, f32[2,320]{1,0:T(2,128)S(1)}, f32[512,320]{1,0:T(8,128)S(1)}, bf16[512,320]{...) custom-call(s32[2]{0:T(128)S(1)} %add_convert_fusion.place, bf16[512,1280]{1,0:T(8,128)(2,1)} %copy-done.32, ...), custom_call_target="tpu_custom_call" | custom-call | flops 1100000000 | bytes 1100000 | tf_op jit(solution)/shard_map/pallas_call | solution.py:88
  417.1 11.3 %shard_map.461 = (bf16[512,1280]{1,0:T(8,128)(2,1)}, f32[9,1280]{1,0:T(8,128)S(1)}, f32[2,320]{1,0:T(2,128)S(1)}, f32[512,320]{1,0:T(8,128)S(1)}, bf16[512,320]{...) custom-call(s32[2]{0:T(128)S(1)} %add_convert_fusion.place, bf16[512,1280]{1,0:T(8,128)(2,1)} %copy-done.31, ...), custom_call_target="tpu_custom_call" | custom-call | flops 1100000000 | bytes 1100000 | tf_op jit(solution)/shard_map/pallas_call | solution.py:88
  453.7 6.5 shard_map.463
  485.4 11.0 %shard_map.464 = (bf16[512,1280]{1,0:T(8,128)(2,1)}, f32[9,1280]{1,0:T(8,128)S(1)}, f32[2,320]{1,0:T(2,128)S(1)}, f32[512,320]{1,0:T(8,128)S(1)}, bf16[512,320]{...) custom-call(s32[2]{0:T(128)S(1)} %add_convert_fusion.place, bf16[512,1280]{1,0:T(8,128)(2,1)} %copy-done.30, ...), custom_call_target="tpu_custom_call" | custom-call | flops 1100000000 | bytes 1100000 | tf_op jit(solution)/shard_map/pallas_call | solution.py:88
  533.6 11.3 %shard_map.467 = (bf16[512,1280]{1,0:T(8,128)(2,1)}, f32[9,1280]{1,0:T(8,128)S(1)}, f32[2,320]{1,0:T(2,128)S(1)}, f32[512,320]{1,0:T(8,128)S(1)}, bf16[512,320]{...) custom-call(s32[2]{0:T(128)S(1)} %add_convert_fusion.place, bf16[512,1280]{1,0:T(8,128)(2,1)} %copy-done.29, ...), custom_call_target="tpu_custom_call" | custom-call | flops 1100000000 | bytes 1100000 | tf_op jit(solution)/shard_map/pallas_call | solution.py:88
  580.5 11.0 %shard_map.470 = (bf16[512,1280]{1,0:T(8,128)(2,1)}, f32[9,1280]{1,0:T(8,128)S(1)}, f32[2,320]{1,0:T(2,128)S(1)}, f32[512,320]{1,0:T(8,128)S(1)}, bf16[512,320]{...) custom-call(s32[2]{0:T(128)S(1)} %add_convert_fusion.place, bf16[512,1280]{1,0:T(8,128)(2,1)} %copy-done.28, ...), custom_call_target="tpu_custom_call" | custom-call | flops 1100000000 | bytes 1100000 | tf_op jit(solution)/shard_map/pallas_call | solution.py:88
  612.5 6.6 shard_map.473
  682.8 8.3 collective-permute-done.87
  705.2 7.0 collective-permute-done.95
  755.6 7.8 all-gather.15.cloned.1.call-done
  770.8 12.2 %psum.29 = f32[]{:T(128)} all-reduce(f32[]{:T(128)S(6)} %add.1082), channel_id=1, replica_groups=mesh['dp'=4,'seq'=8] {'dp'}, use_global_device_ids=true, to_apply=%region_8.9 | all-reduce | flops 1 | bytes 8 | tf_op jit(solution)/shard_map/psum | solution.py:1024
  785.5 26.7 %shard_map.475 = (f32[6,80,2560]{2,1,0:T(8,128)}, f32[6,80,2560]{2,1,0:T(8,128)}, f32[6,80,2560]{2,1,0:T(8,128)}, f32[6,2,320,320]{3,2,1,0:T(8,128)}, f32[6,2,32...) custom-call(f32[1]{0:T(128)} %bitcast.177.factor_ref, bf16[8,256,640]{2,1,0:T(8,128)(2,1)} %bitcast.469, ...), custom_call_target="tpu_custom_call" | custom-call | flops 2500000000 | bytes 2500000 | tf_op jit(solution)/shard_map/pallas_call | solution.py:1040
  824.4 9.2 %all-reduce.3 = (f32[]{:T(128)}, f32[22]{0:T(128)S(1)}, f32[22]{0:T(128)S(1)}) all-reduce(f32[]{:T(128)} %fusion.131, f32[22]{0:T(128)} %get-tuple-element.946, f32[22]{0:T(128)} %get-tuple-element.947), channel_id=1, replica_groups=mesh['dp'=4,'seq'=8] {'dp'}, use_global_device_ids=true, to_apply=%region_5.6 | all-reduce | flops 45 | bytes 360 | tf_op jit(solution)/shard_map/psum | solution.py:1024
  842.2 7.6 multiply_subtract_fusion.1
  (1397 shorter events, 574.5 us)
Async XLA Ops:
  7.2 133.5 %all-gather.9.cloned.1.call-start = ((), (), s32[]{:S(2)}) async-start(), calls=%async_computation | async-start | bytes 13516800 | tf_op jit(solution)/shard_map/all_gather | solution.py:648
  21.9 216.8 %all-gather.11.cloned.1.call-start = ((), (), s32[]{:S(2)}) async-start(), calls=%async_computation.1 | async-start | bytes 7434240 | tf_op jit(solution)/shard_map/all_gather | solution.py:648
  32.2 28.3 %collective-permute-start.6 = (bf16[288,320]{1,0:T(8,128)(2,1)S(1)}, bf16[288,320]{1,0:T(8,128)(2,1)S(1)}, u32[]{:S(2)}, u32[]{:S(2)}) collective-permute-start(bf16[288,320]{1,0:T(8,128)(2,1)S(1)} %get-tuple-element.719), channel_id=1, source_target_pairs={{24,0},{0,8},{8,16},{16,24},{25,1},{1,9},{9,17},{17,25},{26,2},{2,... | collective-permute-start | bytes 552968 | tf_op jit(solution)/shard_map/ppermute | solution.py:664
  32.9 26.2 %collective-permute-start.5 = (bf16[288,320]{1,0:T(8,128)(2,1)S(1)}, bf16[288,320]{1,0:T(8,128)(2,1)S(1)}, u32[]{:S(2)}, u32[]{:S(2)}) collective-permute-start(bf16[288,320]{1,0:T(8,128)(2,1)S(1)} %get-tuple-element.719), channel_id=1, source_target_pairs={{16,0},{24,8},{0,16},{8,24},{17,1},{25,9},{1,17},{9,25},{18,2},{26... | collective-permute-start | bytes 552968 | tf_op jit(solution)/shard_map/ppermute | solution.py:664
  41.8 23.8 %collective-permute-start.3 = (bf16[128,1152]{1,0:T(8,128)(2,1)S(1)}, bf16[128,1152]{1,0:T(8,128)(2,1)S(1)}, u32[]{:S(2)}, u32[]{:S(2)}) collective-permute-start(bf16[128,1152]{1,0:T(8,128)(2,1)S(1)} %get-tuple-element.840), channel_id=1, source_target_pairs={{3,0},{7,1},{0,2},{4,3},{1,4},{5,5},{11,8},{15,9},{8,10},{12,11},{... | collective-permute-start | bytes 884744 | tf_op jit(solution)/shard_map/ppermute | solution.py:621
  69.6 664.1 %all-gather.13.cloned.1.call-start = ((), (), s32[]{:S(2)}) async-start(), calls=%async_computation.2 | async-start | bytes 2949120 | tf_op jit(solution)/shard_map/all_gather | solution.py:1005
  69.7 154.7 %collective-permute-start.26 = (s32[3]{0:T(128)}, s32[3]{0:T(128)}, u32[]{:S(2)}, u32[]{:S(2)}) collective-permute-start(s32[3]{0:T(128)} %param.28), channel_id=1, source_target_pairs={{8,0},{16,8},{24,16},{0,24},{9,1},{17,9},{25,17},{1,25},{10,2},{18... | collective-permute-start | bytes 44 | tf_op jit(solution)/shard_map/ppermute | solution.py:693
  73.8 209.4 %collective-permute-start.28 = (s32[3]{0:T(128)}, s32[3]{0:T(128)}, u32[]{:S(2)}, u32[]{:S(2)}) collective-permute-start(s32[3]{0:T(128)} %param.28), channel_id=1, source_target_pairs={{24,0},{0,8},{8,16},{16,24},{25,1},{1,9},{9,17},{17,25},{26,2},{2,... | collective-permute-start | bytes 44 | tf_op jit(solution)/shard_map/ppermute | solution.py:693
  75.9 219.4 %collective-permute-start.27 = (s32[3]{0:T(128)}, s32[3]{0:T(128)}, u32[]{:S(2)}, u32[]{:S(2)}) collective-permute-start(s32[3]{0:T(128)} %param.28), channel_id=1, source_target_pairs={{16,0},{24,8},{0,16},{8,24},{17,1},{25,9},{1,17},{9,25},{18,2},{26... | collective-permute-start | bytes 44 | tf_op jit(solution)/shard_map/ppermute | solution.py:693
  412.8 22.8 %collective-permute-start.44 = (bf16[2,4,40,640]{3,2,1,0:T(8,128)(2,1)}, bf16[2,4,40,640]{3,2,1,0:T(8,128)(2,1)S(1)}, u32[]{:S(2)}, u32[]{:S(2)}) collective-permute-start(bf16[2,4,40,640]{3,2,1,0:T(8,128)(2,1)} %pad_maximum_fusion.8), channel_id=1, source_target_pairs={{2,0},{3,1},{0,2},{1,3},{6,4},{7,5},{4,6},{5,7},{10,8},{11,9},{8,1... | collective-permute-start | bytes 1228808 | tf_op jit(solution)/shard_map/ppermute | solution.py:868
  438.5 24.8 %collective-permute-start.48 = (f32[4,4,80,640]{3,2,1,0:T(8,128)}, f32[4,4,80,640]{3,2,1,0:T(8,128)}, u32[]{:S(2)}, u32[]{:S(2)}) collective-permute-start(f32[4,4,80,640]{3,2,1,0:T(8,128)} %get-tuple-element.431), channel_id=1, source_target_pairs={{1,0},{0,1},{3,2},{2,3},{5,4},{4,5},{7,6},{6,7},{9,8},{8,9},{11,10... | collective-permute-start | bytes 9830408 | tf_op jit(solution)/shard_map/ppermute | solution.py:865
  469.3 33.5 %collective-permute-start.51 = (f32[96,640]{1,0:T(8,128)}, f32[96,640]{1,0:T(8,128)}, u32[]{:S(2)}, u32[]{:S(2)}) collective-permute-start(f32[96,640]{1,0:T(8,128)} %get-tuple-element.837), channel_id=1, source_target_pairs={{0,8},{8,16},{16,24},{24,0},{1,9},{9,17},{17,25},{25,1},{2,10},{10... | collective-permute-start | bytes 737288 | tf_op jit(solution)/shard_map/ppermute | solution.py:889
  470.0 32.9 %collective-permute-start.53 = (f32[96,640]{1,0:T(8,128)}, f32[96,640]{1,0:T(8,128)}, u32[]{:S(2)}, u32[]{:S(2)}) collective-permute-start(f32[96,640]{1,0:T(8,128)} %get-tuple-element.838), channel_id=1, source_target_pairs={{0,24},{8,0},{16,8},{24,16},{1,25},{9,1},{17,9},{25,17},{2,26},{10... | collective-permute-start | bytes 737288 | tf_op jit(solution)/shard_map/ppermute | solution.py:889
  473.1 29.7 %collective-permute-start.52 = (f32[96,640]{1,0:T(8,128)}, f32[96,640]{1,0:T(8,128)}, u32[]{:S(2)}, u32[]{:S(2)}) collective-permute-start(f32[96,640]{1,0:T(8,128)} %get-tuple-element.839), channel_id=1, source_target_pairs={{0,16},{8,24},{16,0},{24,8},{1,17},{9,25},{17,1},{25,9},{2,18},{10... | collective-permute-start | bytes 737288 | tf_op jit(solution)/shard_map/ppermute | solution.py:889
  474.0 31.1 %collective-permute-start.54 = (bf16[2,4,40,640]{3,2,1,0:T(8,128)(2,1)}, bf16[2,4,40,640]{3,2,1,0:T(8,128)(2,1)}, u32[]{:S(2)}, u32[]{:S(2)}) collective-permute-start(bf16[2,4,40,640]{3,2,1,0:T(8,128)(2,1)} %pad_maximum_fusion.9), channel_id=1, source_target_pairs={{2,0},{3,1},{0,2},{1,3},{6,4},{7,5},{4,6},{5,7},{10,8},{11,9},{8,1... | collective-permute-start | bytes 1228808 | tf_op jit(solution)/shard_map/ppermute | solution.py:868
  476.1 30.0 %collective-permute-start.55 = (bf16[2,4,40,640]{3,2,1,0:T(8,128)(2,1)}, bf16[2,4,40,640]{3,2,1,0:T(8,128)(2,1)}, u32[]{:S(2)}, u32[]{:S(2)}) collective-permute-start(bf16[2,4,40,640]{3,2,1,0:T(8,128)(2,1)} %stack.274), channel_id=1, source_target_pairs={{4,0},{5,1},{6,2},{7,3},{0,4},{1,5},{2,6},{3,7},{12,8},{13,9},{14,... | collective-permute-start | bytes 1228808 | tf_op jit(solution)/shard_map/ppermute | solution.py:868
  525.1 26.1 %collective-permute-start.61 = (f32[80,640]{1,0:T(8,128)}, f32[80,640]{1,0:T(8,128)S(1)}, u32[]{:S(2)}, u32[]{:S(2)}) collective-permute-start(f32[80,640]{1,0:T(8,128)} %get-tuple-element.853), channel_id=1, source_target_pairs={{0,8},{8,16},{16,24},{24,0},{1,9},{9,17},{17,25},{25,1},{2,10},{10... | collective-permute-start | bytes 614408 | tf_op jit(solution)/shard_map/ppermute | solution.py:889
  525.7 25.6 %collective-permute-start.63 = (f32[80,640]{1,0:T(8,128)}, f32[80,640]{1,0:T(8,128)S(1)}, u32[]{:S(2)}, u32[]{:S(2)}) collective-permute-start(f32[80,640]{1,0:T(8,128)} %get-tuple-element.854), channel_id=1, source_target_pairs={{0,24},{8,0},{16,8},{24,16},{1,25},{9,1},{17,9},{25,17},{2,26},{10... | collective-permute-start | bytes 614408 | tf_op jit(solution)/shard_map/ppermute | solution.py:889
  573.7 24.2 %collective-permute-start.71 = (f32[80,640]{1,0:T(8,128)}, f32[80,640]{1,0:T(8,128)S(1)}, u32[]{:S(2)}, u32[]{:S(2)}) collective-permute-start(f32[80,640]{1,0:T(8,128)} %get-tuple-element.850), channel_id=1, source_target_pairs={{0,8},{8,16},{16,24},{24,0},{1,9},{9,17},{17,25},{25,1},{2,10},{10... | collective-permute-start | bytes 614408 | tf_op jit(solution)/shard_map/ppermute | solution.py:889
  573.8 24.1 %collective-permute-start.73 = (f32[80,640]{1,0:T(8,128)}, f32[80,640]{1,0:T(8,128)}, u32[]{:S(2)}, u32[]{:S(2)}) collective-permute-start(f32[80,640]{1,0:T(8,128)} %get-tuple-element.851), channel_id=1, source_target_pairs={{0,24},{8,0},{16,8},{24,16},{1,25},{9,1},{17,9},{25,17},{2,26},{10... | collective-permute-start | bytes 614408 | tf_op jit(solution)/shard_map/ppermute | solution.py:889
  625.2 36.4 %collective-permute-start.84 = (f32[4,4,80,640]{3,2,1,0:T(8,128)}, f32[4,4,80,640]{3,2,1,0:T(8,128)}, u32[]{:S(2)}, u32[]{:S(2)}) collective-permute-start(f32[4,4,80,640]{3,2,1,0:T(8,128)} %get-tuple-element.541), channel_id=1, source_target_pairs={{1,0},{0,1},{3,2},{2,3},{5,4},{4,5},{7,6},{6,7},{9,8},{8,9},{11,10... | collective-permute-start | bytes 9830408 | tf_op jit(solution)/shard_map/ppermute | solution.py:865
  678.5 84.8 %all-gather.15.cloned.1.call-start = ((), (), s32[]{:S(2)}) async-start(), calls=%async_computation.3 | async-start | bytes 3133440 | tf_op jit(solution)/shard_map/all_gather | solution.py:1007
  696.5 26.0 %collective-permute-start.89 = (bf16[80,640]{1,0:T(8,128)(2,1)S(1)}, bf16[80,640]{1,0:T(8,128)(2,1)S(1)}, u32[]{:S(2)}, u32[]{:S(2)}) collective-permute-start(bf16[80,640]{1,0:T(8,128)(2,1)S(1)} %get-tuple-element.844), channel_id=1, source_target_pairs={{0,8},{8,16},{16,24},{24,0},{1,9},{9,17},{17,25},{25,1},{2,10},{10... | collective-permute-start | bytes 307208 | tf_op jit(solution)/shard_map/ppermute | solution.py:889
  696.6 27.0 %collective-permute-start.91 = (bf16[80,640]{1,0:T(8,128)(2,1)S(1)}, bf16[80,640]{1,0:T(8,128)(2,1)S(1)}, u32[]{:S(2)}, u32[]{:S(2)}) collective-permute-start(bf16[80,640]{1,0:T(8,128)(2,1)S(1)} %get-tuple-element.845), channel_id=1, source_target_pairs={{0,24},{8,0},{16,8},{24,16},{1,25},{9,1},{17,9},{25,17},{2,26},{10... | collective-permute-start | bytes 307208 | tf_op jit(solution)/shard_map/ppermute | solution.py:889
  (466 other events, 3789.9 us)
Sparse Core Ops, SparseCore 0:
  22.0 118.7 all-gather.8
  144.2 71.0 all-gather.10
  678.6 35.9 all-gather.12
  733.8 29.4 all-gather.14

commit v7 on v6

--- a/solution.py
+++ b/solution.py
@@ -643,13 +643,11 @@
         lower = lax.dynamic_slice_in_dim(down_proj[l], seq_pos * down_rows, down_rows, 1)
         return [to_bf(block), to_bf(jnp.concatenate([lower[0], lower[1]], 1))]
 
-    def gathered(parts):
-        sizes = [p.shape[0] for p in parts]
-        got = lax.all_gather(jnp.concatenate(parts, 0), ("dp", "seq"), axis=0, tiled=False)
-        return got, sizes
+    def gathered(part):
+        return lax.all_gather(part.reshape(-1, wide), "seq", axis=0, tiled=False)
 
     def cut(got, sizes):
-        got = got.reshape(n_dp, n_seq, sum(sizes), wide)
+        got = got.reshape(n_seq, n_dp, sum(sizes), wide).transpose(1, 0, 2, 3)
         starts = [sum(sizes[:i]) for i in range(len(sizes))]
         return [got[:, :, a : a + n] for a, n in zip(starts, sizes)]
 
@@ -666,21 +664,24 @@
         ]
         return lax.dynamic_slice_in_dim(jnp.stack(got + got), (n_dp - dp_pos) % n_dp, n_dp, 0)
 
-    embed16 = over_dp(to_bf(embed_w)).reshape(-1, D)
     taps16 = over_dp(to_bf(dw_kernel).reshape(LAYERS * 9, -1))
     norms16 = over_dp(to_bf(jnp.stack([norm_gain, norm_bias])))
     taps32 = taps16.transpose(1, 0, 2).reshape(LAYERS, 9, FF).astype(f32)
     norms32 = norms16.transpose(1, 2, 0, 3).reshape(2, -1, D).astype(f32)
     gain32, bias32 = norms32[0], norms32[1]
-    groups = [[0, 1, 2, 3], [4, 5]]
-    extra = [[], [part_of(to_bf(head_w).reshape(-1))]]
+    groups = [[0], [1, 2], [3, 4], [5]]
+    extra = [[], [], [], [part_of(to_bf(head_w).reshape(-1))]]
 
     def layers_of(got, count):
         return [(proj_of(got[2 * i]), got[2 * i + 1].reshape(FF, 2 * D)) for i in range(count)]
 
     parts_of = [more + [p for l in members for p in layer_part(l)] for members, more in zip(groups, extra)]
-    raw = [gathered(parts_of[0])]
-    first_late = groups[1][0]
+    sizes_of = [[p.shape[0] for p in parts] for parts in parts_of]
+    lines = [over_dp(jnp.concatenate(parts, 0)) for parts in parts_of]
+    behind, lines[0] = lax.optimization_barrier((to_bf(embed_w), lines[0]))
+    embed16 = over_dp(behind).reshape(-1, D)
+    raw = [gathered(lines[0])]
+    first_of = {members[0]: n for n, members in enumerate(groups)}
 
     def own(v):
         return lax.dynamic_index_in_dim(v, image, 0, keepdims=False)
@@ -730,9 +731,9 @@
     spread = patches.reshape(img_dev, rows, HALF, 2, -1).transpose(0, 1, 3, 2, 4)
     patch_own = to_team(spread.reshape(img_dev, rows * W, -1))
     e, x = run(2, embed_body, [full, full], patch_own, embed16, ln_first)
-    second, x = lax.optimization_barrier((parts_of[1], x))
-    raw.append(gathered(second))
-    wts = [weights(l, layer) for l, layer in zip(groups[0], layers_of(cut(*raw[0]), len(groups[0])))]
+    lines[1], x = lax.optimization_barrier((lines[1], x))
+    raw += [gathered(line) for line in lines[1:]]
+    wts = [weights(l, layer) for l, layer in zip(groups[0], layers_of(cut(raw[0], sizes_of[0]), len(groups[0])))]
     ln_last = jnp.stack([gain32[-1], bias32[-1]])
 
     half = ((tok, D), bf16)
@@ -769,11 +770,13 @@
             h16=h16, hlow=hlow, hhigh=hhigh,
         )
         shared = (h16, hlow, hhigh, w["taps"], x2, w["w2"])
-        if l + 1 == first_late:
-            got, _ = lax.optimization_barrier((raw[1][0], kv_all))
-            got = cut(got, raw[1][1])
-            head16 = got[0].reshape(n_dp, -1)[:, : head_w.size].reshape(D, CLS)
-            wts += [weights(m, layer) for m, layer in zip(groups[1], layers_of(got[1:], len(groups[1])))]
+        if l + 1 in first_of:
+            n = first_of[l + 1]
+            got, _ = lax.optimization_barrier((raw[n], kv_all))
+            got = cut(got, sizes_of[n])
+            if extra[n]:
+                head16 = got.pop(0).reshape(n_dp, -1)[:, : head_w.size].reshape(D, CLS)
+            wts += [weights(m, layer) for m, layer in zip(groups[n], layers_of(got, len(groups[n])))]
         if l + 1 < LAYERS:
             n = wts[l + 1]
             keep["g16"], keep["slope"], x, a16, q16, r, rn16, kv16 = run(

time: 875 us -> 924 us (1.056)
  local copies, waits for them, and re-layouts: 224 us -> 250 us
  starting transfers between devices: 105 us -> 124 us
    all_gather x2 -> x4, waiting for transfers between devices: 38.6 us -> 0.02 us  [gathered(): return lax.all_gather(part.reshape(-1, wide), 'seq', axis=0, tiled=False)]
    ppermute x9 -> x21, waiting for transfers between devices: 10.5 us -> 48.6 us  [over_dp(): lax.ppermute(v, 'dp', [((d + j) % n_dp, d) for d in range(n_dp)])]
    ppermute x9 -> x21, starting transfers between devices: 15.1 us -> 36.4 us  [over_dp(): lax.ppermute(v, 'dp', [((d + j) % n_dp, d) for d in range(n_dp)])]
    unnamed x841 -> x866, local copies, waits for them, and re-layouts: 113 us -> 115 us
  transfers between devices with their start and end apart: 106 -> 120, of which waited for: 31 -> 35; matrix products, arithmetic and copies ran while one was open for 20% -> 24% of each run, Pallas kernels for 24% -> 23%
where the time goes in v7:
time: 924 us; the launch traced here: 911 us
  local copies, waits for them, and re-layouts  250 us (27%)
  Pallas kernels  249 us (27%)
  starting transfers between devices  124 us (13%)
  waiting for transfers between devices  121 us (13%)
  other arithmetic  115 us (12%)
  between operations  30.8 us (3%)
  blocking collectives  21.4 us (2%)
    pallas_call x28, Pallas kernels, run(): pl.pallas_call(body, out_shape=[jax.ShapeDtypeStruct(s, d) for s, d in ou...  184 us
    unnamed x866, local copies, waits for them, and re-layouts  115 us
    ppermute x21, waiting for transfers between devices, over_dp(): lax.ppermute(v, 'dp', [((d + j) % n_dp, d) for d in range(n_dp)])  48.6 us
    pallas_call x6, Pallas kernels, weight_grads(): pl.pallas_call(functools.partial(weight_grads_body, n_dp, cols, subs), ou...  38.4 us
    ppermute x21, starting transfers between devices, over_dp(): lax.ppermute(v, 'dp', [((d + j) % n_dp, d) for d in range(n_dp)])  36.4 us
    ppermute x32, starting transfers between devices, over_chips(): return lax.ppermute(v, 'seq', [(d ^ bit * subs, d) for d in range(n_seq)])  32.4 us
    ppermute x32, waiting for transfers between devices, over_chips(): return lax.ppermute(v, 'seq', [(d ^ bit * subs, d) for d in range(n_seq)])  29.4 us
    ppermute x18, starting transfers between devices, dp_sum(): total = total + lax.ppermute(of(j).astype(wire[0]), 'dp', pairs).astype(f32)  26.8 us
  transfers between devices with their start and end apart: 120, of which 35 were waited for; matrix products, arithmetic and copies ran while one was open for 24% of the time, Pallas kernels for 23%

profile of v7, /device:TPU:0, one launch (start us, length us, event | category | flops | bytes accessed | tf_op | source)
XLA Modules:
  0.0 911.2 jit_solution(1761841421908138279)
XLA Ops:
  78.4 11.5 %collective-permute-done.11 = bf16[288,320]{1,0:T(8,128)(2,1)S(1)} collective-permute-done((bf16[288,320]{1,0:T(8,128)(2,1)S(1)}, bf16[288,320]{1,0:T(8,128)(2,1)S(1)}, u32[]{:S(2)}, u32[]{:S(2)}) %collective-permute-start.11) | collective-permute-done | bytes 184352 | tf_op jit(solution)/shard_map/ppermute | solution.py:662
  89.9 9.2 %collective-permute-done.12 = bf16[288,320]{1,0:T(8,128)(2,1)S(1)} collective-permute-done((bf16[288,320]{1,0:T(8,128)(2,1)S(1)}, bf16[288,320]{1,0:T(8,128)(2,1)S(1)}, u32[]{:S(2)}, u32[]{:S(2)}) %collective-permute-start.12) | collective-permute-done | bytes 184352 | tf_op jit(solution)/shard_map/ppermute | solution.py:662
  106.7 9.9 %collective-permute-done.25 = bf16[160,640]{1,0:T(8,128)(2,1)S(1)} collective-permute-done((bf16[160,640]{1,0:T(8,128)(2,1)S(1)}, bf16[160,640]{1,0:T(8,128)(2,1)S(1)}, u32[]{:S(2)}, u32[]{:S(2)}) %collective-permute-start.25) | collective-permute-done | bytes 204832 | tf_op jit(solution)/shard_map/ppermute | solution.py:662
  200.4 8.7 shard_map.444
  219.4 8.2 shard_map.446
  268.7 8.3 shard_map.448
  289.4 8.2 shard_map.450
  324.3 8.5 shard_map.452
  358.1 6.5 shard_map.454
  401.1 11.1 %shard_map.456 = (bf16[512,1280]{1,0:T(8,128)(2,1)}, f32[9,1280]{1,0:T(8,128)S(1)}, f32[2,320]{1,0:T(2,128)S(1)}, f32[512,320]{1,0:T(8,128)S(1)}, bf16[512,320]{...) custom-call(s32[2]{0:T(128)S(1)} %add_convert_fusion.place, bf16[512,1280]{1,0:T(8,128)(2,1)} %copy-done.27, ...), custom_call_target="tpu_custom_call" | custom-call | flops 1100000000 | bytes 1100000 | tf_op jit(solution)/shard_map/pallas_call | solution.py:88
  425.0 11.3 %shard_map.458 = (bf16[512,1280]{1,0:T(8,128)(2,1)}, f32[9,1280]{1,0:T(8,128)S(1)}, f32[2,320]{1,0:T(2,128)S(1)}, f32[512,320]{1,0:T(8,128)S(1)}, bf16[512,320]{...) custom-call(s32[2]{0:T(128)S(1)} %add_convert_fusion.place, bf16[512,1280]{1,0:T(8,128)(2,1)} %copy-done.33, ...), custom_call_target="tpu_custom_call" | custom-call | flops 1100000000 | bytes 1100000 | tf_op jit(solution)/shard_map/pallas_call | solution.py:88
  463.6 11.0 %shard_map.461 = (bf16[512,1280]{1,0:T(8,128)(2,1)}, f32[9,1280]{1,0:T(8,128)S(1)}, f32[2,320]{1,0:T(2,128)S(1)}, f32[512,320]{1,0:T(8,128)S(1)}, bf16[512,320]{...) custom-call(s32[2]{0:T(128)S(1)} %add_convert_fusion.place, bf16[512,1280]{1,0:T(8,128)(2,1)} %copy-done.32, ...), custom_call_target="tpu_custom_call" | custom-call | flops 1100000000 | bytes 1100000 | tf_op jit(solution)/shard_map/pallas_call | solution.py:88
  498.8 6.5 shard_map.463
  530.0 11.1 %shard_map.464 = (bf16[512,1280]{1,0:T(8,128)(2,1)}, f32[9,1280]{1,0:T(8,128)S(1)}, f32[2,320]{1,0:T(2,128)S(1)}, f32[512,320]{1,0:T(8,128)S(1)}, bf16[512,320]{...) custom-call(s32[2]{0:T(128)S(1)} %add_convert_fusion.place, bf16[512,1280]{1,0:T(8,128)(2,1)} %copy-done.31, ...), custom_call_target="tpu_custom_call" | custom-call | flops 1100000000 | bytes 1100000 | tf_op jit(solution)/shard_map/pallas_call | solution.py:88
  578.7 11.3 %shard_map.467 = (bf16[512,1280]{1,0:T(8,128)(2,1)}, f32[9,1280]{1,0:T(8,128)S(1)}, f32[2,320]{1,0:T(2,128)S(1)}, f32[512,320]{1,0:T(8,128)S(1)}, bf16[512,320]{...) custom-call(s32[2]{0:T(128)S(1)} %add_convert_fusion.place, bf16[512,1280]{1,0:T(8,128)(2,1)} %copy-done.30, ...), custom_call_target="tpu_custom_call" | custom-call | flops 1100000000 | bytes 1100000 | tf_op jit(solution)/shard_map/pallas_call | solution.py:88
  626.1 11.0 %shard_map.470 = (bf16[512,1280]{1,0:T(8,128)(2,1)}, f32[9,1280]{1,0:T(8,128)S(1)}, f32[2,320]{1,0:T(2,128)S(1)}, f32[512,320]{1,0:T(8,128)S(1)}, bf16[512,320]{...) custom-call(s32[2]{0:T(128)S(1)} %add_convert_fusion.place, bf16[512,1280]{1,0:T(8,128)(2,1)} %copy-done.29, ...), custom_call_target="tpu_custom_call" | custom-call | flops 1100000000 | bytes 1100000 | tf_op jit(solution)/shard_map/pallas_call | solution.py:88
  658.1 6.6 shard_map.473
  728.4 8.6 collective-permute-done.99
  751.1 7.1 collective-permute-done.107
  800.4 8.7 all-gather.19.cloned.1.call-done
  816.6 12.2 %psum.29 = f32[]{:T(128)} all-reduce(f32[]{:T(128)S(6)} %add.1090), channel_id=1, replica_groups=mesh['dp'=4,'seq'=8] {'dp'}, use_global_device_ids=true, to_apply=%region_8.9 | all-reduce | flops 1 | bytes 8 | tf_op jit(solution)/shard_map/psum | solution.py:1027
  831.4 26.7 %shard_map.475 = (f32[6,80,2560]{2,1,0:T(8,128)}, f32[6,80,2560]{2,1,0:T(8,128)}, f32[6,80,2560]{2,1,0:T(8,128)}, f32[6,2,320,320]{3,2,1,0:T(8,128)}, f32[6,2,32...) custom-call(f32[1]{0:T(128)} %bitcast.206.factor_ref, bf16[8,256,640]{2,1,0:T(8,128)(2,1)} %bitcast.521, ...), custom_call_target="tpu_custom_call" | custom-call | flops 2500000000 | bytes 2500000 | tf_op jit(solution)/shard_map/pallas_call | solution.py:1043
  870.4 9.2 %all-reduce.3 = (f32[]{:T(128)}, f32[22]{0:T(128)S(1)}, f32[22]{0:T(128)S(1)}) all-reduce(f32[]{:T(128)} %fusion.131, f32[22]{0:T(128)} %get-tuple-element.977, f32[22]{0:T(128)} %get-tuple-element.978), channel_id=1, replica_groups=mesh['dp'=4,'seq'=8] {'dp'}, use_global_device_ids=true, to_apply=%region_5.6 | all-reduce | flops 45 | bytes 360 | tf_op jit(solution)/shard_map/psum | solution.py:1027
  888.3 7.6 multiply_subtract_fusion.1
  (1470 shorter events, 641.8 us)
Async XLA Ops:
  7.2 155.4 %all-gather.9.cloned.1.call-start = ((), (), s32[]{:S(2)}) async-start(), calls=%async_computation | async-start | bytes 3686400 | tf_op jit(solution)/shard_map/all_gather | solution.py:647
  9.3 27.7 %collective-permute-start.15 = (bf16[2,20,80]{2,1,0:T(8,128)(2,1)}, bf16[2,20,80]{2,1,0:T(8,128)(2,1)S(1)}, u32[]{:S(2)}, u32[]{:S(2)}) collective-permute-start(bf16[2,20,80]{2,1,0:T(8,128)(2,1)} %pad_maximum_fusion.19), channel_id=1, source_target_pairs={{24,0},{0,8},{8,16},{16,24},{25,1},{1,9},{9,17},{17,25},{26,2},{2,... | collective-permute-start | bytes 19208 | tf_op jit(solution)/shard_map/ppermute | solution.py:662
  35.7 28.6 %collective-permute-start.2 = (bf16[160,640]{1,0:T(8,128)(2,1)S(1)}, bf16[160,640]{1,0:T(8,128)(2,1)S(1)}, u32[]{:S(2)}, u32[]{:S(2)}) collective-permute-start(bf16[160,640]{1,0:T(8,128)(2,1)S(1)} %get-tuple-element.750), channel_id=1, source_target_pairs={{24,0},{0,8},{8,16},{16,24},{25,1},{1,9},{9,17},{17,25},{26,2},{2,... | collective-permute-start | bytes 614408 | tf_op jit(solution)/shard_map/ppermute | solution.py:662
  44.4 55.2 %collective-permute-start.6 = (bf16[128,1152]{1,0:T(8,128)(2,1)}, bf16[128,1152]{1,0:T(8,128)(2,1)S(1)}, u32[]{:S(2)}, u32[]{:S(2)}) collective-permute-start(bf16[128,1152]{1,0:T(8,128)(2,1)} %get-tuple-element.871), channel_id=1, source_target_pairs={{3,0},{7,1},{0,2},{4,3},{1,4},{5,5},{11,8},{15,9},{8,10},{12,11},{... | collective-permute-start | bytes 884744 | tf_op jit(solution)/shard_map/ppermute | solution.py:621
  49.4 50.2 %collective-permute-start.5 = (bf16[128,1152]{1,0:T(8,128)(2,1)}, bf16[128,1152]{1,0:T(8,128)(2,1)S(1)}, u32[]{:S(2)}, u32[]{:S(2)}) collective-permute-start(bf16[128,1152]{1,0:T(8,128)(2,1)} %get-tuple-element.872), channel_id=1, source_target_pairs={{2,0},{6,1},{3,2},{7,3},{0,4},{4,5},{10,8},{14,9},{11,10},{15,11},... | collective-permute-start | bytes 884744 | tf_op jit(solution)/shard_map/ppermute | solution.py:621
  60.0 133.4 %all-gather.11.cloned.1.call-start = ((), (), s32[]{:S(2)}) async-start(), calls=%async_computation.1 | async-start | bytes 7372800 | tf_op jit(solution)/shard_map/all_gather | solution.py:647
  60.1 39.4 %collective-permute-start.4 = (bf16[128,1152]{1,0:T(8,128)(2,1)}, bf16[128,1152]{1,0:T(8,128)(2,1)S(1)}, u32[]{:S(2)}, u32[]{:S(2)}) collective-permute-start(bf16[128,1152]{1,0:T(8,128)(2,1)} %get-tuple-element.873), channel_id=1, source_target_pairs={{1,0},{5,1},{2,2},{6,3},{3,4},{7,5},{9,8},{13,9},{10,10},{14,11},{... | collective-permute-start | bytes 884744 | tf_op jit(solution)/shard_map/ppermute | solution.py:621
  62.1 37.4 %collective-permute-start.3 = (bf16[128,1152]{1,0:T(8,128)(2,1)}, bf16[128,1152]{1,0:T(8,128)(2,1)S(1)}, u32[]{:S(2)}, u32[]{:S(2)}) collective-permute-start(bf16[128,1152]{1,0:T(8,128)(2,1)} %get-tuple-element.874), channel_id=1, source_target_pairs={{0,0},{4,1},{1,2},{5,3},{2,4},{6,5},{8,8},{12,9},{9,10},{13,11},{1... | collective-permute-start | bytes 884744 | tf_op jit(solution)/shard_map/ppermute | solution.py:621
  102.8 149.5 %all-gather.13.cloned.1.call-start = ((), (), s32[]{:S(2)}) async-start(), calls=%async_computation.2 | async-start | bytes 7372800 | tf_op jit(solution)/shard_map/all_gather | solution.py:647
  123.8 187.9 %all-gather.15.cloned.1.call-start = ((), (), s32[]{:S(2)}) async-start(), calls=%async_computation.3 | async-start | bytes 4423680 | tf_op jit(solution)/shard_map/all_gather | solution.py:647
  123.8 177.9 %collective-permute-start.38 = (s32[3]{0:T(128)}, s32[3]{0:T(128)}, u32[]{:S(2)}, u32[]{:S(2)}) collective-permute-start(s32[3]{0:T(128)} %param.28), channel_id=1, source_target_pairs={{8,0},{16,8},{24,16},{0,24},{9,1},{17,9},{25,17},{1,25},{10,2},{18... | collective-permute-start | bytes 44 | tf_op jit(solution)/shard_map/ppermute | solution.py:694
  127.8 205.3 %collective-permute-start.40 = (s32[3]{0:T(128)}, s32[3]{0:T(128)}, u32[]{:S(2)}, u32[]{:S(2)}) collective-permute-start(s32[3]{0:T(128)} %param.28), channel_id=1, source_target_pairs={{24,0},{0,8},{8,16},{16,24},{25,1},{1,9},{9,17},{17,25},{26,2},{2,... | collective-permute-start | bytes 44 | tf_op jit(solution)/shard_map/ppermute | solution.py:694
  127.8 216.6 %collective-permute-start.39 = (s32[3]{0:T(128)}, s32[3]{0:T(128)}, u32[]{:S(2)}, u32[]{:S(2)}) collective-permute-start(s32[3]{0:T(128)} %param.28), channel_id=1, source_target_pairs={{16,0},{24,8},{0,16},{8,24},{17,1},{25,9},{1,17},{9,25},{18,2},{26... | collective-permute-start | bytes 44 | tf_op jit(solution)/shard_map/ppermute | solution.py:694
  162.3 617.4 %all-gather.17.cloned.1.call-start = ((), (), s32[]{:S(2)}) async-start(), calls=%async_computation.4 | async-start | bytes 2949120 | tf_op jit(solution)/shard_map/all_gather | solution.py:1008
  514.0 33.5 %collective-permute-start.63 = (f32[96,640]{1,0:T(8,128)}, f32[96,640]{1,0:T(8,128)}, u32[]{:S(2)}, u32[]{:S(2)}) collective-permute-start(f32[96,640]{1,0:T(8,128)} %get-tuple-element.868), channel_id=1, source_target_pairs={{0,8},{8,16},{16,24},{24,0},{1,9},{9,17},{17,25},{25,1},{2,10},{10... | collective-permute-start | bytes 737288 | tf_op jit(solution)/shard_map/ppermute | solution.py:892
  514.6 32.9 %collective-permute-start.65 = (f32[96,640]{1,0:T(8,128)}, f32[96,640]{1,0:T(8,128)}, u32[]{:S(2)}, u32[]{:S(2)}) collective-permute-start(f32[96,640]{1,0:T(8,128)} %get-tuple-element.869), channel_id=1, source_target_pairs={{0,24},{8,0},{16,8},{24,16},{1,25},{9,1},{17,9},{25,17},{2,26},{10... | collective-permute-start | bytes 737288 | tf_op jit(solution)/shard_map/ppermute | solution.py:892
  517.9 29.6 %collective-permute-start.64 = (f32[96,640]{1,0:T(8,128)}, f32[96,640]{1,0:T(8,128)}, u32[]{:S(2)}, u32[]{:S(2)}) collective-permute-start(f32[96,640]{1,0:T(8,128)} %get-tuple-element.870), channel_id=1, source_target_pairs={{0,16},{8,24},{16,0},{24,8},{1,17},{9,25},{17,1},{25,9},{2,18},{10... | collective-permute-start | bytes 737288 | tf_op jit(solution)/shard_map/ppermute | solution.py:892
  518.7 31.0 %collective-permute-start.66 = (bf16[2,4,40,640]{3,2,1,0:T(8,128)(2,1)}, bf16[2,4,40,640]{3,2,1,0:T(8,128)(2,1)}, u32[]{:S(2)}, u32[]{:S(2)}) collective-permute-start(bf16[2,4,40,640]{3,2,1,0:T(8,128)(2,1)} %pad_maximum_fusion.9), channel_id=1, source_target_pairs={{2,0},{3,1},{0,2},{1,3},{6,4},{7,5},{4,6},{5,7},{10,8},{11,9},{8,1... | collective-permute-start | bytes 1228808 | tf_op jit(solution)/shard_map/ppermute | solution.py:871
  521.1 29.6 %collective-permute-start.67 = (bf16[2,4,40,640]{3,2,1,0:T(8,128)(2,1)}, bf16[2,4,40,640]{3,2,1,0:T(8,128)(2,1)}, u32[]{:S(2)}, u32[]{:S(2)}) collective-permute-start(bf16[2,4,40,640]{3,2,1,0:T(8,128)(2,1)} %stack.370), channel_id=1, source_target_pairs={{4,0},{5,1},{6,2},{7,3},{0,4},{1,5},{2,6},{3,7},{12,8},{13,9},{14,... | collective-permute-start | bytes 1228808 | tf_op jit(solution)/shard_map/ppermute | solution.py:871
  570.0 26.4 %collective-permute-start.73 = (f32[80,640]{1,0:T(8,128)}, f32[80,640]{1,0:T(8,128)S(1)}, u32[]{:S(2)}, u32[]{:S(2)}) collective-permute-start(f32[80,640]{1,0:T(8,128)} %get-tuple-element.884), channel_id=1, source_target_pairs={{0,8},{8,16},{16,24},{24,0},{1,9},{9,17},{17,25},{25,1},{2,10},{10... | collective-permute-start | bytes 614408 | tf_op jit(solution)/shard_map/ppermute | solution.py:892
  670.7 36.6 %collective-permute-start.96 = (f32[4,4,80,640]{3,2,1,0:T(8,128)}, f32[4,4,80,640]{3,2,1,0:T(8,128)}, u32[]{:S(2)}, u32[]{:S(2)}) collective-permute-start(f32[4,4,80,640]{3,2,1,0:T(8,128)} %get-tuple-element.541), channel_id=1, source_target_pairs={{1,0},{0,1},{3,2},{2,3},{5,4},{4,5},{7,6},{6,7},{9,8},{8,9},{11,10... | collective-permute-start | bytes 9830408 | tf_op jit(solution)/shard_map/ppermute | solution.py:868
  724.1 85.0 %all-gather.19.cloned.1.call-start = ((), (), s32[]{:S(2)}) async-start(), calls=%async_computation.5 | async-start | bytes 3133440 | tf_op jit(solution)/shard_map/all_gather | solution.py:1010
  741.1 28.2 %collective-permute-start.101 = (bf16[80,640]{1,0:T(8,128)(2,1)S(1)}, bf16[80,640]{1,0:T(8,128)(2,1)S(1)}, u32[]{:S(2)}, u32[]{:S(2)}) collective-permute-start(bf16[80,640]{1,0:T(8,128)(2,1)S(1)} %get-tuple-element.875), channel_id=1, source_target_pairs={{0,8},{8,16},{16,24},{24,0},{1,9},{9,17},{17,25},{25,1},{2,10},{10... | collective-permute-start | bytes 307208 | tf_op jit(solution)/shard_map/ppermute | solution.py:892
  741.2 29.3 %collective-permute-start.103 = (bf16[80,640]{1,0:T(8,128)(2,1)S(1)}, bf16[80,640]{1,0:T(8,128)(2,1)S(1)}, u32[]{:S(2)}, u32[]{:S(2)}) collective-permute-start(bf16[80,640]{1,0:T(8,128)(2,1)S(1)} %get-tuple-element.876), channel_id=1, source_target_pairs={{0,24},{8,0},{16,8},{24,16},{1,25},{9,1},{17,9},{25,17},{2,26},{10... | collective-permute-start | bytes 307208 | tf_op jit(solution)/shard_map/ppermute | solution.py:892
  (484 other events, 3861.5 us)
Sparse Core Ops, SparseCore 0:
  60.1 38.2 all-gather.8
  102.9 45.4 all-gather.10
  150.9 46.6 all-gather.12
  199.3 35.6 all-gather.14
  724.2 35.9 all-gather.16
  779.8 29.2 all-gather.18

commit v8 on v7

--- a/solution.py
+++ b/solution.py
@@ -664,11 +664,6 @@
         ]
         return lax.dynamic_slice_in_dim(jnp.stack(got + got), (n_dp - dp_pos) % n_dp, n_dp, 0)
 
-    taps16 = over_dp(to_bf(dw_kernel).reshape(LAYERS * 9, -1))
-    norms16 = over_dp(to_bf(jnp.stack([norm_gain, norm_bias])))
-    taps32 = taps16.transpose(1, 0, 2).reshape(LAYERS, 9, FF).astype(f32)
-    norms32 = norms16.transpose(1, 2, 0, 3).reshape(2, -1, D).astype(f32)
-    gain32, bias32 = norms32[0], norms32[1]
     groups = [[0], [1, 2], [3, 4], [5]]
     extra = [[], [], [], [part_of(to_bf(head_w).reshape(-1))]]
 
@@ -677,9 +672,27 @@
 
     parts_of = [more + [p for l in members for p in layer_part(l)] for members, more in zip(groups, extra)]
     sizes_of = [[p.shape[0] for p in parts] for parts in parts_of]
-    lines = [over_dp(jnp.concatenate(parts, 0)) for parts in parts_of]
-    behind, lines[0] = lax.optimization_barrier((to_bf(embed_w), lines[0]))
-    embed16 = over_dp(behind).reshape(-1, D)
+    lines = [over_dp(jnp.concatenate(parts, 0)) for parts in parts_of[:2]]
+    norms = jnp.stack([norm_gain, norm_bias])
+    small = jnp.concatenate([to_bf(v).reshape(-1, D) for v in (embed_w, dw_kernel, norms)], 0)
+    small, lines[0] = lax.optimization_barrier((small, lines[0]))
+    small = over_dp(small)
+    marks = (embed_w.shape[0], embed_w.shape[0] + dw_kernel.size // D)
+    embed16 = small[:, : marks[0]].reshape(-1, D)
+    taps32 = small[:, marks[0] : marks[1]].reshape(n_dp, LAYERS * 9, -1).transpose(1, 0, 2)
+    taps32 = taps32.reshape(LAYERS, 9, FF).astype(f32)
+    norms32 = small[:, marks[1] :].reshape(n_dp, 2, -1, row_in).transpose(1, 2, 0, 3)
+    norms32 = norms32.reshape(2, -1, D).astype(f32)
+    gain32, bias32 = norms32[0], norms32[1]
+
+    def total_over_dp(v):
+        got = [v] + [
+            lax.ppermute(v, "dp", [((d + j) % n_dp, d) for d in range(n_dp)])
+            for j in range(1, n_dp)
+        ]
+        index = lax.broadcasted_iota(jnp.int32, (n_dp, 1), 0)
+        rows_of = [jnp.where(index == (dp_pos + j) % n_dp, g, 0.0) for j, g in enumerate(got)]
+        return jnp.sum(sum(rows_of), 0)
     raw = [gathered(lines[0])]
     first_of = {members[0]: n for n, members in enumerate(groups)}
 
@@ -732,7 +745,7 @@
     patch_own = to_team(spread.reshape(img_dev, rows * W, -1))
     e, x = run(2, embed_body, [full, full], patch_own, embed16, ln_first)
     lines[1], x = lax.optimization_barrier((lines[1], x))
-    raw += [gathered(line) for line in lines[1:]]
+    raw.append(gathered(lines[1]))
     wts = [weights(l, layer) for l, layer in zip(groups[0], layers_of(cut(raw[0], sizes_of[0]), len(groups[0])))]
     ln_last = jnp.stack([gain32[-1], bias32[-1]])
 
@@ -749,6 +762,9 @@
     kept = []
     for l in range(LAYERS):
         w = wts[l]
+        if l + 2 < len(groups):
+            parts, kv16 = lax.optimization_barrier((parts_of[l + 2], kv16))
+            raw.append(gathered(over_dp(jnp.concatenate(parts, 0))))
         kv_all = all_keys(kv16)
         o16, lse, x2, b16, h16, edge = run(
             4,
@@ -909,7 +925,9 @@
             return now
         ready = [p for p in pieces if p[0] <= len(stages) + 1]
         now, values = tied(now, [p[1] for p in ready])
-        for n, (p, v) in enumerate(zip(ready, values)):
+        if wire[0] == bf16:
+            values = [v if p[0] else p[1] for p, v in zip(ready, values)]
+        for p, v in zip(ready, values):
             if p[0] < len(stages):
                 p[1] = stages[p[0]](v)
             elif p[0] > len(stages) or p is pieces[0]:
@@ -1024,7 +1042,12 @@
 
     gsq_local = sum(jnp.sum(jnp.square(g.astype(f32))) for g in (early_got, late_got))
     wsq_local = group_sums(tuple((w * w for w in masters)))
-    gsq, wsq, loss = lax.psum((gsq_local, wsq_local, loss_seq), "dp")
+    ends_of = jnp.where(jnp.arange(LANES) == LANES - 1, loss_seq, 0.0)
+    first_sums = total_over_dp(
+        jnp.where(jnp.arange(LANES) == LANES - 2, gsq_local, ends_of)
+        + jnp.pad(wsq_local, (0, LANES - wsq_local.shape[0]))
+    )
+    gsq, wsq, loss = first_sums[LANES - 2], first_sums[: 4 + 3 * LAYERS], first_sums[LANES - 1]
     grad_norm = jnp.sqrt(gsq)
     factor = jnp.minimum(1.0, clip_limit / grad_norm)
 
@@ -1064,11 +1087,8 @@
         new_m.append(m2)
         new_v.append(v2)
         updates.append(u)
-    usq = lax.psum(
-        group_sums(
-            tuple((u * u for u in updates)), jnp.sum(got[6][:, 0, : 4 + 3 * LAYERS], 0)
-        ),
-        "dp",
+    usq = total_over_dp(
+        group_sums(tuple((u * u for u in updates)), jnp.sum(got[6][:, 0, : 4 + 3 * LAYERS], 0))
     )
     wnorm = jnp.sqrt(wsq)
     unorm = jnp.sqrt(usq)

time: 924 us -> 886 us (0.959)
  blocking collectives: 21.4 us -> 0 us
  local copies, waits for them, and re-layouts: 250 us -> 231 us
  starting transfers between devices: 124 us -> 135 us
  waiting for transfers between devices: 121 us -> 111 us
    psum x2 -> x0, blocking collectives: 21.4 us -> none  [per_device(): gsq, wsq, loss = lax.psum((gsq_local, wsq_local, loss_seq), 'dp')]
    unnamed x866 -> x853, local copies, waits for them, and re-layouts: 115 us -> 101 us
    ppermute x21 -> x15, waiting for transfers between devices: 48.6 us -> 34.6 us  [over_dp(): lax.ppermute(v, 'dp', [((d + j) % n_dp, d) for d in range(n_dp)])]
    ppermute x0 -> x6, starting transfers between devices: none -> 9.41 us  [total_over_dp(): lax.ppermute(v, 'dp', [((d + j) % n_dp, d) for d in range(n_dp)])]
    ppermute x21 -> x15, starting transfers between devices: 36.4 us -> 34.4 us  [over_dp(): lax.ppermute(v, 'dp', [((d + j) % n_dp, d) for d in range(n_dp)])]
  transfers between devices with their start and end apart: 120 -> 120, of which waited for: 35 -> 34; matrix products, arithmetic and copies ran while one was open for 24% -> 23% of each run, Pallas kernels for 23% -> 24%
where the time goes in v8:
time: 886 us; the launch traced here: 874 us
  Pallas kernels  250 us (28%)
  local copies, waits for them, and re-layouts  231 us (26%)
  starting transfers between devices  135 us (15%)
  other arithmetic  116 us (13%)
  waiting for transfers between devices  111 us (13%)
  between operations  30.8 us (3%)
    pallas_call x28, Pallas kernels, run(): pl.pallas_call(body, out_shape=[jax.ShapeDtypeStruct(s, d) for s, d in ou...  184 us
    unnamed x853, local copies, waits for them, and re-layouts  101 us
    ppermute x32, waiting for transfers between devices, over_chips(): return lax.ppermute(v, 'seq', [(d ^ bit * subs, d) for d in range(n_seq)])  38.5 us
    pallas_call x6, Pallas kernels, weight_grads(): pl.pallas_call(functools.partial(weight_grads_body, n_dp, cols, subs), ou...  38.3 us
    ppermute x15, waiting for transfers between devices, over_dp(): lax.ppermute(v, 'dp', [((d + j) % n_dp, d) for d in range(n_dp)])  34.6 us
    ppermute x15, starting transfers between devices, over_dp(): lax.ppermute(v, 'dp', [((d + j) % n_dp, d) for d in range(n_dp)])  34.4 us
    ppermute x32, starting transfers between devices, over_chips(): return lax.ppermute(v, 'seq', [(d ^ bit * subs, d) for d in range(n_seq)])  34.2 us
    ppermute x18, starting transfers between devices, dp_sum(): total = total + lax.ppermute(of(j).astype(wire[0]), 'dp', pairs).astype(f32)  27.5 us
  transfers between devices with their start and end apart: 120, of which 34 were waited for; matrix products, arithmetic and copies ran while one was open for 23% of the time, Pallas kernels for 24%

profile of v8, /device:TPU:0, one launch (start us, length us, event | category | flops | bytes accessed | tf_op | source)
XLA Modules:
  0.0 874.0 jit_solution(17015042075261787849)
XLA Ops:
  96.2 6.5 collective-permute-start.21
  105.1 11.6 %collective-permute-done.19 = bf16[160,640]{1,0:T(8,128)(2,1)S(1)} collective-permute-done((bf16[160,640]{1,0:T(8,128)(2,1)S(1)}, bf16[160,640]{1,0:T(8,128)(2,1)S(1)}, u32[]{:S(2)}, u32[]{:S(2)}) %collective-permute-start.19) | collective-permute-done | bytes 204832 | tf_op jit(solution)/shard_map/ppermute | solution.py:662
  159.3 8.2 shard_map.444
  212.8 8.3 shard_map.446
  257.4 8.4 shard_map.448
  278.1 8.2 shard_map.450
  315.1 8.6 shard_map.452
  347.9 6.5 shard_map.454
  387.7 11.0 %shard_map.456 = (bf16[512,1280]{1,0:T(8,128)(2,1)}, f32[9,1280]{1,0:T(8,128)S(1)}, f32[2,320]{1,0:T(2,128)S(1)}, f32[512,320]{1,0:T(8,128)S(1)}, bf16[512,320]{...) custom-call(s32[2]{0:T(128)S(1)} %add_convert_fusion.place, bf16[512,1280]{1,0:T(8,128)(2,1)} %copy-done.25, ...), custom_call_target="tpu_custom_call" | custom-call | flops 1100000000 | bytes 1100000 | tf_op jit(solution)/shard_map/pallas_call | solution.py:88
  403.4 6.4 shard_map.457
  412.3 11.4 %shard_map.458 = (bf16[512,1280]{1,0:T(8,128)(2,1)}, f32[9,1280]{1,0:T(8,128)S(1)}, f32[2,320]{1,0:T(2,128)S(1)}, f32[512,320]{1,0:T(8,128)S(1)}, bf16[512,320]{...) custom-call(s32[2]{0:T(128)S(1)} %add_convert_fusion.place, bf16[512,1280]{1,0:T(8,128)(2,1)} %copy-done.31, ...), custom_call_target="tpu_custom_call" | custom-call | flops 1100000000 | bytes 1100000 | tf_op jit(solution)/shard_map/pallas_call | solution.py:88
  437.2 6.6 shard_map.460
  454.6 11.0 %shard_map.461 = (bf16[512,1280]{1,0:T(8,128)(2,1)}, f32[9,1280]{1,0:T(8,128)S(1)}, f32[2,320]{1,0:T(2,128)S(1)}, f32[512,320]{1,0:T(8,128)S(1)}, bf16[512,320]{...) custom-call(s32[2]{0:T(128)S(1)} %add_convert_fusion.place, bf16[512,1280]{1,0:T(8,128)(2,1)} %copy-done.30, ...), custom_call_target="tpu_custom_call" | custom-call | flops 1100000000 | bytes 1100000 | tf_op jit(solution)/shard_map/pallas_call | solution.py:88
  490.9 6.5 shard_map.463
  519.1 11.2 %shard_map.464 = (bf16[512,1280]{1,0:T(8,128)(2,1)}, f32[9,1280]{1,0:T(8,128)S(1)}, f32[2,320]{1,0:T(2,128)S(1)}, f32[512,320]{1,0:T(8,128)S(1)}, bf16[512,320]{...) custom-call(s32[2]{0:T(128)S(1)} %add_convert_fusion.place, bf16[512,1280]{1,0:T(8,128)(2,1)} %copy-done.29, ...), custom_call_target="tpu_custom_call" | custom-call | flops 1100000000 | bytes 1100000 | tf_op jit(solution)/shard_map/pallas_call | solution.py:88
  546.8 6.4 shard_map.466
  566.6 11.3 %shard_map.467 = (bf16[512,1280]{1,0:T(8,128)(2,1)}, f32[9,1280]{1,0:T(8,128)S(1)}, f32[2,320]{1,0:T(2,128)S(1)}, f32[512,320]{1,0:T(8,128)S(1)}, bf16[512,320]{...) custom-call(s32[2]{0:T(128)S(1)} %add_convert_fusion.place, bf16[512,1280]{1,0:T(8,128)(2,1)} %copy-done.28, ...), custom_call_target="tpu_custom_call" | custom-call | flops 1100000000 | bytes 1100000 | tf_op jit(solution)/shard_map/pallas_call | solution.py:88
  594.1 6.4 shard_map.469
  616.9 11.1 %shard_map.470 = (bf16[512,1280]{1,0:T(8,128)(2,1)}, f32[9,1280]{1,0:T(8,128)S(1)}, f32[2,320]{1,0:T(2,128)S(1)}, f32[512,320]{1,0:T(8,128)S(1)}, bf16[512,320]{...) custom-call(s32[2]{0:T(128)S(1)} %add_convert_fusion.place, bf16[512,1280]{1,0:T(8,128)(2,1)} %copy-done.27, ...), custom_call_target="tpu_custom_call" | custom-call | flops 1100000000 | bytes 1100000 | tf_op jit(solution)/shard_map/pallas_call | solution.py:88
  642.1 6.6 shard_map.473
  657.5 8.6 collective-permute-done.79
  708.9 9.4 %collective-permute-done.90 = bf16[2,4,40,640]{3,2,1,0:T(8,128)(2,1)S(1)} collective-permute-done((bf16[2,4,40,640]{3,2,1,0:T(8,128)(2,1)S(1)}, bf16[2,4,40,640]{3,2,1,0:T(8,128)(2,1)S(1)}, u32[]{:S(2)}, u32[]{:S(2)}) %collective-permute-start.90) | collective-permute-done | bytes 409632 | tf_op jit(solution)/shard_map/ppermute | solution.py:887
  731.4 6.9 collective-permute-done.98
  806.5 26.9 %shard_map.475 = (f32[6,80,2560]{2,1,0:T(8,128)}, f32[6,80,2560]{2,1,0:T(8,128)}, f32[6,80,2560]{2,1,0:T(8,128)}, f32[6,2,320,320]{3,2,1,0:T(8,128)}, f32[6,2,32...) custom-call(f32[1]{0:T(128)} %bitcast.200.factor_ref, bf16[8,256,640]{2,1,0:T(8,128)(2,1)} %bitcast.502, ...), custom_call_target="tpu_custom_call" | custom-call | flops 2500000000 | bytes 2500000 | tf_op jit(solution)/shard_map/pallas_call | solution.py:1066
  (1458 shorter events, 619.1 us)
Async XLA Ops:
  7.2 81.5 %all-gather.9.cloned.1.call-start = ((), (), s32[]{:S(2)}) async-start(), calls=%async_computation | async-start | bytes 3686400 | tf_op jit(solution)/shard_map/all_gather | solution.py:647
  28.4 27.0 %collective-permute-start.6 = (bf16[160,640]{1,0:T(8,128)(2,1)S(1)}, bf16[160,640]{1,0:T(8,128)(2,1)S(1)}, u32[]{:S(2)}, u32[]{:S(2)}) collective-permute-start(bf16[160,640]{1,0:T(8,128)(2,1)S(1)} %get-tuple-element.751), channel_id=1, source_target_pairs={{24,0},{0,8},{8,16},{16,24},{25,1},{1,9},{9,17},{17,25},{26,2},{2,... | collective-permute-start | bytes 614408 | tf_op jit(solution)/shard_map/ppermute | solution.py:662
  37.6 30.6 %collective-permute-start.3 = (bf16[128,1152]{1,0:T(8,128)(2,1)}, bf16[128,1152]{1,0:T(8,128)(2,1)S(1)}, u32[]{:S(2)}, u32[]{:S(2)}) collective-permute-start(bf16[128,1152]{1,0:T(8,128)(2,1)} %get-tuple-element.871), channel_id=1, source_target_pairs={{3,0},{7,1},{0,2},{4,3},{1,4},{5,5},{11,8},{15,9},{8,10},{12,11},{... | collective-permute-start | bytes 884744 | tf_op jit(solution)/shard_map/ppermute | solution.py:621
  41.9 26.2 %collective-permute-start.2 = (bf16[128,1152]{1,0:T(8,128)(2,1)}, bf16[128,1152]{1,0:T(8,128)(2,1)S(1)}, u32[]{:S(2)}, u32[]{:S(2)}) collective-permute-start(bf16[128,1152]{1,0:T(8,128)(2,1)} %get-tuple-element.872), channel_id=1, source_target_pairs={{2,0},{6,1},{3,2},{7,3},{0,4},{4,5},{10,8},{14,9},{11,10},{15,11},... | collective-permute-start | bytes 884744 | tf_op jit(solution)/shard_map/ppermute | solution.py:621
  46.6 103.1 %all-gather.11.cloned.1.call-start = ((), (), s32[]{:S(2)}) async-start(), calls=%async_computation.1 | async-start | bytes 7372800 | tf_op jit(solution)/shard_map/all_gather | solution.py:647
  84.4 164.2 %all-gather.13.cloned.1.call-start = ((), (), s32[]{:S(2)}) async-start(), calls=%async_computation.2 | async-start | bytes 7372800 | tf_op jit(solution)/shard_map/all_gather | solution.py:647
  119.8 187.8 %all-gather.15.cloned.1.call-start = ((), (), s32[]{:S(2)}) async-start(), calls=%async_computation.3 | async-start | bytes 4423680 | tf_op jit(solution)/shard_map/all_gather | solution.py:647
  187.4 571.8 %all-gather.17.cloned.1.call-start = ((), (), s32[]{:S(2)}) async-start(), calls=%async_computation.4 | async-start | bytes 2949120 | tf_op jit(solution)/shard_map/all_gather | solution.py:1026
  187.5 102.8 %collective-permute-start.32 = (s32[3]{0:T(128)}, s32[3]{0:T(128)}, u32[]{:S(2)}, u32[]{:S(2)}) collective-permute-start(s32[3]{0:T(128)} %param.28), channel_id=1, source_target_pairs={{8,0},{16,8},{24,16},{0,24},{9,1},{17,9},{25,17},{1,25},{10,2},{18... | collective-permute-start | bytes 44 | tf_op jit(solution)/shard_map/ppermute | solution.py:707
  192.2 131.8 %collective-permute-start.34 = (s32[3]{0:T(128)}, s32[3]{0:T(128)S(1)}, u32[]{:S(2)}, u32[]{:S(2)}) collective-permute-start(s32[3]{0:T(128)} %param.28), channel_id=1, source_target_pairs={{24,0},{0,8},{8,16},{16,24},{25,1},{1,9},{9,17},{17,25},{26,2},{2,... | collective-permute-start | bytes 44 | tf_op jit(solution)/shard_map/ppermute | solution.py:707
  192.7 142.0 %collective-permute-start.33 = (s32[3]{0:T(128)}, s32[3]{0:T(128)}, u32[]{:S(2)}, u32[]{:S(2)}) collective-permute-start(s32[3]{0:T(128)} %param.28), channel_id=1, source_target_pairs={{16,0},{24,8},{0,16},{8,24},{17,1},{25,9},{1,17},{9,25},{18,2},{26... | collective-permute-start | bytes 44 | tf_op jit(solution)/shard_map/ppermute | solution.py:707
  506.1 30.6 %collective-permute-start.54 = (f32[96,640]{1,0:T(8,128)}, f32[96,640]{1,0:T(8,128)}, u32[]{:S(2)}, u32[]{:S(2)}) collective-permute-start(f32[96,640]{1,0:T(8,128)} %get-tuple-element.868), channel_id=1, source_target_pairs={{0,8},{8,16},{16,24},{24,0},{1,9},{9,17},{17,25},{25,1},{2,10},{10... | collective-permute-start | bytes 737288 | tf_op jit(solution)/shard_map/ppermute | solution.py:908
  509.2 27.5 %collective-permute-start.56 = (f32[96,640]{1,0:T(8,128)}, f32[96,640]{1,0:T(8,128)}, u32[]{:S(2)}, u32[]{:S(2)}) collective-permute-start(f32[96,640]{1,0:T(8,128)} %get-tuple-element.869), channel_id=1, source_target_pairs={{0,24},{8,0},{16,8},{24,16},{1,25},{9,1},{17,9},{25,17},{2,26},{10... | collective-permute-start | bytes 737288 | tf_op jit(solution)/shard_map/ppermute | solution.py:908
  509.9 26.8 %collective-permute-start.55 = (f32[96,640]{1,0:T(8,128)}, f32[96,640]{1,0:T(8,128)}, u32[]{:S(2)}, u32[]{:S(2)}) collective-permute-start(f32[96,640]{1,0:T(8,128)} %get-tuple-element.870), channel_id=1, source_target_pairs={{0,16},{8,24},{16,0},{24,8},{1,17},{9,25},{17,1},{25,9},{2,18},{10... | collective-permute-start | bytes 737288 | tf_op jit(solution)/shard_map/ppermute | solution.py:908
  511.5 26.8 %collective-permute-start.57 = (bf16[2,4,40,640]{3,2,1,0:T(8,128)(2,1)}, bf16[2,4,40,640]{3,2,1,0:T(8,128)(2,1)}, u32[]{:S(2)}, u32[]{:S(2)}) collective-permute-start(bf16[2,4,40,640]{3,2,1,0:T(8,128)(2,1)} %pad_maximum_fusion.9), channel_id=1, source_target_pairs={{2,0},{3,1},{0,2},{1,3},{6,4},{7,5},{4,6},{5,7},{10,8},{11,9},{8,1... | collective-permute-start | bytes 1228808 | tf_op jit(solution)/shard_map/ppermute | solution.py:887
  514.0 25.4 %collective-permute-start.58 = (bf16[2,4,40,640]{3,2,1,0:T(8,128)(2,1)}, bf16[2,4,40,640]{3,2,1,0:T(8,128)(2,1)}, u32[]{:S(2)}, u32[]{:S(2)}) collective-permute-start(bf16[2,4,40,640]{3,2,1,0:T(8,128)(2,1)} %stack.318), channel_id=1, source_target_pairs={{4,0},{5,1},{6,2},{7,3},{0,4},{1,5},{2,6},{3,7},{12,8},{13,9},{14,... | collective-permute-start | bytes 1228808 | tf_op jit(solution)/shard_map/ppermute | solution.py:887
  558.6 25.7 %collective-permute-start.64 = (f32[80,640]{1,0:T(8,128)}, f32[80,640]{1,0:T(8,128)S(1)}, u32[]{:S(2)}, u32[]{:S(2)}) collective-permute-start(f32[80,640]{1,0:T(8,128)} %get-tuple-element.884), channel_id=1, source_target_pairs={{0,8},{8,16},{16,24},{24,0},{1,9},{9,17},{17,25},{25,1},{2,10},{10... | collective-permute-start | bytes 614408 | tf_op jit(solution)/shard_map/ppermute | solution.py:908
  560.2 24.2 %collective-permute-start.66 = (f32[80,640]{1,0:T(8,128)}, f32[80,640]{1,0:T(8,128)S(1)}, u32[]{:S(2)}, u32[]{:S(2)}) collective-permute-start(f32[80,640]{1,0:T(8,128)} %get-tuple-element.885), channel_id=1, source_target_pairs={{0,24},{8,0},{16,8},{24,16},{1,25},{9,1},{17,9},{25,17},{2,26},{10... | collective-permute-start | bytes 614408 | tf_op jit(solution)/shard_map/ppermute | solution.py:908
  610.1 25.0 %collective-permute-start.74 = (f32[80,640]{1,0:T(8,128)}, f32[80,640]{1,0:T(8,128)S(1)}, u32[]{:S(2)}, u32[]{:S(2)}) collective-permute-start(f32[80,640]{1,0:T(8,128)} %get-tuple-element.881), channel_id=1, source_target_pairs={{0,8},{8,16},{16,24},{24,0},{1,9},{9,17},{17,25},{25,1},{2,10},{10... | collective-permute-start | bytes 614408 | tf_op jit(solution)/shard_map/ppermute | solution.py:908
  638.2 29.4 %collective-permute-start.81 = (f32[4,4,80,640]{3,2,1,0:T(8,128)}, f32[4,4,80,640]{3,2,1,0:T(8,128)}, u32[]{:S(2)}, u32[]{:S(2)}) collective-permute-start(f32[4,4,80,640]{3,2,1,0:T(8,128)} %get-tuple-element.540), channel_id=1, source_target_pairs={{1,0},{0,1},{3,2},{2,3},{5,4},{4,5},{7,6},{6,7},{9,8},{8,9},{11,10... | collective-permute-start | bytes 9830408 | tf_op jit(solution)/shard_map/ppermute | solution.py:884
  648.7 31.6 %collective-permute-start.87 = (f32[4,4,80,640]{3,2,1,0:T(8,128)}, f32[4,4,80,640]{3,2,1,0:T(8,128)}, u32[]{:S(2)}, u32[]{:S(2)}) collective-permute-start(f32[4,4,80,640]{3,2,1,0:T(8,128)} %get-tuple-element.551), channel_id=1, source_target_pairs={{1,0},{0,1},{3,2},{2,3},{5,4},{4,5},{7,6},{6,7},{9,8},{8,9},{11,10... | collective-permute-start | bytes 9830408 | tf_op jit(solution)/shard_map/ppermute | solution.py:884
  703.5 86.8 %all-gather.19.cloned.1.call-start = ((), (), s32[]{:S(2)}) async-start(), calls=%async_computation.5 | async-start | bytes 3133440 | tf_op jit(solution)/shard_map/all_gather | solution.py:1028
  722.1 26.8 %collective-permute-start.92 = (bf16[80,640]{1,0:T(8,128)(2,1)S(1)}, bf16[80,640]{1,0:T(8,128)(2,1)S(1)}, u32[]{:S(2)}, u32[]{:S(2)}) collective-permute-start(bf16[80,640]{1,0:T(8,128)(2,1)S(1)} %get-tuple-element.875), channel_id=1, source_target_pairs={{0,8},{8,16},{16,24},{24,0},{1,9},{9,17},{17,25},{25,1},{2,10},{10... | collective-permute-start | bytes 307208 | tf_op jit(solution)/shard_map/ppermute | solution.py:908
  722.1 27.8 %collective-permute-start.94 = (bf16[80,640]{1,0:T(8,128)(2,1)S(1)}, bf16[80,640]{1,0:T(8,128)(2,1)S(1)}, u32[]{:S(2)}, u32[]{:S(2)}) collective-permute-start(bf16[80,640]{1,0:T(8,128)(2,1)S(1)} %get-tuple-element.876), channel_id=1, source_target_pairs={{0,24},{8,0},{16,8},{24,16},{1,25},{9,1},{17,9},{25,17},{2,26},{10... | collective-permute-start | bytes 307208 | tf_op jit(solution)/shard_map/ppermute | solution.py:908
  (480 other events, 4128.5 us)
Sparse Core Ops, SparseCore 0:
  46.7 39.1 all-gather.8
  88.4 48.9 all-gather.10
  139.9 46.6 all-gather.12
  188.3 37.8 all-gather.14
  703.7 36.0 all-gather.16
  759.3 30.9 all-gather.18

commit v9 on v8

--- a/solution.py
+++ b/solution.py
@@ -93,6 +93,22 @@
         compiler_params=pltpu.CompilerParams(vmem_limit_bytes=48 << 20),
         cost_estimate=cost(us),
     )(*scalars, *args)
+
+
+class Rows:
+    def __init__(self, ref, start):
+        self.ref, self.start = ref, start
+
+    def __getitem__(self, at):
+        rows, *rest = at if isinstance(at, tuple) else (at,)
+        return self.ref[(slice(self.start + rows.start, self.start + rows.stop), *rest)]
+
+
+def shifted(body, starts):
+    def call(*refs):
+        return body(*[Rows(r, starts[n]) if n in starts else r for n, r in enumerate(refs)])
+
+    return call
 
 
 def cells_of(v):
@@ -644,10 +660,10 @@
         return [to_bf(block), to_bf(jnp.concatenate([lower[0], lower[1]], 1))]
 
     def gathered(part):
-        return lax.all_gather(part.reshape(-1, wide), "seq", axis=0, tiled=False)
+        return lax.all_gather(part, ("dp", "seq"), axis=0, tiled=False)
 
     def cut(got, sizes):
-        got = got.reshape(n_seq, n_dp, sum(sizes), wide).transpose(1, 0, 2, 3)
+        got = got.reshape(n_dp, n_seq, sum(sizes), wide)
         starts = [sum(sizes[:i]) for i in range(len(sizes))]
         return [got[:, :, a : a + n] for a, n in zip(starts, sizes)]
 
@@ -664,23 +680,22 @@
         ]
         return lax.dynamic_slice_in_dim(jnp.stack(got + got), (n_dp - dp_pos) % n_dp, n_dp, 0)
 
-    groups = [[0], [1, 2], [3, 4], [5]]
-    extra = [[], [], [], [part_of(to_bf(head_w).reshape(-1))]]
+    groups = [[0, 1, 2], [3, 4, 5]]
+    extra = [[], [part_of(to_bf(head_w).reshape(-1))]]
 
     def layers_of(got, count):
         return [(proj_of(got[2 * i]), got[2 * i + 1].reshape(FF, 2 * D)) for i in range(count)]
 
     parts_of = [more + [p for l in members for p in layer_part(l)] for members, more in zip(groups, extra)]
     sizes_of = [[p.shape[0] for p in parts] for parts in parts_of]
-    lines = [over_dp(jnp.concatenate(parts, 0)) for parts in parts_of[:2]]
+    lines = [jnp.concatenate(parts, 0) for parts in parts_of]
     norms = jnp.stack([norm_gain, norm_bias])
     small = jnp.concatenate([to_bf(v).reshape(-1, D) for v in (embed_w, dw_kernel, norms)], 0)
-    small, lines[0] = lax.optimization_barrier((small, lines[0]))
     small = over_dp(small)
     marks = (embed_w.shape[0], embed_w.shape[0] + dw_kernel.size // D)
     embed16 = small[:, : marks[0]].reshape(-1, D)
     taps32 = small[:, marks[0] : marks[1]].reshape(n_dp, LAYERS * 9, -1).transpose(1, 0, 2)
-    taps32 = taps32.reshape(LAYERS, 9, FF).astype(f32)
+    taps32 = taps32.reshape(LAYERS * 9, FF).astype(f32)
     norms32 = small[:, marks[1] :].reshape(n_dp, 2, -1, row_in).transpose(1, 2, 0, 3)
     norms32 = norms32.reshape(2, -1, D).astype(f32)
     gain32, bias32 = norms32[0], norms32[1]
@@ -726,7 +741,6 @@
     ).astype(f32)
 
     def weights(l, layer):
-        base = 1 + 3 * l
         return dict(
             wq=layer[0][:, :D],
             wkv=layer[0][:, D : 3 * D],
@@ -734,9 +748,9 @@
             w1=layer[0][:, 4 * D :],
             wsr=layer[1][:, :D],
             w2=layer[1][:, D:],
-            taps=taps32[l],
-            gain=gain32[base : base + 3],
-            bias=bias32[base : base + 3],
+            taps=taps32,
+            gain=gain32,
+            bias=bias32,
         )
 
     full = ((tok, D), f32)
@@ -757,18 +771,15 @@
 
     w = wts[0]
     a16, q16, r, rn16, kv16 = run(
-        2, first_body, input_outs, x, w["gain"], w["bias"], w["wq"], w["wsr"], w["wkv"]
+        2, shifted(first_body, {1: 1, 2: 1}), input_outs, x, w["gain"], w["bias"], w["wq"], w["wsr"], w["wkv"]
     )
     kept = []
     for l in range(LAYERS):
         w = wts[l]
-        if l + 2 < len(groups):
-            parts, kv16 = lax.optimization_barrier((parts_of[l + 2], kv16))
-            raw.append(gathered(over_dp(jnp.concatenate(parts, 0))))
         kv_all = all_keys(kv16)
         o16, lse, x2, b16, h16, edge = run(
             4,
-            middle_body,
+            shifted(middle_body, {5: 1 + 3 * l, 6: 1 + 3 * l}),
             [half, ((HEADS, tok), f32), full, half, wide16, row16],
             q16,
             kv_all,
@@ -797,7 +808,7 @@
             n = wts[l + 1]
             keep["g16"], keep["slope"], x, a16, q16, r, rn16, kv16 = run(
                 8,
-                join_body,
+                shifted(join_body, {4: 9 * l, 7: 4 + 3 * l, 8: 4 + 3 * l}),
                 [wide16, ((tok, FF), f32), full] + input_outs,
                 *shared,
                 n["gain"],
@@ -810,7 +821,7 @@
         else:
             keep["g16"], keep["slope"], x, pool = run(
                 7,
-                last_body,
+                shifted(last_body, {4: 9 * l}),
                 [wide16, ((tok, FF), f32), full, ((1, D), f32)],
                 *shared,
                 ln_last,
@@ -949,7 +960,7 @@
         dz16 = advance(dz16)
         dh16, d_taps, dln2, dx2, dy2, dq16, dkv = run(
             11,
-            block_back_body,
+            shifted(block_back_body, {7: 9 * l, 10: 1 + 3 * l}),
             [wide16, ((9, FF), f32), ln_out, full, half, half, ((team * keys_own, 2 * D), f32)],
             k["h16"], k["hlow"], k["hhigh"], dz16, zlow, zhigh, w["taps"], w["w1"], k["x2"], w["gain"], dx,
             w["wo"], k["q16"], k["kv"], shut, k["lse"],
@@ -964,7 +975,7 @@
         if l:
             dr16, dln, dx, dy16, dz16, edge = run(
                 6,
-                join_back_body,
+                shifted(join_back_body, {4: 1 + 3 * l}),
                 [((keys_own, D), bf16), ((4, D), f32), full, half, wide16, row16],
                 *shared,
                 wts[l - 1]["w2"],
@@ -974,7 +985,7 @@
         else:
             dr16, dln, de16, dln_first = run(
                 3,
-                first_back_body,
+                shifted(first_back_body, {3: 1}),
                 [((keys_own, D), bf16), ((4, D), f32), half, ln_out],
                 *shared,
                 e,

time: 886 us -> 811 us (0.915)
  local copies, waits for them, and re-layouts: 231 us -> 148 us
  waiting for transfers between devices: 111 us -> 150 us
  starting transfers between devices: 135 us -> 109 us
    all_gather x4 -> x2, waiting for transfers between devices: 0.02 us -> 65.7 us  [gathered(): return lax.all_gather(part, ('dp', 'seq'), axis=0, tiled=False)]
    ppermute x15 -> x3, starting transfers between devices: 34.4 us -> 6.96 us  [over_dp(): lax.ppermute(v, 'dp', [((d + j) % n_dp, d) for d in range(n_dp)])]
    ppermute x15 -> x3, waiting for transfers between devices: 34.6 us -> 10 us  [over_dp(): lax.ppermute(v, 'dp', [((d + j) % n_dp, d) for d in range(n_dp)])]
    unnamed x853 -> x712, local copies, waits for them, and re-layouts: 101 us -> 76.2 us
    squeeze x7 -> x2, local copies, waits for them, and re-layouts: 9.79 us -> 0.18 us  [per_device(): gain32, bias32 = (norms32[0], norms32[1])]
    slice x12 -> x3, local copies, waits for them, and re-layouts: 18.3 us -> 12.3 us  [cut(): return [got[:, :, a:a + n] for a, n in zip(starts, sizes)]]
  transfers between devices with their start and end apart: 120 -> 106, of which waited for: 34 -> 29; matrix products, arithmetic and copies ran while one was open for 23% -> 18% of each run, Pallas kernels for 24% -> 26%
where the time goes in v9:
time: 811 us; the launch traced here: 802 us
  Pallas kernels  249 us (31%)
  waiting for transfers between devices  150 us (18%)
  local copies, waits for them, and re-layouts  148 us (18%)
  other arithmetic  117 us (14%)
  starting transfers between devices  109 us (13%)
  between operations  30.2 us (4%)
    pallas_call x28, Pallas kernels, run(): pl.pallas_call(body, out_shape=[jax.ShapeDtypeStruct(s, d) for s, d in ou...  183 us
    unnamed x712, local copies, waits for them, and re-layouts  76.2 us
    all_gather x2, waiting for transfers between devices, gathered(): return lax.all_gather(part, ('dp', 'seq'), axis=0, tiled=False)  65.7 us
    pallas_call x6, Pallas kernels, weight_grads(): pl.pallas_call(functools.partial(weight_grads_body, n_dp, cols, subs), ou...  38.5 us
    ppermute x32, starting transfers between devices, over_chips(): return lax.ppermute(v, 'seq', [(d ^ bit * subs, d) for d in range(n_seq)])  34 us
    ppermute x32, waiting for transfers between devices, over_chips(): return lax.ppermute(v, 'seq', [(d ^ bit * subs, d) for d in range(n_seq)])  33.3 us
    pallas_call x1, Pallas kernels, per_device(): pl.pallas_call(functools.partial(update_body, cols, subs, late), grid=(LA...  26.9 us
    ppermute x18, starting transfers between devices, dp_sum(): total = total + lax.ppermute(of(j).astype(wire[0]), 'dp', pairs).astype(f32)  26.7 us
  transfers between devices with their start and end apart: 106, of which 29 were waited for; matrix products, arithmetic and copies ran while one was open for 18% of the time, Pallas kernels for 26%

profile of v9, /device:TPU:0, one launch (start us, length us, event | category | flops | bytes accessed | tf_op | source)
XLA Modules:
  0.0 802.4 jit_solution(16199977574261062343)
XLA Ops:
  40.9 10.0 %collective-permute-done.4 = bf16[352,320]{1,0:T(8,128)(2,1)S(1)} collective-permute-done((bf16[352,320]{1,0:T(8,128)(2,1)S(1)}, bf16[352,320]{1,0:T(8,128)(2,1)S(1)}, u32[]{:S(2)}, u32[]{:S(2)}) %collective-permute-start.4) | collective-permute-done | bytes 225312 | tf_op jit(solution)/shard_map/ppermute | solution.py:678
  83.5 37.2 %all-gather.9.cloned.1.call-done = bf16[7680,640]{1,0:T(8,128)(2,1)} async-done(((bf16[240,640]{1,0:T(8,128)(2,1)}), bf16[7680,640]{1,0:T(8,128)(2,1)}) %all-gather.9.cloned.1.call-update) | async-done | bytes 9830416 | tf_op jit(solution)/shard_map/all_gather | solution.py:663
  142.4 8.6 %shard_map.444 = (bf16[512,1280]{1,0:T(8,128)(2,1)}, f32[512,1280]{1,0:T(8,128)}, f32[512,320]{1,0:T(8,128)S(1)}, bf16[512,320]{1,0:T(8,128)(2,1)S(1)}, bf16[512...) custom-call(s32[2]{0:T(128)S(1)} %add_convert_fusion.refs_0_.place, ...), custom_call_target="tpu_custom_call" | custom-call | flops 800000000 | bytes 800000 | tf_op jit(solution)/shard_map/pallas_call | solution.py:88
  161.8 8.2 %shard_map.446 = (bf16[512,1280]{1,0:T(8,128)(2,1)}, f32[512,1280]{1,0:T(8,128)}, f32[512,320]{1,0:T(8,128)S(1)}, bf16[512,320]{1,0:T(8,128)(2,1)S(1)}, bf16[512...) custom-call(s32[2]{0:T(128)S(1)} %add_convert_fusion.refs_0_.place, ...), custom_call_target="tpu_custom_call" | custom-call | flops 800000000 | bytes 800000 | tf_op jit(solution)/shard_map/pallas_call | solution.py:88
  181.1 28.5 %all-gather.11.cloned.1.call-done = bf16[8192,640]{1,0:T(8,128)(2,1)} async-done(((bf16[256,640]{1,0:T(8,128)(2,1)}), bf16[8192,640]{1,0:T(8,128)(2,1)}) %all-gather.11.cloned.1.call-update) | async-done | bytes 10485776 | tf_op jit(solution)/shard_map/all_gather | solution.py:663
  218.6 8.2 %shard_map.448 = (bf16[512,1280]{1,0:T(8,128)(2,1)}, f32[512,1280]{1,0:T(8,128)}, f32[512,320]{1,0:T(8,128)S(1)}, bf16[512,320]{1,0:T(8,128)(2,1)S(1)}, bf16[512...) custom-call(s32[2]{0:T(128)S(1)} %add_convert_fusion.refs_0_.place, ...), custom_call_target="tpu_custom_call" | custom-call | flops 800000000 | bytes 800000 | tf_op jit(solution)/shard_map/pallas_call | solution.py:88
  238.9 8.3 %shard_map.450 = (bf16[512,1280]{1,0:T(8,128)(2,1)}, f32[512,1280]{1,0:T(8,128)}, f32[512,320]{1,0:T(8,128)S(1)}, bf16[512,320]{1,0:T(8,128)(2,1)S(1)}, bf16[512...) custom-call(s32[2]{0:T(128)S(1)} %add_convert_fusion.refs_0_.place, ...), custom_call_target="tpu_custom_call" | custom-call | flops 800000000 | bytes 800000 | tf_op jit(solution)/shard_map/pallas_call | solution.py:88
  258.1 8.1 %shard_map.452 = (bf16[512,1280]{1,0:T(8,128)(2,1)}, f32[512,1280]{1,0:T(8,128)}, f32[512,320]{1,0:T(8,128)S(1)}, bf16[512,320]{1,0:T(8,128)(2,1)S(1)}, bf16[512...) custom-call(s32[2]{0:T(128)S(1)} %add_convert_fusion.refs_0_.place, ...), custom_call_target="tpu_custom_call" | custom-call | flops 800000000 | bytes 800000 | tf_op jit(solution)/shard_map/pallas_call | solution.py:88
  286.4 6.7 shard_map.454
  321.2 11.1 %shard_map.456 = (bf16[512,1280]{1,0:T(8,128)(2,1)}, f32[9,1280]{1,0:T(8,128)S(1)}, f32[2,320]{1,0:T(2,128)S(1)}, f32[512,320]{1,0:T(8,128)S(1)}, bf16[512,320]{...) custom-call(s32[2]{0:T(128)S(1)} %add_convert_fusion.refs_0_.place, ...), custom_call_target="tpu_custom_call" | custom-call | flops 1100000000 | bytes 1100000 | tf_op jit(solution)/shard_map/pallas_call | solution.py:88
  335.8 6.5 shard_map.457
  344.7 11.1 %shard_map.458 = (bf16[512,1280]{1,0:T(8,128)(2,1)}, f32[9,1280]{1,0:T(8,128)S(1)}, f32[2,320]{1,0:T(2,128)S(1)}, f32[512,320]{1,0:T(8,128)S(1)}, bf16[512,320]{...) custom-call(s32[2]{0:T(128)S(1)} %add_convert_fusion.refs_0_.place, ...), custom_call_target="tpu_custom_call" | custom-call | flops 1100000000 | bytes 1100000 | tf_op jit(solution)/shard_map/pallas_call | solution.py:88
  369.1 6.4 shard_map.460
  386.6 11.3 %shard_map.461 = (bf16[512,1280]{1,0:T(8,128)(2,1)}, f32[9,1280]{1,0:T(8,128)S(1)}, f32[2,320]{1,0:T(2,128)S(1)}, f32[512,320]{1,0:T(8,128)S(1)}, bf16[512,320]{...) custom-call(s32[2]{0:T(128)S(1)} %add_convert_fusion.refs_0_.place, ...), custom_call_target="tpu_custom_call" | custom-call | flops 1100000000 | bytes 1100000 | tf_op jit(solution)/shard_map/pallas_call | solution.py:88
  420.5 6.5 shard_map.463
  448.5 11.1 %shard_map.464 = (bf16[512,1280]{1,0:T(8,128)(2,1)}, f32[9,1280]{1,0:T(8,128)S(1)}, f32[2,320]{1,0:T(2,128)S(1)}, f32[512,320]{1,0:T(8,128)S(1)}, bf16[512,320]{...) custom-call(s32[2]{0:T(128)S(1)} %add_convert_fusion.refs_0_.place, ...), custom_call_target="tpu_custom_call" | custom-call | flops 1100000000 | bytes 1100000 | tf_op jit(solution)/shard_map/pallas_call | solution.py:88
  476.2 6.4 shard_map.466
  495.2 11.3 %shard_map.467 = (bf16[512,1280]{1,0:T(8,128)(2,1)}, f32[9,1280]{1,0:T(8,128)S(1)}, f32[2,320]{1,0:T(2,128)S(1)}, f32[512,320]{1,0:T(8,128)S(1)}, bf16[512,320]{...) custom-call(s32[2]{0:T(128)S(1)} %add_convert_fusion.refs_0_.place, ...), custom_call_target="tpu_custom_call" | custom-call | flops 1100000000 | bytes 1100000 | tf_op jit(solution)/shard_map/pallas_call | solution.py:88
  542.9 11.0 %shard_map.470 = (bf16[512,1280]{1,0:T(8,128)(2,1)}, f32[9,1280]{1,0:T(8,128)S(1)}, f32[2,320]{1,0:T(2,128)S(1)}, f32[512,320]{1,0:T(8,128)S(1)}, bf16[512,320]{...) custom-call(s32[2]{0:T(128)S(1)} %add_convert_fusion.refs_0_.place, ...), custom_call_target="tpu_custom_call" | custom-call | flops 1100000000 | bytes 1100000 | tf_op jit(solution)/shard_map/pallas_call | solution.py:88
  569.8 6.6 shard_map.473
  584.8 9.3 %collective-permute-done.67 = f32[4,40,640]{2,1,0:T(8,128)} collective-permute-done((f32[4,40,640]{2,1,0:T(8,128)}, f32[4,40,640]{2,1,0:T(8,128)}, u32[]{:S(2)}, u32[]{:S(2)}) %collective-permute-start.67) | collective-permute-done | bytes 409632 | tf_op jit(solution)/shard_map/ppermute | solution.py:898
  637.8 7.0 collective-permute-done.78
  661.2 6.5 collective-permute-done.86
  735.0 26.9 %shard_map.475 = (f32[6,80,2560]{2,1,0:T(8,128)}, f32[6,80,2560]{2,1,0:T(8,128)}, f32[6,80,2560]{2,1,0:T(8,128)}, f32[6,2,320,320]{3,2,1,0:T(8,128)}, f32[6,2,32...) custom-call(f32[1]{0:T(128)} %bitcast.159.factor_ref, bf16[8,256,640]{2,1,0:T(8,128)(2,1)} %bitcast.383, ...), custom_call_target="tpu_custom_call" | custom-call | flops 2500000000 | bytes 2500000 | tf_op jit(solution)/shard_map/pallas_call | solution.py:1077
  (1257 shorter events, 499.3 us)
Async XLA Ops:
  7.2 113.5 %all-gather.9.cloned.1.call-start = ((), (), s32[]{:S(2)}) async-start(), calls=%async_computation | async-start | bytes 10137600 | tf_op jit(solution)/shard_map/all_gather | solution.py:663
  18.8 190.8 %all-gather.11.cloned.1.call-start = ((), (), s32[]{:S(2)}) async-start(), calls=%async_computation.1 | async-start | bytes 10813440 | tf_op jit(solution)/shard_map/all_gather | solution.py:663
  21.7 33.6 %collective-permute-start.6 = (bf16[352,320]{1,0:T(8,128)(2,1)S(1)}, bf16[352,320]{1,0:T(8,128)(2,1)S(1)}, u32[]{:S(2)}, u32[]{:S(2)}) collective-permute-start(bf16[352,320]{1,0:T(8,128)(2,1)S(1)} %get-tuple-element.698), channel_id=1, source_target_pairs={{24,0},{0,8},{8,16},{16,24},{25,1},{1,9},{9,17},{17,25},{26,2},{2,... | collective-permute-start | bytes 675848 | tf_op jit(solution)/shard_map/ppermute | solution.py:678
  24.7 28.2 %collective-permute-start.5 = (bf16[352,320]{1,0:T(8,128)(2,1)S(1)}, bf16[352,320]{1,0:T(8,128)(2,1)S(1)}, u32[]{:S(2)}, u32[]{:S(2)}) collective-permute-start(bf16[352,320]{1,0:T(8,128)(2,1)S(1)} %get-tuple-element.698), channel_id=1, source_target_pairs={{16,0},{24,8},{0,16},{8,24},{17,1},{25,9},{1,17},{9,25},{18,2},{26... | collective-permute-start | bytes 675848 | tf_op jit(solution)/shard_map/ppermute | solution.py:678
  30.6 31.0 %collective-permute-start.3 = (bf16[128,1152]{1,0:T(8,128)(2,1)S(1)}, bf16[128,1152]{1,0:T(8,128)(2,1)S(1)}, u32[]{:S(2)}, u32[]{:S(2)}) collective-permute-start(bf16[128,1152]{1,0:T(8,128)(2,1)S(1)} %get-tuple-element.818), channel_id=1, source_target_pairs={{3,0},{7,1},{0,2},{4,3},{1,4},{5,5},{11,8},{15,9},{8,10},{12,11},{... | collective-permute-start | bytes 884744 | tf_op jit(solution)/shard_map/ppermute | solution.py:637
  34.0 27.5 %collective-permute-start.2 = (bf16[128,1152]{1,0:T(8,128)(2,1)S(1)}, bf16[128,1152]{1,0:T(8,128)(2,1)S(1)}, u32[]{:S(2)}, u32[]{:S(2)}) collective-permute-start(bf16[128,1152]{1,0:T(8,128)(2,1)S(1)} %get-tuple-element.819), channel_id=1, source_target_pairs={{2,0},{6,1},{3,2},{7,3},{0,4},{4,5},{10,8},{14,9},{11,10},{15,11},... | collective-permute-start | bytes 884744 | tf_op jit(solution)/shard_map/ppermute | solution.py:637
  63.8 624.7 %all-gather.13.cloned.1.call-start = ((), (), s32[]{:S(2)}) async-start(), calls=%async_computation.2 | async-start | bytes 2949120 | tf_op jit(solution)/shard_map/all_gather | solution.py:1037
  63.9 106.5 %collective-permute-start.20 = (s32[3]{0:T(128)S(1)}, s32[3]{0:T(128)}, u32[]{:S(2)}, u32[]{:S(2)}) collective-permute-start(s32[3]{0:T(128)S(1)} %copy-done.321), channel_id=1, source_target_pairs={{8,0},{16,8},{24,16},{0,24},{9,1},{17,9},{25,17},{1,25},{10,2},{18... | collective-permute-start | bytes 44 | tf_op jit(solution)/shard_map/ppermute | solution.py:722
  69.8 196.8 %collective-permute-start.22 = (s32[3]{0:T(128)S(1)}, s32[3]{0:T(128)}, u32[]{:S(2)}, u32[]{:S(2)}) collective-permute-start(s32[3]{0:T(128)S(1)} %copy-done.321), channel_id=1, source_target_pairs={{24,0},{0,8},{8,16},{16,24},{25,1},{1,9},{9,17},{17,25},{26,2},{2,... | collective-permute-start | bytes 44 | tf_op jit(solution)/shard_map/ppermute | solution.py:722
  71.2 206.1 %collective-permute-start.21 = (s32[3]{0:T(128)S(1)}, s32[3]{0:T(128)}, u32[]{:S(2)}, u32[]{:S(2)}) collective-permute-start(s32[3]{0:T(128)S(1)} %copy-done.321), channel_id=1, source_target_pairs={{16,0},{24,8},{0,16},{8,24},{17,1},{25,9},{1,17},{9,25},{18,2},{26... | collective-permute-start | bytes 44 | tf_op jit(solution)/shard_map/ppermute | solution.py:722
  180.8 36.7 %collective-permute-start.12 = (bf16[64,1280]{1,0:T(8,128)(2,1)}, bf16[64,1280]{1,0:T(8,128)(2,1)}, u32[]{:S(2)}, u32[]{:S(2)}) collective-permute-start(bf16[64,1280]{1,0:T(8,128)(2,1)} %get-tuple-element.319), channel_id=1, source_target_pairs={{1,0},{0,1},{3,2},{2,3},{5,4},{4,5},{7,6},{6,7},{9,8},{8,9},{11,10... | collective-permute-start | bytes 491528 | tf_op jit(solution)/shard_map/ppermute | solution.py:603
  436.0 30.0 %collective-permute-start.42 = (f32[96,640]{1,0:T(8,128)}, f32[96,640]{1,0:T(8,128)}, u32[]{:S(2)}, u32[]{:S(2)}) collective-permute-start(f32[96,640]{1,0:T(8,128)} %get-tuple-element.815), channel_id=1, source_target_pairs={{0,8},{8,16},{16,24},{24,0},{1,9},{9,17},{17,25},{25,1},{2,10},{10... | collective-permute-start | bytes 737288 | tf_op jit(solution)/shard_map/ppermute | solution.py:919
  437.3 28.8 %collective-permute-start.44 = (f32[96,640]{1,0:T(8,128)}, f32[96,640]{1,0:T(8,128)}, u32[]{:S(2)}, u32[]{:S(2)}) collective-permute-start(f32[96,640]{1,0:T(8,128)} %get-tuple-element.816), channel_id=1, source_target_pairs={{0,24},{8,0},{16,8},{24,16},{1,25},{9,1},{17,9},{25,17},{2,26},{10... | collective-permute-start | bytes 737288 | tf_op jit(solution)/shard_map/ppermute | solution.py:919
  439.9 26.2 %collective-permute-start.43 = (f32[96,640]{1,0:T(8,128)}, f32[96,640]{1,0:T(8,128)}, u32[]{:S(2)}, u32[]{:S(2)}) collective-permute-start(f32[96,640]{1,0:T(8,128)} %get-tuple-element.817), channel_id=1, source_target_pairs={{0,16},{8,24},{16,0},{24,8},{1,17},{9,25},{17,1},{25,9},{2,18},{10... | collective-permute-start | bytes 737288 | tf_op jit(solution)/shard_map/ppermute | solution.py:919
  440.7 27.0 %collective-permute-start.45 = (bf16[2,4,40,640]{3,2,1,0:T(8,128)(2,1)}, bf16[2,4,40,640]{3,2,1,0:T(8,128)(2,1)}, u32[]{:S(2)}, u32[]{:S(2)}) collective-permute-start(bf16[2,4,40,640]{3,2,1,0:T(8,128)(2,1)} %pad_maximum_fusion.9), channel_id=1, source_target_pairs={{2,0},{3,1},{0,2},{1,3},{6,4},{7,5},{4,6},{5,7},{10,8},{11,9},{8,1... | collective-permute-start | bytes 1228808 | tf_op jit(solution)/shard_map/ppermute | solution.py:898
  442.8 25.9 %collective-permute-start.46 = (bf16[2,4,40,640]{3,2,1,0:T(8,128)(2,1)}, bf16[2,4,40,640]{3,2,1,0:T(8,128)(2,1)}, u32[]{:S(2)}, u32[]{:S(2)}) collective-permute-start(bf16[2,4,40,640]{3,2,1,0:T(8,128)(2,1)} %stack.222), channel_id=1, source_target_pairs={{4,0},{5,1},{6,2},{7,3},{0,4},{1,5},{2,6},{3,7},{12,8},{13,9},{14,... | collective-permute-start | bytes 1228808 | tf_op jit(solution)/shard_map/ppermute | solution.py:898
  487.7 25.2 %collective-permute-start.52 = (f32[80,640]{1,0:T(8,128)}, f32[80,640]{1,0:T(8,128)}, u32[]{:S(2)}, u32[]{:S(2)}) collective-permute-start(f32[80,640]{1,0:T(8,128)} %get-tuple-element.831), channel_id=1, source_target_pairs={{0,8},{8,16},{16,24},{24,0},{1,9},{9,17},{17,25},{25,1},{2,10},{10... | collective-permute-start | bytes 614408 | tf_op jit(solution)/shard_map/ppermute | solution.py:919
  535.9 25.9 %collective-permute-start.62 = (f32[80,640]{1,0:T(8,128)}, f32[80,640]{1,0:T(8,128)S(1)}, u32[]{:S(2)}, u32[]{:S(2)}) collective-permute-start(f32[80,640]{1,0:T(8,128)} %get-tuple-element.828), channel_id=1, source_target_pairs={{0,8},{8,16},{16,24},{24,0},{1,9},{9,17},{17,25},{25,1},{2,10},{10... | collective-permute-start | bytes 614408 | tf_op jit(solution)/shard_map/ppermute | solution.py:919
  536.0 25.8 %collective-permute-start.64 = (f32[80,640]{1,0:T(8,128)}, f32[80,640]{1,0:T(8,128)S(1)}, u32[]{:S(2)}, u32[]{:S(2)}) collective-permute-start(f32[80,640]{1,0:T(8,128)} %get-tuple-element.829), channel_id=1, source_target_pairs={{0,24},{8,0},{16,8},{24,16},{1,25},{9,1},{17,9},{25,17},{2,26},{10... | collective-permute-start | bytes 614408 | tf_op jit(solution)/shard_map/ppermute | solution.py:919
  565.9 30.4 %collective-permute-start.69 = (f32[4,4,80,640]{3,2,1,0:T(8,128)}, f32[4,4,80,640]{3,2,1,0:T(8,128)}, u32[]{:S(2)}, u32[]{:S(2)}) collective-permute-start(f32[4,4,80,640]{3,2,1,0:T(8,128)} %get-tuple-element.514), channel_id=1, source_target_pairs={{1,0},{0,1},{3,2},{2,3},{5,4},{4,5},{7,6},{6,7},{9,8},{8,9},{11,10... | collective-permute-start | bytes 9830408 | tf_op jit(solution)/shard_map/ppermute | solution.py:895
  576.4 32.1 %collective-permute-start.75 = (f32[4,4,80,640]{3,2,1,0:T(8,128)}, f32[4,4,80,640]{3,2,1,0:T(8,128)}, u32[]{:S(2)}, u32[]{:S(2)}) collective-permute-start(f32[4,4,80,640]{3,2,1,0:T(8,128)} %get-tuple-element.525), channel_id=1, source_target_pairs={{1,0},{0,1},{3,2},{2,3},{5,4},{4,5},{7,6},{6,7},{9,8},{8,9},{11,10... | collective-permute-start | bytes 9830408 | tf_op jit(solution)/shard_map/ppermute | solution.py:895
  633.7 84.3 %all-gather.15.cloned.1.call-start = ((), (), s32[]{:S(2)}) async-start(), calls=%async_computation.3 | async-start | bytes 3133440 | tf_op jit(solution)/shard_map/all_gather | solution.py:1039
  650.0 27.0 %collective-permute-start.80 = (bf16[80,640]{1,0:T(8,128)(2,1)S(1)}, bf16[80,640]{1,0:T(8,128)(2,1)S(1)}, u32[]{:S(2)}, u32[]{:S(2)}) collective-permute-start(bf16[80,640]{1,0:T(8,128)(2,1)S(1)} %get-tuple-element.822), channel_id=1, source_target_pairs={{0,8},{8,16},{16,24},{24,0},{1,9},{9,17},{17,25},{25,1},{2,10},{10... | collective-permute-start | bytes 307208 | tf_op jit(solution)/shard_map/ppermute | solution.py:919
  650.1 27.9 %collective-permute-start.82 = (bf16[80,640]{1,0:T(8,128)(2,1)S(1)}, bf16[80,640]{1,0:T(8,128)(2,1)S(1)}, u32[]{:S(2)}, u32[]{:S(2)}) collective-permute-start(bf16[80,640]{1,0:T(8,128)(2,1)S(1)} %get-tuple-element.823), channel_id=1, source_target_pairs={{0,24},{8,0},{16,8},{24,16},{1,25},{9,1},{17,9},{25,17},{2,26},{10... | collective-permute-start | bytes 307208 | tf_op jit(solution)/shard_map/ppermute | solution.py:919
  (414 other events, 3412.3 us)
Sparse Core Ops, SparseCore 0:
  18.9 101.7 all-gather.8
  124.1 85.3 all-gather.10
  633.9 35.1 all-gather.12
  688.7 29.3 all-gather.14

commit v10 on v9

--- a/solution.py
+++ b/solution.py
@@ -680,7 +680,7 @@
         ]
         return lax.dynamic_slice_in_dim(jnp.stack(got + got), (n_dp - dp_pos) % n_dp, n_dp, 0)
 
-    groups = [[0, 1, 2], [3, 4, 5]]
+    groups = [[0, 1, 2, 3], [4, 5]]
     extra = [[], [part_of(to_bf(head_w).reshape(-1))]]
 
     def layers_of(got, count):
@@ -927,7 +927,7 @@
     def tied(value, others):
         return lax.optimization_barrier((value, others))
 
-    wire = [f32]
+    wire, free = ([f32], [False])
     stages = [pair_sum, plane_first, plane_second]
     pieces = []
 
@@ -936,7 +936,7 @@
             return now
         ready = [p for p in pieces if p[0] <= len(stages) + 1]
         now, values = tied(now, [p[1] for p in ready])
-        if wire[0] == bf16:
+        if free[0]:
             values = [v if p[0] else p[1] for p, v in zip(ready, values)]
         for p, v in zip(ready, values):
             if p[0] < len(stages):
@@ -970,6 +970,8 @@
             first, _ = tied(waiting[0], dkv)
             pieces.append([0, weight_grads(first, *waiting[1:])])
         dkv_own = own_keys(dkv)
+        if l == 0:
+            wire[0] = bf16
         dq16 = advance(dq16)
         shared = (dkv_own, w["wkv"], k["r"], w["gain"], dq16, w["wq"], w["wsr"], k["x"], dx2)
         if l:
@@ -997,7 +999,7 @@
             jnp.concatenate([dln[0:2], dln2[0:1]], 0),
             jnp.concatenate([dln[2:4], dln2[1:2]], 0),
         )
-    wire[0] = bf16
+    free[0] = True
     pieces.append([0, weight_grads(*waiting)])
     de16 = advance(de16)
     (d_embed,) = run(3, embed_back_body, [((embed16.shape[0], D), f32)], patch_own, de16)

time: 811 us -> 801 us (0.988)
  other arithmetic: 117 us -> 108 us
    all_gather x2, waiting for transfers between devices: 65.7 us -> 51.3 us  [gathered(): return lax.all_gather(part, ('dp', 'seq'), axis=0, tiled=False)]
    ppermute x18, waiting for transfers between devices: 12.1 us -> 20.7 us  [dp_sum(): total = total + lax.ppermute(of(j).astype(wire[0]), 'dp', pairs).astype(f32)]
    unnamed x712 -> x726, local copies, waits for them, and re-layouts: 76.2 us -> 79 us
  transfers between devices with their start and end apart: 106 -> 106, of which waited for: 29 -> 31; matrix products, arithmetic and copies ran while one was open for 18% -> 17% of each run, Pallas kernels for 26% -> 25%
where the time goes in v10:
time: 801 us; the launch traced here: 793 us
  Pallas kernels  248 us (31%)
  local copies, waits for them, and re-layouts  153 us (19%)
  waiting for transfers between devices  143 us (18%)
  starting transfers between devices  110 us (14%)
  other arithmetic  108 us (13%)
  between operations  30.1 us (4%)
    pallas_call x28, Pallas kernels, run(): pl.pallas_call(body, out_shape=[jax.ShapeDtypeStruct(s, d) for s, d in ou...  183 us
    unnamed x726, local copies, waits for them, and re-layouts  79 us
    all_gather x2, waiting for transfers between devices, gathered(): return lax.all_gather(part, ('dp', 'seq'), axis=0, tiled=False)  51.3 us
    pallas_call x6, Pallas kernels, weight_grads(): pl.pallas_call(functools.partial(weight_grads_body, n_dp, cols, subs), ou...  38.3 us
    ppermute x32, starting transfers between devices, over_chips(): return lax.ppermute(v, 'seq', [(d ^ bit * subs, d) for d in range(n_seq)])  34.8 us
    ppermute x32, waiting for transfers between devices, over_chips(): return lax.ppermute(v, 'seq', [(d ^ bit * subs, d) for d in range(n_seq)])  31.7 us
    pallas_call x1, Pallas kernels, per_device(): pl.pallas_call(functools.partial(update_body, cols, subs, late), grid=(LA...  26.9 us
    ppermute x18, starting transfers between devices, dp_sum(): total = total + lax.ppermute(of(j).astype(wire[0]), 'dp', pairs).astype(f32)  25.9 us
  transfers between devices with their start and end apart: 106, of which 31 were waited for; matrix products, arithmetic and copies ran while one was open for 17% of the time, Pallas kernels for 25%

profile of v10, /device:TPU:0, one launch (start us, length us, event | category | flops | bytes accessed | tf_op | source)
XLA Modules:
  0.0 792.9 jit_solution(6909726100724063986)
XLA Ops:
  40.9 12.6 %collective-permute-done.4 = bf16[352,320]{1,0:T(8,128)(2,1)S(1)} collective-permute-done((bf16[352,320]{1,0:T(8,128)(2,1)S(1)}, bf16[352,320]{1,0:T(8,128)(2,1)S(1)}, u32[]{:S(2)}, u32[]{:S(2)}) %collective-permute-start.4) | collective-permute-done | bytes 225312 | tf_op jit(solution)/shard_map/ppermute | solution.py:678
  66.5 6.5 collective-permute-start.20
  86.3 51.3 %all-gather.9.cloned.1.call-done = bf16[10240,640]{1,0:T(8,128)(2,1)} async-done(((bf16[320,640]{1,0:T(8,128)(2,1)}), bf16[10240,640]{1,0:T(8,128)(2,1)}) %all-gather.9.cloned.1.call-update) | async-done | bytes 13107216 | tf_op jit(solution)/shard_map/all_gather | solution.py:663
  137.6 7.6 fusion.146
  162.6 8.4 %shard_map.444 = (bf16[512,1280]{1,0:T(8,128)(2,1)}, f32[512,1280]{1,0:T(8,128)}, f32[512,320]{1,0:T(8,128)S(1)}, bf16[512,320]{1,0:T(8,128)(2,1)S(1)}, bf16[512...) custom-call(s32[2]{0:T(128)S(1)} %add_convert_fusion.refs_0_.place, ...), custom_call_target="tpu_custom_call" | custom-call | flops 800000000 | bytes 800000 | tf_op jit(solution)/shard_map/pallas_call | solution.py:88
  182.6 8.4 %shard_map.446 = (bf16[512,1280]{1,0:T(8,128)(2,1)}, f32[512,1280]{1,0:T(8,128)}, f32[512,320]{1,0:T(8,128)S(1)}, bf16[512,320]{1,0:T(8,128)(2,1)S(1)}, bf16[512...) custom-call(s32[2]{0:T(128)S(1)} %add_convert_fusion.refs_0_.place, ...), custom_call_target="tpu_custom_call" | custom-call | flops 800000000 | bytes 800000 | tf_op jit(solution)/shard_map/pallas_call | solution.py:88
  202.0 8.6 %shard_map.448 = (bf16[512,1280]{1,0:T(8,128)(2,1)}, f32[512,1280]{1,0:T(8,128)}, f32[512,320]{1,0:T(8,128)S(1)}, bf16[512,320]{1,0:T(8,128)(2,1)S(1)}, bf16[512...) custom-call(s32[2]{0:T(128)S(1)} %add_convert_fusion.refs_0_.place, ...), custom_call_target="tpu_custom_call" | custom-call | flops 800000000 | bytes 800000 | tf_op jit(solution)/shard_map/pallas_call | solution.py:88
  229.5 8.3 %shard_map.450 = (bf16[512,1280]{1,0:T(8,128)(2,1)}, f32[512,1280]{1,0:T(8,128)}, f32[512,320]{1,0:T(8,128)S(1)}, bf16[512,320]{1,0:T(8,128)(2,1)S(1)}, bf16[512...) custom-call(s32[2]{0:T(128)S(1)} %add_convert_fusion.refs_0_.place, ...), custom_call_target="tpu_custom_call" | custom-call | flops 800000000 | bytes 800000 | tf_op jit(solution)/shard_map/pallas_call | solution.py:88
  248.1 8.3 %shard_map.452 = (bf16[512,1280]{1,0:T(8,128)(2,1)}, f32[512,1280]{1,0:T(8,128)}, f32[512,320]{1,0:T(8,128)S(1)}, bf16[512,320]{1,0:T(8,128)(2,1)S(1)}, bf16[512...) custom-call(s32[2]{0:T(128)S(1)} %add_convert_fusion.refs_0_.place, ...), custom_call_target="tpu_custom_call" | custom-call | flops 800000000 | bytes 800000 | tf_op jit(solution)/shard_map/pallas_call | solution.py:88
  277.1 6.6 shard_map.454
  311.7 11.3 %shard_map.456 = (bf16[512,1280]{1,0:T(8,128)(2,1)}, f32[9,1280]{1,0:T(8,128)S(1)}, f32[2,320]{1,0:T(2,128)S(1)}, f32[512,320]{1,0:T(8,128)S(1)}, bf16[512,320]{...) custom-call(s32[2]{0:T(128)S(1)} %add_convert_fusion.refs_0_.place, ...), custom_call_target="tpu_custom_call" | custom-call | flops 1100000000 | bytes 1100000 | tf_op jit(solution)/shard_map/pallas_call | solution.py:88
  326.3 6.5 shard_map.457
  335.2 11.0 %shard_map.458 = (bf16[512,1280]{1,0:T(8,128)(2,1)}, f32[9,1280]{1,0:T(8,128)S(1)}, f32[2,320]{1,0:T(2,128)S(1)}, f32[512,320]{1,0:T(8,128)S(1)}, bf16[512,320]{...) custom-call(s32[2]{0:T(128)S(1)} %add_convert_fusion.refs_0_.place, ...), custom_call_target="tpu_custom_call" | custom-call | flops 1100000000 | bytes 1100000 | tf_op jit(solution)/shard_map/pallas_call | solution.py:88
  360.1 6.4 shard_map.460
  374.0 11.1 %shard_map.461 = (bf16[512,1280]{1,0:T(8,128)(2,1)}, f32[9,1280]{1,0:T(8,128)S(1)}, f32[2,320]{1,0:T(2,128)S(1)}, f32[512,320]{1,0:T(8,128)S(1)}, bf16[512,320]{...) custom-call(s32[2]{0:T(128)S(1)} %add_convert_fusion.refs_0_.place, ...), custom_call_target="tpu_custom_call" | custom-call | flops 1100000000 | bytes 1100000 | tf_op jit(solution)/shard_map/pallas_call | solution.py:88
  407.6 6.5 shard_map.463
  436.4 11.3 %shard_map.464 = (bf16[512,1280]{1,0:T(8,128)(2,1)}, f32[9,1280]{1,0:T(8,128)S(1)}, f32[2,320]{1,0:T(2,128)S(1)}, f32[512,320]{1,0:T(8,128)S(1)}, bf16[512,320]{...) custom-call(s32[2]{0:T(128)S(1)} %add_convert_fusion.refs_0_.place, ...), custom_call_target="tpu_custom_call" | custom-call | flops 1100000000 | bytes 1100000 | tf_op jit(solution)/shard_map/pallas_call | solution.py:88
  464.4 6.4 shard_map.466
  483.4 11.0 %shard_map.467 = (bf16[512,1280]{1,0:T(8,128)(2,1)}, f32[9,1280]{1,0:T(8,128)S(1)}, f32[2,320]{1,0:T(2,128)S(1)}, f32[512,320]{1,0:T(8,128)S(1)}, bf16[512,320]{...) custom-call(s32[2]{0:T(128)S(1)} %add_convert_fusion.refs_0_.place, ...), custom_call_target="tpu_custom_call" | custom-call | flops 1100000000 | bytes 1100000 | tf_op jit(solution)/shard_map/pallas_call | solution.py:88
  510.1 6.4 shard_map.469
  523.9 10.8 %shard_map.470 = (bf16[512,1280]{1,0:T(8,128)(2,1)}, f32[9,1280]{1,0:T(8,128)S(1)}, f32[2,320]{1,0:T(2,128)S(1)}, f32[512,320]{1,0:T(8,128)S(1)}, bf16[512,320]{...) custom-call(s32[2]{0:T(128)S(1)} %add_convert_fusion.refs_0_.place, ...), custom_call_target="tpu_custom_call" | custom-call | flops 1100000000 | bytes 1100000 | tf_op jit(solution)/shard_map/pallas_call | solution.py:88
  549.7 8.2 %collective-permute-done.63 = f32[80,640]{1,0:T(8,128)S(1)} collective-permute-done((f32[80,640]{1,0:T(8,128)}, f32[80,640]{1,0:T(8,128)S(1)}, u32[]{:S(2)}, u32[]{:S(2)}) %collective-permute-start.63) | collective-permute-done | bytes 204832 | tf_op jit(solution)/shard_map/ppermute | solution.py:919
  626.5 9.4 %collective-permute-done.78 = bf16[2,4,40,640]{3,2,1,0:T(8,128)(2,1)S(1)} collective-permute-done((bf16[2,4,40,640]{3,2,1,0:T(8,128)(2,1)S(1)}, bf16[2,4,40,640]{3,2,1,0:T(8,128)(2,1)S(1)}, u32[]{:S(2)}, u32[]{:S(2)}) %collective-permute-start.78) | collective-permute-done | bytes 409632 | tf_op jit(solution)/shard_map/ppermute | solution.py:898
  725.7 26.9 %shard_map.475 = (f32[6,80,2560]{2,1,0:T(8,128)}, f32[6,80,2560]{2,1,0:T(8,128)}, f32[6,80,2560]{2,1,0:T(8,128)}, f32[6,2,320,320]{3,2,1,0:T(8,128)}, f32[6,2,32...) custom-call(f32[1]{0:T(128)} %bitcast.159.factor_ref, bf16[8,256,640]{2,1,0:T(8,128)(2,1)} %bitcast.384, ...), custom_call_target="tpu_custom_call" | custom-call | flops 2500000000 | bytes 2500000 | tf_op jit(solution)/shard_map/pallas_call | solution.py:1079
  (1272 shorter events, 493.1 us)
Async XLA Ops:
  7.2 130.4 %all-gather.9.cloned.1.call-start = ((), (), s32[]{:S(2)}) async-start(), calls=%async_computation | async-start | bytes 13516800 | tf_op jit(solution)/shard_map/all_gather | solution.py:663
  19.7 195.4 %all-gather.11.cloned.1.call-start = ((), (), s32[]{:S(2)}) async-start(), calls=%async_computation.1 | async-start | bytes 7434240 | tf_op jit(solution)/shard_map/all_gather | solution.py:663
  22.7 35.2 %collective-permute-start.6 = (bf16[352,320]{1,0:T(8,128)(2,1)S(1)}, bf16[352,320]{1,0:T(8,128)(2,1)S(1)}, u32[]{:S(2)}, u32[]{:S(2)}) collective-permute-start(bf16[352,320]{1,0:T(8,128)(2,1)S(1)} %get-tuple-element.698), channel_id=1, source_target_pairs={{24,0},{0,8},{8,16},{16,24},{25,1},{1,9},{9,17},{17,25},{26,2},{2,... | collective-permute-start | bytes 675848 | tf_op jit(solution)/shard_map/ppermute | solution.py:678
  25.7 29.8 %collective-permute-start.5 = (bf16[352,320]{1,0:T(8,128)(2,1)S(1)}, bf16[352,320]{1,0:T(8,128)(2,1)S(1)}, u32[]{:S(2)}, u32[]{:S(2)}) collective-permute-start(bf16[352,320]{1,0:T(8,128)(2,1)S(1)} %get-tuple-element.698), channel_id=1, source_target_pairs={{16,0},{24,8},{0,16},{8,24},{17,1},{25,9},{1,17},{9,25},{18,2},{26... | collective-permute-start | bytes 675848 | tf_op jit(solution)/shard_map/ppermute | solution.py:678
  28.3 25.2 %collective-permute-start.4 = (bf16[352,320]{1,0:T(8,128)(2,1)S(1)}, bf16[352,320]{1,0:T(8,128)(2,1)S(1)}, u32[]{:S(2)}, u32[]{:S(2)}) collective-permute-start(bf16[352,320]{1,0:T(8,128)(2,1)S(1)} %get-tuple-element.698), channel_id=1, source_target_pairs={{8,0},{16,8},{24,16},{0,24},{9,1},{17,9},{25,17},{1,25},{10,2},{18... | collective-permute-start | bytes 675848 | tf_op jit(solution)/shard_map/ppermute | solution.py:678
  31.5 32.6 %collective-permute-start.3 = (bf16[128,1152]{1,0:T(8,128)(2,1)S(1)}, bf16[128,1152]{1,0:T(8,128)(2,1)S(1)}, u32[]{:S(2)}, u32[]{:S(2)}) collective-permute-start(bf16[128,1152]{1,0:T(8,128)(2,1)S(1)} %get-tuple-element.816), channel_id=1, source_target_pairs={{3,0},{7,1},{0,2},{4,3},{1,4},{5,5},{11,8},{15,9},{8,10},{12,11},{... | collective-permute-start | bytes 884744 | tf_op jit(solution)/shard_map/ppermute | solution.py:637
  34.9 29.1 %collective-permute-start.2 = (bf16[128,1152]{1,0:T(8,128)(2,1)S(1)}, bf16[128,1152]{1,0:T(8,128)(2,1)S(1)}, u32[]{:S(2)}, u32[]{:S(2)}) collective-permute-start(bf16[128,1152]{1,0:T(8,128)(2,1)S(1)} %get-tuple-element.817), channel_id=1, source_target_pairs={{2,0},{6,1},{3,2},{7,3},{0,4},{4,5},{10,8},{14,9},{11,10},{15,11},... | collective-permute-start | bytes 884744 | tf_op jit(solution)/shard_map/ppermute | solution.py:637
  66.5 612.1 %all-gather.13.cloned.1.call-start = ((), (), s32[]{:S(2)}) async-start(), calls=%async_computation.2 | async-start | bytes 2949120 | tf_op jit(solution)/shard_map/all_gather | solution.py:1039
  66.5 145.8 %collective-permute-start.20 = (s32[3]{0:T(128)S(1)}, s32[3]{0:T(128)}, u32[]{:S(2)}, u32[]{:S(2)}) collective-permute-start(s32[3]{0:T(128)S(1)} %copy-done.328), channel_id=1, source_target_pairs={{8,0},{16,8},{24,16},{0,24},{9,1},{17,9},{25,17},{1,25},{10,2},{18... | collective-permute-start | bytes 44 | tf_op jit(solution)/shard_map/ppermute | solution.py:722
  73.0 184.0 %collective-permute-start.22 = (s32[3]{0:T(128)S(1)}, s32[3]{0:T(128)}, u32[]{:S(2)}, u32[]{:S(2)}) collective-permute-start(s32[3]{0:T(128)S(1)} %copy-done.328), channel_id=1, source_target_pairs={{24,0},{0,8},{8,16},{16,24},{25,1},{1,9},{9,17},{17,25},{26,2},{2,... | collective-permute-start | bytes 44 | tf_op jit(solution)/shard_map/ppermute | solution.py:722
  74.3 193.7 %collective-permute-start.21 = (s32[3]{0:T(128)S(1)}, s32[3]{0:T(128)}, u32[]{:S(2)}, u32[]{:S(2)}) collective-permute-start(s32[3]{0:T(128)S(1)} %copy-done.328), channel_id=1, source_target_pairs={{16,0},{24,8},{0,16},{8,24},{17,1},{25,9},{1,17},{9,25},{18,2},{26... | collective-permute-start | bytes 44 | tf_op jit(solution)/shard_map/ppermute | solution.py:722
  370.3 22.0 %collective-permute-start.35 = (bf16[2,4,40,640]{3,2,1,0:T(8,128)(2,1)S(1)}, bf16[2,4,40,640]{3,2,1,0:T(8,128)(2,1)S(1)}, u32[]{:S(2)}, u32[]{:S(2)}) collective-permute-start(bf16[2,4,40,640]{3,2,1,0:T(8,128)(2,1)S(1)} %pad_maximum_fusion.8), channel_id=1, source_target_pairs={{2,0},{3,1},{0,2},{1,3},{6,4},{7,5},{4,6},{5,7},{10,8},{11,9},{8,1... | collective-permute-start | bytes 1228808 | tf_op jit(solution)/shard_map/ppermute | solution.py:898
  423.1 31.1 %collective-permute-start.42 = (f32[96,640]{1,0:T(8,128)}, f32[96,640]{1,0:T(8,128)}, u32[]{:S(2)}, u32[]{:S(2)}) collective-permute-start(f32[96,640]{1,0:T(8,128)} %get-tuple-element.813), channel_id=1, source_target_pairs={{0,8},{8,16},{16,24},{24,0},{1,9},{9,17},{17,25},{25,1},{2,10},{10... | collective-permute-start | bytes 737288 | tf_op jit(solution)/shard_map/ppermute | solution.py:919
  424.0 30.3 %collective-permute-start.44 = (f32[96,640]{1,0:T(8,128)}, f32[96,640]{1,0:T(8,128)}, u32[]{:S(2)}, u32[]{:S(2)}) collective-permute-start(f32[96,640]{1,0:T(8,128)} %get-tuple-element.814), channel_id=1, source_target_pairs={{0,24},{8,0},{16,8},{24,16},{1,25},{9,1},{17,9},{25,17},{2,26},{10... | collective-permute-start | bytes 737288 | tf_op jit(solution)/shard_map/ppermute | solution.py:919
  427.0 27.3 %collective-permute-start.43 = (f32[96,640]{1,0:T(8,128)}, f32[96,640]{1,0:T(8,128)}, u32[]{:S(2)}, u32[]{:S(2)}) collective-permute-start(f32[96,640]{1,0:T(8,128)} %get-tuple-element.815), channel_id=1, source_target_pairs={{0,16},{8,24},{16,0},{24,8},{1,17},{9,25},{17,1},{25,9},{2,18},{10... | collective-permute-start | bytes 737288 | tf_op jit(solution)/shard_map/ppermute | solution.py:919
  427.8 28.0 %collective-permute-start.45 = (bf16[2,4,40,640]{3,2,1,0:T(8,128)(2,1)}, bf16[2,4,40,640]{3,2,1,0:T(8,128)(2,1)}, u32[]{:S(2)}, u32[]{:S(2)}) collective-permute-start(bf16[2,4,40,640]{3,2,1,0:T(8,128)(2,1)} %pad_maximum_fusion.9), channel_id=1, source_target_pairs={{2,0},{3,1},{0,2},{1,3},{6,4},{7,5},{4,6},{5,7},{10,8},{11,9},{8,1... | collective-permute-start | bytes 1228808 | tf_op jit(solution)/shard_map/ppermute | solution.py:898
  429.9 27.0 %collective-permute-start.46 = (bf16[2,4,40,640]{3,2,1,0:T(8,128)(2,1)}, bf16[2,4,40,640]{3,2,1,0:T(8,128)(2,1)}, u32[]{:S(2)}, u32[]{:S(2)}) collective-permute-start(bf16[2,4,40,640]{3,2,1,0:T(8,128)(2,1)} %stack.222), channel_id=1, source_target_pairs={{4,0},{5,1},{6,2},{7,3},{0,4},{1,5},{2,6},{3,7},{12,8},{13,9},{14,... | collective-permute-start | bytes 1228808 | tf_op jit(solution)/shard_map/ppermute | solution.py:898
  475.8 25.0 %collective-permute-start.52 = (f32[80,640]{1,0:T(8,128)}, f32[80,640]{1,0:T(8,128)S(1)}, u32[]{:S(2)}, u32[]{:S(2)}) collective-permute-start(f32[80,640]{1,0:T(8,128)} %get-tuple-element.829), channel_id=1, source_target_pairs={{0,8},{8,16},{16,24},{24,0},{1,9},{9,17},{17,25},{25,1},{2,10},{10... | collective-permute-start | bytes 614408 | tf_op jit(solution)/shard_map/ppermute | solution.py:919
  476.4 24.4 %collective-permute-start.54 = (f32[80,640]{1,0:T(8,128)}, f32[80,640]{1,0:T(8,128)}, u32[]{:S(2)}, u32[]{:S(2)}) collective-permute-start(f32[80,640]{1,0:T(8,128)} %get-tuple-element.830), channel_id=1, source_target_pairs={{0,24},{8,0},{16,8},{24,16},{1,25},{9,1},{17,9},{25,17},{2,26},{10... | collective-permute-start | bytes 614408 | tf_op jit(solution)/shard_map/ppermute | solution.py:919
  560.6 25.0 %collective-permute-start.69 = (f32[4,4,80,640]{3,2,1,0:T(8,128)}, f32[4,4,80,640]{3,2,1,0:T(8,128)}, u32[]{:S(2)}, u32[]{:S(2)}) collective-permute-start(f32[4,4,80,640]{3,2,1,0:T(8,128)} %get-tuple-element.514), channel_id=1, source_target_pairs={{1,0},{0,1},{3,2},{2,3},{5,4},{4,5},{7,6},{6,7},{9,8},{8,9},{11,10... | collective-permute-start | bytes 9830408 | tf_op jit(solution)/shard_map/ppermute | solution.py:895
  570.9 27.4 %collective-permute-start.75 = (f32[4,4,80,640]{3,2,1,0:T(8,128)}, f32[4,4,80,640]{3,2,1,0:T(8,128)}, u32[]{:S(2)}, u32[]{:S(2)}) collective-permute-start(f32[4,4,80,640]{3,2,1,0:T(8,128)} %get-tuple-element.525), channel_id=1, source_target_pairs={{1,0},{0,1},{3,2},{2,3},{5,4},{4,5},{7,6},{6,7},{9,8},{8,9},{11,10... | collective-permute-start | bytes 9830408 | tf_op jit(solution)/shard_map/ppermute | solution.py:895
  622.2 86.2 %all-gather.15.cloned.1.call-start = ((), (), s32[]{:S(2)}) async-start(), calls=%async_computation.3 | async-start | bytes 3133440 | tf_op jit(solution)/shard_map/all_gather | solution.py:1041
  640.1 26.4 %collective-permute-start.80 = (bf16[80,640]{1,0:T(8,128)(2,1)S(1)}, bf16[80,640]{1,0:T(8,128)(2,1)S(1)}, u32[]{:S(2)}, u32[]{:S(2)}) collective-permute-start(bf16[80,640]{1,0:T(8,128)(2,1)S(1)} %get-tuple-element.820), channel_id=1, source_target_pairs={{0,8},{8,16},{16,24},{24,0},{1,9},{9,17},{17,25},{25,1},{2,10},{10... | collective-permute-start | bytes 307208 | tf_op jit(solution)/shard_map/ppermute | solution.py:919
  640.2 27.5 %collective-permute-start.82 = (bf16[80,640]{1,0:T(8,128)(2,1)S(1)}, bf16[80,640]{1,0:T(8,128)(2,1)S(1)}, u32[]{:S(2)}, u32[]{:S(2)}) collective-permute-start(bf16[80,640]{1,0:T(8,128)(2,1)S(1)} %get-tuple-element.821), channel_id=1, source_target_pairs={{0,24},{8,0},{16,8},{24,16},{1,25},{9,1},{17,9},{25,17},{2,26},{10... | collective-permute-start | bytes 307208 | tf_op jit(solution)/shard_map/ppermute | solution.py:919
  (421 other events, 3323.0 us)
Sparse Core Ops, SparseCore 0:
  19.8 117.7 all-gather.8
  141.0 71.0 all-gather.10
  622.3 35.3 all-gather.12
  678.7 29.7 all-gather.14
